TPU v7x, 128 devices: a whole 4x4x4 slice. The times are simulated.
128 devices in a mesh: section: 8 (over x, z_hi), ctx: 16 (over z_lo, y, core).
Axes of the slice: x: 4, y: 4, z: 4 (z_hi: 2, z_lo: 2; z = z_hi * 2 + z_lo), core: 2. Of those that a mesh axis runs over, the one named last changes fastest.
Arguments:
- acts: bfloat16 [8, 2048, 12288], P('section', 'ctx'), may hold values from -6 to 6
- cots: bfloat16 [8, 2048, 4096], P('section', 'ctx'), may hold values from -1.1953125 to 1.1953125
- kern: float32 [8, 7, 12288], P('section'), may hold values from -2 to 2
- filt: bfloat16 [8, 4096, 2048], P('section', 'ctx'), may hold values from -9 to 9
- skip: float32 [8, 4096], P('section'), may hold values from 0.5 to 1.5
Outputs:
- output: bfloat16 [8, 2048, 4096], P('section', 'ctx')
- input_grad: bfloat16 [8, 2048, 12288], P('section', 'ctx')
- kern_grad: float32 [8, 7, 12288], P('section')
- filt_grad: float32 [8, 4096, 2048], P('section', 'ctx')
- skip_grad: float32 [8, 4096], P('section', 'ctx')
All inputs are finite; a program needn't handle non-finite values.
Results may differ from a plain program's by a relative error of at most 0.023.
Values may be sent and summed in bfloat16 or wider, within the bound.
No kernel may reach another device: no remote copies, remote signals or barrier semaphores. Data moves between devices by JAX's collectives and lax.ppermute only.
A program may use at most 192 MiB of HBM per device.

v0:
```python
import math

import jax
import jax.numpy as jnp
from jax import lax
from jax.sharding import PartitionSpec as P


def passed_along(value, axis, steps):
    count = lax.axis_size(axis)
    pairs = [(source, (source + steps) % count) for source in range(count)]
    return lax.ppermute(value, axis, pairs)


def from_behind(block, axis, distance):
    devices = range(lax.axis_size(axis))
    route = [(i - distance, i) for i in devices if i - distance in devices]
    return lax.ppermute(block, axis, route)


def factor_length(total):
    best = 2
    for divisor in range(2, math.isqrt(total) + 1):
        if total % divisor == 0 and divisor % 2 == 0:
            best = divisor
    return (best, total // best)


def phases(rows, cols, total):
    left = jnp.arange(rows, dtype=jnp.int32)[:, None]
    right = jnp.arange(cols, dtype=jnp.int32)[None, :]
    return (left * right % total).astype(jnp.float32) * (2.0 * math.pi / total)


def block_table(cos_t, sin_t, sign):
    top = jnp.stack([cos_t, sign * sin_t], axis=1)
    bottom = jnp.stack([-sign * sin_t, cos_t], axis=1)
    return jnp.stack([top, bottom], axis=0)


def make_tables(first, second):
    total = first * second
    outer = phases(first, first // 2, first)
    twist = phases(first, second, total)
    inner = phases(second, second, second)
    outer_pair = jnp.stack([jnp.cos(outer), -jnp.sin(outer)], axis=0)
    inner_cos = jnp.cos(inner)
    inner_sin = jnp.sin(inner)
    return (
        outer_pair,
        jnp.cos(twist),
        jnp.sin(twist),
        block_table(inner_cos, inner_sin, 1.0),
        block_table(inner_cos, inner_sin, -1.0),
    )


def contract(form, table, values):
    return jnp.einsum(form, table, values, precision=lax.Precision.HIGH)


def contract_narrow(form, table, values):
    upper = table.astype(jnp.bfloat16)
    lower = (table - upper.astype(jnp.float32)).astype(jnp.bfloat16)
    return jnp.einsum(form, upper, values, preferred_element_type=jnp.float32) + jnp.einsum(
        form, lower, values, preferred_element_type=jnp.float32
    )


def forward_transform(signal, tables):
    outer_pair, twist_cos, twist_sin, inner_fwd, inner_inv = tables
    first, second = twist_cos.shape
    columns = signal.shape[1]
    blocked = signal.reshape(first // 2, second, columns)
    spread = contract_narrow("pkm,mjc->pkjc", outer_pair, blocked)
    a_real = spread[0]
    a_imag = spread[1]
    b_real = a_real * twist_cos[:, :, None] + a_imag * twist_sin[:, :, None]
    b_imag = a_imag * twist_cos[:, :, None] - a_real * twist_sin[:, :, None]
    stacked = jnp.stack([b_real, b_imag], axis=0)
    return contract("pqsj,skjc->pkqc", inner_fwd, stacked)


def cmul(left, right, conj_right):
    if conj_right:
        return jnp.stack(
            [left[0] * right[0] + left[1] * right[1], left[1] * right[0] - left[0] * right[1]],
            axis=0,
        )
    return jnp.stack(
        [left[0] * right[0] - left[1] * right[1], left[0] * right[1] + left[1] * right[0]], axis=0
    )


def inverse_transform(spectrum, tables):
    outer_pair, twist_cos, twist_sin, inner_fwd, inner_inv = tables
    first, second = twist_cos.shape
    columns = spectrum.shape[3]
    back = contract("pjsq,skqc->pkjc", inner_inv, spectrum)
    g_real = back[0] * twist_cos[:, :, None] - back[1] * twist_sin[:, :, None]
    g_imag = back[0] * twist_sin[:, :, None] + back[1] * twist_cos[:, :, None]
    result = contract("skm,skjc->mjc", outer_pair, jnp.stack([g_real, g_imag], axis=0))
    return result.reshape(first // 2 * second, columns) / (first * second)


def on_device(acts, cots, kern, filt, skip):
    source = passed_along(acts, "section", 1)[0]
    incoming = passed_along(cots, "section", -1)[0]
    taps = kern.shape[1]
    margin = taps - 1
    tokens_dev, feats = source.shape
    width = feats // 3
    groups = lax.axis_size("ctx")
    chans = width // groups
    seq_len = tokens_dev * groups
    before = from_behind(source[tokens_dev - margin :], "ctx", 1)
    padded = jnp.concatenate([before, source], axis=0).astype(jnp.float32)
    weights = kern[0]
    feature = sum(
        (
            weights[offset][None, :] * padded[margin - offset : margin - offset + tokens_dev]
            for offset in range(taps)
        )
    )
    query = feature[:, :width]
    keyed = feature[:, width : 2 * width]
    value = feature[:, 2 * width :]
    gated = (keyed * value).astype(jnp.bfloat16)
    gain_all = skip[0]
    gain_part = lax.dynamic_slice_in_dim(gain_all, lax.axis_index("ctx") * chans, chans)
    first, second = factor_length(2 * seq_len)
    tables = make_tables(first, second)
    filt_spec = forward_transform(filt[0].T, tables)
    grad_in = incoming.astype(jnp.float32)
    grad_mix = (grad_in * query).astype(jnp.bfloat16)
    gated_part = lax.all_to_all(gated, "ctx", split_axis=1, concat_axis=0, tiled=True)
    gated_f = gated_part.astype(jnp.float32)
    gated_spec = forward_transform(gated_part, tables)
    mixed = inverse_transform(cmul(gated_spec, filt_spec, False), tables)
    mixed_part = mixed.astype(jnp.bfloat16)
    mixed_seq = lax.all_to_all(mixed_part, "ctx", split_axis=0, concat_axis=1, tiled=True)
    grad_part = lax.all_to_all(grad_mix, "ctx", split_axis=1, concat_axis=0, tiled=True)
    gated_f, gated_spec = (gated_f, gated_spec)
    grad_f = grad_part.astype(jnp.float32)
    grad_spec = forward_transform(grad_part, tables)
    back = inverse_transform(cmul(grad_spec, filt_spec, True), tables)
    filt_grad = inverse_transform(cmul(grad_spec, gated_spec, True), tables)
    through = (back + gain_part[None, :] * grad_f).astype(jnp.bfloat16)
    skip_grad = jnp.sum(grad_f * gated_f, axis=0)
    through_part, filt_grad, skip_grad = (through, filt_grad, skip_grad)
    through_seq = lax.all_to_all(through_part, "ctx", split_axis=0, concat_axis=1, tiled=True)
    inner = mixed_seq.astype(jnp.float32) + gain_all[None, :] * gated.astype(jnp.float32)
    output = (query * inner).astype(jnp.bfloat16)
    through_f = through_seq.astype(jnp.float32)
    feat_grad = jnp.concatenate([grad_in * inner, through_f * value, through_f * keyed], axis=1)
    after = from_behind(feat_grad[:margin].astype(jnp.bfloat16), "ctx", -1).astype(jnp.float32)
    extended = jnp.concatenate([feat_grad, after], axis=0)
    input_grad = sum(
        (
            weights[offset][None, :] * extended[offset : offset + tokens_dev]
            for offset in range(taps)
        )
    ).astype(jnp.bfloat16)
    partial_kern = jnp.sum(
        jnp.stack(
            [
                feat_grad * padded[margin - offset : margin - offset + tokens_dev]
                for offset in range(taps)
            ],
            axis=0,
        ),
        axis=1,
    )
    kern_grad = lax.psum(partial_kern.astype(jnp.bfloat16), "ctx").astype(jnp.float32)
    return (output[None], input_grad[None], kern_grad[None], filt_grad.T[None], skip_grad[None])


def solution(mesh):
    return jax.shard_map(
        on_device,
        mesh=mesh,
        in_specs=(
            P("section", "ctx", None),
            P("section", "ctx", None),
            P("section", None, None),
            P("section", "ctx", None),
            P("section", None),
        ),
        out_specs=(
            P("section", "ctx", None),
            P("section", "ctx", None),
            P("section", None, None),
            P("section", "ctx", None),
            P("section", "ctx"),
        ),
        check_vma=False,
    )
```

profile of v0, /device:TPU:1, one launch (start us, length us, event | category | flops | bytes accessed | tf_op | source)
XLA Modules:
  0.0 614.2 jit_solution(2262165847482371102)
XLA Ops:
  9.5 6.6 %collective-permute-start.2 = (bf16[1,128,4096]{1,2,0:T(8,128)(2,1)}, bf16[1,128,4096]{1,2,0:T(8,128)(2,1)S(1)}, u32[]{:S(2)}, u32[]{:S(2)}) collective-permute-start(bf16[1,128,4096]{1,2,0:T(8,128)(2,1)} %copy.84), channel_id=1, source_target_pairs={{0,112},{16,0},{32,16},{48,32},{64,48},{80,64},{96,80},{112,96},{1... | collective-permute-start | bytes 3145736 | tf_op jit(solution)/shard_map/ppermute | solution.py:12
  16.1 4.6 copy.69
  23.2 82.2 %collective-permute-done = bf16[1,128,12288]{1,2,0:T(8,128)(2,1)} collective-permute-done((bf16[1,128,12288]{1,2,0:T(8,128)(2,1)}, bf16[1,128,12288]{1,2,0:T(8,128)(2,1)}, u32[]{:S(2)}, u32[]{:S(2)}) %collective-permute-start) | collective-permute-done | bytes 3145760 | tf_op jit(solution)/shard_map/ppermute | solution.py:12
  105.4 3.6 slice_bitcast_fusion
  109.0 3.9 copy.70
  112.9 3.6 collective-permute-start.1
  119.3 3.6 copy.71
  123.0 4.7 maximum_convert_fusion
  127.8 24.5 %multiply_add_fusion = f32[128,12288]{0,1:T(8,128)} fusion(f32[134,12288]{0,1:T(8,128)S(1)} %maximum_convert_fusion, f32[12288]{0:T(1024)S(1)} %bitcast.243, f32[12288]{0:T(1024)S(1)} %bitcast.245, f32[12288]{0:T(1024)S(1)} %bitcast.235, f32[12288]{0:T(1024)S(1)} %bitcast.237, f32[12288]{0:T(1024)S(1)} %bitcast.239, f32[12288]{0:T(1024)S(1)} %bitcast.241, ...), kind=kLoop, calls=%fused_computation.60 | loop fusion | flops 20447232 | bytes 50675712 | tf_op jit(solution)/shard_map/add | solution.py:119
  155.5 6.2 %all-to-all-start.2 = ((bf16[128,16,256]{0,2,1:T(8,128)(2,1)}), bf16[128,16,256]{0,2,1:T(8,128)(2,1)S(1)}, u32[]{:S(2)}, u32[]{:S(2)}) async-start(bf16[128,16,256]{0,2,1:T(8,128)(2,1)} %bitcast.232), calls=%async_computation.2 | async-start | bytes 2097152 | tf_op jit(solution)/shard_map/all_to_all | solution.py:142
  163.0 4.6 convolution_add_fusion.1
  167.6 10.0 %all-to-all-done.2 = bf16[128,16,256]{0,2,1:T(8,128)(2,1)S(1)} async-done(((bf16[128,16,256]{0,2,1:T(8,128)(2,1)}), bf16[128,16,256]{0,2,1:T(8,128)(2,1)S(1)}, u32[]{:S(2)}, u32[]{:S(2)}) %all-to-all-start.2) | async-done | bytes 1048608 | tf_op jit(solution)/shard_map/all_to_all | solution.py:142
  181.8 7.3 %multiply_add_fusion.5 = (f32[1,64,64,256]{3,1,2,0:T(8,128)}, f32[1,64,64,256]{3,1,2,0:T(8,128)}, f32[1,64,64,256]{3,1,2,0:T(8,128)}, f32[1,64,64,256]{3,1,2,0:T(8,128)}) fusion(f32[2,64,64,256]{3,1,2,0:T(8,128)S(1)} %convolution_add_fusion, f32[64,64]{0,1:T(8,128)S(1)} %get-tuple-element.64, f32[64,64]{0,1:T(8,128)S(1)} %get-tuple-element.65, ...), kind=kLoop, calls=%fused_computation.70 | loop fusion | flops 12582912 | bytes 33587200 | tf_op jit(solution)/shard_map/add | solution.py:78
  189.1 4.1 maximum_bitcast_fusion.4
  193.2 4.1 maximum_bitcast_fusion.1
  197.3 8.5 %fusion.40 = f32[2,64,64,256]{3,2,0,1:T(8,128)S(1)} fusion(f32[2,64,64,256,1]{3,1,2,0,4:T(8,128)S(1)} %maximum_bitcast_fusion.4, f32[1,64,2,64]{3,1,2,0:T(8,128)S(1)} %get-tuple-element.57, f32[1,64,2,64]{3,1,2,0:T(8,128)S(1)} %get-tuple-element.60), kind=kOutput, calls=%fused_computation.84 | convolution fusion | flops 1610629120 | bytes 16842752 | tf_op jit(solution)/shard_map/pqsj,skjc->pkqc/dot_general | solution.py:59
  205.8 8.7 %fusion.37 = f32[2,64,64,256]{3,2,0,1:T(8,128)S(1)} fusion(f32[2,64,64,256,1]{3,1,2,0,4:T(8,128)S(1)} %maximum_bitcast_fusion.1, f32[1,64,2,64]{3,1,2,0:T(8,128)S(1)} %get-tuple-element.57, f32[1,64,2,64]{3,1,2,0:T(8,128)S(1)} %get-tuple-element.60), kind=kOutput, calls=%fused_computation.83 | convolution fusion | flops 1610629120 | bytes 16842752 | tf_op jit(solution)/shard_map/pqsj,skjc->pkqc/dot_general | solution.py:59
  214.5 4.7 multiply_add_fusion.4
  220.3 6.5 %fusion.44 = f32[64,256,2,64]{1,3,2,0:T(8,128)S(1)} fusion(f32[1,64,64,256]{3,2,0,1:T(8,128)} %get-tuple-element.23, f32[1,64,64,256]{3,2,0,1:T(8,128)} %get-tuple-element.22, f32[1,64,2,64]{3,1,2,0:T(8,128)S(1)} %get-tuple-element.61, f32[1,64,2,64]{3,1,2,0:T(8,128)S(1)} %get-tuple-element.56), kind=kOutput, calls=%fused_computation.86 | convolution fusion | flops 1612726272 | bytes 16842752 | tf_op jit(solution)/shard_map/pjsq,skqc->pkjc/dot_general | solution.py:59
  226.8 4.9 copy.164
  241.0 18.8 %all_to_all.52 = bf16[16,128,256]{1,2,0:T(8,128)(2,1)S(1)} all-to-all(bf16[16,128,256]{1,2,0:T(8,128)(2,1)S(1)} %fusion.48), channel_id=1, replica_groups=mesh['section'=8,'ctx'=16] {'ctx'}, dimensions={0} | all-to-all | bytes 2097152 | tf_op jit(solution)/shard_map/all_to_all | solution.py:151
  259.8 4.0 bitcast_multiply_fusion.4
  264.7 20.2 %all_to_all.53 = bf16[128,16,256]{0,2,1:T(8,128)(2,1)} all-to-all(bf16[128,16,256]{0,2,1:T(8,128)(2,1)S(1)} %bitcast.220), channel_id=1, replica_groups=mesh['section'=8,'ctx'=16] {'ctx'}, dimensions={1} | all-to-all | bytes 2097152 | tf_op jit(solution)/shard_map/all_to_all | solution.py:136
  292.5 4.2 maximum_bitcast_fusion
  296.7 14.0 %fusion.34 = f32[2,64,64,256]{3,2,0,1:T(8,128)} fusion(f32[2,64,64,256,1]{3,1,2,0,4:T(8,128)} %maximum_bitcast_fusion, f32[1,64,2,64]{3,1,2,0:T(8,128)S(1)} %get-tuple-element.57, f32[1,64,2,64]{3,1,2,0:T(8,128)S(1)} %get-tuple-element.60), kind=kOutput, calls=%fused_computation.82 | convolution fusion | flops 1610629120 | bytes 16842752 | tf_op jit(solution)/shard_map/pqsj,skjc->pkqc/dot_general | solution.py:59
  310.7 11.9 %multiply_add_fusion.2 = (f32[1,64,64,256]{3,2,0,1:T(8,128)}, f32[1,64,64,256]{3,2,0,1:T(8,128)}, f32[1,64,64,256]{3,2,0,1:T(8,128)}, f32[1,64,64,256]{3,2,0,1:T(8,128)}) fusion(f32[2,64,64,256]{3,2,0,1:T(8,128)S(1)} %bitcast.212, f32[2,64,64,256]{3,2,0,1:T(8,128)} %fusion.34, f32[2,64,64,256]{3,2,0,1:T(8,128)} %copy-done.8), kind=kLoop, calls=%fused_computation.64 | loop fusion | flops 12582912 | bytes 41943040 | tf_op jit(solution)/shard_map/add | solution.py:87
  322.5 6.4 %fusion.45 = f32[64,256,2,64]{1,3,2,0:T(8,128)S(1)} fusion(f32[1,64,64,256]{3,2,0,1:T(8,128)} %get-tuple-element.38, f32[1,64,64,256]{3,2,0,1:T(8,128)} %get-tuple-element.39, f32[1,64,2,64]{3,1,2,0:T(8,128)S(1)} %get-tuple-element.61, f32[1,64,2,64]{3,1,2,0:T(8,128)S(1)} %get-tuple-element.56), kind=kOutput, calls=%fused_computation.87 | convolution fusion | flops 1612726272 | bytes 16842752 | tf_op jit(solution)/shard_map/pjsq,skqc->pkjc/dot_general | solution.py:59
  329.0 4.9 copy.165
  333.8 6.5 %fusion.43 = f32[64,256,2,64]{1,3,2,0:T(8,128)S(1)} fusion(f32[1,64,64,256]{3,2,0,1:T(8,128)} %get-tuple-element.21, f32[1,64,64,256]{3,2,0,1:T(8,128)} %get-tuple-element.20, f32[1,64,2,64]{3,1,2,0:T(8,128)S(1)} %get-tuple-element.61, f32[1,64,2,64]{3,1,2,0:T(8,128)S(1)} %get-tuple-element.56), kind=kOutput, calls=%fused_computation.85 | convolution fusion | flops 1612726272 | bytes 16842752 | tf_op jit(solution)/shard_map/pjsq,skqc->pkjc/dot_general | solution.py:59
  340.3 8.2 %copy.163 = f32[64,256,2,64]{1,0,3,2:T(8,128)} copy(f32[64,256,2,64]{1,3,2,0:T(8,128)S(1)} %fusion.43) | data formatting | bytes 16777216 | tf_op jit(solution)/shard_map/pjsq,skqc->pkjc/dot_general | solution.py:59
  348.5 7.9 %multiply_subtract_fusion = (f32[1,64,64,256]{3,1,2,0:T(8,128)}, f32[1,64,64,256]{3,1,2,0:T(8,128)}, f32[1,64,64,256]{3,1,2,0:T(8,128)S(1)}, f32[1,64,64,256]{3,1,2,0:T(8,128)}) fusion(f32[2,64,64,256]{3,1,2,0:T(8,128)} %bitcast.217, f32[64,64]{0,1:T(8,128)S(1)} %get-tuple-element.64, f32[64,64]{0,1:T(8,128)S(1)} %get-tuple-element.65, ...), kind=kLoop, calls=%fused_computation.62 | loop fusion | flops 12582912 | bytes 33587200 | tf_op jit(solution)/shard_map/sub | solution.py:100
  356.3 5.1 fusion.51
  363.0 5.1 all-to-all-start.1
  368.2 5.3 bitcast_multiply_fusion
  389.9 3.8 convert_multiply_fusion.1
  393.7 6.7 %pad_maximum_fusion.1 = bf16[128,12288]{0,1:T(8,128)(2,1)} fusion(f32[128,4096]{0,1:T(8,128)S(1)} %copy-done.1, f32[128,4096]{0,1:T(8,128)S(1)} %get-tuple-element.40, f32[128,4096]{0,1:T(8,128)S(1)} %get-tuple-element.43), kind=kLoop, calls=%fused_computation.52 | loop fusion | flops 9437184 | bytes 9437184 | tf_op jit(solution)/shard_map/concatenate | solution.py:155
  400.4 10.1 %bitcast_dynamic-update-slice_fusion.6 = f32[7,128,12288]{1,2,0:T(8,128)} fusion(f32[134,12288]{0,1:T(8,128)} %copy-done, f32[128,4096]{0,1:T(8,128)S(1)} %copy-done.1, f32[128,4096]{0,1:T(8,128)S(1)} %get-tuple-element.40, f32[128,4096]{0,1:T(8,128)S(1)} %get-tuple-element.43), kind=kLoop, calls=%fused_computation.59 | loop fusion | flops 4718591 | bytes 18874368
  416.7 10.0 %bitcast_dynamic-update-slice_fusion.5 = f32[7,128,12288]{1,2,0:T(8,128)} fusion(f32[7,128,12288]{1,2,0:T(8,128)} %bitcast_dynamic-update-slice_fusion.6, f32[134,12288]{0,1:T(8,128)} %copy-done, f32[128,4096]{0,1:T(8,128)} %get-tuple-element.41, f32[128,4096]{0,1:T(8,128)S(1)} %get-tuple-element.40, f32[128,4096]{0,1:T(8,128)} %copy-done.4), kind=kLoop, calls=%fused_computation.58 | loop fusion | flops 4718592 | bytes 18874368
  426.6 10.3 %bitcast_dynamic-update-slice_fusion.4 = f32[7,128,12288]{1,2,0:T(8,128)} fusion(f32[7,128,12288]{1,2,0:T(8,128)} %bitcast_dynamic-update-slice_fusion.5, f32[134,12288]{0,1:T(8,128)} %copy-done, f32[128,4096]{0,1:T(8,128)S(1)} %copy-done.2, f32[128,4096]{0,1:T(8,128)S(1)} %get-tuple-element.40, f32[128,4096]{0,1:T(8,128)S(1)} %copy-done.5), kind=kLoop, calls=%fused_computation.57 | loop fusion | flops 4718592 | bytes 18874368
  437.0 7.4 %bitcast_dynamic-update-slice_fusion.3 = f32[7,128,12288]{1,2,0:T(8,128)} fusion(f32[7,128,12288]{1,2,0:T(8,128)} %bitcast_dynamic-update-slice_fusion.4, f32[134,12288]{0,1:T(8,128)S(1)} %bitcast.210, f32[128,4096]{0,1:T(8,128)S(1)} %copy-done.2, f32[128,4096]{0,1:T(8,128)S(1)} %get-tuple-element.40, f32[128,4096]{0,1:T(8,128)S(1)} %copy-done.5), kind=kLoop, calls=%fused_computation.56 | loop fusion | flops 4718592 | bytes 18874368
  444.3 7.3 %bitcast_dynamic-update-slice_fusion.2 = f32[7,128,12288]{1,2,0:T(8,128)} fusion(f32[7,128,12288]{1,2,0:T(8,128)} %bitcast_dynamic-update-slice_fusion.3, f32[134,12288]{0,1:T(8,128)S(1)} %bitcast.210, f32[128,4096]{0,1:T(8,128)S(1)} %copy-done.2, f32[128,4096]{0,1:T(8,128)S(1)} %get-tuple-element.40, f32[128,4096]{0,1:T(8,128)S(1)} %copy-done.5), kind=kLoop, calls=%fused_computation.55 | loop fusion | flops 4718592 | bytes 18874368
  451.6 7.6 %bitcast_dynamic-update-slice_fusion.1 = f32[7,128,12288]{1,2,0:T(8,128)} fusion(f32[7,128,12288]{1,2,0:T(8,128)} %bitcast_dynamic-update-slice_fusion.2, f32[134,12288]{0,1:T(8,128)S(1)} %bitcast.210, f32[128,4096]{0,1:T(8,128)S(1)} %copy-done.2, f32[128,4096]{0,1:T(8,128)S(1)} %get-tuple-element.40, f32[128,4096]{0,1:T(8,128)S(1)} %copy-done.5), kind=kLoop, calls=%fused_computation.54 | loop fusion | flops 4718592 | bytes 18874368
  459.2 7.2 %bitcast_dynamic-update-slice_fusion = f32[7,128,12288]{1,2,0:T(8,128)} fusion(f32[7,128,12288]{1,2,0:T(8,128)} %bitcast_dynamic-update-slice_fusion.1, f32[134,12288]{0,1:T(8,128)S(1)} %bitcast.210, f32[128,4096]{0,1:T(8,128)S(1)} %copy-done.2, f32[128,4096]{0,1:T(8,128)S(1)} %get-tuple-element.40, f32[128,4096]{0,1:T(8,128)S(1)} %copy-done.5), kind=kLoop, calls=%fused_computation.53 | loop fusion | flops 4718592 | bytes 18874368 | tf_op jit(solution)/shard_map/stack | solution.py:165
  467.7 20.5 %reduce_sum.18 = bf16[7,12288]{1,0:T(8,128)(2,1)S(1)} reduce(f32[7,128,12288]{1,2,0:T(8,128)} %bitcast_dynamic-update-slice_fusion, f32[]{:T(128)} %constant.55.clone.1), dimensions={1}, to_apply=%region_0.1 | reduce | flops 10924032 | bytes 44212228 | tf_op jit(solution)/shard_map/reduce_sum | solution.py:164
  492.7 12.3 %pad_maximum_fusion = f32[134,12288]{0,1:T(8,128)} fusion(f32[6,12288]{0,1:T(8,128)} %copy.94, f32[128,4096]{0,1:T(8,128)} %get-tuple-element.41, f32[128,4096]{0,1:T(8,128)S(1)} %get-tuple-element.40, f32[128,4096]{0,1:T(8,128)} %copy-done.4), kind=kLoop, calls=%fused_computation | loop fusion | flops 4939776 | bytes 13172736 | tf_op jit(solution)/shard_map/concatenate | solution.py:157
  505.1 31.6 %fusion.46 = bf16[1,128,12288]{1,2,0:T(8,128)(2,1)} fusion(f32[134,12288]{0,1:T(8,128)} %pad_maximum_fusion, f32[12288]{0:T(1024)S(1)} %bitcast.244, f32[12288]{0:T(1024)S(1)} %bitcast.246, f32[12288]{0:T(1024)S(1)} %bitcast.236, f32[12288]{0:T(1024)S(1)} %bitcast.238, f32[12288]{0:T(1024)S(1)} %bitcast.240, f32[12288]{0:T(1024)S(1)} %bitcast.242, ...), kind=kLoop, calls=%fused_computation.89 | loop fusion | flops 25165824 | bytes 47529984 | tf_op jit(solution)/shard_map/broadcast_in_dim | solution.py:175
  536.6 4.6 copy.99
  541.3 63.8 %all-reduce.2.cloned.1.call-done = bf16[1,7,12288]{2,0,1:T(2,128)(2,1)} async-done(((bf16[1,7,12288]{2,0,1:T(2,128)(2,1)}), bf16[1,7,12288]{2,0,1:T(2,128)(2,1)}) %all-reduce.2.cloned.1.call-update) | async-done | bytes 172048 | tf_op jit(solution)/shard_map/psum | solution.py:174
  (123 shorter events, 67.3 us)
Async XLA Ops:
  7.2 15.3 %copy-start.29 = (f32[1,7,12288]{2,0,1:T(1,128)S(1)}, f32[1,7,12288]{2,0,1:T(1,128)}, u32[]{:S(2)}) copy-start(f32[1,7,12288]{2,0,1:T(1,128)} %param.7) | copy-start | bytes 1032196
  9.5 142.9 %collective-permute-start.2 = (bf16[1,128,4096]{1,2,0:T(8,128)(2,1)}, bf16[1,128,4096]{1,2,0:T(8,128)(2,1)S(1)}, u32[]{:S(2)}, u32[]{:S(2)}) collective-permute-start(bf16[1,128,4096]{1,2,0:T(8,128)(2,1)} %copy.84), channel_id=1, source_target_pairs={{0,112},{16,0},{32,16},{48,32},{64,48},{80,64},{96,80},{112,96},{1... | collective-permute-start | bytes 3145736 | tf_op jit(solution)/shard_map/ppermute | solution.py:12
  20.7 96.9 %copy-start.14 = (bf16[1,256,2048]{2,1,0:T(8,128)(2,1)S(1)}, bf16[1,256,2048]{2,1,0:T(8,128)(2,1)}, u32[]{:S(2)}) copy-start(bf16[1,256,2048]{2,1,0:T(8,128)(2,1)} %param.8) | copy-start | bytes 3145732
  20.7 84.7 %collective-permute-start = (bf16[1,128,12288]{1,2,0:T(8,128)(2,1)}, bf16[1,128,12288]{1,2,0:T(8,128)(2,1)}, u32[]{:S(2)}, u32[]{:S(2)}) collective-permute-start(bf16[1,128,12288]{1,2,0:T(8,128)(2,1)} %copy.69), channel_id=1, source_target_pairs={{0,16},{16,32},{32,48},{48,64},{64,80},{80,96},{96,112},{112,0},{1... | collective-permute-start | bytes 9437192 | tf_op jit(solution)/shard_map/ppermute | solution.py:12
  23.2 104.5 %copy-start.15 = (f32[1,1,12288]{2,0,1:T(1,128)}, f32[1,1,12288]{2,0,1:T(1,128)S(1)}, u32[]{:S(2)}) copy-start(f32[1,1,12288]{2,0,1:T(1,128)S(1)} %get-tuple-element.45) | copy-start | bytes 147460
  112.9 6.5 %collective-permute-start.1 = (bf16[6,12288]{1,0:T(8,128)(2,1)}, bf16[6,12288]{1,0:T(8,128)(2,1)}, u32[]{:S(2)}, u32[]{:S(2)}) collective-permute-start(bf16[6,12288]{1,0:T(8,128)(2,1)} %copy.70), channel_id=1, source_target_pairs={{0,1},{1,2},{2,3},{3,4},{4,5},{5,6},{6,7},{7,8},{8,9},{9,10},{10,1... | collective-permute-start | bytes 442376 | tf_op jit(solution)/shard_map/ppermute | solution.py:18
  123.0 4.8 copy-start.17
  123.0 4.8 copy-start.19
  123.0 4.8 copy-start.21
  123.0 4.8 copy-start.23
  123.0 4.8 copy-start.25
  123.0 4.8 copy-start.27
  127.7 24.6 %copy-start = (f32[134,12288]{0,1:T(8,128)}, f32[134,12288]{0,1:T(8,128)S(1)}, u32[]{:S(2)}) copy-start(f32[134,12288]{0,1:T(8,128)S(1)} %maximum_convert_fusion) | copy-start | bytes 19759108
  152.3 10.7 %copy-start.13 = (bf16[1,128,4096]{1,2,0:T(8,128)(2,1)}, bf16[1,128,4096]{1,2,0:T(8,128)(2,1)S(1)}, u32[]{:S(2)}) copy-start(bf16[1,128,4096]{1,2,0:T(8,128)(2,1)S(1)} %collective-permute-done.2) | copy-start | bytes 3145732
  155.5 22.1 %all-to-all-start.2 = ((bf16[128,16,256]{0,2,1:T(8,128)(2,1)}), bf16[128,16,256]{0,2,1:T(8,128)(2,1)S(1)}, u32[]{:S(2)}, u32[]{:S(2)}) async-start(bf16[128,16,256]{0,2,1:T(8,128)(2,1)} %bitcast.232), calls=%async_computation.2 | async-start | bytes 2097152 | tf_op jit(solution)/shard_map/all_to_all | solution.py:142
  178.1 2.6 slice-start.5
  179.4 2.4 slice-start.6
  205.8 8.7 %copy-start.7 = (f32[2,64,64,256]{3,2,0,1:T(8,128)}, f32[2,64,64,256]{3,2,0,1:T(8,128)S(1)}, u32[]{:S(2)}) copy-start(f32[2,64,64,256]{3,2,0,1:T(8,128)S(1)} %fusion.40) | copy-start | bytes 25165828
  214.5 5.8 copy-start.8
  236.1 4.5 copy-start.31
  263.7 1.0 copy-start.9
  287.1 2.6 copy-start.11
  292.5 18.2 %slice-start.3 = ((s8[8388608]{0:T(1024)(128)(4,1)}), s8[4194304]{0:T(1024)(128)(4,1)S(1)}, s32[]{:S(2)}) async-start(s8[8388608]{0:T(1024)(128)(4,1)} %bitcast.211), calls=%async_computation.8 | async-start | bytes 8388608
  296.7 14.0 %slice-start.4 = ((s8[8388608]{0:T(1024)(128)(4,1)}), s8[4194304]{0:T(1024)(128)(4,1)S(1)}, s32[]{:S(2)}) async-start(s8[8388608]{0:T(1024)(128)(4,1)} %bitcast.211), calls=%async_computation.9 | async-start | bytes 8388608
  363.0 21.2 %all-to-all-start.1 = ((bf16[16,128,256]{2,1,0:T(8,128)(2,1)}), bf16[16,128,256]{2,1,0:T(8,128)(2,1)}, u32[]{:S(2)}, u32[]{:S(2)}) async-start(bf16[16,128,256]{2,1,0:T(8,128)(2,1)} %bitcast.231), calls=%async_computation.1 | async-start | bytes 2097152 | tf_op jit(solution)/shard_map/all_to_all | solution.py:141
  368.2 236.8 %all-reduce.2.cloned.1.call-start = ((), (), s32[]{:S(2)}) async-start(), calls=%async_computation.4 | async-start | bytes 688128 | tf_op jit(solution)/shard_map/psum | solution.py:174
  376.1 13.9 %copy-start.30 = (f32[1,4096]{1,0:T(1,128)S(1)}, f32[1,4096]{1,0:T(1,128)}, u32[]{:S(2)}) copy-start(f32[1,4096]{1,0:T(1,128)} %param.9) | copy-start | bytes 49156
  381.1 8.8 %copy-start.10 = (bf16[128,4096]{0,1:T(8,128)(2,1)S(1)}, bf16[128,4096]{0,1:T(8,128)(2,1)}, u32[]{:S(2)}) copy-start(bf16[128,4096]{0,1:T(8,128)(2,1)} %copy-done.9) | copy-start | bytes 3145732
  389.9 3.8 copy-start.1
  393.7 16.8 %copy-start.4 = (f32[128,4096]{0,1:T(8,128)}, f32[128,4096]{0,1:T(8,128)S(1)}, u32[]{:S(2)}) copy-start(f32[128,4096]{0,1:T(8,128)S(1)} %get-tuple-element.43) | copy-start | bytes 6291460
  413.7 12.9 %copy-start.2 = (f32[128,4096]{0,1:T(8,128)S(1)}, f32[128,4096]{0,1:T(8,128)}, u32[]{:S(2)}) copy-start(f32[128,4096]{0,1:T(8,128)} %get-tuple-element.41) | copy-start | bytes 6291460
  413.8 12.9 %copy-start.5 = (f32[128,4096]{0,1:T(8,128)S(1)}, f32[128,4096]{0,1:T(8,128)}, u32[]{:S(2)}) copy-start(f32[128,4096]{0,1:T(8,128)} %copy-done.4) | copy-start | bytes 6291460
  413.8 75.4 %collective-permute-start.3 = (bf16[6,12288]{1,0:T(8,128)(2,1)S(1)}, bf16[6,12288]{1,0:T(8,128)(2,1)S(1)}, u32[]{:S(2)}, u32[]{:S(2)}) collective-permute-start(bf16[6,12288]{1,0:T(8,128)(2,1)S(1)} %copy.93), channel_id=1, source_target_pairs={{1,0},{2,1},{3,2},{4,3},{5,4},{6,5},{7,6},{8,7},{9,8},{10,9},{11,1... | collective-permute-start | bytes 442376 | tf_op jit(solution)/shard_map/ppermute | solution.py:18
  416.6 20.3 %slice-start = ((s8[12582912]{0:T(1024)(128)(4,1)}), s8[4194304]{0:T(1024)(128)(4,1)S(1)}, s32[]{:S(2)}) async-start(s8[12582912]{0:T(1024)(128)(4,1)} %bitcast.209), calls=%async_computation.5 | async-start | bytes 8388608
  416.7 20.3 %slice-start.1 = ((s8[12582912]{0:T(1024)(128)(4,1)}), s8[4194304]{0:T(1024)(128)(4,1)S(1)}, s32[]{:S(2)}) async-start(s8[12582912]{0:T(1024)(128)(4,1)} %bitcast.209), calls=%async_computation.6 | async-start | bytes 8388608
  426.6 10.3 %slice-start.2 = ((s8[12582912]{0:T(1024)(128)(4,1)}), s8[4194304]{0:T(1024)(128)(4,1)S(1)}, s32[]{:S(2)}) async-start(s8[12582912]{0:T(1024)(128)(4,1)} %bitcast.209), calls=%async_computation.7 | async-start | bytes 8388608
  459.2 7.2 %copy-start.12 = (bf16[128,4096]{0,1:T(8,128)(2,1)S(1)}, bf16[128,4096]{0,1:T(8,128)(2,1)}, u32[]{:S(2)}) copy-start(bf16[128,4096]{0,1:T(8,128)(2,1)} %get-tuple-element.44) | copy-start | bytes 3145732
  492.6 12.3 %copy-start.3 = (f32[128,4096]{0,1:T(8,128)S(1)}, f32[128,4096]{0,1:T(8,128)}, u32[]{:S(2)}) copy-start(f32[128,4096]{0,1:T(8,128)} %get-tuple-element.41) | copy-start | bytes 6291460
  492.6 12.3 %copy-start.6 = (f32[128,4096]{0,1:T(8,128)S(1)}, f32[128,4096]{0,1:T(8,128)}, u32[]{:S(2)}) copy-start(f32[128,4096]{0,1:T(8,128)} %copy-done.4) | copy-start | bytes 6291460
  492.7 12.3 %copy-start.16 = (f32[1,1,12288]{2,0,1:T(1,128)S(1)}, f32[1,1,12288]{2,0,1:T(1,128)}, u32[]{:S(2)}) copy-start(f32[1,1,12288]{2,0,1:T(1,128)} %copy-done.15) | copy-start | bytes 147460
  492.7 12.3 %copy-start.18 = (f32[1,1,12288]{2,0,1:T(1,128)S(1)}, f32[1,1,12288]{2,0,1:T(1,128)}, u32[]{:S(2)}) copy-start(f32[1,1,12288]{2,0,1:T(1,128)} %get-tuple-element.46) | copy-start | bytes 147460
  492.7 12.4 %copy-start.20 = (f32[1,1,12288]{2,0,1:T(1,128)S(1)}, f32[1,1,12288]{2,0,1:T(1,128)}, u32[]{:S(2)}) copy-start(f32[1,1,12288]{2,0,1:T(1,128)} %get-tuple-element.47) | copy-start | bytes 147460
  492.7 12.4 %copy-start.22 = (f32[1,1,12288]{2,0,1:T(1,128)S(1)}, f32[1,1,12288]{2,0,1:T(1,128)}, u32[]{:S(2)}) copy-start(f32[1,1,12288]{2,0,1:T(1,128)} %get-tuple-element.48) | copy-start | bytes 147460
  492.7 12.4 %copy-start.24 = (f32[1,1,12288]{2,0,1:T(1,128)S(1)}, f32[1,1,12288]{2,0,1:T(1,128)}, u32[]{:S(2)}) copy-start(f32[1,1,12288]{2,0,1:T(1,128)} %get-tuple-element.49) | copy-start | bytes 147460
  492.7 12.4 %copy-start.26 = (f32[1,1,12288]{2,0,1:T(1,128)S(1)}, f32[1,1,12288]{2,0,1:T(1,128)}, u32[]{:S(2)}) copy-start(f32[1,1,12288]{2,0,1:T(1,128)} %get-tuple-element.50) | copy-start | bytes 147460
  492.7 12.4 %copy-start.28 = (f32[1,1,12288]{2,0,1:T(1,128)S(1)}, f32[1,1,12288]{2,0,1:T(1,128)}, u32[]{:S(2)}) copy-start(f32[1,1,12288]{2,0,1:T(1,128)} %get-tuple-element.51) | copy-start | bytes 147460
Sparse Core Ops, SparseCore 0:
  489.2 115.7 all-reduce.1
where the time goes:
time: 625 us; the launch traced here: 614 us
  other arithmetic  228 us (36%)
  waiting for transfers between devices  159 us (25%)
  matrix products  76.2 us (12%)
  local copies, waits for them, and re-layouts  72.4 us (12%)
  blocking collectives  38.9 us (6%)
  starting transfers between devices  24.5 us (4%)
  between operations  14.9 us (2%)
    ppermute x2, waiting for transfers between devices, passed_along(): return lax.ppermute(value, axis, pairs)  82.2 us
    dot_general x9, matrix products, contract(): return jnp.einsum(form, table, values, precision=lax.Precision.HIGH)  63.9 us
    psum x1, waiting for transfers between devices, on_device(): lax.psum(partial_kern.astype(jnp.bfloat16), 'ctx').astype(jnp.float32)  63.8 us
    unnamed x9, other arithmetic  52.6 us
    broadcast_in_dim x1, other arithmetic, on_device(): input_grad[None]  31.6 us
    add x1, other arithmetic, on_device(): sum((weights[offset][None, :] * padded[margin - offset:margin - offset +...  24.5 us
    reduce_sum x1, other arithmetic, on_device(): jnp.sum(jnp.stack([feat_grad * padded[margin - offset:margin - offset + t...  20.5 us
    all_to_all x1, blocking collectives, on_device(): lax.all_to_all(gated, 'ctx', split_axis=1, concat_axis=0, tiled=True)  20.2 us
  transfers between devices with their start and end apart: 7, of which 5 were waited for; matrix products, arithmetic and copies ran while one was open for 31% of the time, Pallas kernels for 0%

commit v1 on v0

v1 whole, which is shorter than its diff:
```python
import math

import jax
import jax.numpy as jnp
import ml_dtypes
import numpy as np
from jax import lax
from jax.experimental import pallas as pl
from jax.experimental.pallas import tpu as pltpu
from jax.sharding import PartitionSpec as P

TAPS = 7
HALO = 8
ROOT = math.sqrt(0.5)
F32 = jnp.float32
BF16 = jnp.bfloat16
MIB = 1 << 20


def passed_along(value, axis, steps):
    count = lax.axis_size(axis)
    pairs = [(source, (source + steps) % count) for source in range(count)]
    return lax.ppermute(value, axis, pairs)


def from_behind(block, axis, distance):
    devices = range(lax.axis_size(axis))
    route = [(i - distance, i) for i in devices if i - distance in devices]
    return lax.ppermute(block, axis, route)


def leaf_angles():
    angles = [math.pi / 2]
    for _ in range(3):
        angles = [half for angle in angles for half in (angle / 2, angle / 2 + math.pi)]
    return angles


def leaf_tables(length):
    leaf = length // 8
    order = np.arange(leaf)
    tables = []
    for angle in leaf_angles():
        phase = (angle + 2.0 * np.pi * order[:, None]) / leaf * order[None, :]
        real, imag = np.cos(phase), np.sin(phase)
        tables.append(np.block([[real, -imag], [imag, real]]))
    table = np.stack(tables)
    back = table.transpose(0, 2, 1) / length
    return table.astype(ml_dtypes.bfloat16), back.astype(ml_dtypes.bfloat16)


def turned(pair, angle):
    real, imag = pair
    cos, sin = math.cos(angle), math.sin(angle)
    return real * cos - imag * sin, real * sin + imag * cos


def split_rings(parts):
    low, high = [], []
    for lower, upper in zip(parts[:4], parts[4:]):
        scaled = upper * ROOT
        low.append((lower + scaled, scaled))
        high.append((lower - scaled, -scaled))
    rings = [(math.pi / 4, low), (math.pi / 4 + math.pi, high)]
    while len(rings[0][1]) > 1:
        finer = []
        for angle, pieces in rings:
            half = len(pieces) // 2
            plus, minus = [], []
            for lower, upper in zip(pieces[:half], pieces[half:]):
                real, imag = turned(upper, angle / 2)
                plus.append((lower[0] + real, lower[1] + imag))
                minus.append((lower[0] - real, lower[1] - imag))
            finer += [(angle / 2, plus), (angle / 2 + math.pi, minus)]
        rings = finer
    return [pieces[0] for _, pieces in rings]


def join_rings(leaves):
    angles = [math.pi / 4, math.pi / 4 + math.pi]
    angles = [half for angle in angles for half in (angle / 2, angle / 2 + math.pi)]
    groups = [[leaf] for leaf in leaves]
    while len(groups) > 2:
        merged = []
        for index in range(0, len(groups), 2):
            angle = angles[index // 2] if len(groups) == 8 else [math.pi / 4, math.pi / 4 + math.pi][index // 2]
            lower, upper = [], []
            for plus, minus in zip(groups[index], groups[index + 1]):
                lower.append((plus[0] + minus[0], plus[1] + minus[1]))
                upper.append(turned((plus[0] - minus[0], plus[1] - minus[1]), -angle / 2))
            merged.append(lower + upper)
        groups = merged
    lower, upper = [], []
    for plus, minus in zip(groups[0], groups[1]):
        lower.append(plus[0] + minus[0])
        upper.append(((plus[0] - minus[0]) + (plus[1] - minus[1])) * ROOT)
    return lower + upper


def filter_kernel(filt_ref, table_ref, spec_ref, rings):
    chans, length = filt_ref.shape
    leaf = length // 8
    step = pl.program_id(0)

    @pl.when(step == 0)
    def _():
        @pl.loop(0, chans // 16)
        def _(strip):
            rows = pl.ds(pl.multiple_of(strip * 16, 16), 16)
            for lane in range(0, leaf, 128):
                parts = [
                    filt_ref[rows, piece * leaf + lane : piece * leaf + lane + 128].astype(F32)
                    for piece in range(8)
                ]
                for index, (real, imag) in enumerate(split_rings(parts)):
                    rings[index, rows, lane : lane + 128] = real.astype(BF16)
                    rings[index, rows, leaf + lane : leaf + lane + 128] = imag.astype(BF16)

    spec_ref[0] = lax.dot_general(
        table_ref[0], rings[step], (((1,), (1,)), ((), ())), preferred_element_type=F32
    )


def filter_spectrum(filt, table):
    chans, length = filt.shape
    wide = length // 4
    return pl.pallas_call(
        filter_kernel,
        out_shape=jax.ShapeDtypeStruct((8, wide, chans), F32),
        grid=(8,),
        in_specs=[
            pl.BlockSpec((chans, length), lambda j: (0, 0)),
            pl.BlockSpec((1, wide, wide), lambda j: (j, 0, 0)),
        ],
        out_specs=pl.BlockSpec((1, wide, chans), lambda j: (j, 0, 0)),
        scratch_shapes=[pltpu.VMEM((8, chans, wide), BF16)],
        compiler_params=pltpu.CompilerParams(vmem_limit_bytes=24 * MIB),
        cost_estimate=pl.CostEstimate(
            flops=16 * wide * wide * chans, bytes_accessed=10 * MIB, transcendentals=0
        ),
        name="filter_spectrum",
    )(filt, table)


def tap_rows(kern_ref, lanes):
    return [kern_ref[tap : tap + 1, lanes] for tap in range(TAPS)]


def feature_rows(held, role, taps, start, count):
    total = taps[0] * held[role, pl.ds(start, count), :]
    for tap in range(1, TAPS):
        total = total + taps[tap] * held[role, pl.ds(start - tap, count), :]
    return total


def feature_kernel(*refs):
    sources, befores, kerns = refs[0:3], refs[3:6], refs[6:9]
    incoming_ref, moved_ref, feats_ref, held = refs[9:]
    rows, lanes_all = incoming_ref.shape
    for lane in range(0, lanes_all, 128):
        lanes = slice(lane, lane + 128)
        taps = []
        for role in range(3):
            held[role, 0:HALO, :] = befores[role][:, lanes].astype(F32)
            held[role, HALO : HALO + rows, :] = sources[role][:, lanes].astype(F32)
            taps.append(tap_rows(kerns[role], lanes))
        for row in range(0, rows, 16):
            span = slice(row, row + 16)
            query, keyed, value = [
                feature_rows(held, role, taps[role], HALO + row, 16) for role in range(3)
            ]
            feats_ref[0, span, lanes] = query
            feats_ref[1, span, lanes] = keyed
            feats_ref[2, span, lanes] = value
            moved_ref[0, 0, span, lanes] = (keyed * value).astype(BF16)
            moved_ref[0, 1, span, lanes] = (incoming_ref[span, lanes].astype(F32) * query).astype(BF16)


def featurize(source, before, incoming, weights, groups):
    rows, width = incoming.shape
    chans = width // groups

    def roles(height):
        return [
            pl.BlockSpec((height, chans), lambda d, role=role: (0, role * groups + d)) for role in range(3)
        ]

    return pl.pallas_call(
        feature_kernel,
        out_shape=(
            jax.ShapeDtypeStruct((groups, 2, rows, chans), BF16),
            jax.ShapeDtypeStruct((3, rows, width), F32),
        ),
        grid=(groups,),
        in_specs=roles(rows) + roles(HALO) + roles(TAPS) + [pl.BlockSpec((rows, chans), lambda d: (0, d))],
        out_specs=(
            pl.BlockSpec((1, 2, rows, chans), lambda d: (d, 0, 0, 0)),
            pl.BlockSpec((3, rows, chans), lambda d: (0, 0, d)),
        ),
        scratch_shapes=[pltpu.VMEM((3, HALO + rows, 128), F32)],
        compiler_params=pltpu.CompilerParams(vmem_limit_bytes=16 * MIB),
        cost_estimate=pl.CostEstimate(
            flops=45 * rows * width, bytes_accessed=24 * rows * width, transcendentals=0
        ),
        name="featurize",
    )(source, source, source, before, before, before, weights, weights, weights, incoming)


def long_kernel(
    moved_ref, spec_ref, table_ref, back_ref, gain_ref, sent_ref, filt_ref, skip_ref, rings, products, joined, turned_ref
):
    groups, _, rows, chans = moved_ref.shape
    leaf = groups * rows // 8
    per_piece = leaf // rows
    step = pl.program_id(0)

    @pl.when(step == 0)
    def _():
        @pl.loop(0, rows // 16)
        def _(strip):
            inside = pl.ds(pl.multiple_of(strip * 16, 16), 16)
            for part in range(per_piece):
                real_rows = pl.ds(pl.multiple_of(part * rows + strip * 16, 16), 16)
                imag_rows = pl.ds(pl.multiple_of(leaf + part * rows + strip * 16, 16), 16)
                for kind in range(2):
                    for lane in range(0, chans, 128):
                        lanes = slice(lane, lane + 128)
                        parts = [
                            moved_ref[piece * per_piece + part, kind, inside, lanes].astype(F32)
                            for piece in range(8)
                        ]
                        into = slice(kind * chans + lane, kind * chans + lane + 128)
                        for index, (real, imag) in enumerate(split_rings(parts)):
                            rings[index, real_rows, into] = real.astype(BF16)
                            rings[index, imag_rows, into] = imag.astype(BF16)

    both = jnp.dot(table_ref[0], rings[step], preferred_element_type=F32)
    g_real, g_imag = both[:leaf, :chans], both[leaf:, :chans]
    d_real, d_imag = both[:leaf, chans:], both[leaf:, chans:]
    f_real, f_imag = spec_ref[0, :leaf], spec_ref[0, leaf:]
    products[:leaf, 0:chans] = (g_real * f_real - g_imag * f_imag).astype(BF16)
    products[leaf:, 0:chans] = (g_real * f_imag + g_imag * f_real).astype(BF16)
    products[:leaf, chans : 2 * chans] = (d_real * f_real + d_imag * f_imag).astype(BF16)
    products[leaf:, chans : 2 * chans] = (d_imag * f_real - d_real * f_imag).astype(BF16)
    products[:leaf, 2 * chans :] = (d_real * g_real + d_imag * g_imag).astype(BF16)
    products[leaf:, 2 * chans :] = (d_imag * g_real - d_real * g_imag).astype(BF16)
    joined[step] = jnp.dot(back_ref[0], products[...], preferred_element_type=F32)

    @pl.when(step == 7)
    def _():
        skip_ref[...] = jnp.zeros_like(skip_ref)

        @pl.loop(0, rows // 16)
        def _(strip):
            inside = pl.ds(pl.multiple_of(strip * 16, 16), 16)
            for part in range(per_piece):
                real_rows = pl.ds(pl.multiple_of(part * rows + strip * 16, 16), 16)
                imag_rows = pl.ds(pl.multiple_of(leaf + part * rows + strip * 16, 16), 16)
                for lane in range(0, chans, 128):
                    lanes = slice(lane, lane + 128)
                    gain = gain_ref[0:1, lanes]
                    for kind in range(3):
                        column = slice(kind * chans + lane, kind * chans + lane + 128)
                        leaves = [
                            (joined[index, real_rows, column], joined[index, imag_rows, column])
                            for index in range(8)
                        ]
                        total = jnp.zeros((16, 128), F32)
                        for piece, result in enumerate(join_rings(leaves)):
                            owner = piece * per_piece + part
                            if kind == 0:
                                sent_ref[owner, 0, inside, lanes] = result.astype(BF16)
                            elif kind == 1:
                                grad = moved_ref[owner, 1, inside, lanes].astype(F32)
                                sent_ref[owner, 1, inside, lanes] = (result + gain * grad).astype(BF16)
                                total = total + grad * moved_ref[owner, 0, inside, lanes].astype(F32)
                            else:
                                into = pl.ds(pl.multiple_of(owner * rows + strip * 16, 16), 16)
                                turned_ref[into, lanes] = result
                        if kind == 1:
                            skip_ref[0:1, lanes] += jnp.sum(total, axis=0, keepdims=True)

        for piece in range(groups):
            span = slice(piece * rows, (piece + 1) * rows)
            filt_ref[:, span] = turned_ref[span, :].T
        for owner in range(groups - 1):
            sent_ref[owner, :, rows : rows + HALO, :] = sent_ref[owner + 1, :, 0:HALO, :]
        sent_ref[groups - 1, :, rows : rows + HALO, :] = jnp.zeros((2, HALO, chans), BF16)


def long_convolutions(moved, spectrum, table, back, gain):
    groups, _, rows, chans = moved.shape
    length = groups * rows
    wide = length // 4
    whole = pl.Buffered(1)
    return pl.pallas_call(
        long_kernel,
        out_shape=(
            jax.ShapeDtypeStruct((groups, 2, rows + HALO, chans), BF16),
            jax.ShapeDtypeStruct((chans, length), F32),
            jax.ShapeDtypeStruct((1, chans), F32),
        ),
        grid=(8,),
        in_specs=[
            pl.BlockSpec(moved.shape, lambda j: (0, 0, 0, 0), pipeline_mode=whole),
            pl.BlockSpec((1, wide, chans), lambda j: (j, 0, 0)),
            pl.BlockSpec((1, wide, wide), lambda j: (j, 0, 0)),
            pl.BlockSpec((1, wide, wide), lambda j: (j, 0, 0)),
            pl.BlockSpec((1, chans), lambda j: (0, 0)),
        ],
        out_specs=(
            pl.BlockSpec((groups, 2, rows + HALO, chans), lambda j: (0, 0, 0, 0), pipeline_mode=whole),
            pl.BlockSpec((chans, length), lambda j: (0, 0), pipeline_mode=whole),
            pl.BlockSpec((1, chans), lambda j: (0, 0)),
        ),
        scratch_shapes=[
            pltpu.VMEM((8, wide, 2 * chans), BF16),
            pltpu.VMEM((wide, 3 * chans), BF16),
            pltpu.VMEM((8, wide, 3 * chans), F32),
            pltpu.VMEM((length, chans), F32),
        ],
        compiler_params=pltpu.CompilerParams(vmem_limit_bytes=48 * MIB),
        cost_estimate=pl.CostEstimate(
            flops=80 * wide * wide * chans, bytes_accessed=20 * MIB, transcendentals=0
        ),
        name="long_convolutions",
    )(moved, spectrum, table, back, gain)


def gradient_kernel(*refs):
    sources, befores, afters, kerns = refs[0:3], refs[3:6], refs[6:9], refs[9:12]
    incoming_ref, later_ref, feats_ref, back_ref, gain_ref = refs[12:17]
    output_ref, partial_ref, grad_hbm = refs[17:20]
    held, grads, slots, sems = refs[20:]
    rows, chans = incoming_ref.shape
    width = grad_hbm.shape[1] // 3
    step = pl.program_id(0)
    slot = lax.rem(step, 2)

    def write_back(role, slot_at, step_at):
        start = pl.multiple_of(role * width + step_at * chans, 128)
        return pltpu.make_async_copy(
            slots.at[slot_at, role], grad_hbm.at[:, pl.ds(start, chans)], sems.at[slot_at, role]
        )

    @pl.when(step >= 2)
    def _():
        for role in range(3):
            write_back(role, slot, step - 2).wait()

    for lane in range(0, chans, 128):
        lanes = slice(lane, lane + 128)
        gain = gain_ref[0:1, lanes]
        taps = []
        for role in range(3):
            held[role, 0:HALO, :] = befores[role][:, lanes].astype(F32)
            held[role, HALO : HALO + rows, :] = sources[role][:, lanes].astype(F32)
            held[role, HALO + rows : HALO + rows + HALO, :] = afters[role][:, lanes].astype(F32)
            taps.append(tap_rows(kerns[role], lanes))

        def feature_grads(keyed, value, grad_in, mixed, through, span):
            gated = (keyed * value).astype(BF16).astype(F32)
            inner = mixed + gain * gated
            grads[0, span, :] = grad_in * inner
            grads[1, span, :] = through * value
            grads[2, span, :] = through * keyed
            return inner

        for row in range(0, rows, 16):
            span = slice(row, row + 16)
            inner = feature_grads(
                feats_ref[1, span, lanes],
                feats_ref[2, span, lanes],
                incoming_ref[span, lanes].astype(F32),
                back_ref[0, 0, span, lanes].astype(F32),
                back_ref[0, 1, span, lanes].astype(F32),
                span,
            )
            output_ref[span, lanes] = (feats_ref[0, span, lanes] * inner).astype(BF16)
        span = slice(rows, rows + HALO)
        feature_grads(
            feature_rows(held, 1, taps[1], HALO + rows, HALO),
            feature_rows(held, 2, taps[2], HALO + rows, HALO),
            later_ref[:, lanes].astype(F32),
            back_ref[0, 0, span, lanes].astype(F32),
            back_ref[0, 1, span, lanes].astype(F32),
            span,
        )
        for role in range(3):
            sums = [jnp.zeros((16, 128), F32) for _ in range(TAPS)]
            for row in range(0, rows, 16):
                here = grads[role, row : row + 16, :]
                total = taps[role][0] * here
                sums[0] = sums[0] + here * held[role, HALO + row : HALO + row + 16, :]
                for tap in range(1, TAPS):
                    total = total + taps[role][tap] * grads[role, row + tap : row + tap + 16, :]
                    sums[tap] = sums[tap] + here * held[role, HALO + row - tap : HALO + row - tap + 16, :]
                slots[slot, role, row : row + 16, lanes] = total.astype(BF16)
            rows_out = [jnp.sum(one, axis=0, keepdims=True) for one in sums]
            rows_out.append(jnp.zeros((1, 128), F32))
            partial_ref[0, role, :, lanes] = jnp.concatenate(rows_out, axis=0).astype(BF16)

    for role in range(3):
        write_back(role, slot, step).start()

    @pl.when(step == pl.num_programs(0) - 1)
    def _():
        for role in range(3):
            write_back(role, 1 - slot, step - 1).wait()
            write_back(role, slot, step).wait()


def gradients(source, before, after, weights, incoming, later, feats, back, gain):
    rows, width = incoming.shape
    groups = back.shape[0]
    chans = width // groups

    def roles(height):
        return [
            pl.BlockSpec((height, chans), lambda d, role=role: (0, role * groups + d)) for role in range(3)
        ]

    return pl.pallas_call(
        gradient_kernel,
        out_shape=(
            jax.ShapeDtypeStruct((rows, width), BF16),
            jax.ShapeDtypeStruct((groups, 3, HALO, chans), BF16),
            jax.ShapeDtypeStruct((rows, 3 * width), BF16),
        ),
        grid=(groups,),
        in_specs=roles(rows)
        + roles(HALO)
        + roles(HALO)
        + roles(TAPS)
        + [
            pl.BlockSpec((rows, chans), lambda d: (0, d)),
            pl.BlockSpec((HALO, chans), lambda d: (0, d)),
            pl.BlockSpec((3, rows, chans), lambda d: (0, 0, d)),
            pl.BlockSpec((1, 2, rows + HALO, chans), lambda d: (d, 0, 0, 0)),
            pl.BlockSpec((1, chans), lambda d: (0, d)),
        ],
        out_specs=(
            pl.BlockSpec((rows, chans), lambda d: (0, d)),
            pl.BlockSpec((1, 3, HALO, chans), lambda d: (d, 0, 0, 0)),
            pl.BlockSpec(memory_space=pl.ANY),
        ),
        scratch_shapes=[
            pltpu.VMEM((3, rows + 2 * HALO, 128), F32),
            pltpu.VMEM((3, rows + HALO, 128), F32),
            pltpu.VMEM((2, 3, rows, chans), BF16),
            pltpu.SemaphoreType.DMA((2, 3)),
        ],
        compiler_params=pltpu.CompilerParams(vmem_limit_bytes=16 * MIB),
        cost_estimate=pl.CostEstimate(
            flops=100 * rows * width, bytes_accessed=32 * rows * width, transcendentals=0
        ),
        name="featurizer_gradients",
    )(
        *[source] * 3,
        *[before] * 3,
        *[after] * 3,
        *[weights] * 3,
        incoming,
        later,
        feats,
        back,
        gain,
    )


def on_device(acts, cots, kern, filt, skip):
    source = passed_along(acts, "section", 1)[0]
    incoming = passed_along(cots, "section", -1)[0]
    rows, feats_all = source.shape
    groups = lax.axis_size("ctx")
    chans = filt.shape[1]
    weights = kern[0]
    before = from_behind(source[rows - HALO :], "ctx", 1)
    after = from_behind(source[:HALO], "ctx", -1)
    later = from_behind(incoming[:HALO], "ctx", -1)
    table, back = (jnp.asarray(one) for one in leaf_tables(rows * groups))
    spectrum = filter_spectrum(filt[0], table)
    gain = lax.dynamic_slice_in_dim(skip, lax.axis_index("ctx") * chans, chans, axis=1)

    moved, feats = featurize(source, before, incoming, weights, groups)
    moved = lax.all_to_all(moved, "ctx", split_axis=0, concat_axis=0, tiled=True)
    sent, filt_grad, skip_grad = long_convolutions(moved, spectrum, table, back, gain)
    sent = lax.all_to_all(sent, "ctx", split_axis=0, concat_axis=0, tiled=True)
    output, partial, input_grad = gradients(
        source, before, after, weights, incoming, later, feats, sent, skip
    )
    partial = lax.all_to_all(partial, "ctx", split_axis=0, concat_axis=0, tiled=True)
    summed = jnp.sum(partial.astype(F32), axis=0, keepdims=True).astype(BF16)
    everyone = jnp.broadcast_to(summed, partial.shape)
    everyone = lax.all_to_all(everyone, "ctx", split_axis=0, concat_axis=0, tiled=True)
    kern_grad = everyone[:, :, :TAPS].transpose(2, 1, 0, 3).reshape(TAPS, feats_all).astype(F32)
    return (output[None], input_grad[None], kern_grad[None], filt_grad[None], skip_grad)


def solution(mesh):
    return jax.shard_map(
        on_device,
        mesh=mesh,
        in_specs=(
            P("section", "ctx", None),
            P("section", "ctx", None),
            P("section", None, None),
            P("section", "ctx", None),
            P("section", None),
        ),
        out_specs=(
            P("section", "ctx", None),
            P("section", "ctx", None),
            P("section", None, None),
            P("section", "ctx", None),
            P("section", "ctx"),
        ),
        check_vma=False,
    )
```

time: 625 us -> 249 us (0.40); the launches traced: 614 us -> 248 us
  other arithmetic: 228 us -> 0.06 us
  matrix products: 76.2 us -> 0 us
  local copies, waits for them, and re-layouts: 72.4 us -> 24 us
  Pallas kernels: 0 us -> 42.5 us
  waiting for transfers between devices: 159 us -> 132 us
  blocking collectives: 38.9 us -> 22 us
  between operations: 14.9 us -> 0.78 us
    dot_general x15 -> x0, matrix products: 76.2 us -> none  [the longest x9 63.9 us: contract(): return jnp.einsum(form, table, values, precision=lax.Precision.HIGH)]
    psum x1 -> x0, waiting for transfers between devices: 63.8 us -> none  [on_device(): lax.psum(partial_kern.astype(jnp.bfloat16), 'ctx').astype(jnp.float32)]
    unnamed x9 -> x0, other arithmetic: 52.6 us -> none
    add x5 -> x0, other arithmetic: 49.9 us -> none  [the longest x1 24.5 us: on_device(): sum((weights[offset][None, :] * padded[margin - offset:margin - offset +...]
    pallas_call x0 -> x4, Pallas kernels: none -> 42.5 us  [the longest x1 19.1 us: long_convolutions(): pl.pallas_call(long_kernel, out_shape=(jax.ShapeDtypeStruct((groups, 2, r...]
    broadcast_in_dim x2 -> x0, other arithmetic: 33.6 us -> none  [the longest x1 31.6 us: on_device(): input_grad[None]]
    ppermute x2 -> x3, waiting for transfers between devices: 0.27 us -> 27.4 us  [from_behind(): return lax.ppermute(block, axis, route)]
    reduce_sum x2 -> x1, other arithmetic: 22.6 us -> 0.04 us  [on_device(): summed = jnp.sum(partial.astype(F32), axis=0, keepdims=True).astype(BF16)]
  transfers between devices with their start and end apart: 7 -> 7, of which waited for: 5 -> 4; matrix products, arithmetic and copies ran while one was open for 31% -> 1% of each run, Pallas kernels for 0% -> 2%
where the time goes in v1:
time: 249 us; the launch traced here: 248 us
  waiting for transfers between devices  132 us (53%)
  Pallas kernels  42.5 us (17%)
  starting transfers between devices  26.5 us (11%)
  local copies, waits for them, and re-layouts  24 us (10%)
  blocking collectives  22 us (9%)
    ppermute x2, waiting for transfers between devices, passed_along(): return lax.ppermute(value, axis, pairs)  87.3 us
    ppermute x3, waiting for transfers between devices, from_behind(): return lax.ppermute(block, axis, route)  27.4 us
    unnamed x35, local copies, waits for them, and re-layouts  20.7 us
    pallas_call x1, Pallas kernels, long_convolutions(): pl.pallas_call(long_kernel, out_shape=(jax.ShapeDtypeStruct((groups, 2, r...  19.1 us
    all_to_all x1, waiting for transfers between devices, on_device(): lax.all_to_all(moved, 'ctx', split_axis=0, concat_axis=0, tiled=True)  17.8 us
    pallas_call x1, Pallas kernels, gradients(): pl.pallas_call(gradient_kernel, out_shape=(jax.ShapeDtypeStruct((rows, wi...  14.4 us
    all_to_all x1, blocking collectives, on_device(): lax.all_to_all(partial, 'ctx', split_axis=0, concat_axis=0, tiled=True)  12.3 us
    all_to_all x1, blocking collectives, on_device(): lax.all_to_all(everyone, 'ctx', split_axis=0, concat_axis=0, tiled=True)  9.68 us
  transfers between devices with their start and end apart: 7, of which 4 were waited for; matrix products, arithmetic and copies ran while one was open for 1% of the time, Pallas kernels for 2%

profile of v1, /device:TPU:1, one launch (start us, length us, event | category | flops | bytes accessed | tf_op | source)
XLA Modules:
  0.0 248.3 jit_solution(17467572660444124046)
XLA Ops:
  0.6 4.5 %collective-permute-start = (bf16[1,128,12288]{2,1,0:T(8,128)(2,1)}, bf16[1,128,12288]{2,1,0:T(8,128)(2,1)S(1)}, u32[]{:S(2)}, u32[]{:S(2)}) collective-permute-start(bf16[1,128,12288]{2,1,0:T(8,128)(2,1)} %param.7), channel_id=1, source_target_pairs={{0,16},{16,32},{32,48},{48,64},{64,80},{80,96},{96,112},{112,0},{1... | collective-permute-start | bytes 9437192 | tf_op jit(solution)/shard_map/ppermute | solution.py:23
  5.1 2.3 collective-permute-start.3
  7.4 87.3 %collective-permute-done = bf16[1,128,12288]{2,1,0:T(8,128)(2,1)S(1)} collective-permute-done((bf16[1,128,12288]{2,1,0:T(8,128)(2,1)}, bf16[1,128,12288]{2,1,0:T(8,128)(2,1)S(1)}, u32[]{:S(2)}, u32[]{:S(2)}) %collective-permute-start) | collective-permute-done | bytes 3145760 | tf_op jit(solution)/shard_map/ppermute | solution.py:23
  94.7 0.7 slice_bitcast_fusion
  95.4 4.6 %collective-permute-start.1 = (bf16[8,12288]{1,0:T(8,128)(2,1)S(1)}, bf16[8,12288]{1,0:T(8,128)(2,1)S(1)}, u32[]{:S(2)}, u32[]{:S(2)}) collective-permute-start(bf16[8,12288]{1,0:T(8,128)(2,1)S(1)} %get-tuple-element.32), channel_id=1, source_target_pairs={{0,1},{1,2},{2,3},{3,4},{4,5},{5,6},{6,7},{7,8},{8,9},{9,10},{10,1... | collective-permute-start | bytes 589832 | tf_op jit(solution)/shard_map/ppermute | solution.py:29
  100.0 1.2 copy.20
  101.2 0.0 collective-permute-done.3
  101.2 0.0 copy-start.4
  101.2 1.4 collective-permute-done.1.refs_3_.refs_4_.refs_5_
  102.6 0.0 copy-start
  102.6 5.2 %featurize.1 = (bf16[16,2,128,256]{3,2,1,0:T(8,128)(2,1)S(1)}, f32[3,128,4096]{2,1,0:T(8,128)S(1)}) custom-call(bf16[128,12288]{1,0:T(8,128)(2,1)S(1)} %bitcast.19, bf16[128,12288]{1,0:T(8,128)(2,1)S(1)} %bitcast.20, bf16[128,12288]{1,0:T(8,128)(2,1)S(1)} %bitcast.21, bf16[8,12288]{1,0:T(8,128)(2,1)S(1)} %collective-permute-done.1.refs_3_.refs_4_.refs_5_, ...), custom_call_target="tpu_custom_call" | custom-call | flops 23592960 | bytes 12582912 | tf_op jit(solution)/shard_map/featurize/pallas_call | solution.py:188
  107.8 0.0 copy-done.4
  107.8 0.0 copy-done
  107.8 0.0 copy-start.2
  107.8 2.6 %copy-done.2 = f32[3,128,4096]{2,1,0:T(8,128)} copy-done((f32[3,128,4096]{2,1,0:T(8,128)}, f32[3,128,4096]{2,1,0:T(8,128)S(1)}, u32[]{:S(2)}) %copy-start.2) | copy-done | bytes 6291480
  110.5 0.0 copy-start.9
  110.5 1.3 copy-done.9
  111.8 6.2 %all-to-all-start = ((bf16[16,2,128,256]{3,2,1,0:T(8,128)(2,1)}), bf16[16,2,128,256]{3,2,1,0:T(8,128)(2,1)}, u32[]{:S(2)}, u32[]{:S(2)}) async-start(bf16[16,2,128,256]{3,2,1,0:T(8,128)(2,1)} %copy-done.9), calls=%async_computation | async-start | bytes 4194304 | tf_op jit(solution)/shard_map/all_to_all | solution.py:486
  118.0 2.2 copy-done.6
  120.2 1.2 copy-done.12
  121.4 3.8 %filter_spectrum.1.spec_ref = f32[8,512,256]{2,1,0:T(8,128)S(1)} custom-call(bf16[256,2048]{1,0:T(8,128)(2,1)S(1)} %bitcast.33, bf16[8,512,512]{2,1,0:T(8,128)(2,1)S(1)} %copy-done.6), custom_call_target="tpu_custom_call" | custom-call | flops 1073741824 | bytes 10485760 | tf_op jit(solution)/shard_map/filter_spectrum/pallas_call | solution.py:127
  125.3 0.0 copy-start.7
  125.3 2.1 copy-done.7
  127.3 0.0 copy-done.15
  127.3 0.6 constant_dynamic-slice_fusion.gain_ref
  127.9 17.8 %all-to-all-done.moved_ref = bf16[16,2,128,256]{3,2,1,0:T(8,128)(2,1)} async-done(((bf16[16,2,128,256]{3,2,1,0:T(8,128)(2,1)}), bf16[16,2,128,256]{3,2,1,0:T(8,128)(2,1)}, u32[]{:S(2)}, u32[]{:S(2)}) %all-to-all-start) | async-done | bytes 2097184 | tf_op jit(solution)/shard_map/all_to_all | solution.py:486
  145.7 0.7 copy-done.16
  146.4 19.1 %long_convolutions.1 = (bf16[16,2,136,256]{3,2,1,0:T(8,128)(2,1)S(1)}, f32[256,2048]{1,0:T(8,128)}, f32[1,256]{1,0:T(1,128)}) custom-call(bf16[16,2,128,256]{3,2,1,0:T(8,128)(2,1)} %all-to-all-done.moved_ref, f32[8,512,256]{2,1,0:T(8,128)} %copy-done.7, bf16[8,512,512]{2,1,0:T(8,128)(2,1)} %constant.17.clone.table_ref, ...), custom_call_target="tpu_custom_call" | custom-call | flops 5368709120 | bytes 20971520 | tf_op jit(solution)/shard_map/long_convolutions/pallas_call | solution.py:296
  165.5 1.4 copy-done.8
  166.9 4.8 %all-to-all-start.1 = ((bf16[16,2,136,256]{3,2,1,0:T(8,128)(2,1)}), bf16[16,2,136,256]{3,2,1,0:T(8,128)(2,1)}, u32[]{:S(2)}, u32[]{:S(2)}) async-start(bf16[16,2,136,256]{3,2,1,0:T(8,128)(2,1)} %copy-done.8), calls=%async_computation.1 | async-start | bytes 4456448 | tf_op jit(solution)/shard_map/all_to_all | solution.py:488
  171.6 2.2 collective-permute-start.2
  173.8 0.8 slice_bitcast_fusion.2
  174.7 1.9 collective-permute-start.4
  176.6 26.0 %collective-permute-done.4.refs_13_ = bf16[8,4096]{1,0:T(8,128)(2,1)S(1)} collective-permute-done((bf16[8,4096]{1,0:T(8,128)(2,1)S(1)}, bf16[8,4096]{1,0:T(8,128)(2,1)S(1)}, u32[]{:S(2)}, u32[]{:S(2)}) %collective-permute-start.4) | collective-permute-done | bytes 65568 | tf_op jit(solution)/shard_map/ppermute | solution.py:29
  202.6 0.6 copy-done.13
  203.2 0.0 collective-permute-done.2.refs_6_.refs_7_.refs_8_
  203.2 0.7 copy-done.10
  203.9 0.0 all-to-all-done.1.refs_15_
  203.9 0.9 copy-done.1
  204.9 2.8 %copy-done.3 = f32[3,128,4096]{2,1,0:T(8,128)S(1)} copy-done((f32[3,128,4096]{2,1,0:T(8,128)S(1)}, f32[3,128,4096]{2,1,0:T(8,128)}, u32[]{:S(2)}) %copy-start.3) | copy-done | bytes 6291480
  207.6 1.2 copy-done.5
  208.9 0.9 copy-done.11
  209.8 0.8 copy-done.14
  210.6 14.4 %featurizer_gradients.1 = (bf16[128,4096]{1,0:T(8,128)(2,1)}, bf16[16,3,8,256]{3,2,1,0:T(8,128)(2,1)S(1)}, bf16[128,12288]{1,0:T(8,128)(2,1)}) custom-call(bf16[128,12288]{1,0:T(8,128)(2,1)S(1)} %bitcast.22, bf16[128,12288]{1,0:T(8,128)(2,1)S(1)} %bitcast.23, bf16[128,12288]{1,0:T(8,128)(2,1)S(1)} %bitcast.24, bf16[8,12288]{1,0:T(8,128)(2,1)S(1)} %copy-done.1, ...), custom_call_target="tpu_custom_call" | custom-call | flops 52428800 | bytes 16777216 | tf_op jit(solution)/shard_map/featurizer_gradients/pallas_call | solution.py:423
  225.0 12.3 %all_to_all.20 = bf16[16,3,8,256]{3,2,1,0:T(8,128)(2,1)S(1)} all-to-all(bf16[16,3,8,256]{3,2,1,0:T(8,128)(2,1)S(1)} %get-tuple-element.18), channel_id=1, replica_groups=mesh['section'=8,'ctx'=16] {'ctx'}, dimensions={0} | all-to-all | bytes 393216 | tf_op jit(solution)/shard_map/all_to_all | solution.py:492
  237.4 9.7 %all_to_all.21 = bf16[16,3,8,256]{3,2,1,0:T(8,128)(2,1)S(1)} all-to-all(bf16[16,3,8,256]{3,2,1,0:T(8,128)(2,1)S(1)} %broadcast_in_dim.18), channel_id=1, replica_groups=mesh['section'=8,'ctx'=16] {'ctx'}, dimensions={0} | all-to-all | bytes 393216 | tf_op jit(solution)/shard_map/all_to_all | solution.py:495
  247.1 0.1 copy.16
  247.2 1.1 reshape.31
  (15 shorter events, 0.1 us)
Async XLA Ops:
  0.6 94.0 %collective-permute-start = (bf16[1,128,12288]{2,1,0:T(8,128)(2,1)}, bf16[1,128,12288]{2,1,0:T(8,128)(2,1)S(1)}, u32[]{:S(2)}, u32[]{:S(2)}) collective-permute-start(bf16[1,128,12288]{2,1,0:T(8,128)(2,1)} %param.7), channel_id=1, source_target_pairs={{0,16},{16,32},{32,48},{48,64},{64,80},{80,96},{96,112},{112,0},{1... | collective-permute-start | bytes 9437192 | tf_op jit(solution)/shard_map/ppermute | solution.py:23
  5.1 96.1 %collective-permute-start.3 = (bf16[1,128,4096]{2,1,0:T(8,128)(2,1)}, bf16[1,128,4096]{2,1,0:T(8,128)(2,1)S(1)}, u32[]{:S(2)}, u32[]{:S(2)}) collective-permute-start(bf16[1,128,4096]{2,1,0:T(8,128)(2,1)} %param.8), channel_id=1, source_target_pairs={{0,112},{16,0},{32,16},{48,32},{64,48},{80,64},{96,80},{112,96},{1... | collective-permute-start | bytes 3145736 | tf_op jit(solution)/shard_map/ppermute | solution.py:23
  95.4 7.2 %collective-permute-start.1 = (bf16[8,12288]{1,0:T(8,128)(2,1)S(1)}, bf16[8,12288]{1,0:T(8,128)(2,1)S(1)}, u32[]{:S(2)}, u32[]{:S(2)}) collective-permute-start(bf16[8,12288]{1,0:T(8,128)(2,1)S(1)} %get-tuple-element.32), channel_id=1, source_target_pairs={{0,1},{1,2},{2,3},{3,4},{4,5},{5,6},{6,7},{7,8},{8,9},{9,10},{10,1... | collective-permute-start | bytes 589832 | tf_op jit(solution)/shard_map/ppermute | solution.py:29
  101.2 6.6 %copy-start.4 = (bf16[1,128,4096]{2,1,0:T(8,128)(2,1)}, bf16[1,128,4096]{2,1,0:T(8,128)(2,1)S(1)}, u32[]{:S(2)}) copy-start(bf16[1,128,4096]{2,1,0:T(8,128)(2,1)S(1)} %collective-permute-done.3) | copy-start | bytes 3145732
  102.6 5.2 %copy-start = (bf16[8,12288]{1,0:T(8,128)(2,1)}, bf16[8,12288]{1,0:T(8,128)(2,1)S(1)}, u32[]{:S(2)}) copy-start(bf16[8,12288]{1,0:T(8,128)(2,1)S(1)} %collective-permute-done.1.refs_3_.refs_4_.refs_5_) | copy-start | bytes 589828
  107.8 2.6 %copy-start.2 = (f32[3,128,4096]{2,1,0:T(8,128)}, f32[3,128,4096]{2,1,0:T(8,128)S(1)}, u32[]{:S(2)}) copy-start(f32[3,128,4096]{2,1,0:T(8,128)S(1)} %get-tuple-element.13.refs_14_) | copy-start | bytes 18874372
  110.5 1.3 copy-start.9
  111.8 33.9 %all-to-all-start = ((bf16[16,2,128,256]{3,2,1,0:T(8,128)(2,1)}), bf16[16,2,128,256]{3,2,1,0:T(8,128)(2,1)}, u32[]{:S(2)}, u32[]{:S(2)}) async-start(bf16[16,2,128,256]{3,2,1,0:T(8,128)(2,1)} %copy-done.9), calls=%async_computation | async-start | bytes 4194304 | tf_op jit(solution)/shard_map/all_to_all | solution.py:486
  118.0 2.2 copy-start.6
  120.2 1.2 copy-start.12
  121.4 5.9 %copy-start.15 = (f32[1,4096]{1,0:T(1,128)S(1)}, f32[1,4096]{1,0:T(1,128)}, u32[]{:S(2)}) copy-start(f32[1,4096]{1,0:T(1,128)} %refs_16_.1) | copy-start | bytes 49156
  125.3 2.1 copy-start.7
  145.7 0.7 copy-start.16
  165.5 1.4 copy-start.8
  166.9 37.0 %all-to-all-start.1 = ((bf16[16,2,136,256]{3,2,1,0:T(8,128)(2,1)}), bf16[16,2,136,256]{3,2,1,0:T(8,128)(2,1)}, u32[]{:S(2)}, u32[]{:S(2)}) async-start(bf16[16,2,136,256]{3,2,1,0:T(8,128)(2,1)} %copy-done.8), calls=%async_computation.1 | async-start | bytes 4456448 | tf_op jit(solution)/shard_map/all_to_all | solution.py:488
  171.6 31.6 %collective-permute-start.2 = (bf16[8,12288]{1,0:T(8,128)(2,1)}, bf16[8,12288]{1,0:T(8,128)(2,1)S(1)}, u32[]{:S(2)}, u32[]{:S(2)}) collective-permute-start(bf16[8,12288]{1,0:T(8,128)(2,1)} %get-tuple-element.31), channel_id=1, source_target_pairs={{1,0},{2,1},{3,2},{4,3},{5,4},{6,5},{7,6},{8,7},{9,8},{10,9},{11,1... | collective-permute-start | bytes 589832 | tf_op jit(solution)/shard_map/ppermute | solution.py:29
  174.7 27.9 %collective-permute-start.4 = (bf16[8,4096]{1,0:T(8,128)(2,1)S(1)}, bf16[8,4096]{1,0:T(8,128)(2,1)S(1)}, u32[]{:S(2)}, u32[]{:S(2)}) collective-permute-start(bf16[8,4096]{1,0:T(8,128)(2,1)S(1)} %slice_bitcast_fusion.2), channel_id=1, source_target_pairs={{1,0},{2,1},{3,2},{4,3},{5,4},{6,5},{7,6},{8,7},{9,8},{10,9},{11,1... | collective-permute-start | bytes 196616 | tf_op jit(solution)/shard_map/ppermute | solution.py:29
  202.6 0.6 copy-start.13
  203.2 0.7 copy-start.10
  203.9 0.9 copy-start.1
  204.8 2.8 %copy-start.3 = (f32[3,128,4096]{2,1,0:T(8,128)S(1)}, f32[3,128,4096]{2,1,0:T(8,128)}, u32[]{:S(2)}) copy-start(f32[3,128,4096]{2,1,0:T(8,128)} %copy-done.2) | copy-start | bytes 18874372
  207.6 1.2 copy-start.5
  208.9 0.9 copy-start.11
  209.8 0.8 copy-start.14

commit v2 on v1

--- a/solution.py
+++ b/solution.py
@@ -1,3 +1,4 @@
+import functools
 import math
 
 import jax
@@ -15,6 +16,11 @@
 F32 = jnp.float32
 BF16 = jnp.bfloat16
 MIB = 1 << 20
+CHUNKS = 2
+
+
+def in_hbm(*arrays):
+    return [pltpu.with_memory_space_constraint(array, pltpu.HBM) for array in arrays]
 
 
 def passed_along(value, axis, steps):
@@ -126,7 +132,7 @@
     wide = length // 4
     return pl.pallas_call(
         filter_kernel,
-        out_shape=jax.ShapeDtypeStruct((8, wide, chans), F32),
+        out_shape=pltpu.HBM((8, wide, chans), F32),
         grid=(8,),
         in_specs=[
             pl.BlockSpec((chans, length), lambda j: (0, 0)),
@@ -134,12 +140,45 @@
         ],
         out_specs=pl.BlockSpec((1, wide, chans), lambda j: (j, 0, 0)),
         scratch_shapes=[pltpu.VMEM((8, chans, wide), BF16)],
-        compiler_params=pltpu.CompilerParams(vmem_limit_bytes=24 * MIB),
+        compiler_params=pltpu.CompilerParams(vmem_limit_bytes=12 * MIB),
         cost_estimate=pl.CostEstimate(
             flops=16 * wide * wide * chans, bytes_accessed=10 * MIB, transcendentals=0
         ),
         name="filter_spectrum",
-    )(filt, table)
+    )(*in_hbm(filt, table))
+
+
+def pick_kernel(chunk, wide_ref, wide_out, sems):
+    lanes = wide_out.shape[1] // sems.shape[0]
+    copies = [
+        pltpu.make_async_copy(
+            wide_ref.at[:, pl.ds((CHUNKS * piece + chunk) * lanes, lanes)],
+            wide_out.at[:, pl.ds(piece * lanes, lanes)],
+            sems.at[piece],
+        )
+        for piece in range(sems.shape[0])
+    ]
+    for copy in copies:
+        copy.start()
+    for copy in copies:
+        copy.wait()
+
+
+def pick_chunk(array, chunk, lanes):
+    rows, width = array.shape
+    pieces = width // CHUNKS // lanes
+    return pl.pallas_call(
+        functools.partial(pick_kernel, chunk),
+        out_shape=pltpu.HBM((rows, width // CHUNKS), array.dtype),
+        in_specs=[pl.BlockSpec(memory_space=pl.ANY)],
+        out_specs=pl.BlockSpec(memory_space=pl.ANY),
+        scratch_shapes=[pltpu.SemaphoreType.DMA((pieces,))],
+        compiler_params=pltpu.CompilerParams(vmem_limit_bytes=2 * MIB),
+        cost_estimate=pl.CostEstimate(
+            flops=0, bytes_accessed=2 * rows * width, transcendentals=0
+        ),
+        name="pick_chunk",
+    )(*in_hbm(array))
 
 
 def tap_rows(kern_ref, lanes):
@@ -176,39 +215,41 @@
             moved_ref[0, 1, span, lanes] = (incoming_ref[span, lanes].astype(F32) * query).astype(BF16)
 
 
-def featurize(source, before, incoming, weights, groups):
+def featurize(source, before, incoming, weights, groups, chunk):
     rows, width = incoming.shape
     chans = width // groups
 
-    def roles(height):
+    def roles(height, step=1, first=0):
         return [
-            pl.BlockSpec((height, chans), lambda d, role=role: (0, role * groups + d)) for role in range(3)
+            pl.BlockSpec((height, chans), lambda d, role=role: (0, (role * groups + d) * step + first))
+            for role in range(3)
         ]
 
     return pl.pallas_call(
         feature_kernel,
         out_shape=(
-            jax.ShapeDtypeStruct((groups, 2, rows, chans), BF16),
-            jax.ShapeDtypeStruct((3, rows, width), F32),
+            pltpu.HBM((groups, 2, rows, chans), BF16),
+            pltpu.HBM((3, rows, width), F32),
         ),
         grid=(groups,),
-        in_specs=roles(rows) + roles(HALO) + roles(TAPS) + [pl.BlockSpec((rows, chans), lambda d: (0, d))],
+        in_specs=roles(rows) + roles(HALO) + roles(TAPS, CHUNKS, chunk) + [pl.BlockSpec((rows, chans), lambda d: (0, d))],
         out_specs=(
             pl.BlockSpec((1, 2, rows, chans), lambda d: (d, 0, 0, 0)),
             pl.BlockSpec((3, rows, chans), lambda d: (0, 0, d)),
         ),
         scratch_shapes=[pltpu.VMEM((3, HALO + rows, 128), F32)],
-        compiler_params=pltpu.CompilerParams(vmem_limit_bytes=16 * MIB),
+        compiler_params=pltpu.CompilerParams(vmem_limit_bytes=6 * MIB),
         cost_estimate=pl.CostEstimate(
             flops=45 * rows * width, bytes_accessed=24 * rows * width, transcendentals=0
         ),
         name="featurize",
-    )(source, source, source, before, before, before, weights, weights, weights, incoming)
+    )(*[source] * 3, *[before] * 3, *in_hbm(*[weights] * 3), incoming)
 
 
 def long_kernel(
-    moved_ref, spec_ref, table_ref, back_ref, gain_ref, sent_ref, filt_ref, skip_ref, rings, products, joined, turned_ref
+    moved_ref, spec_ref, table_ref, back_ref, gain_ref, *refs
 ):
+    sent_ref, filt_ref, skip_ref, rings, products, joined, turned_ref = refs[-7:]
     groups, _, rows, chans = moved_ref.shape
     leaf = groups * rows // 8
     per_piece = leaf // rows
@@ -288,29 +329,31 @@
         sent_ref[groups - 1, :, rows : rows + HALO, :] = jnp.zeros((2, HALO, chans), BF16)
 
 
-def long_convolutions(moved, spectrum, table, back, gain):
+def long_convolutions(moved, spectrum, table, back, gain, chunk, earlier):
     groups, _, rows, chans = moved.shape
     length = groups * rows
     wide = length // 4
     whole = pl.Buffered(1)
     return pl.pallas_call(
         long_kernel,
+        input_output_aliases={5: 1} if earlier else {},
         out_shape=(
-            jax.ShapeDtypeStruct((groups, 2, rows + HALO, chans), BF16),
-            jax.ShapeDtypeStruct((chans, length), F32),
-            jax.ShapeDtypeStruct((1, chans), F32),
+            pltpu.HBM((groups, 2, rows + HALO, chans), BF16),
+            pltpu.HBM((CHUNKS * chans, length), F32),
+            pltpu.HBM((1, chans), F32),
         ),
         grid=(8,),
         in_specs=[
             pl.BlockSpec(moved.shape, lambda j: (0, 0, 0, 0), pipeline_mode=whole),
-            pl.BlockSpec((1, wide, chans), lambda j: (j, 0, 0)),
+            pl.BlockSpec((1, wide, chans), lambda j: (j, 0, chunk)),
             pl.BlockSpec((1, wide, wide), lambda j: (j, 0, 0)),
             pl.BlockSpec((1, wide, wide), lambda j: (j, 0, 0)),
-            pl.BlockSpec((1, chans), lambda j: (0, 0)),
-        ],
+            pl.BlockSpec((1, chans), lambda j: (0, chunk)),
+        ]
+        + [pl.BlockSpec(memory_space=pl.ANY)] * len(earlier),
         out_specs=(
             pl.BlockSpec((groups, 2, rows + HALO, chans), lambda j: (0, 0, 0, 0), pipeline_mode=whole),
-            pl.BlockSpec((chans, length), lambda j: (0, 0), pipeline_mode=whole),
+            pl.BlockSpec((chans, length), lambda j: (chunk, 0), pipeline_mode=whole),
             pl.BlockSpec((1, chans), lambda j: (0, 0)),
         ),
         scratch_shapes=[
@@ -319,26 +362,25 @@
             pltpu.VMEM((8, wide, 3 * chans), F32),
             pltpu.VMEM((length, chans), F32),
         ],
-        compiler_params=pltpu.CompilerParams(vmem_limit_bytes=48 * MIB),
+        compiler_params=pltpu.CompilerParams(vmem_limit_bytes=20 * MIB),
         cost_estimate=pl.CostEstimate(
             flops=80 * wide * wide * chans, bytes_accessed=20 * MIB, transcendentals=0
         ),
         name="long_convolutions",
-    )(moved, spectrum, table, back, gain)
-
-
-def gradient_kernel(*refs):
+    )(moved, *in_hbm(spectrum, table, back, gain, *earlier))
+
+
+def gradient_kernel(chunk, *refs):
     sources, befores, afters, kerns = refs[0:3], refs[3:6], refs[6:9], refs[9:12]
     incoming_ref, later_ref, feats_ref, back_ref, gain_ref = refs[12:17]
-    output_ref, partial_ref, grad_hbm = refs[17:20]
-    held, grads, slots, sems = refs[20:]
+    output_ref, partial_ref, grad_hbm, held, grads, slots, sems = refs[-7:]
     rows, chans = incoming_ref.shape
     width = grad_hbm.shape[1] // 3
     step = pl.program_id(0)
     slot = lax.rem(step, 2)
 
     def write_back(role, slot_at, step_at):
-        start = pl.multiple_of(role * width + step_at * chans, 128)
+        start = pl.multiple_of(role * width + (step_at * CHUNKS + chunk) * chans, 128)
         return pltpu.make_async_copy(
             slots.at[slot_at, role], grad_hbm.at[:, pl.ds(start, chans)], sems.at[slot_at, role]
         )
@@ -410,37 +452,40 @@
             write_back(role, slot, step).wait()
 
 
-def gradients(source, before, after, weights, incoming, later, feats, back, gain):
+def gradients(source, before, after, weights, incoming, later, feats, back, gain, chunk, earlier):
     rows, width = incoming.shape
     groups = back.shape[0]
     chans = width // groups
 
-    def roles(height):
+    def roles(height, step=1, first=0):
         return [
-            pl.BlockSpec((height, chans), lambda d, role=role: (0, role * groups + d)) for role in range(3)
+            pl.BlockSpec((height, chans), lambda d, role=role: (0, (role * groups + d) * step + first))
+            for role in range(3)
         ]
 
     return pl.pallas_call(
-        gradient_kernel,
+        functools.partial(gradient_kernel, chunk),
+        input_output_aliases={17: 0, 18: 2} if earlier else {},
         out_shape=(
-            jax.ShapeDtypeStruct((rows, width), BF16),
-            jax.ShapeDtypeStruct((groups, 3, HALO, chans), BF16),
-            jax.ShapeDtypeStruct((rows, 3 * width), BF16),
+            pltpu.HBM((rows, CHUNKS * width), BF16),
+            pltpu.HBM((groups, 3, HALO, chans), BF16),
+            pltpu.HBM((rows, 3 * CHUNKS * width), BF16),
         ),
         grid=(groups,),
         in_specs=roles(rows)
         + roles(HALO)
         + roles(HALO)
-        + roles(TAPS)
+        + roles(TAPS, CHUNKS, chunk)
         + [
             pl.BlockSpec((rows, chans), lambda d: (0, d)),
             pl.BlockSpec((HALO, chans), lambda d: (0, d)),
             pl.BlockSpec((3, rows, chans), lambda d: (0, 0, d)),
             pl.BlockSpec((1, 2, rows + HALO, chans), lambda d: (d, 0, 0, 0)),
-            pl.BlockSpec((1, chans), lambda d: (0, d)),
-        ],
+            pl.BlockSpec((1, chans), lambda d: (0, d * CHUNKS + chunk)),
+        ]
+        + [pl.BlockSpec(memory_space=pl.ANY)] * len(earlier),
         out_specs=(
-            pl.BlockSpec((rows, chans), lambda d: (0, d)),
+            pl.BlockSpec((rows, chans), lambda d: (0, d * CHUNKS + chunk)),
             pl.BlockSpec((1, 3, HALO, chans), lambda d: (d, 0, 0, 0)),
             pl.BlockSpec(memory_space=pl.ANY),
         ),
@@ -450,7 +495,7 @@
             pltpu.VMEM((2, 3, rows, chans), BF16),
             pltpu.SemaphoreType.DMA((2, 3)),
         ],
-        compiler_params=pltpu.CompilerParams(vmem_limit_bytes=16 * MIB),
+        compiler_params=pltpu.CompilerParams(vmem_limit_bytes=8 * MIB),
         cost_estimate=pl.CostEstimate(
             flops=100 * rows * width, bytes_accessed=32 * rows * width, transcendentals=0
         ),
@@ -459,42 +504,54 @@
         *[source] * 3,
         *[before] * 3,
         *[after] * 3,
-        *[weights] * 3,
+        *in_hbm(*[weights] * 3),
         incoming,
         later,
-        feats,
+        *in_hbm(feats),
         back,
-        gain,
+        *in_hbm(gain, *earlier),
     )
 
 
 def on_device(acts, cots, kern, filt, skip):
-    source = passed_along(acts, "section", 1)[0]
-    incoming = passed_along(cots, "section", -1)[0]
-    rows, feats_all = source.shape
+    rows, feats_all = acts.shape[1:]
     groups = lax.axis_size("ctx")
     chans = filt.shape[1]
+    part = chans // CHUNKS
     weights = kern[0]
-    before = from_behind(source[rows - HALO :], "ctx", 1)
-    after = from_behind(source[:HALO], "ctx", -1)
-    later = from_behind(incoming[:HALO], "ctx", -1)
     table, back = (jnp.asarray(one) for one in leaf_tables(rows * groups))
     spectrum = filter_spectrum(filt[0], table)
     gain = lax.dynamic_slice_in_dim(skip, lax.axis_index("ctx") * chans, chans, axis=1)
 
-    moved, feats = featurize(source, before, incoming, weights, groups)
-    moved = lax.all_to_all(moved, "ctx", split_axis=0, concat_axis=0, tiled=True)
-    sent, filt_grad, skip_grad = long_convolutions(moved, spectrum, table, back, gain)
-    sent = lax.all_to_all(sent, "ctx", split_axis=0, concat_axis=0, tiled=True)
-    output, partial, input_grad = gradients(
-        source, before, after, weights, incoming, later, feats, sent, skip
-    )
-    partial = lax.all_to_all(partial, "ctx", split_axis=0, concat_axis=0, tiled=True)
-    summed = jnp.sum(partial.astype(F32), axis=0, keepdims=True).astype(BF16)
-    everyone = jnp.broadcast_to(summed, partial.shape)
-    everyone = lax.all_to_all(everyone, "ctx", split_axis=0, concat_axis=0, tiled=True)
-    kern_grad = everyone[:, :, :TAPS].transpose(2, 1, 0, 3).reshape(TAPS, feats_all).astype(F32)
-    return (output[None], input_grad[None], kern_grad[None], filt_grad[None], skip_grad)
+    arrived = []
+    for chunk in range(CHUNKS):
+        leaving = pick_chunk(acts[0], chunk, part), pick_chunk(cots[0], chunk, part)
+        if arrived:
+            leaving, arrived[-1] = lax.optimization_barrier((leaving, arrived[-1]))
+        arrived.append((passed_along(leaving[0], "section", 1), passed_along(leaving[1], "section", -1)))
+
+    partials, skips, filters, results = [], [], (), ()
+    for chunk, (source, incoming) in enumerate(arrived):
+        before = from_behind(source[rows - HALO :], "ctx", 1)
+        after = from_behind(source[:HALO], "ctx", -1)
+        later = from_behind(incoming[:HALO], "ctx", -1)
+        moved, feats = featurize(source, before, incoming, weights, groups, chunk)
+        moved = lax.all_to_all(moved, "ctx", split_axis=0, concat_axis=0, tiled=True)
+        sent, *filters, skip_grad = long_convolutions(moved, spectrum, table, back, gain, chunk, filters)
+        sent = lax.all_to_all(sent, "ctx", split_axis=0, concat_axis=0, tiled=True)
+        output, partial, input_grad = gradients(
+            source, before, after, weights, incoming, later, feats, sent, skip, chunk, results
+        )
+        results = (output, input_grad)
+        skips.append(skip_grad)
+        partial = lax.all_to_all(partial, "ctx", split_axis=0, concat_axis=0, tiled=True)
+        summed = jnp.sum(partial.astype(F32), axis=0, keepdims=True).astype(BF16)
+        everyone = jnp.broadcast_to(summed, partial.shape)
+        everyone = lax.all_to_all(everyone, "ctx", split_axis=0, concat_axis=0, tiled=True)
+        partials.append(everyone[:, :, :TAPS].transpose(2, 1, 0, 3).astype(F32))
+    kern_grad = jnp.stack(partials, axis=3).reshape(TAPS, feats_all)
+    skip_grad = jnp.concatenate(skips, axis=1)
+    return (results[0][None], results[1][None], kern_grad[None], filters[0][None], skip_grad)
 
 
 def solution(mesh):

time: 249 us -> 370 us (1.49)
  Pallas kernels: 42.5 us -> 215 us
  waiting for transfers between devices: 132 us -> 72.3 us
  starting transfers between devices: 26.5 us -> 71.1 us
  blocking collectives: 22 us -> 0 us
  local copies, waits for them, and re-layouts: 24 us -> 7.05 us
    pallas_call x4 -> x11, Pallas kernels: 42.5 us -> 215 us  [the longest x4 133 us: pick_chunk(): pl.pallas_call(functools.partial(pick_kernel, chunk), out_shape=pltpu.HBM...]
    ppermute x2 -> x4, waiting for transfers between devices: 87.3 us -> 0.01 us  [passed_along(): return lax.ppermute(value, axis, pairs)]
    all_to_all x2 -> x0, blocking collectives: 22 us -> none  [the longest x1 12.3 us: on_device(): lax.all_to_all(partial, 'ctx', split_axis=0, concat_axis=0, tiled=True)]
    all_to_all x0 -> x4, starting transfers between devices: none -> 18.8 us  [the longest x2 10.9 us: on_device(): lax.all_to_all(partial, 'ctx', split_axis=0, concat_axis=0, tiled=True)]
    unnamed x35 -> x13, local copies, waits for them, and re-layouts: 20.7 us -> 2.04 us
    all_to_all x1 -> x2, waiting for transfers between devices: 0.01 us -> 14.5 us  [on_device(): sent = lax.all_to_all(sent, 'ctx', split_axis=0, concat_axis=0, tiled=True)]
    all_to_all x0 -> x4, waiting for transfers between devices: none -> 11.2 us  [the longest x2 5.83 us: on_device(): lax.all_to_all(partial, 'ctx', split_axis=0, concat_axis=0, tiled=True)]
    ppermute x3 -> x6, starting transfers between devices: 8.71 us -> 16.2 us  [from_behind(): return lax.ppermute(block, axis, route)]
  transfers between devices with their start and end apart: 7 -> 18, of which waited for: 4 -> 8; matrix products, arithmetic and copies ran while one was open for 1% -> 1% of each run, Pallas kernels for 2% -> 45%
where the time goes in v2:
time: 370 us; the launch traced here: 367 us
  Pallas kernels  215 us (58%)
  waiting for transfers between devices  72.3 us (20%)
  starting transfers between devices  71.1 us (19%)
  local copies, waits for them, and re-layouts  7.05 us (2%)
    pallas_call x4, Pallas kernels, pick_chunk(): pl.pallas_call(functools.partial(pick_kernel, chunk), out_shape=pltpu.HBM...  133 us
    pallas_call x2, Pallas kernels, long_convolutions(): pl.pallas_call(long_kernel, input_output_aliases={5: 1} if earlier else {...  28.5 us
    ppermute x6, waiting for transfers between devices, from_behind(): return lax.ppermute(block, axis, route)  25.7 us
    pallas_call x2, Pallas kernels, gradients(): pl.pallas_call(functools.partial(gradient_kernel, chunk), input_output_al...  25.4 us
    all_to_all x2, waiting for transfers between devices, on_device(): lax.all_to_all(moved, 'ctx', split_axis=0, concat_axis=0, tiled=True)  20.9 us
    pallas_call x2, Pallas kernels, featurize(): pl.pallas_call(feature_kernel, out_shape=(pltpu.HBM((groups, 2, rows, cha...  19.2 us
    ppermute x6, starting transfers between devices, from_behind(): return lax.ppermute(block, axis, route)  16.2 us
    all_to_all x2, waiting for transfers between devices, on_device(): sent = lax.all_to_all(sent, 'ctx', split_axis=0, concat_axis=0, tiled=True)  14.5 us
  transfers between devices with their start and end apart: 18, of which 8 were waited for; matrix products, arithmetic and copies ran while one was open for 1% of the time, Pallas kernels for 45%

profile of v2, /device:TPU:1, one launch (start us, length us, event | category | flops | bytes accessed | tf_op | source)
XLA Modules:
  0.0 366.8 jit_solution(10027422521645100164)
XLA Ops:
  0.6 49.2 %pick_chunk.6 = bf16[128,6144]{1,0:T(8,128)(2,1)} custom-call(bf16[128,12288]{1,0:T(8,128)(2,1)} %bitcast.34), custom_call_target="tpu_custom_call" | custom-call | bytes 3145728 | tf_op jit(solution)/shard_map/pick_chunk/pallas_call | solution.py:170
  49.8 4.5 %collective-permute-start = (bf16[128,6144]{1,0:T(8,128)(2,1)}, bf16[128,6144]{1,0:T(8,128)(2,1)S(1)}, u32[]{:S(2)}, u32[]{:S(2)}) collective-permute-start(bf16[128,6144]{1,0:T(8,128)(2,1)} %pick_chunk.6), channel_id=1, source_target_pairs={{0,16},{16,32},{32,48},{48,64},{64,80},{80,96},{96,112},{112,0},{1... | collective-permute-start | bytes 4718600 | tf_op jit(solution)/shard_map/ppermute | solution.py:29
  54.3 17.1 %pick_chunk.7 = bf16[128,2048]{1,0:T(8,128)(2,1)} custom-call(bf16[128,4096]{1,0:T(8,128)(2,1)} %bitcast.36), custom_call_target="tpu_custom_call" | custom-call | bytes 1048576 | tf_op jit(solution)/shard_map/pick_chunk/pallas_call | solution.py:170
  71.4 2.3 collective-permute-start.1
  73.7 49.2 %pick_chunk.4 = bf16[128,6144]{1,0:T(8,128)(2,1)} custom-call(bf16[128,12288]{1,0:T(8,128)(2,1)} %bitcast.35), custom_call_target="tpu_custom_call" | custom-call | bytes 3145728 | tf_op jit(solution)/shard_map/pick_chunk/pallas_call | solution.py:170
  122.9 0.0 copy-start.2
  122.9 17.1 %pick_chunk.5 = bf16[128,2048]{1,0:T(8,128)(2,1)} custom-call(bf16[128,4096]{1,0:T(8,128)(2,1)} %bitcast.37), custom_call_target="tpu_custom_call" | custom-call | bytes 1048576 | tf_op jit(solution)/shard_map/pick_chunk/pallas_call | solution.py:170
  140.1 0.8 collective-permute-start.2
  140.9 4.6 %collective-permute-start.7 = (bf16[8,6144]{1,0:T(8,128)(2,1)S(1)}, bf16[8,6144]{1,0:T(8,128)(2,1)S(1)}, u32[]{:S(2)}, u32[]{:S(2)}) collective-permute-start(bf16[8,6144]{1,0:T(8,128)(2,1)S(1)} %get-tuple-element.61), channel_id=1, source_target_pairs={{0,1},{1,2},{2,3},{3,4},{4,5},{5,6},{6,7},{7,8},{8,9},{9,10},{10,1... | collective-permute-start | bytes 294920 | tf_op jit(solution)/shard_map/ppermute | solution.py:35
  145.6 1.0 copy.33
  146.5 0.7 collective-permute-done.7.refs_3_.refs_4_.refs_5_
  147.2 9.3 %featurize.3 = (bf16[16,2,128,128]{3,2,1,0:T(8,128)(2,1)}, f32[3,128,2048]{2,1,0:T(8,128)}) custom-call(bf16[128,6144]{1,0:T(8,128)(2,1)S(1)} %collective-permute-done.refs_0_.refs_1_.refs_2_, bf16[128,6144]{1,0:T(8,128)(2,1)S(1)} %collective-permute-done.refs_0_.refs_1_.refs_2_, bf16[128,6144]{1,0:T(8,128)(2,1)S(1)} %collective-permute-done.refs_0_.refs_1_.refs_2_, ...), custom_call_target="tpu_custom_call" | custom-call | flops 11796480 | bytes 6291456 | tf_op jit(solution)/shard_map/featurize/pallas_call | solution.py:228
  156.4 6.2 %all-to-all-start.1 = ((bf16[16,2,128,128]{3,2,1,0:T(8,128)(2,1)}), bf16[16,2,128,128]{3,2,1,0:T(8,128)(2,1)}, u32[]{:S(2)}, u32[]{:S(2)}) async-start(bf16[16,2,128,128]{3,2,1,0:T(8,128)(2,1)} %get-tuple-element.31), calls=%async_computation.1 | async-start | bytes 2097152 | tf_op jit(solution)/shard_map/all_to_all | solution.py:539
  162.6 9.0 %filter_spectrum.1.spec_ref = f32[8,512,256]{2,1,0:T(8,128)} custom-call(bf16[256,2048]{1,0:T(8,128)(2,1)} %bitcast.40, bf16[8,512,512]{2,1,0:T(8,128)(2,1)} %constant.18.clone.table_ref), custom_call_target="tpu_custom_call" | custom-call | flops 1073741824 | bytes 10485760 | tf_op jit(solution)/shard_map/filter_spectrum/pallas_call | solution.py:133
  171.6 1.2 constant_dynamic-slice_fusion.gain_ref
  172.8 5.6 %collective-permute-start.5 = (bf16[128,2048]{1,0:T(8,128)(2,1)}, bf16[128,2048]{1,0:T(8,128)(2,1)}, u32[]{:S(2)}, u32[]{:S(2)}) collective-permute-start(bf16[128,2048]{1,0:T(8,128)(2,1)} %pick_chunk.5), channel_id=1, source_target_pairs={{0,112},{16,0},{32,16},{48,32},{64,48},{80,64},{96,80},{112,96},{1... | collective-permute-start | bytes 1572872 | tf_op jit(solution)/shard_map/ppermute | solution.py:29
  178.5 20.9 %all-to-all-done.1.moved_ref = bf16[16,2,128,128]{3,2,1,0:T(8,128)(2,1)} async-done(((bf16[16,2,128,128]{3,2,1,0:T(8,128)(2,1)}), bf16[16,2,128,128]{3,2,1,0:T(8,128)(2,1)}, u32[]{:S(2)}, u32[]{:S(2)}) %all-to-all-start.1) | async-done | bytes 1048608 | tf_op jit(solution)/shard_map/all_to_all | solution.py:539
  199.4 14.2 %long_convolutions.2 = (bf16[16,2,136,128]{3,2,1,0:T(8,128)(2,1)}, f32[256,2048]{1,0:T(8,128)}, f32[1,128]{1,0:T(1,128)}) custom-call(bf16[16,2,128,128]{3,2,1,0:T(8,128)(2,1)} %all-to-all-done.1.moved_ref, f32[8,512,256]{2,1,0:T(8,128)} %filter_spectrum.1.spec_ref, bf16[8,512,512]{2,1,0:T(8,128)(2,1)} %constant.18.clone.table_ref, ...), custom_call_target="tpu_custom_call" | custom-call | flops 2684354560 | bytes 20971520 | tf_op jit(solution)/shard_map/long_convolutions/pallas_call | solution.py:337
  213.6 5.1 %all-to-all-start.3 = ((bf16[16,2,136,128]{3,2,1,0:T(8,128)(2,1)}), bf16[16,2,136,128]{3,2,1,0:T(8,128)(2,1)}, u32[]{:S(2)}, u32[]{:S(2)}) async-start(bf16[16,2,136,128]{3,2,1,0:T(8,128)(2,1)} %get-tuple-element.35), calls=%async_computation.3 | async-start | bytes 2228224 | tf_op jit(solution)/shard_map/all_to_all | solution.py:541
  218.7 0.0 collective-permute-done.2.refs_0_.refs_1_.refs_2_
  218.7 3.5 collective-permute-start.3
  222.2 11.0 %collective-permute-done.3.refs_3_.refs_4_.refs_5_ = bf16[8,6144]{1,0:T(8,128)(2,1)S(1)} collective-permute-done((bf16[8,6144]{1,0:T(8,128)(2,1)S(1)}, bf16[8,6144]{1,0:T(8,128)(2,1)S(1)}, u32[]{:S(2)}, u32[]{:S(2)}) %collective-permute-start.3) | collective-permute-done | bytes 98336 | tf_op jit(solution)/shard_map/ppermute | solution.py:35
  233.2 9.9 %featurize.2 = (bf16[16,2,128,128]{3,2,1,0:T(8,128)(2,1)}, f32[3,128,2048]{2,1,0:T(8,128)}) custom-call(bf16[128,6144]{1,0:T(8,128)(2,1)S(1)} %collective-permute-done.2.refs_0_.refs_1_.refs_2_, bf16[128,6144]{1,0:T(8,128)(2,1)S(1)} %collective-permute-done.2.refs_0_.refs_1_.refs_2_, bf16[128,6144]{1,0:T(8,128)(2,1)S(1)} %collective-permute-done.2.refs_0_.refs_1_.refs_2_, ...), custom_call_target="tpu_custom_call" | custom-call | flops 11796480 | bytes 6291456 | tf_op jit(solution)/shard_map/featurize/pallas_call | solution.py:228
  243.2 6.0 %all-to-all-start = ((bf16[16,2,128,128]{3,2,1,0:T(8,128)(2,1)}), bf16[16,2,128,128]{3,2,1,0:T(8,128)(2,1)}, u32[]{:S(2)}, u32[]{:S(2)}) async-start(bf16[16,2,128,128]{3,2,1,0:T(8,128)(2,1)} %get-tuple-element.28), calls=%async_computation | async-start | bytes 2097152 | tf_op jit(solution)/shard_map/all_to_all | solution.py:539
  249.1 2.1 collective-permute-start.8
  251.2 0.8 slice.29
  251.9 1.9 collective-permute-start.9
  253.9 10.8 %collective-permute-done.9.refs_13_ = bf16[8,2048]{1,0:T(8,128)(2,1)S(1)} collective-permute-done((bf16[8,2048]{1,0:T(8,128)(2,1)S(1)}, bf16[8,2048]{1,0:T(8,128)(2,1)S(1)}, u32[]{:S(2)}, u32[]{:S(2)}) %collective-permute-start.9) | collective-permute-done | bytes 32800 | tf_op jit(solution)/shard_map/ppermute | solution.py:35
  264.7 1.0 copy-done.1
  265.7 12.9 %featurizer_gradients.2 = (bf16[128,4096]{1,0:T(8,128)(2,1)}, bf16[16,3,8,128]{3,2,1,0:T(8,128)(2,1)}, bf16[128,12288]{1,0:T(8,128)(2,1)}) custom-call(bf16[128,6144]{1,0:T(8,128)(2,1)S(1)} %collective-permute-done.refs_0_.refs_1_.refs_2_, bf16[128,6144]{1,0:T(8,128)(2,1)S(1)} %collective-permute-done.refs_0_.refs_1_.refs_2_, ...), custom_call_target="tpu_custom_call" | custom-call | flops 26214400 | bytes 8388608 | tf_op jit(solution)/shard_map/featurizer_gradients/pallas_call | solution.py:466
  278.6 4.6 %all-to-all-start.4 = ((bf16[16,3,8,128]{3,2,1,0:T(8,128)(2,1)}), bf16[16,3,8,128]{3,2,1,0:T(8,128)(2,1)S(1)}, u32[]{:S(2)}, u32[]{:S(2)}) async-start(bf16[16,3,8,128]{3,2,1,0:T(8,128)(2,1)} %get-tuple-element.40), calls=%async_computation.4 | async-start | bytes 196608 | tf_op jit(solution)/shard_map/all_to_all | solution.py:547
  283.2 14.3 %long_convolutions.3 = (bf16[16,2,136,128]{3,2,1,0:T(8,128)(2,1)}, f32[256,2048]{1,0:T(8,128)}, f32[1,128]{1,0:T(1,128)}) custom-call(bf16[16,2,128,128]{3,2,1,0:T(8,128)(2,1)} %all-to-all-done.moved_ref, f32[8,512,256]{2,1,0:T(8,128)} %filter_spectrum.1.spec_ref, bf16[8,512,512]{2,1,0:T(8,128)(2,1)} %constant.18.clone.table_ref, ...), custom_call_target="tpu_custom_call", output_to_operand_aliasing={{1}: (5, {})} | custom-call | flops 2684354560 | bytes 20971520 | tf_op jit(solution)/shard_map/long_convolutions/pallas_call | solution.py:337
  297.5 5.7 %all-to-all-start.2 = ((bf16[16,2,136,128]{3,2,1,0:T(8,128)(2,1)}), bf16[16,2,136,128]{3,2,1,0:T(8,128)(2,1)S(1)}, u32[]{:S(2)}, u32[]{:S(2)}) async-start(bf16[16,2,136,128]{3,2,1,0:T(8,128)(2,1)} %get-tuple-element.33), calls=%async_computation.2 | async-start | bytes 2228224 | tf_op jit(solution)/shard_map/all_to_all | solution.py:541
  303.3 2.0 collective-permute-start.4
  305.3 14.5 %all-to-all-done.2.refs_15_ = bf16[16,2,136,128]{3,2,1,0:T(8,128)(2,1)S(1)} async-done(((bf16[16,2,136,128]{3,2,1,0:T(8,128)(2,1)}), bf16[16,2,136,128]{3,2,1,0:T(8,128)(2,1)S(1)}, u32[]{:S(2)}, u32[]{:S(2)}) %all-to-all-start.2) | async-done | bytes 1114144 | tf_op jit(solution)/shard_map/all_to_all | solution.py:541
  319.8 0.7 broadcast_in_dim.23
  320.5 4.0 %all-to-all-start.5 = ((bf16[16,3,8,128]{3,2,1,0:T(8,128)(2,1)}), bf16[16,3,8,128]{3,2,1,0:T(8,128)(2,1)S(1)}, u32[]{:S(2)}, u32[]{:S(2)}) async-start(bf16[16,3,8,128]{3,2,1,0:T(8,128)(2,1)} %broadcast_in_dim.23), calls=%async_computation.5 | async-start | bytes 196608 | tf_op jit(solution)/shard_map/all_to_all | solution.py:550
  324.5 0.8 slice.34
  325.3 2.1 collective-permute-start.6
  327.4 3.2 collective-permute-done.6.refs_13_
  330.6 12.6 %featurizer_gradients.3 = (bf16[128,4096]{1,0:T(8,128)(2,1)}, bf16[16,3,8,128]{3,2,1,0:T(8,128)(2,1)}, bf16[128,12288]{1,0:T(8,128)(2,1)}) custom-call(bf16[128,6144]{1,0:T(8,128)(2,1)S(1)} %collective-permute-done.2.refs_0_.refs_1_.refs_2_, ...), custom_call_target="tpu_custom_call", output_to_operand_aliasing={{0}: (17, {}), {2}: (18, {})} | custom-call | flops 26214400 | bytes 8388608 | tf_op jit(solution)/shard_map/featurizer_gradients/pallas_call | solution.py:466
  343.2 6.3 %all-to-all-start.6 = ((bf16[16,3,8,128]{3,2,1,0:T(8,128)(2,1)}), bf16[16,3,8,128]{3,2,1,0:T(8,128)(2,1)S(1)}, u32[]{:S(2)}, u32[]{:S(2)}) async-start(bf16[16,3,8,128]{3,2,1,0:T(8,128)(2,1)} %get-tuple-element.41), calls=%async_computation.6 | async-start | bytes 196608 | tf_op jit(solution)/shard_map/all_to_all | solution.py:547
  349.5 5.8 %all-to-all-done.6 = bf16[16,3,8,128]{3,2,1,0:T(8,128)(2,1)S(1)} async-done(((bf16[16,3,8,128]{3,2,1,0:T(8,128)(2,1)}), bf16[16,3,8,128]{3,2,1,0:T(8,128)(2,1)S(1)}, u32[]{:S(2)}, u32[]{:S(2)}) %all-to-all-start.6) | async-done | bytes 98336 | tf_op jit(solution)/shard_map/all_to_all | solution.py:547
  355.4 0.7 broadcast_in_dim.24
  356.0 3.9 %all-to-all-start.7 = ((bf16[16,3,8,128]{3,2,1,0:T(8,128)(2,1)}), bf16[16,3,8,128]{3,2,1,0:T(8,128)(2,1)S(1)}, u32[]{:S(2)}, u32[]{:S(2)}) async-start(bf16[16,3,8,128]{3,2,1,0:T(8,128)(2,1)} %broadcast_in_dim.24), calls=%async_computation.7 | async-start | bytes 196608 | tf_op jit(solution)/shard_map/all_to_all | solution.py:550
  359.9 0.6 pad_maximum_fusion
  360.5 5.3 %all-to-all-done.7 = bf16[16,3,8,128]{3,2,1,0:T(8,128)(2,1)S(1)} async-done(((bf16[16,3,8,128]{3,2,1,0:T(8,128)(2,1)}), bf16[16,3,8,128]{3,2,1,0:T(8,128)(2,1)S(1)}, u32[]{:S(2)}, u32[]{:S(2)}) %all-to-all-start.7) | async-done | bytes 98336 | tf_op jit(solution)/shard_map/all_to_all | solution.py:550
  365.9 0.9 copy.25
  (24 shorter events, 0.2 us)
Async XLA Ops:
  49.8 90.3 %collective-permute-start = (bf16[128,6144]{1,0:T(8,128)(2,1)}, bf16[128,6144]{1,0:T(8,128)(2,1)S(1)}, u32[]{:S(2)}, u32[]{:S(2)}) collective-permute-start(bf16[128,6144]{1,0:T(8,128)(2,1)} %pick_chunk.6), channel_id=1, source_target_pairs={{0,16},{16,32},{32,48},{48,64},{64,80},{80,96},{96,112},{112,0},{1... | collective-permute-start | bytes 4718600 | tf_op jit(solution)/shard_map/ppermute | solution.py:29
  71.4 68.6 %collective-permute-start.1 = (bf16[128,2048]{1,0:T(8,128)(2,1)}, bf16[128,2048]{1,0:T(8,128)(2,1)S(1)}, u32[]{:S(2)}, u32[]{:S(2)}) collective-permute-start(bf16[128,2048]{1,0:T(8,128)(2,1)} %pick_chunk.7), channel_id=1, source_target_pairs={{0,112},{16,0},{32,16},{48,32},{64,48},{80,64},{96,80},{112,96},{1... | collective-permute-start | bytes 1572872 | tf_op jit(solution)/shard_map/ppermute | solution.py:29
  122.9 22.6 %copy-start.2 = (f32[1,7,12288]{2,0,1:T(1,128)S(1)}, f32[1,7,12288]{2,0,1:T(1,128)}, u32[]{:S(2)}) copy-start(f32[1,7,12288]{2,0,1:T(1,128)} %param.9) | copy-start | bytes 1032196
  140.1 16.4 %copy-start = (bf16[128,2048]{1,0:T(8,128)(2,1)}, bf16[128,2048]{1,0:T(8,128)(2,1)S(1)}, u32[]{:S(2)}) copy-start(bf16[128,2048]{1,0:T(8,128)(2,1)S(1)} %collective-permute-done.1.refs_9_.refs_12_) | copy-start | bytes 1572868
  140.1 78.6 %collective-permute-start.2 = (bf16[128,6144]{1,0:T(8,128)(2,1)}, bf16[128,6144]{1,0:T(8,128)(2,1)S(1)}, u32[]{:S(2)}, u32[]{:S(2)}) collective-permute-start(bf16[128,6144]{1,0:T(8,128)(2,1)} %pick_chunk.4), channel_id=1, source_target_pairs={{0,16},{16,32},{32,48},{48,64},{64,80},{80,96},{96,112},{112,0},{1... | collective-permute-start | bytes 4718600 | tf_op jit(solution)/shard_map/ppermute | solution.py:29
  140.9 6.2 %collective-permute-start.7 = (bf16[8,6144]{1,0:T(8,128)(2,1)S(1)}, bf16[8,6144]{1,0:T(8,128)(2,1)S(1)}, u32[]{:S(2)}, u32[]{:S(2)}) collective-permute-start(bf16[8,6144]{1,0:T(8,128)(2,1)S(1)} %get-tuple-element.61), channel_id=1, source_target_pairs={{0,1},{1,2},{2,3},{3,4},{4,5},{5,6},{6,7},{7,8},{8,9},{9,10},{10,1... | collective-permute-start | bytes 294920 | tf_op jit(solution)/shard_map/ppermute | solution.py:35
  156.4 43.0 %all-to-all-start.1 = ((bf16[16,2,128,128]{3,2,1,0:T(8,128)(2,1)}), bf16[16,2,128,128]{3,2,1,0:T(8,128)(2,1)}, u32[]{:S(2)}, u32[]{:S(2)}) async-start(bf16[16,2,128,128]{3,2,1,0:T(8,128)(2,1)} %get-tuple-element.31), calls=%async_computation.1 | async-start | bytes 2097152 | tf_op jit(solution)/shard_map/all_to_all | solution.py:539
  172.8 49.4 %collective-permute-start.5 = (bf16[128,2048]{1,0:T(8,128)(2,1)}, bf16[128,2048]{1,0:T(8,128)(2,1)}, u32[]{:S(2)}, u32[]{:S(2)}) collective-permute-start(bf16[128,2048]{1,0:T(8,128)(2,1)} %pick_chunk.5), channel_id=1, source_target_pairs={{0,112},{16,0},{32,16},{48,32},{64,48},{80,64},{96,80},{112,96},{1... | collective-permute-start | bytes 1572872 | tf_op jit(solution)/shard_map/ppermute | solution.py:29
  213.6 29.6 %all-to-all-start.3 = ((bf16[16,2,136,128]{3,2,1,0:T(8,128)(2,1)}), bf16[16,2,136,128]{3,2,1,0:T(8,128)(2,1)}, u32[]{:S(2)}, u32[]{:S(2)}) async-start(bf16[16,2,136,128]{3,2,1,0:T(8,128)(2,1)} %get-tuple-element.35), calls=%async_computation.3 | async-start | bytes 2228224 | tf_op jit(solution)/shard_map/all_to_all | solution.py:541
  218.7 14.6 %collective-permute-start.3 = (bf16[8,6144]{1,0:T(8,128)(2,1)S(1)}, bf16[8,6144]{1,0:T(8,128)(2,1)S(1)}, u32[]{:S(2)}, u32[]{:S(2)}) collective-permute-start(bf16[8,6144]{1,0:T(8,128)(2,1)S(1)} %get-tuple-element.63), channel_id=1, source_target_pairs={{0,1},{1,2},{2,3},{3,4},{4,5},{5,6},{6,7},{7,8},{8,9},{9,10},{10,1... | collective-permute-start | bytes 294920 | tf_op jit(solution)/shard_map/ppermute | solution.py:35
  243.2 35.5 %all-to-all-start = ((bf16[16,2,128,128]{3,2,1,0:T(8,128)(2,1)}), bf16[16,2,128,128]{3,2,1,0:T(8,128)(2,1)}, u32[]{:S(2)}, u32[]{:S(2)}) async-start(bf16[16,2,128,128]{3,2,1,0:T(8,128)(2,1)} %get-tuple-element.28), calls=%async_computation | async-start | bytes 2097152 | tf_op jit(solution)/shard_map/all_to_all | solution.py:539
  249.1 15.6 %collective-permute-start.8 = (bf16[8,6144]{1,0:T(8,128)(2,1)S(1)}, bf16[8,6144]{1,0:T(8,128)(2,1)S(1)}, u32[]{:S(2)}, u32[]{:S(2)}) collective-permute-start(bf16[8,6144]{1,0:T(8,128)(2,1)S(1)} %get-tuple-element.60), channel_id=1, source_target_pairs={{1,0},{2,1},{3,2},{4,3},{5,4},{6,5},{7,6},{8,7},{9,8},{10,9},{11,1... | collective-permute-start | bytes 294920 | tf_op jit(solution)/shard_map/ppermute | solution.py:35
  251.9 12.8 %collective-permute-start.9 = (bf16[8,2048]{1,0:T(8,128)(2,1)S(1)}, bf16[8,2048]{1,0:T(8,128)(2,1)S(1)}, u32[]{:S(2)}, u32[]{:S(2)}) collective-permute-start(bf16[8,2048]{1,0:T(8,128)(2,1)S(1)} %slice.29), channel_id=1, source_target_pairs={{1,0},{2,1},{3,2},{4,3},{5,4},{6,5},{7,6},{8,7},{9,8},{10,9},{11,1... | collective-permute-start | bytes 98312 | tf_op jit(solution)/shard_map/ppermute | solution.py:35
  264.7 1.0 copy-start.1
  278.6 18.9 %all-to-all-start.4 = ((bf16[16,3,8,128]{3,2,1,0:T(8,128)(2,1)}), bf16[16,3,8,128]{3,2,1,0:T(8,128)(2,1)S(1)}, u32[]{:S(2)}, u32[]{:S(2)}) async-start(bf16[16,3,8,128]{3,2,1,0:T(8,128)(2,1)} %get-tuple-element.40), calls=%async_computation.4 | async-start | bytes 196608 | tf_op jit(solution)/shard_map/all_to_all | solution.py:547
  297.5 22.3 %all-to-all-start.2 = ((bf16[16,2,136,128]{3,2,1,0:T(8,128)(2,1)}), bf16[16,2,136,128]{3,2,1,0:T(8,128)(2,1)S(1)}, u32[]{:S(2)}, u32[]{:S(2)}) async-start(bf16[16,2,136,128]{3,2,1,0:T(8,128)(2,1)} %get-tuple-element.33), calls=%async_computation.2 | async-start | bytes 2228224 | tf_op jit(solution)/shard_map/all_to_all | solution.py:541
  303.3 27.3 %collective-permute-start.4 = (bf16[8,6144]{1,0:T(8,128)(2,1)S(1)}, bf16[8,6144]{1,0:T(8,128)(2,1)S(1)}, u32[]{:S(2)}, u32[]{:S(2)}) collective-permute-start(bf16[8,6144]{1,0:T(8,128)(2,1)S(1)} %get-tuple-element.62), channel_id=1, source_target_pairs={{1,0},{2,1},{3,2},{4,3},{5,4},{6,5},{7,6},{8,7},{9,8},{10,9},{11,1... | collective-permute-start | bytes 294920 | tf_op jit(solution)/shard_map/ppermute | solution.py:35
  320.5 22.7 %all-to-all-start.5 = ((bf16[16,3,8,128]{3,2,1,0:T(8,128)(2,1)}), bf16[16,3,8,128]{3,2,1,0:T(8,128)(2,1)S(1)}, u32[]{:S(2)}, u32[]{:S(2)}) async-start(bf16[16,3,8,128]{3,2,1,0:T(8,128)(2,1)} %broadcast_in_dim.23), calls=%async_computation.5 | async-start | bytes 196608 | tf_op jit(solution)/shard_map/all_to_all | solution.py:550
  325.3 5.3 %collective-permute-start.6 = (bf16[8,2048]{1,0:T(8,128)(2,1)S(1)}, bf16[8,2048]{1,0:T(8,128)(2,1)S(1)}, u32[]{:S(2)}, u32[]{:S(2)}) collective-permute-start(bf16[8,2048]{1,0:T(8,128)(2,1)S(1)} %slice.34), channel_id=1, source_target_pairs={{1,0},{2,1},{3,2},{4,3},{5,4},{6,5},{7,6},{8,7},{9,8},{10,9},{11,1... | collective-permute-start | bytes 98312 | tf_op jit(solution)/shard_map/ppermute | solution.py:35
  330.6 29.3 %copy-start.3 = (f32[1,128]{1,0:T(1,128)S(1)}, f32[1,128]{1,0:T(1,128)}, u32[]{:S(2)}) copy-start(f32[1,128]{1,0:T(1,128)} %get-tuple-element.43) | copy-start | bytes 1540
  330.6 29.3 %copy-start.4 = (f32[1,128]{1,0:T(1,128)S(1)}, f32[1,128]{1,0:T(1,128)}, u32[]{:S(2)}) copy-start(f32[1,128]{1,0:T(1,128)} %get-tuple-element.44) | copy-start | bytes 1540
  343.2 12.2 %all-to-all-start.6 = ((bf16[16,3,8,128]{3,2,1,0:T(8,128)(2,1)}), bf16[16,3,8,128]{3,2,1,0:T(8,128)(2,1)S(1)}, u32[]{:S(2)}, u32[]{:S(2)}) async-start(bf16[16,3,8,128]{3,2,1,0:T(8,128)(2,1)} %get-tuple-element.41), calls=%async_computation.6 | async-start | bytes 196608 | tf_op jit(solution)/shard_map/all_to_all | solution.py:547
  356.0 9.8 %all-to-all-start.7 = ((bf16[16,3,8,128]{3,2,1,0:T(8,128)(2,1)}), bf16[16,3,8,128]{3,2,1,0:T(8,128)(2,1)S(1)}, u32[]{:S(2)}, u32[]{:S(2)}) async-start(bf16[16,3,8,128]{3,2,1,0:T(8,128)(2,1)} %broadcast_in_dim.24), calls=%async_computation.7 | async-start | bytes 196608 | tf_op jit(solution)/shard_map/all_to_all | solution.py:550

commit v3 on v1

v3 whole, which is shorter than its diff:
```python
import math

import jax
import jax.numpy as jnp
import ml_dtypes
import numpy as np
from jax import lax
from jax.experimental import pallas as pl
from jax.experimental.pallas import tpu as pltpu
from jax.sharding import PartitionSpec as P

TAPS = 7
HALO = 8
EXTRA = 32
ROOT = math.sqrt(0.5)
F32 = jnp.float32
BF16 = jnp.bfloat16
MIB = 1 << 20


def in_hbm(*arrays):
    return [pltpu.with_memory_space_constraint(array, pltpu.HBM) for array in arrays]


def passed_along(value, axis, steps):
    count = lax.axis_size(axis)
    pairs = [(source, (source + steps) % count) for source in range(count)]
    return lax.ppermute(value, axis, pairs)


def handed_over(value, steps, partner):
    sections, groups = lax.axis_size("section"), lax.axis_size("ctx")
    pairs = [
        (section * groups + place, (section + steps) % sections * groups + (place ^ partner))
        for section in range(sections)
        for place in range(groups)
    ]
    return lax.ppermute(value, ("section", "ctx"), pairs)


def leaf_angles():
    angles = [math.pi / 2]
    for _ in range(3):
        angles = [half for angle in angles for half in (angle / 2, angle / 2 + math.pi)]
    return angles


def leaf_tables(length):
    leaf = length // 8
    order = np.arange(leaf)
    tables = []
    for angle in leaf_angles():
        phase = (angle + 2.0 * np.pi * order[:, None]) / leaf * order[None, :]
        real, imag = np.cos(phase), np.sin(phase)
        tables.append(np.block([[real, -imag], [imag, real]]))
    table = np.stack(tables)
    back = table.transpose(0, 2, 1) / length
    return table.astype(ml_dtypes.bfloat16), back.astype(ml_dtypes.bfloat16)


def turned(pair, angle):
    real, imag = pair
    cos, sin = math.cos(angle), math.sin(angle)
    return real * cos - imag * sin, real * sin + imag * cos


def split_rings(parts):
    low, high = [], []
    for lower, upper in zip(parts[:4], parts[4:]):
        scaled = upper * ROOT
        low.append((lower + scaled, scaled))
        high.append((lower - scaled, -scaled))
    rings = [(math.pi / 4, low), (math.pi / 4 + math.pi, high)]
    while len(rings[0][1]) > 1:
        finer = []
        for angle, pieces in rings:
            half = len(pieces) // 2
            plus, minus = [], []
            for lower, upper in zip(pieces[:half], pieces[half:]):
                real, imag = turned(upper, angle / 2)
                plus.append((lower[0] + real, lower[1] + imag))
                minus.append((lower[0] - real, lower[1] - imag))
            finer += [(angle / 2, plus), (angle / 2 + math.pi, minus)]
        rings = finer
    return [pieces[0] for _, pieces in rings]


def join_rings(leaves):
    angles = [math.pi / 4, math.pi / 4 + math.pi]
    angles = [half for angle in angles for half in (angle / 2, angle / 2 + math.pi)]
    groups = [[leaf] for leaf in leaves]
    while len(groups) > 2:
        merged = []
        for index in range(0, len(groups), 2):
            angle = angles[index // 2] if len(groups) == 8 else [math.pi / 4, math.pi / 4 + math.pi][index // 2]
            lower, upper = [], []
            for plus, minus in zip(groups[index], groups[index + 1]):
                lower.append((plus[0] + minus[0], plus[1] + minus[1]))
                upper.append(turned((plus[0] - minus[0], plus[1] - minus[1]), -angle / 2))
            merged.append(lower + upper)
        groups = merged
    lower, upper = [], []
    for plus, minus in zip(groups[0], groups[1]):
        lower.append(plus[0] + minus[0])
        upper.append(((plus[0] - minus[0]) + (plus[1] - minus[1])) * ROOT)
    return lower + upper


def filter_kernel(filt_ref, table_ref, spec_ref, rings):
    chans, length = filt_ref.shape
    leaf = length // 8
    step = pl.program_id(0)

    @pl.when(step == 0)
    def _():
        @pl.loop(0, chans // 16)
        def _(strip):
            rows = pl.ds(pl.multiple_of(strip * 16, 16), 16)
            for lane in range(0, leaf, 128):
                parts = [
                    filt_ref[rows, piece * leaf + lane : piece * leaf + lane + 128].astype(F32)
                    for piece in range(8)
                ]
                for index, (real, imag) in enumerate(split_rings(parts)):
                    rings[index, rows, lane : lane + 128] = real.astype(BF16)
                    rings[index, rows, leaf + lane : leaf + lane + 128] = imag.astype(BF16)

    spec_ref[0] = lax.dot_general(
        table_ref[0], rings[step], (((1,), (1,)), ((), ())), preferred_element_type=F32
    )


def filter_spectrum(filt, table):
    chans, length = filt.shape
    wide = length // 4
    return pl.pallas_call(
        filter_kernel,
        out_shape=pltpu.HBM((8, wide, chans), F32),
        grid=(8,),
        in_specs=[
            pl.BlockSpec((chans, length), lambda j: (0, 0)),
            pl.BlockSpec((1, wide, wide), lambda j: (j, 0, 0)),
        ],
        out_specs=pl.BlockSpec((1, wide, chans), lambda j: (j, 0, 0)),
        scratch_shapes=[pltpu.VMEM((8, chans, wide), BF16)],
        compiler_params=pltpu.CompilerParams(vmem_limit_bytes=12 * MIB),
        cost_estimate=pl.CostEstimate(
            flops=16 * wide * wide * chans, bytes_accessed=10 * MIB, transcendentals=0
        ),
        name="filter_spectrum",
    )(*in_hbm(filt, table))


def piece_kernel(me_ref, *refs):
    groups = len(refs) - 3
    step = pl.program_id(0)
    for partner in range(groups):

        @pl.when(step == partner)
        def _(partner=partner):
            for role in range(3):
                refs[3 + partner][role] = refs[role][...]


def pieces_for_owners(me, acts, groups):
    rows, feats_all = acts.shape
    chans = feats_all // 3 // groups
    return pl.pallas_call(
        piece_kernel,
        out_shape=[pltpu.HBM((3, rows, chans), BF16)] * groups,
        grid_spec=pltpu.PrefetchScalarGridSpec(
            num_scalar_prefetch=1,
            grid=(groups,),
            in_specs=[
                pl.BlockSpec((rows, chans), lambda k, me, role=role: (0, role * groups + (me[0] ^ k)))
                for role in range(3)
            ],
            out_specs=[pl.BlockSpec((3, rows, chans), lambda k, me: (0, 0, 0), pipeline_mode=pl.Buffered(1))] * groups,
        ),
        compiler_params=pltpu.CompilerParams(vmem_limit_bytes=8 * MIB),
        cost_estimate=pl.CostEstimate(
            flops=0, bytes_accessed=4 * rows * feats_all, transcendentals=0
        ),
        name="pieces_for_owners",
    )(me, *in_hbm(acts, acts, acts))


def split_kernel(wide_ref, pieces_ref):
    pieces_ref[0] = wide_ref[...]


def split_columns(array, groups):
    rows, width = array.shape
    return pl.pallas_call(
        split_kernel,
        out_shape=pltpu.HBM((groups, rows, width // groups), array.dtype),
        grid=(groups,),
        in_specs=[pl.BlockSpec((rows, width // groups), lambda d: (0, d))],
        out_specs=pl.BlockSpec((1, rows, width // groups), lambda d: (d, 0, 0)),
        compiler_params=pltpu.CompilerParams(vmem_limit_bytes=4 * MIB),
        cost_estimate=pl.CostEstimate(flops=0, bytes_accessed=4 * rows * width, transcendentals=0),
        name="split_columns",
    )(*in_hbm(array))


def fetch_pieces(me_ref, pieces, source, sems):
    for partner, piece in enumerate(pieces):
        block = me_ref[0] ^ partner
        pltpu.make_async_copy(piece, source.at[block], sems.at[block]).start()


def feature_kernel(me_ref, *refs):
    groups = len(refs) - 7
    pieces = refs[:groups]
    taps_ref, incoming_ref, moved_ref, feats_ref, source, held, sems = refs[groups:]
    _, rows, chans = incoming_ref.shape
    step = pl.program_id(0)

    @pl.when(step == 0)
    def _():
        fetch_pieces(me_ref, pieces, source, sems)
        held[:, :, rows:, :] = jnp.zeros((3, chans // 128, HALO, 128), F32)

    pltpu.make_async_copy(pieces[0], source.at[step], sems.at[step]).wait()
    for part in range(chans // 128):
        lanes = slice(part * 128, part * 128 + 128)
        taps = []
        for role in range(3):
            held[role, part, 0:HALO, :] = held[role, part, rows : rows + HALO, :]
            held[role, part, HALO:, :] = source[step, role, :, lanes].astype(F32)
            taps.append([taps_ref[role, tap : tap + 1, lanes] for tap in range(TAPS)])
        for row in range(0, rows, 16):
            span = slice(row, row + 16)
            features = []
            for role in range(3):
                total = taps[role][0] * held[role, part, HALO + row : HALO + row + 16, :]
                for tap in range(1, TAPS):
                    total = total + taps[role][tap] * held[role, part, HALO + row - tap : HALO + row - tap + 16, :]
                feats_ref[0, role, span, lanes] = total
                features.append(total)
            query, keyed, value = features
            moved_ref[0, 0, span, lanes] = (keyed * value).astype(BF16)
            moved_ref[0, 1, span, lanes] = (incoming_ref[0, span, lanes].astype(F32) * query).astype(BF16)


def featurize(me, pieces, taps, incoming):
    groups, rows, chans = incoming.shape
    return pl.pallas_call(
        feature_kernel,
        out_shape=(
            pltpu.HBM((groups, 2, rows, chans), BF16),
            pltpu.HBM((groups, 3, rows, chans), F32),
        ),
        grid=(groups,),
        in_specs=[pl.BlockSpec(memory_space=pltpu.SMEM)]
        + [pl.BlockSpec(memory_space=pl.ANY)] * groups
        + [
            pl.BlockSpec((3, HALO, chans), lambda p: (0, 0, 0)),
            pl.BlockSpec((1, rows, chans), lambda p: (p, 0, 0)),
        ],
        out_specs=(
            pl.BlockSpec((1, 2, rows, chans), lambda p: (p, 0, 0, 0)),
            pl.BlockSpec((1, 3, rows, chans), lambda p: (p, 0, 0, 0)),
        ),
        scratch_shapes=[
            pltpu.VMEM((groups, 3, rows, chans), BF16),
            pltpu.VMEM((3, chans // 128, HALO + rows, 128), F32),
            pltpu.SemaphoreType.DMA((groups,)),
        ],
        compiler_params=pltpu.CompilerParams(vmem_limit_bytes=12 * MIB),
        cost_estimate=pl.CostEstimate(
            flops=45 * groups * rows * chans, bytes_accessed=24 * groups * rows * chans, transcendentals=0
        ),
        name="featurize",
    )(me, *pieces, taps, incoming)


def long_kernel(
    moved_ref, spec_ref, table_ref, back_ref, gain_ref, sent_ref, filt_ref, skip_ref, rings, products, joined, turned_ref
):
    groups, _, rows, chans = moved_ref.shape
    leaf = groups * rows // 8
    per_piece = leaf // rows
    step = pl.program_id(0)

    @pl.when(step == 0)
    def _():
        @pl.loop(0, rows // 16)
        def _(strip):
            inside = pl.ds(pl.multiple_of(strip * 16, 16), 16)
            for part in range(per_piece):
                real_rows = pl.ds(pl.multiple_of(part * rows + strip * 16, 16), 16)
                imag_rows = pl.ds(pl.multiple_of(leaf + part * rows + strip * 16, 16), 16)
                for kind in range(2):
                    for lane in range(0, chans, 128):
                        lanes = slice(lane, lane + 128)
                        parts = [
                            moved_ref[piece * per_piece + part, kind, inside, lanes].astype(F32)
                            for piece in range(8)
                        ]
                        into = slice(kind * chans + lane, kind * chans + lane + 128)
                        for index, (real, imag) in enumerate(split_rings(parts)):
                            rings[index, real_rows, into] = real.astype(BF16)
                            rings[index, imag_rows, into] = imag.astype(BF16)

    both = jnp.dot(table_ref[0], rings[step], preferred_element_type=F32)
    g_real, g_imag = both[:leaf, :chans], both[leaf:, :chans]
    d_real, d_imag = both[:leaf, chans:], both[leaf:, chans:]
    f_real, f_imag = spec_ref[0, :leaf], spec_ref[0, leaf:]
    products[:leaf, 0:chans] = (g_real * f_real - g_imag * f_imag).astype(BF16)
    products[leaf:, 0:chans] = (g_real * f_imag + g_imag * f_real).astype(BF16)
    products[:leaf, chans : 2 * chans] = (d_real * f_real + d_imag * f_imag).astype(BF16)
    products[leaf:, chans : 2 * chans] = (d_imag * f_real - d_real * f_imag).astype(BF16)
    products[:leaf, 2 * chans :] = (d_real * g_real + d_imag * g_imag).astype(BF16)
    products[leaf:, 2 * chans :] = (d_imag * g_real - d_real * g_imag).astype(BF16)
    joined[step] = jnp.dot(back_ref[0], products[...], preferred_element_type=F32)

    @pl.when(step == 7)
    def _():
        skip_ref[...] = jnp.zeros_like(skip_ref)

        @pl.loop(0, rows // 16)
        def _(strip):
            inside = pl.ds(pl.multiple_of(strip * 16, 16), 16)
            for part in range(per_piece):
                real_rows = pl.ds(pl.multiple_of(part * rows + strip * 16, 16), 16)
                imag_rows = pl.ds(pl.multiple_of(leaf + part * rows + strip * 16, 16), 16)
                for lane in range(0, chans, 128):
                    lanes = slice(lane, lane + 128)
                    gain = gain_ref[0:1, lanes]
                    for kind in range(3):
                        column = slice(kind * chans + lane, kind * chans + lane + 128)
                        leaves = [
                            (joined[index, real_rows, column], joined[index, imag_rows, column])
                            for index in range(8)
                        ]
                        total = jnp.zeros((16, 128), F32)
                        for piece, result in enumerate(join_rings(leaves)):
                            owner = piece * per_piece + part
                            if kind == 0:
                                sent_ref[owner, 0, inside, lanes] = result.astype(BF16)
                            elif kind == 1:
                                grad = moved_ref[owner, 1, inside, lanes].astype(F32)
                                sent_ref[owner, 1, inside, lanes] = (result + gain * grad).astype(BF16)
                                total = total + grad * moved_ref[owner, 0, inside, lanes].astype(F32)
                            else:
                                into = pl.ds(pl.multiple_of(owner * rows + strip * 16, 16), 16)
                                turned_ref[into, lanes] = result
                        if kind == 1:
                            skip_ref[0:1, lanes] += jnp.sum(total, axis=0, keepdims=True)

        for piece in range(groups):
            span = slice(piece * rows, (piece + 1) * rows)
            filt_ref[:, span] = turned_ref[span, :].T


def long_convolutions(moved, spectrum, table, back, gain):
    groups, _, rows, chans = moved.shape
    length = groups * rows
    wide = length // 4
    whole = pl.Buffered(1)
    return pl.pallas_call(
        long_kernel,
        out_shape=(
            pltpu.HBM((groups, 2, rows, chans), BF16),
            pltpu.HBM((chans, length), F32),
            pltpu.HBM((1, chans), F32),
        ),
        grid=(8,),
        in_specs=[
            pl.BlockSpec(moved.shape, lambda j: (0, 0, 0, 0), pipeline_mode=whole),
            pl.BlockSpec((1, wide, chans), lambda j: (j, 0, 0)),
            pl.BlockSpec((1, wide, wide), lambda j: (j, 0, 0)),
            pl.BlockSpec((1, wide, wide), lambda j: (j, 0, 0)),
            pl.BlockSpec((1, chans), lambda j: (0, 0)),
        ],
        out_specs=(
            pl.BlockSpec((groups, 2, rows, chans), lambda j: (0, 0, 0, 0), pipeline_mode=whole),
            pl.BlockSpec((chans, length), lambda j: (0, 0), pipeline_mode=whole),
            pl.BlockSpec((1, chans), lambda j: (0, 0)),
        ),
        scratch_shapes=[
            pltpu.VMEM((8, wide, 2 * chans), BF16),
            pltpu.VMEM((wide, 3 * chans), BF16),
            pltpu.VMEM((8, wide, 3 * chans), F32),
            pltpu.VMEM((length, chans), F32),
        ],
        compiler_params=pltpu.CompilerParams(vmem_limit_bytes=38 * MIB),
        cost_estimate=pl.CostEstimate(
            flops=80 * wide * wide * chans, bytes_accessed=20 * MIB, transcendentals=0
        ),
        name="long_convolutions",
    )(*in_hbm(moved, spectrum, table, back, gain))


def gradient_kernel(me_ref, *refs):
    groups = len(refs) - 14
    pieces = refs[:groups]
    taps_ref, incoming_ref, feats_ref, back_ref, gain_ref, ready_hbm = refs[groups : groups + 6]
    source, grads, sums, slots, last, sems, slot_sems, last_sems = refs[groups + 6 :]
    _, rows, chans = incoming_ref.shape
    step = pl.program_id(0)
    block = groups - 1 - step
    slot = lax.rem(step, 2)

    def write_back(slot_at, block_at):
        return pltpu.make_async_copy(
            slots.at[slot_at], ready_hbm.at[block_at, pl.ds(0, 4 * rows)], slot_sems.at[slot_at]
        )

    @pl.when(step == 0)
    def _():
        fetch_pieces(me_ref, pieces, source, sems)
        grads[:, :, 0:HALO, :] = jnp.zeros((3, chans // 128, HALO, 128), F32)
        sums[...] = jnp.zeros_like(sums)

    @pl.when(step >= 2)
    def _():
        write_back(slot, block + 2).wait()

    pltpu.make_async_copy(pieces[0], source.at[block], sems.at[block]).wait()
    for part in range(chans // 128):
        lanes = slice(part * 128, part * 128 + 128)
        gain = gain_ref[0:1, lanes]
        for role in range(3):
            grads[role, part, rows : rows + HALO, :] = grads[role, part, 0:HALO, :]
        for row in range(0, rows, 16):
            span = slice(row, row + 16)
            query, keyed, value = [feats_ref[0, role, span, lanes] for role in range(3)]
            gated = (keyed * value).astype(BF16).astype(F32)
            inner = back_ref[0, 0, span, lanes].astype(F32) + gain * gated
            through = back_ref[0, 1, span, lanes].astype(F32)
            grads[0, part, span, :] = incoming_ref[0, span, lanes].astype(F32) * inner
            grads[1, part, span, :] = through * value
            grads[2, part, span, :] = through * keyed
            slots[slot, span, lanes] = (query * inner).astype(BF16)
        for role in range(3):
            taps = [taps_ref[role, tap : tap + 1, lanes] for tap in range(TAPS)]
            parts = [jnp.zeros((16, 128), F32) for _ in range(TAPS)]
            for row in range(0, rows, 16):
                here = source[block, role, row : row + 16, lanes].astype(F32)
                total = jnp.zeros((16, 128), F32)
                for tap in range(TAPS):
                    ahead = grads[role, part, row + tap : row + tap + 16, :]
                    total = total + taps[tap] * ahead
                    parts[tap] = parts[tap] + here * ahead
                start = (1 + role) * rows + row
                slots[slot, start : start + 16, lanes] = total.astype(BF16)
            for tap in range(TAPS):
                sums[role, tap, :, lanes] += parts[tap][0:8] + parts[tap][8:16]

    write_back(slot, block).start()

    @pl.when(step == groups - 1)
    def _():
        rows_out = []
        for role in range(3):
            for tap in range(TAPS):
                rows_out.append(jnp.sum(sums[role, tap], axis=0, keepdims=True))
            rows_out.append(jnp.zeros((HALO - TAPS, chans), F32))
        rows_out.append(jnp.zeros((EXTRA - 3 * HALO, chans), F32))
        last[...] = jnp.concatenate(rows_out, axis=0).astype(BF16)
        copies = [
            pltpu.make_async_copy(last, ready_hbm.at[owner, pl.ds(4 * rows, EXTRA)], last_sems.at[owner])
            for owner in range(groups)
        ]
        for copy in copies:
            copy.start()
        write_back(1 - slot, block + 1).wait()
        write_back(slot, block).wait()
        for copy in copies:
            copy.wait()


def gradients(me, pieces, taps, incoming, feats, back, gain):
    groups, rows, chans = incoming.shape
    last = groups - 1
    return pl.pallas_call(
        gradient_kernel,
        out_shape=pltpu.HBM((groups, 4 * rows + EXTRA, chans), BF16),
        grid=(groups,),
        in_specs=[pl.BlockSpec(memory_space=pltpu.SMEM)]
        + [pl.BlockSpec(memory_space=pl.ANY)] * groups
        + [
            pl.BlockSpec((3, HALO, chans), lambda p: (0, 0, 0)),
            pl.BlockSpec((1, rows, chans), lambda p: (last - p, 0, 0)),
            pl.BlockSpec((1, 3, rows, chans), lambda p: (last - p, 0, 0, 0)),
            pl.BlockSpec((1, 2, rows, chans), lambda p: (last - p, 0, 0, 0)),
            pl.BlockSpec((1, chans), lambda p: (0, 0)),
        ],
        out_specs=pl.BlockSpec(memory_space=pl.ANY),
        scratch_shapes=[
            pltpu.VMEM((groups, 3, rows, chans), BF16),
            pltpu.VMEM((3, chans // 128, rows + HALO, 128), F32),
            pltpu.VMEM((3, TAPS, 8, chans), F32),
            pltpu.VMEM((2, 4 * rows, chans), BF16),
            pltpu.VMEM((EXTRA, chans), BF16),
            pltpu.SemaphoreType.DMA((groups,)),
            pltpu.SemaphoreType.DMA((2,)),
            pltpu.SemaphoreType.DMA((groups,)),
        ],
        compiler_params=pltpu.CompilerParams(vmem_limit_bytes=12 * MIB),
        cost_estimate=pl.CostEstimate(
            flops=100 * groups * rows * chans, bytes_accessed=32 * groups * rows * chans, transcendentals=0
        ),
        name="featurizer_gradients",
    )(me, *pieces, taps, incoming, *in_hbm(feats, back, gain))


def place_kernel(held_ref, output_ref, grad_ref):
    step = pl.program_id(0)
    chans = held_ref.shape[2]

    def place(into):
        for owner in range(held_ref.shape[0]):
            into[:, owner * chans : (owner + 1) * chans] = held_ref[owner]

    @pl.when(step < 4)
    def _():
        place(output_ref)

    @pl.when(step >= 4)
    def _():
        place(grad_ref)


def place_columns(held, rows):
    groups, _, chans = held.shape
    some = groups // 4
    return pl.pallas_call(
        place_kernel,
        out_shape=(
            pltpu.HBM((rows, groups * chans), BF16),
            pltpu.HBM((rows, 3 * groups * chans), BF16),
        ),
        grid=(16,),
        in_specs=[pl.BlockSpec((some, rows, chans), lambda i: (lax.rem(i, 4), lax.div(i, 4), 0))],
        out_specs=(
            pl.BlockSpec((rows, some * chans), lambda i: (0, jnp.minimum(i, 3))),
            pl.BlockSpec((rows, some * chans), lambda i: (0, jnp.maximum(i - 4, 0))),
        ),
        compiler_params=pltpu.CompilerParams(vmem_limit_bytes=4 * MIB),
        cost_estimate=pl.CostEstimate(
            flops=0, bytes_accessed=16 * groups * rows * chans, transcendentals=0
        ),
        name="place_columns",
    )(*in_hbm(held))


def on_device(acts, cots, kern, filt, skip):
    rows, feats_all = acts.shape[1:]
    groups = lax.axis_size("ctx")
    chans = filt.shape[1]
    place = lax.axis_index("ctx").astype(jnp.int32)
    me = place[None]

    pieces = pieces_for_owners(me, acts[0], groups)
    incoming, pieces = lax.optimization_barrier((split_columns(cots[0], groups), pieces))
    incoming = passed_along(incoming, "section", -1)
    pieces = [handed_over(piece, 1, partner) for partner, piece in enumerate(pieces)]
    half = groups // 2
    incoming, pieces[:half] = lax.optimization_barrier((incoming, pieces[:half]))
    incoming = lax.all_to_all(incoming, "ctx", split_axis=0, concat_axis=0, tiled=True)

    table, back = (jnp.asarray(one) for one in leaf_tables(rows * groups))
    spectrum = filter_spectrum(filt[0], table)
    gain = lax.dynamic_slice_in_dim(skip, place * chans, chans, axis=1)
    taps = kern[0].reshape(TAPS, 3, groups, chans)
    taps = lax.dynamic_index_in_dim(taps, place, axis=2, keepdims=False).transpose(1, 0, 2)
    taps = jnp.pad(taps, ((0, 0), (0, HALO - TAPS), (0, 0)))

    moved, feats = featurize(me, pieces, taps, incoming)
    sent, filt_grad, skip_grad = long_convolutions(moved, spectrum, table, back, gain)
    ready = gradients(me, pieces, taps, incoming, feats, sent, gain)
    ready = lax.all_to_all(ready, "ctx", split_axis=0, concat_axis=0, tiled=True)
    output, input_grad = place_columns(ready, rows)
    sums = ready[:, 4 * rows : 4 * rows + 3 * HALO].reshape(groups, 3, HALO, chans)[:, :, :TAPS]
    kern_grad = sums.transpose(2, 1, 0, 3).reshape(TAPS, feats_all).astype(F32)
    return (output[None], input_grad[None], kern_grad[None], filt_grad[None], skip_grad)


def solution(mesh):
    return jax.shard_map(
        on_device,
        mesh=mesh,
        in_specs=(
            P("section", "ctx", None),
            P("section", "ctx", None),
            P("section", None, None),
            P("section", "ctx", None),
            P("section", None),
        ),
        out_specs=(
            P("section", "ctx", None),
            P("section", "ctx", None),
            P("section", None, None),
            P("section", "ctx", None),
            P("section", "ctx"),
        ),
        check_vma=False,
    )
```

time: 249 us -> 261 us (1.048)
  waiting for transfers between devices: 132 us -> 45.4 us
  Pallas kernels: 42.5 us -> 89.6 us
  blocking collectives: 22 us -> 55.6 us
  starting transfers between devices: 26.5 us -> 53.5 us
  local copies, waits for them, and re-layouts: 24 us -> 11.4 us
    ppermute x2 -> x1, waiting for transfers between devices: 87.3 us -> 0.01 us  [passed_along(): return lax.ppermute(value, axis, pairs)]
    pallas_call x4 -> x7, Pallas kernels: 42.5 us -> 89.6 us  [the longest x1 20 us: long_convolutions(): pl.pallas_call(long_kernel, out_shape=(pltpu.HBM((groups, 2, rows, chans)...]
    ppermute x3 -> x16, starting transfers between devices: 8.71 us -> 42.9 us  [handed_over(): return lax.ppermute(value, ('section', 'ctx'), pairs)]
    all_to_all x2 -> x1, blocking collectives: 22 us -> 55.6 us  [on_device(): lax.all_to_all(ready, 'ctx', split_axis=0, concat_axis=0, tiled=True)]
    ppermute x3 -> x16, waiting for transfers between devices: 27.4 us -> 45.4 us  [handed_over(): return lax.ppermute(value, ('section', 'ctx'), pairs)]
    all_to_all x2 -> x1, waiting for transfers between devices: 17.8 us -> 0.01 us  [on_device(): lax.all_to_all(incoming, 'ctx', split_axis=0, concat_axis=0, tiled=True)]
    unnamed x35 -> x26, local copies, waits for them, and re-layouts: 20.7 us -> 8.75 us
    all_to_all x2 -> x1, starting transfers between devices: 11 us -> 3.89 us  [on_device(): lax.all_to_all(incoming, 'ctx', split_axis=0, concat_axis=0, tiled=True)]
  transfers between devices with their start and end apart: 7 -> 18, of which waited for: 4 -> 7; matrix products, arithmetic and copies ran while one was open for 1% -> 2% of each run, Pallas kernels for 2% -> 4%
where the time goes in v3:
time: 261 us; the launch traced here: 259 us
  Pallas kernels  89.6 us (34%)
  blocking collectives  55.6 us (21%)
  starting transfers between devices  53.5 us (20%)
  waiting for transfers between devices  45.4 us (17%)
  local copies, waits for them, and re-layouts  11.4 us (4%)
    all_to_all x1, blocking collectives, on_device(): lax.all_to_all(ready, 'ctx', split_axis=0, concat_axis=0, tiled=True)  55.6 us
    ppermute x16, waiting for transfers between devices, handed_over(): return lax.ppermute(value, ('section', 'ctx'), pairs)  45.4 us
    ppermute x16, starting transfers between devices, handed_over(): return lax.ppermute(value, ('section', 'ctx'), pairs)  42.9 us
    pallas_call x1, Pallas kernels, long_convolutions(): pl.pallas_call(long_kernel, out_shape=(pltpu.HBM((groups, 2, rows, chans)...  20 us
    pallas_call x1, Pallas kernels, gradients(): pl.pallas_call(gradient_kernel, out_shape=pltpu.HBM((groups, 4 * rows + E...  18.8 us
    pallas_call x1, Pallas kernels, featurize(): pl.pallas_call(feature_kernel, out_shape=(pltpu.HBM((groups, 2, rows, cha...  12.5 us
    pallas_call x1, Pallas kernels, place_columns(): pl.pallas_call(place_kernel, out_shape=(pltpu.HBM((rows, groups * chans),...  10.3 us
    pallas_call x1, Pallas kernels, pieces_for_owners(): pl.pallas_call(piece_kernel, out_shape=[pltpu.HBM((3, rows, chans), BF16)...  10 us
  transfers between devices with their start and end apart: 18, of which 7 were waited for; matrix products, arithmetic and copies ran while one was open for 2% of the time, Pallas kernels for 4%

profile of v3, /device:TPU:1, one launch (start us, length us, event | category | flops | bytes accessed | tf_op | source)
XLA Modules:
  0.0 258.9 jit_solution(2701199421000404077)
XLA Ops:
  0.6 0.0 copy-start
  0.7 8.9 %split_columns.1 = bf16[16,128,256]{2,1,0:T(8,128)(2,1)} custom-call(bf16[128,4096]{1,0:T(8,128)(2,1)} %bitcast.26), custom_call_target="tpu_custom_call" | custom-call | bytes 2097152 | tf_op jit(solution)/shard_map/split_columns/pallas_call | solution.py:194
  9.5 10.0 %pieces_for_owners.1 = (bf16[3,128,256]{2,1,0:T(8,128)(2,1)}, bf16[3,128,256]{2,1,0:T(8,128)(2,1)}, bf16[3,128,256]{2,1,0:T(8,128)(2,1)}, bf16[3,128,256]{2,1,0:...) custom-call(s32[1]{0:T(128)} %bitcast.me_ref, ...), custom_call_target="tpu_custom_call" | custom-call | bytes 6291456 | tf_op jit(solution)/shard_map/pieces_for_owners/pallas_call | solution.py:168
  19.6 6.7 %collective-permute-start = (bf16[16,128,256]{2,1,0:T(8,128)(2,1)S(1)}, bf16[16,128,256]{2,1,0:T(8,128)(2,1)}, u32[]{:S(2)}, u32[]{:S(2)}) collective-permute-start(bf16[16,128,256]{2,1,0:T(8,128)(2,1)S(1)} %copy-done.11), channel_id=1, source_target_pairs={{0,112},{16,0},{32,16},{48,32},{64,48},{80,64},{96,80},{112,96},{1... | collective-permute-start | bytes 3145736 | tf_op jit(solution)/shard_map/ppermute | solution.py:28
  26.2 2.8 %collective-permute-start.2 = (bf16[3,128,256]{2,1,0:T(8,128)(2,1)}, bf16[3,128,256]{2,1,0:T(8,128)(2,1)S(1)}, u32[]{:S(2)}, u32[]{:S(2)}) collective-permute-start(bf16[3,128,256]{2,1,0:T(8,128)(2,1)} %get-tuple-element.72), channel_id=1, source_target_pairs={{0,17},{1,16},{2,19},{3,18},{4,21},{5,20},{6,23},{7,22},{8,25},{9,... | collective-permute-start | bytes 589832 | tf_op jit(solution)/shard_map/ppermute | solution.py:38
  29.0 0.8 collective-permute-start.3
  29.9 3.4 %collective-permute-start.4 = (bf16[3,128,256]{2,1,0:T(8,128)(2,1)}, bf16[3,128,256]{2,1,0:T(8,128)(2,1)S(1)}, u32[]{:S(2)}, u32[]{:S(2)}) collective-permute-start(bf16[3,128,256]{2,1,0:T(8,128)(2,1)} %get-tuple-element.74), channel_id=1, source_target_pairs={{0,19},{1,18},{2,17},{3,16},{4,23},{5,22},{6,21},{7,20},{8,27},{9,... | collective-permute-start | bytes 589832 | tf_op jit(solution)/shard_map/ppermute | solution.py:38
  33.3 27.3 %collective-permute-done.1.refs_0_ = bf16[3,128,256]{2,1,0:T(8,128)(2,1)S(1)} collective-permute-done((bf16[3,128,256]{2,1,0:T(8,128)(2,1)}, bf16[3,128,256]{2,1,0:T(8,128)(2,1)S(1)}, u32[]{:S(2)}, u32[]{:S(2)}) %collective-permute-start.1) | collective-permute-done | bytes 196640 | tf_op jit(solution)/shard_map/ppermute | solution.py:38
  60.6 6.2 %collective-permute-start.5 = (bf16[3,128,256]{2,1,0:T(8,128)(2,1)}, bf16[3,128,256]{2,1,0:T(8,128)(2,1)S(1)}, u32[]{:S(2)}, u32[]{:S(2)}) collective-permute-start(bf16[3,128,256]{2,1,0:T(8,128)(2,1)} %get-tuple-element.75), channel_id=1, source_target_pairs={{0,20},{1,21},{2,22},{3,23},{4,16},{5,17},{6,18},{7,19},{8,28},{9,... | collective-permute-start | bytes 589832 | tf_op jit(solution)/shard_map/ppermute | solution.py:38
  66.8 4.5 %collective-permute-start.6 = (bf16[3,128,256]{2,1,0:T(8,128)(2,1)}, bf16[3,128,256]{2,1,0:T(8,128)(2,1)S(1)}, u32[]{:S(2)}, u32[]{:S(2)}) collective-permute-start(bf16[3,128,256]{2,1,0:T(8,128)(2,1)} %get-tuple-element.76), channel_id=1, source_target_pairs={{0,21},{1,20},{2,23},{3,22},{4,17},{5,16},{6,19},{7,18},{8,29},{9,... | collective-permute-start | bytes 589832 | tf_op jit(solution)/shard_map/ppermute | solution.py:38
  71.3 2.4 collective-permute-start.7
  73.7 3.1 %collective-permute-start.8 = (bf16[3,128,256]{2,1,0:T(8,128)(2,1)}, bf16[3,128,256]{2,1,0:T(8,128)(2,1)S(1)}, u32[]{:S(2)}, u32[]{:S(2)}) collective-permute-start(bf16[3,128,256]{2,1,0:T(8,128)(2,1)} %get-tuple-element.78), channel_id=1, source_target_pairs={{0,23},{1,22},{2,21},{3,20},{4,19},{5,18},{6,17},{7,16},{8,31},{9,... | collective-permute-start | bytes 589832 | tf_op jit(solution)/shard_map/ppermute | solution.py:38
  76.8 3.6 %collective-permute-done.6.refs_5_ = bf16[3,128,256]{2,1,0:T(8,128)(2,1)S(1)} collective-permute-done((bf16[3,128,256]{2,1,0:T(8,128)(2,1)}, bf16[3,128,256]{2,1,0:T(8,128)(2,1)S(1)}, u32[]{:S(2)}, u32[]{:S(2)}) %collective-permute-start.6) | collective-permute-done | bytes 196640 | tf_op jit(solution)/shard_map/ppermute | solution.py:38
  80.3 4.1 %collective-permute-done.7.refs_6_ = bf16[3,128,256]{2,1,0:T(8,128)(2,1)S(1)} collective-permute-done((bf16[3,128,256]{2,1,0:T(8,128)(2,1)}, bf16[3,128,256]{2,1,0:T(8,128)(2,1)S(1)}, u32[]{:S(2)}, u32[]{:S(2)}) %collective-permute-start.7) | collective-permute-done | bytes 196640 | tf_op jit(solution)/shard_map/ppermute | solution.py:38
  84.5 4.2 %collective-permute-done.8.refs_7_ = bf16[3,128,256]{2,1,0:T(8,128)(2,1)S(1)} collective-permute-done((bf16[3,128,256]{2,1,0:T(8,128)(2,1)}, bf16[3,128,256]{2,1,0:T(8,128)(2,1)S(1)}, u32[]{:S(2)}, u32[]{:S(2)}) %collective-permute-start.8) | collective-permute-done | bytes 196640 | tf_op jit(solution)/shard_map/ppermute | solution.py:38
  88.7 3.9 %all-to-all-start = ((bf16[16,128,256]{2,1,0:T(8,128)(2,1)}), bf16[16,128,256]{2,1,0:T(8,128)(2,1)S(1)}, u32[]{:S(2)}, u32[]{:S(2)}) async-start(bf16[16,128,256]{2,1,0:T(8,128)(2,1)} %collective-permute-done), calls=%async_computation | async-start | bytes 2097152 | tf_op jit(solution)/shard_map/all_to_all | solution.py:563
  92.6 1.7 collective-permute-start.9
  94.3 0.3 collective-permute-start.10
  94.6 3.9 %collective-permute-start.11 = (bf16[3,128,256]{2,1,0:T(8,128)(2,1)}, bf16[3,128,256]{2,1,0:T(8,128)(2,1)S(1)}, u32[]{:S(2)}, u32[]{:S(2)}) collective-permute-start(bf16[3,128,256]{2,1,0:T(8,128)(2,1)} %get-tuple-element.89), channel_id=1, source_target_pairs={{0,26},{1,27},{2,24},{3,25},{4,30},{5,31},{6,28},{7,29},{8,18},{9,... | collective-permute-start | bytes 589832 | tf_op jit(solution)/shard_map/ppermute | solution.py:38
  98.5 0.4 collective-permute-start.12
  98.8 5.6 %collective-permute-start.13 = (bf16[3,128,256]{2,1,0:T(8,128)(2,1)}, bf16[3,128,256]{2,1,0:T(8,128)(2,1)}, u32[]{:S(2)}, u32[]{:S(2)}) collective-permute-start(bf16[3,128,256]{2,1,0:T(8,128)(2,1)} %get-tuple-element.91), channel_id=1, source_target_pairs={{0,28},{1,29},{2,30},{3,31},{4,24},{5,25},{6,26},{7,27},{8,20},{9,... | collective-permute-start | bytes 589832 | tf_op jit(solution)/shard_map/ppermute | solution.py:38
  104.5 2.5 reduce
  107.0 1.8 copy.15
  108.8 0.9 constant_dynamic-slice_fusion.1
  109.8 0.8 collective-permute-start.14
  110.6 5.8 %collective-permute-start.15 = (bf16[3,128,256]{2,1,0:T(8,128)(2,1)}, bf16[3,128,256]{2,1,0:T(8,128)(2,1)S(1)}, u32[]{:S(2)}, u32[]{:S(2)}) collective-permute-start(bf16[3,128,256]{2,1,0:T(8,128)(2,1)} %get-tuple-element.93), channel_id=1, source_target_pairs={{0,30},{1,31},{2,28},{3,29},{4,26},{5,27},{6,24},{7,25},{8,22},{9,... | collective-permute-start | bytes 589832 | tf_op jit(solution)/shard_map/ppermute | solution.py:38
  116.3 1.3 collective-permute-start.16
  117.6 9.1 %filter_spectrum.1.spec_ref = f32[8,512,256]{2,1,0:T(8,128)} custom-call(bf16[256,2048]{1,0:T(8,128)(2,1)} %bitcast.25, bf16[8,512,512]{2,1,0:T(8,128)(2,1)} %constant.21.clone.table_ref), custom_call_target="tpu_custom_call" | custom-call | flops 1073741824 | bytes 10485760 | tf_op jit(solution)/shard_map/filter_spectrum/pallas_call | solution.py:136
  126.8 0.5 constant_dynamic-slice_fusion.gain_ref.refs_20_
  127.3 0.2 collective-permute-done.14.refs_13_
  127.5 0.7 copy-done.1
  128.2 1.9 collective-permute-done.15.refs_14_
  130.1 0.7 copy-done.4
  130.7 4.1 %collective-permute-done.16.refs_15_ = bf16[3,128,256]{2,1,0:T(8,128)(2,1)S(1)} collective-permute-done((bf16[3,128,256]{2,1,0:T(8,128)(2,1)}, bf16[3,128,256]{2,1,0:T(8,128)(2,1)S(1)}, u32[]{:S(2)}, u32[]{:S(2)}) %collective-permute-start.16) | collective-permute-done | bytes 196640 | tf_op jit(solution)/shard_map/ppermute | solution.py:38
  134.8 0.7 copy-done.7
  135.5 0.9 copy-done.2
  136.5 0.9 copy-done.5
  137.4 0.9 copy-done.8
  138.3 12.5 %featurize.1 = (bf16[16,2,128,256]{3,2,1,0:T(8,128)(2,1)}, f32[16,3,128,256]{3,2,1,0:T(8,128)}) custom-call(s32[1]{0:T(128)} %bitcast.me_ref, bf16[3,128,256]{2,1,0:T(8,128)(2,1)S(1)} %collective-permute-done.1.refs_0_, bf16[3,128,256]{2,1,0:T(8,128)(2,1)S(1)} %collective-permute-done.2.refs_1_, bf16[3,128,256]{2,1,0:T(8,128)(2,1)S(1)} %collective-permute-done.3.refs_2_, ...), custom_call_target="tpu_custom_call" | custom-call | flops 23592960 | bytes 12582912 | tf_op jit(solution)/shard_map/featurize/pallas_call | solution.py:248
  150.8 0.0 copy-start.3
  150.8 0.0 copy-start.6
  150.9 20.0 %long_convolutions.1 = (bf16[16,2,128,256]{3,2,1,0:T(8,128)(2,1)}, f32[256,2048]{1,0:T(8,128)}, f32[1,256]{1,0:T(1,128)}) custom-call(bf16[16,2,128,256]{3,2,1,0:T(8,128)(2,1)} %get-tuple-element.97.moved_ref, f32[8,512,256]{2,1,0:T(8,128)} %filter_spectrum.1.spec_ref, bf16[8,512,512]{2,1,0:T(8,128)(2,1)} %constant.21.clone.table_ref, ...), custom_call_target="tpu_custom_call" | custom-call | flops 5368709120 | bytes 20971520 | tf_op jit(solution)/shard_map/long_convolutions/pallas_call | solution.py:362
  170.8 18.8 %featurizer_gradients.1 = bf16[16,544,256]{2,1,0:T(8,128)(2,1)} custom-call(s32[1]{0:T(128)} %bitcast.me_ref, bf16[3,128,256]{2,1,0:T(8,128)(2,1)S(1)} %collective-permute-done.1.refs_0_, bf16[3,128,256]{2,1,0:T(8,128)(2,1)S(1)} %collective-permute-done.2.refs_1_, bf16[3,128,256]{2,1,0:T(8,128)(2,1)S(1)} %collective-permute-done.3.refs_2_, ...), custom_call_target="tpu_custom_call" | custom-call | flops 52428800 | bytes 16777216 | tf_op jit(solution)/shard_map/featurizer_gradients/pallas_call | solution.py:478
  189.7 55.6 %all_to_all.10.held_ref = bf16[16,544,256]{2,1,0:T(8,128)(2,1)S(1)} all-to-all(bf16[16,544,256]{2,1,0:T(8,128)(2,1)} %featurizer_gradients.1), channel_id=1, replica_groups=mesh['section'=8,'ctx'=16] {'ctx'}, dimensions={0} | all-to-all | bytes 8912896 | tf_op jit(solution)/shard_map/all_to_all | solution.py:575
  245.3 2.1 copy-done.10
  247.4 0.1 copy.13
  247.6 1.1 reshape.27
  248.6 10.3 %place_columns.1 = (bf16[128,4096]{1,0:T(8,128)(2,1)}, bf16[128,12288]{1,0:T(8,128)(2,1)}) custom-call(bf16[16,544,256]{2,1,0:T(8,128)(2,1)} %copy-done.10), custom_call_target="tpu_custom_call" | custom-call | bytes 8388608 | tf_op jit(solution)/shard_map/place_columns/pallas_call | solution.py:530
  (30 shorter events, 0.1 us)
Async XLA Ops:
  0.6 126.1 %copy-start = (f32[1,4096]{1,0:T(1,128)S(1)}, f32[1,4096]{1,0:T(1,128)}, u32[]{:S(2)}) copy-start(f32[1,4096]{1,0:T(1,128)} %param.11) | copy-start | bytes 49156
  9.5 10.0 %copy-start.11 = (bf16[16,128,256]{2,1,0:T(8,128)(2,1)S(1)}, bf16[16,128,256]{2,1,0:T(8,128)(2,1)}, u32[]{:S(2)}) copy-start(bf16[16,128,256]{2,1,0:T(8,128)(2,1)} %split_columns.1) | copy-start | bytes 3145732
  19.6 69.1 %collective-permute-start = (bf16[16,128,256]{2,1,0:T(8,128)(2,1)S(1)}, bf16[16,128,256]{2,1,0:T(8,128)(2,1)}, u32[]{:S(2)}, u32[]{:S(2)}) collective-permute-start(bf16[16,128,256]{2,1,0:T(8,128)(2,1)S(1)} %copy-done.11), channel_id=1, source_target_pairs={{0,112},{16,0},{32,16},{48,32},{64,48},{80,64},{96,80},{112,96},{1... | collective-permute-start | bytes 3145736 | tf_op jit(solution)/shard_map/ppermute | solution.py:28
  26.2 34.3 %collective-permute-start.1 = (bf16[3,128,256]{2,1,0:T(8,128)(2,1)}, bf16[3,128,256]{2,1,0:T(8,128)(2,1)S(1)}, u32[]{:S(2)}, u32[]{:S(2)}) collective-permute-start(bf16[3,128,256]{2,1,0:T(8,128)(2,1)} %get-tuple-element.71), channel_id=1, source_target_pairs={{0,16},{1,17},{2,18},{3,19},{4,20},{5,21},{6,22},{7,23},{8,24},{9,... | collective-permute-start | bytes 589832 | tf_op jit(solution)/shard_map/ppermute | solution.py:38
  26.2 40.6 %collective-permute-start.2 = (bf16[3,128,256]{2,1,0:T(8,128)(2,1)}, bf16[3,128,256]{2,1,0:T(8,128)(2,1)S(1)}, u32[]{:S(2)}, u32[]{:S(2)}) collective-permute-start(bf16[3,128,256]{2,1,0:T(8,128)(2,1)} %get-tuple-element.72), channel_id=1, source_target_pairs={{0,17},{1,16},{2,19},{3,18},{4,21},{5,20},{6,23},{7,22},{8,25},{9,... | collective-permute-start | bytes 589832 | tf_op jit(solution)/shard_map/ppermute | solution.py:38
  29.0 42.3 %collective-permute-start.3 = (bf16[3,128,256]{2,1,0:T(8,128)(2,1)}, bf16[3,128,256]{2,1,0:T(8,128)(2,1)S(1)}, u32[]{:S(2)}, u32[]{:S(2)}) collective-permute-start(bf16[3,128,256]{2,1,0:T(8,128)(2,1)} %get-tuple-element.73), channel_id=1, source_target_pairs={{0,18},{1,19},{2,16},{3,17},{4,22},{5,23},{6,20},{7,21},{8,26},{9,... | collective-permute-start | bytes 589832 | tf_op jit(solution)/shard_map/ppermute | solution.py:38
  29.9 43.8 %collective-permute-start.4 = (bf16[3,128,256]{2,1,0:T(8,128)(2,1)}, bf16[3,128,256]{2,1,0:T(8,128)(2,1)S(1)}, u32[]{:S(2)}, u32[]{:S(2)}) collective-permute-start(bf16[3,128,256]{2,1,0:T(8,128)(2,1)} %get-tuple-element.74), channel_id=1, source_target_pairs={{0,19},{1,18},{2,17},{3,16},{4,23},{5,22},{6,21},{7,20},{8,27},{9,... | collective-permute-start | bytes 589832 | tf_op jit(solution)/shard_map/ppermute | solution.py:38
  60.6 16.2 %collective-permute-start.5 = (bf16[3,128,256]{2,1,0:T(8,128)(2,1)}, bf16[3,128,256]{2,1,0:T(8,128)(2,1)S(1)}, u32[]{:S(2)}, u32[]{:S(2)}) collective-permute-start(bf16[3,128,256]{2,1,0:T(8,128)(2,1)} %get-tuple-element.75), channel_id=1, source_target_pairs={{0,20},{1,21},{2,22},{3,23},{4,16},{5,17},{6,18},{7,19},{8,28},{9,... | collective-permute-start | bytes 589832 | tf_op jit(solution)/shard_map/ppermute | solution.py:38
  66.8 13.5 %collective-permute-start.6 = (bf16[3,128,256]{2,1,0:T(8,128)(2,1)}, bf16[3,128,256]{2,1,0:T(8,128)(2,1)S(1)}, u32[]{:S(2)}, u32[]{:S(2)}) collective-permute-start(bf16[3,128,256]{2,1,0:T(8,128)(2,1)} %get-tuple-element.76), channel_id=1, source_target_pairs={{0,21},{1,20},{2,23},{3,22},{4,17},{5,16},{6,19},{7,18},{8,29},{9,... | collective-permute-start | bytes 589832 | tf_op jit(solution)/shard_map/ppermute | solution.py:38
  71.3 13.2 %collective-permute-start.7 = (bf16[3,128,256]{2,1,0:T(8,128)(2,1)}, bf16[3,128,256]{2,1,0:T(8,128)(2,1)S(1)}, u32[]{:S(2)}, u32[]{:S(2)}) collective-permute-start(bf16[3,128,256]{2,1,0:T(8,128)(2,1)} %get-tuple-element.77), channel_id=1, source_target_pairs={{0,22},{1,23},{2,20},{3,21},{4,18},{5,19},{6,16},{7,17},{8,30},{9,... | collective-permute-start | bytes 589832 | tf_op jit(solution)/shard_map/ppermute | solution.py:38
  73.7 15.0 %collective-permute-start.8 = (bf16[3,128,256]{2,1,0:T(8,128)(2,1)}, bf16[3,128,256]{2,1,0:T(8,128)(2,1)S(1)}, u32[]{:S(2)}, u32[]{:S(2)}) collective-permute-start(bf16[3,128,256]{2,1,0:T(8,128)(2,1)} %get-tuple-element.78), channel_id=1, source_target_pairs={{0,23},{1,22},{2,21},{3,20},{4,19},{5,18},{6,17},{7,16},{8,31},{9,... | collective-permute-start | bytes 589832 | tf_op jit(solution)/shard_map/ppermute | solution.py:38
  88.7 46.9 %all-to-all-start = ((bf16[16,128,256]{2,1,0:T(8,128)(2,1)}), bf16[16,128,256]{2,1,0:T(8,128)(2,1)S(1)}, u32[]{:S(2)}, u32[]{:S(2)}) async-start(bf16[16,128,256]{2,1,0:T(8,128)(2,1)} %collective-permute-done), calls=%async_computation | async-start | bytes 2097152 | tf_op jit(solution)/shard_map/all_to_all | solution.py:563
  92.6 17.2 %collective-permute-start.9 = (bf16[3,128,256]{2,1,0:T(8,128)(2,1)}, bf16[3,128,256]{2,1,0:T(8,128)(2,1)S(1)}, u32[]{:S(2)}, u32[]{:S(2)}) collective-permute-start(bf16[3,128,256]{2,1,0:T(8,128)(2,1)} %get-tuple-element.87), channel_id=1, source_target_pairs={{0,24},{1,25},{2,26},{3,27},{4,28},{5,29},{6,30},{7,31},{8,16},{9,... | collective-permute-start | bytes 589832 | tf_op jit(solution)/shard_map/ppermute | solution.py:38
  94.3 16.3 %collective-permute-start.10 = (bf16[3,128,256]{2,1,0:T(8,128)(2,1)}, bf16[3,128,256]{2,1,0:T(8,128)(2,1)S(1)}, u32[]{:S(2)}, u32[]{:S(2)}) collective-permute-start(bf16[3,128,256]{2,1,0:T(8,128)(2,1)} %get-tuple-element.88), channel_id=1, source_target_pairs={{0,25},{1,24},{2,27},{3,26},{4,29},{5,28},{6,31},{7,30},{8,17},{9,... | collective-permute-start | bytes 589832 | tf_op jit(solution)/shard_map/ppermute | solution.py:38
  94.6 21.7 %collective-permute-start.11 = (bf16[3,128,256]{2,1,0:T(8,128)(2,1)}, bf16[3,128,256]{2,1,0:T(8,128)(2,1)S(1)}, u32[]{:S(2)}, u32[]{:S(2)}) collective-permute-start(bf16[3,128,256]{2,1,0:T(8,128)(2,1)} %get-tuple-element.89), channel_id=1, source_target_pairs={{0,26},{1,27},{2,24},{3,25},{4,30},{5,31},{6,28},{7,29},{8,18},{9,... | collective-permute-start | bytes 589832 | tf_op jit(solution)/shard_map/ppermute | solution.py:38
  98.5 28.8 %collective-permute-start.12 = (bf16[3,128,256]{2,1,0:T(8,128)(2,1)}, bf16[3,128,256]{2,1,0:T(8,128)(2,1)S(1)}, u32[]{:S(2)}, u32[]{:S(2)}) collective-permute-start(bf16[3,128,256]{2,1,0:T(8,128)(2,1)} %get-tuple-element.90), channel_id=1, source_target_pairs={{0,27},{1,26},{2,25},{3,24},{4,31},{5,30},{6,29},{7,28},{8,19},{9,... | collective-permute-start | bytes 589832 | tf_op jit(solution)/shard_map/ppermute | solution.py:38
  98.8 28.5 %collective-permute-start.13 = (bf16[3,128,256]{2,1,0:T(8,128)(2,1)}, bf16[3,128,256]{2,1,0:T(8,128)(2,1)}, u32[]{:S(2)}, u32[]{:S(2)}) collective-permute-start(bf16[3,128,256]{2,1,0:T(8,128)(2,1)} %get-tuple-element.91), channel_id=1, source_target_pairs={{0,28},{1,29},{2,30},{3,31},{4,24},{5,25},{6,26},{7,27},{8,20},{9,... | collective-permute-start | bytes 589832 | tf_op jit(solution)/shard_map/ppermute | solution.py:38
  109.8 17.7 %collective-permute-start.14 = (bf16[3,128,256]{2,1,0:T(8,128)(2,1)}, bf16[3,128,256]{2,1,0:T(8,128)(2,1)S(1)}, u32[]{:S(2)}, u32[]{:S(2)}) collective-permute-start(bf16[3,128,256]{2,1,0:T(8,128)(2,1)} %get-tuple-element.92), channel_id=1, source_target_pairs={{0,29},{1,28},{2,31},{3,30},{4,25},{5,24},{6,27},{7,26},{8,21},{9,... | collective-permute-start | bytes 589832 | tf_op jit(solution)/shard_map/ppermute | solution.py:38
  110.6 19.5 %collective-permute-start.15 = (bf16[3,128,256]{2,1,0:T(8,128)(2,1)}, bf16[3,128,256]{2,1,0:T(8,128)(2,1)S(1)}, u32[]{:S(2)}, u32[]{:S(2)}) collective-permute-start(bf16[3,128,256]{2,1,0:T(8,128)(2,1)} %get-tuple-element.93), channel_id=1, source_target_pairs={{0,30},{1,31},{2,28},{3,29},{4,26},{5,27},{6,24},{7,25},{8,22},{9,... | collective-permute-start | bytes 589832 | tf_op jit(solution)/shard_map/ppermute | solution.py:38
  116.3 18.5 %collective-permute-start.16 = (bf16[3,128,256]{2,1,0:T(8,128)(2,1)}, bf16[3,128,256]{2,1,0:T(8,128)(2,1)S(1)}, u32[]{:S(2)}, u32[]{:S(2)}) collective-permute-start(bf16[3,128,256]{2,1,0:T(8,128)(2,1)} %get-tuple-element.94), channel_id=1, source_target_pairs={{0,31},{1,30},{2,29},{3,28},{4,27},{5,26},{6,25},{7,24},{8,23},{9,... | collective-permute-start | bytes 589832 | tf_op jit(solution)/shard_map/ppermute | solution.py:38
  127.5 0.7 copy-start.1
  130.1 0.7 copy-start.4
  134.8 0.7 copy-start.7
  135.5 0.9 copy-start.2
  136.5 0.9 copy-start.5
  137.4 0.9 copy-start.8
  150.8 20.0 %copy-start.3 = (bf16[3,128,256]{2,1,0:T(8,128)(2,1)S(1)}, bf16[3,128,256]{2,1,0:T(8,128)(2,1)}, u32[]{:S(2)}) copy-start(bf16[3,128,256]{2,1,0:T(8,128)(2,1)} %copy-done.1) | copy-start | bytes 589828
  150.8 20.0 %copy-start.6 = (bf16[3,128,256]{2,1,0:T(8,128)(2,1)S(1)}, bf16[3,128,256]{2,1,0:T(8,128)(2,1)}, u32[]{:S(2)}) copy-start(bf16[3,128,256]{2,1,0:T(8,128)(2,1)} %copy-done.4) | copy-start | bytes 589828
  150.8 20.0 %copy-start.9 = (bf16[3,128,256]{2,1,0:T(8,128)(2,1)S(1)}, bf16[3,128,256]{2,1,0:T(8,128)(2,1)}, u32[]{:S(2)}) copy-start(bf16[3,128,256]{2,1,0:T(8,128)(2,1)} %copy-done.7) | copy-start | bytes 589828
  245.3 2.1 copy-start.10

commit v4 on v3

v4 whole, which is shorter than its diff:
```python
import functools
import math

import jax
import jax.numpy as jnp
import ml_dtypes
import numpy as np
from jax import lax
from jax.experimental import pallas as pl
from jax.experimental.pallas import tpu as pltpu
from jax.sharding import PartitionSpec as P

TAPS = 7
HALO = 8
EXTRA = 32
CHUNKS = 2
OWNER_MIB = 34
GATE = 4
ROOT = math.sqrt(0.5)
F32 = jnp.float32
BF16 = jnp.bfloat16
MIB = 1 << 20


def in_hbm(*arrays):
    return [pltpu.with_memory_space_constraint(array, pltpu.HBM) for array in arrays]


def passed_along(value, axis, steps):
    count = lax.axis_size(axis)
    pairs = [(source, (source + steps) % count) for source in range(count)]
    return lax.ppermute(value, axis, pairs)


def handed_over(value, steps, partner):
    sections, groups = lax.axis_size("section"), lax.axis_size("ctx")
    pairs = [
        (section * groups + place, (section + steps) % sections * groups + (place ^ partner))
        for section in range(sections)
        for place in range(groups)
    ]
    return lax.ppermute(value, ("section", "ctx"), pairs)


def leaf_angles():
    angles = [math.pi / 2]
    for _ in range(3):
        angles = [half for angle in angles for half in (angle / 2, angle / 2 + math.pi)]
    return angles


def leaf_tables(length):
    leaf = length // 8
    order = np.arange(leaf)
    tables = []
    for angle in leaf_angles():
        phase = (angle + 2.0 * np.pi * order[:, None]) / leaf * order[None, :]
        real, imag = np.cos(phase), np.sin(phase)
        tables.append(np.block([[real, -imag], [imag, real]]))
    table = np.stack(tables)
    back = table.transpose(0, 2, 1) / length
    return table.astype(ml_dtypes.bfloat16), back.astype(ml_dtypes.bfloat16)


def turned(pair, angle):
    real, imag = pair
    cos, sin = math.cos(angle), math.sin(angle)
    return real * cos - imag * sin, real * sin + imag * cos


def split_rings(parts):
    low, high = [], []
    for lower, upper in zip(parts[:4], parts[4:]):
        scaled = upper * ROOT
        low.append((lower + scaled, scaled))
        high.append((lower - scaled, -scaled))
    rings = [(math.pi / 4, low), (math.pi / 4 + math.pi, high)]
    while len(rings[0][1]) > 1:
        finer = []
        for angle, pieces in rings:
            half = len(pieces) // 2
            plus, minus = [], []
            for lower, upper in zip(pieces[:half], pieces[half:]):
                real, imag = turned(upper, angle / 2)
                plus.append((lower[0] + real, lower[1] + imag))
                minus.append((lower[0] - real, lower[1] - imag))
            finer += [(angle / 2, plus), (angle / 2 + math.pi, minus)]
        rings = finer
    return [pieces[0] for _, pieces in rings]


def join_rings(leaves):
    angles = [math.pi / 4, math.pi / 4 + math.pi]
    angles = [half for angle in angles for half in (angle / 2, angle / 2 + math.pi)]
    groups = [[leaf] for leaf in leaves]
    while len(groups) > 2:
        merged = []
        for index in range(0, len(groups), 2):
            angle = angles[index // 2] if len(groups) == 8 else [math.pi / 4, math.pi / 4 + math.pi][index // 2]
            lower, upper = [], []
            for plus, minus in zip(groups[index], groups[index + 1]):
                lower.append((plus[0] + minus[0], plus[1] + minus[1]))
                upper.append(turned((plus[0] - minus[0], plus[1] - minus[1]), -angle / 2))
            merged.append(lower + upper)
        groups = merged
    lower, upper = [], []
    for plus, minus in zip(groups[0], groups[1]):
        lower.append(plus[0] + minus[0])
        upper.append(((plus[0] - minus[0]) + (plus[1] - minus[1])) * ROOT)
    return lower + upper


def filter_kernel(filt_ref, table_ref, spec_ref, rings):
    chans, length = filt_ref.shape
    leaf = length // 8
    step = pl.program_id(0)

    @pl.when(step == 0)
    def _():
        @pl.loop(0, chans // 16)
        def _(strip):
            rows = pl.ds(pl.multiple_of(strip * 16, 16), 16)
            for lane in range(0, leaf, 128):
                parts = [
                    filt_ref[rows, piece * leaf + lane : piece * leaf + lane + 128].astype(F32)
                    for piece in range(8)
                ]
                for index, (real, imag) in enumerate(split_rings(parts)):
                    rings[index, rows, lane : lane + 128] = real.astype(BF16)
                    rings[index, rows, leaf + lane : leaf + lane + 128] = imag.astype(BF16)

    spec_ref[0] = lax.dot_general(
        table_ref[0], rings[step], (((1,), (1,)), ((), ())), preferred_element_type=F32
    )


def filter_spectrum(filt, table):
    chans, length = filt.shape
    wide = length // 4
    return pl.pallas_call(
        filter_kernel,
        out_shape=pltpu.HBM((8, wide, chans), F32),
        grid=(8,),
        in_specs=[
            pl.BlockSpec((chans, length), lambda j: (0, 0)),
            pl.BlockSpec((1, wide, wide), lambda j: (j, 0, 0)),
        ],
        out_specs=pl.BlockSpec((1, wide, chans), lambda j: (j, 0, 0)),
        scratch_shapes=[pltpu.VMEM((8, chans, wide), BF16)],
        compiler_params=pltpu.CompilerParams(vmem_limit_bytes=12 * MIB),
        cost_estimate=pl.CostEstimate(
            flops=16 * wide * wide * chans, bytes_accessed=10 * MIB, transcendentals=0
        ),
        name="filter_spectrum",
    )(*in_hbm(filt, table))


def wait_all(copies):
    for copy in copies:
        copy.start()
    for copy in copies:
        copy.wait()


def leave_kernel(me_ref, wide_ref, leaving_ref, sems):
    chips, roles, _, chans = leaving_ref.shape
    width = wide_ref.shape[1] // roles
    copies = []
    for chip in range(chips):
        start = (me_ref[0] ^ (2 * chip + 1)) * chans
        for role in range(roles):
            columns = pl.ds(pl.multiple_of(role * width + start, 128), chans)
            copies.append(
                pltpu.make_async_copy(wide_ref.at[:, columns], leaving_ref.at[chip, role], sems.at[chip, role])
            )
    wait_all(copies)


def piece_kernel(me_ref, wide_ref, came_ref, *refs):
    *pieces, sems = refs
    _, roles, _, chans = pieces[0].shape
    width = wide_ref.shape[1] // roles
    copies = []
    for chip, piece in enumerate(pieces):
        start = (me_ref[0] ^ (2 * chip)) * chans
        for role in range(roles):
            columns = pl.ds(pl.multiple_of(role * width + start, 128), chans)
            copies.append(pltpu.make_async_copy(wide_ref.at[:, columns], piece.at[0, role], sems.at[chip, role]))
        copies.append(pltpu.make_async_copy(came_ref.at[chip], piece.at[1], sems.at[chip, roles]))
    wait_all(copies)


def leaving_pieces(me, wide, groups, roles):
    rows, width = wide.shape
    chans = width // roles // groups
    return pl.pallas_call(
        leave_kernel,
        out_shape=jax.ShapeDtypeStruct((groups // 2, roles, rows, chans), BF16),
        in_specs=[pl.BlockSpec(memory_space=pltpu.SMEM), pl.BlockSpec(memory_space=pl.ANY)],
        out_specs=pl.BlockSpec(memory_space=pltpu.VMEM),
        scratch_shapes=[pltpu.SemaphoreType.DMA((groups // 2, roles))],
        compiler_params=pltpu.CompilerParams(vmem_limit_bytes=4 * MIB),
        cost_estimate=pl.CostEstimate(flops=0, bytes_accessed=2 * rows * width, transcendentals=0),
        name="leaving_pieces",
    )(me, *in_hbm(wide))


def pieces_for_owners(me, wide, came, groups):
    chips, roles, rows, chans = came.shape
    return pl.pallas_call(
        piece_kernel,
        out_shape=[jax.ShapeDtypeStruct((2, roles, rows, chans), BF16)] * chips,
        in_specs=[pl.BlockSpec(memory_space=pltpu.SMEM), pl.BlockSpec(memory_space=pl.ANY), pl.BlockSpec(memory_space=pltpu.VMEM)],
        out_specs=[pl.BlockSpec(memory_space=pltpu.VMEM)] * chips,
        scratch_shapes=[pltpu.SemaphoreType.DMA((chips, roles + 1))],
        compiler_params=pltpu.CompilerParams(vmem_limit_bytes=8 * MIB),
        cost_estimate=pl.CostEstimate(flops=0, bytes_accessed=8 * chips * roles * rows * chans, transcendentals=0),
        name="pieces_for_owners",
    )(me, *in_hbm(wide), came)


def split_kernel(wide_ref, pieces_ref, sems):
    groups, _, part = pieces_ref.shape
    wait_all(
        [
            pltpu.make_async_copy(
                wide_ref.at[:, pl.ds(owner * part, part)], pieces_ref.at[owner], sems.at[owner]
            )
            for owner in range(groups)
        ]
    )


def split_columns(wide, groups):
    rows, width = wide.shape
    return pl.pallas_call(
        split_kernel,
        out_shape=jax.ShapeDtypeStruct((groups, rows, width // groups), BF16),
        in_specs=[pl.BlockSpec(memory_space=pl.ANY)],
        out_specs=pl.BlockSpec(memory_space=pltpu.VMEM),
        scratch_shapes=[pltpu.SemaphoreType.DMA((groups,))],
        compiler_params=pltpu.CompilerParams(vmem_limit_bytes=4 * MIB),
        cost_estimate=pl.CostEstimate(flops=0, bytes_accessed=4 * rows * width, transcendentals=0),
        name="split_columns",
    )(*in_hbm(wide))


def featurize(step, source, incoming, taps_ref, held, feats, moved):
    _, rows, chans = incoming.shape
    for part in range(chans // 128):
        lanes = slice(part * 128, part * 128 + 128)
        taps = []
        for role in range(3):
            held[role, part, 0:HALO, :] = held[role, part, rows : rows + HALO, :]
            held[role, part, HALO:, :] = source[step, role, :, lanes].astype(F32)
            taps.append([taps_ref[role, tap : tap + 1, lanes] for tap in range(TAPS)])
        for row in range(0, rows, 16):
            span = slice(row, row + 16)
            features = []
            for role in range(3):
                total = taps[role][0] * held[role, part, HALO + row : HALO + row + 16, :]
                for tap in range(1, TAPS):
                    total = total + taps[role][tap] * held[role, part, HALO + row - tap : HALO + row - tap + 16, :]
                feats[step, role, span, lanes] = total
                features.append(total)
            query, keyed, value = features
            moved[step, 0, span, lanes] = (keyed * value).astype(BF16)
            moved[step, 1, span, lanes] = (incoming[step, span, lanes].astype(F32) * query).astype(BF16)


def split_all(moved, rings):
    groups, _, rows, chans = moved.shape
    leaf = groups * rows // 8
    per_piece = leaf // rows

    @pl.loop(0, rows // 16)
    def _(strip):
        inside = pl.ds(pl.multiple_of(strip * 16, 16), 16)
        for part in range(per_piece):
            real_rows = pl.ds(pl.multiple_of(part * rows + strip * 16, 16), 16)
            imag_rows = pl.ds(pl.multiple_of(leaf + part * rows + strip * 16, 16), 16)
            for kind in range(2):
                for lane in range(0, chans, 128):
                    lanes = slice(lane, lane + 128)
                    parts = [
                        moved[piece * per_piece + part, kind, inside, lanes].astype(F32) for piece in range(8)
                    ]
                    into = slice(kind * chans + lane, kind * chans + lane + 128)
                    for index, (real, imag) in enumerate(split_rings(parts)):
                        rings[index, real_rows, into] = real.astype(BF16)
                        rings[index, imag_rows, into] = imag.astype(BF16)


def multiply_ring(step, rings, table, back, spec, products, joined):
    chans = spec.shape[2]
    leaf = spec.shape[1] // 2
    both = jnp.dot(table[step], rings[step], preferred_element_type=F32)
    g_real, g_imag = both[:leaf, :chans], both[leaf:, :chans]
    d_real, d_imag = both[:leaf, chans:], both[leaf:, chans:]
    f_real, f_imag = spec[step, :leaf], spec[step, leaf:]
    products[:leaf, 0:chans] = (g_real * f_real - g_imag * f_imag).astype(BF16)
    products[leaf:, 0:chans] = (g_real * f_imag + g_imag * f_real).astype(BF16)
    products[:leaf, chans : 2 * chans] = (d_real * f_real + d_imag * f_imag).astype(BF16)
    products[leaf:, chans : 2 * chans] = (d_imag * f_real - d_real * f_imag).astype(BF16)
    products[:leaf, 2 * chans :] = (d_real * g_real + d_imag * g_imag).astype(BF16)
    products[leaf:, 2 * chans :] = (d_imag * g_real - d_real * g_imag).astype(BF16)
    joined[step] = jnp.dot(back[step], products[...], preferred_element_type=F32)


def join_all(joined, moved, gain_ref, sent, flat, skip_ref):
    groups, _, rows, chans = moved.shape
    leaf = groups * rows // 8
    per_piece = leaf // rows
    skip_ref[...] = jnp.zeros_like(skip_ref)

    @pl.loop(0, rows // 16)
    def _(strip):
        inside = pl.ds(pl.multiple_of(strip * 16, 16), 16)
        for part in range(per_piece):
            real_rows = pl.ds(pl.multiple_of(part * rows + strip * 16, 16), 16)
            imag_rows = pl.ds(pl.multiple_of(leaf + part * rows + strip * 16, 16), 16)
            for lane in range(0, chans, 128):
                lanes = slice(lane, lane + 128)
                gain = gain_ref[0:1, lanes]
                for kind in range(3):
                    column = slice(kind * chans + lane, kind * chans + lane + 128)
                    leaves = [
                        (joined[index, real_rows, column], joined[index, imag_rows, column]) for index in range(8)
                    ]
                    total = jnp.zeros((16, 128), F32)
                    for piece, result in enumerate(join_rings(leaves)):
                        owner = piece * per_piece + part
                        if kind == 0:
                            sent[owner, 0, inside, lanes] = result.astype(BF16)
                        elif kind == 1:
                            grad = moved[owner, 1, inside, lanes].astype(F32)
                            sent[owner, 1, inside, lanes] = (result + gain * grad).astype(BF16)
                            total = total + grad * moved[owner, 0, inside, lanes].astype(F32)
                        else:
                            into = pl.ds(pl.multiple_of(owner * rows + strip * 16, 16), 16)
                            flat[into, lanes] = result
                    if kind == 1:
                        skip_ref[0:1, lanes] += jnp.sum(total, axis=0, keepdims=True)


def gradients(block, slot, source, incoming, feats, sent, taps_ref, gain_ref, grads, sums, slots):
    _, rows, chans = incoming.shape
    for part in range(chans // 128):
        lanes = slice(part * 128, part * 128 + 128)
        gain = gain_ref[0:1, lanes]
        for role in range(3):
            grads[role, part, rows : rows + HALO, :] = grads[role, part, 0:HALO, :]
        for row in range(0, rows, 16):
            span = slice(row, row + 16)
            query, keyed, value = [feats[block, role, span, lanes] for role in range(3)]
            gated = (keyed * value).astype(BF16).astype(F32)
            inner = sent[block, 0, span, lanes].astype(F32) + gain * gated
            through = sent[block, 1, span, lanes].astype(F32)
            grads[0, part, span, :] = incoming[block, span, lanes].astype(F32) * inner
            grads[1, part, span, :] = through * value
            grads[2, part, span, :] = through * keyed
            slots[slot, span, lanes] = (query * inner).astype(BF16)
        for role in range(3):
            taps = [taps_ref[role, tap : tap + 1, lanes] for tap in range(TAPS)]
            parts = [jnp.zeros((16, 128), F32) for _ in range(TAPS)]
            for row in range(0, rows, 16):
                here = source[block, role, row : row + 16, lanes].astype(F32)
                total = jnp.zeros((16, 128), F32)
                for tap in range(TAPS):
                    ahead = grads[role, part, row + tap : row + tap + 16, :]
                    total = total + taps[tap] * ahead
                    parts[tap] = parts[tap] + here * ahead
                start = (1 + role) * rows + row
                slots[slot, start : start + 16, lanes] = total.astype(BF16)
            for tap in range(TAPS):
                sums[role, tap, :, lanes] += parts[tap][0:8] + parts[tap][8:16]


def owner_kernel(chunk, groups, me_ref, *refs):
    pieces = refs[: groups // 2]
    incoming_hbm, spec_hbm, table_hbm, back_hbm, taps_ref, gain_ref = refs[groups // 2 : groups // 2 + 6]
    (
        ready_hbm, filt_hbm, skip_ref,
        source, incoming, spec, table, back, held, feats, moved, rings, products, joined, sent, flat, turned_flat,
        grads, sums, slots, last,
        piece_sems, incoming_sem, spec_sems, table_sems, back_sems, filt_sem, slot_sems, last_sems,
    ) = refs[-29:]
    _, rows, chans = incoming.shape

    lanes = pl.ds(chunk * chans, chans)
    incoming_copy = pltpu.make_async_copy(incoming_hbm.at[:, :, lanes], incoming, incoming_sem.at[0])
    incoming_copy.start()
    for partner in range(groups):
        block = me_ref[0] ^ partner
        piece = pieces[partner // 2].at[partner % 2, :, :, lanes]
        pltpu.make_async_copy(piece, source.at[block], piece_sems.at[block]).start()
    loads = []
    for ring in range(8):
        loads.append(
            [
                pltpu.make_async_copy(table_hbm.at[ring], table.at[ring], table_sems.at[ring]),
                pltpu.make_async_copy(spec_hbm.at[ring, :, lanes], spec.at[ring], spec_sems.at[ring]),
                pltpu.make_async_copy(back_hbm.at[ring], back.at[ring], back_sems.at[ring]),
            ]
        )
        for copy in loads[-1]:
            copy.start()
    held[:, :, rows:, :] = jnp.zeros((3, chans // 128, HALO, 128), F32)
    grads[:, :, 0:HALO, :] = jnp.zeros((3, chans // 128, HALO, 128), F32)
    sums[...] = jnp.zeros_like(sums)
    incoming_copy.wait()

    @pl.loop(0, groups)
    def _(step):
        pltpu.make_async_copy(pieces[0].at[0, :, :, lanes], source.at[step], piece_sems.at[step]).wait()
        featurize(step, source, incoming, taps_ref, held, feats, moved)

    split_all(moved, rings)

    @pl.loop(0, 8)
    def _(step):
        pltpu.make_async_copy(table_hbm.at[step], table.at[step], table_sems.at[step]).wait()
        pltpu.make_async_copy(spec_hbm.at[step, :, lanes], spec.at[step], spec_sems.at[step]).wait()
        pltpu.make_async_copy(back_hbm.at[step], back.at[step], back_sems.at[step]).wait()
        multiply_ring(step, rings, table, back, spec, products, joined)

    join_all(joined, moved, gain_ref, sent, flat, skip_ref)
    for block in range(groups):
        span = slice(block * rows, (block + 1) * rows)
        turned_flat[:, span] = flat[span, :].T
    filt_copy = pltpu.make_async_copy(turned_flat, filt_hbm.at[pl.ds(chunk * chans, chans)], filt_sem.at[0])
    filt_copy.start()

    def write_back(slot_at, block_at):
        return pltpu.make_async_copy(
            slots.at[slot_at], ready_hbm.at[block_at, pl.ds(0, 4 * rows)], slot_sems.at[slot_at]
        )

    @pl.loop(0, groups)
    def _(step):
        block = groups - 1 - step
        slot = lax.rem(step, 2)

        @pl.when(step >= 2)
        def _():
            write_back(slot, block + 2).wait()

        gradients(block, slot, source, incoming, feats, sent, taps_ref, gain_ref, grads, sums, slots)
        write_back(slot, block).start()

    rows_out = []
    for role in range(3):
        for tap in range(TAPS):
            rows_out.append(jnp.sum(sums[role, tap], axis=0, keepdims=True))
        rows_out.append(jnp.zeros((HALO - TAPS, chans), F32))
    rows_out.append(jnp.zeros((EXTRA - 3 * HALO, chans), F32))
    last[...] = jnp.concatenate(rows_out, axis=0).astype(BF16)
    wait_all(
        [
            pltpu.make_async_copy(last, ready_hbm.at[owner, pl.ds(4 * rows, EXTRA)], last_sems.at[owner])
            for owner in range(groups)
        ]
    )
    write_back(groups % 2, 1).wait()
    write_back((groups + 1) % 2, 0).wait()
    filt_copy.wait()


def owner_work(me, pieces, incoming, spectrum, table, back, taps, gain, chunk, earlier):
    groups, rows, chans = incoming.shape
    chans = chans // CHUNKS
    length = groups * rows
    wide = length // 4
    parts = chans // 128
    flops = 80 * wide * wide * chans + 200 * length * chans
    return pl.pallas_call(
        functools.partial(owner_kernel, chunk, groups),
        input_output_aliases={groups // 2 + 7: 1} if earlier else {},
        out_shape=(
            pltpu.HBM((groups, 4 * rows + EXTRA, chans), BF16),
            pltpu.HBM((CHUNKS * chans, length), F32),
            jax.ShapeDtypeStruct((1, chans), F32),
        ),
        in_specs=[pl.BlockSpec(memory_space=pltpu.SMEM)]
        + [pl.BlockSpec(memory_space=pl.ANY)] * (groups // 2 + 4)
        + [pl.BlockSpec(memory_space=pltpu.VMEM)] * 2
        + [pl.BlockSpec(memory_space=pl.ANY)] * len(earlier),
        out_specs=(
            pl.BlockSpec(memory_space=pl.ANY),
            pl.BlockSpec(memory_space=pl.ANY),
            pl.BlockSpec(memory_space=pltpu.VMEM),
        ),
        scratch_shapes=[
            pltpu.VMEM((groups, 3, rows, chans), BF16),
            pltpu.VMEM((groups, rows, chans), BF16),
            pltpu.VMEM((8, wide, chans), F32),
            pltpu.VMEM((8, wide, wide), BF16),
            pltpu.VMEM((8, wide, wide), BF16),
            pltpu.VMEM((3, parts, HALO + rows, 128), F32),
            pltpu.VMEM((groups, 3, rows, chans), F32),
            pltpu.VMEM((groups, 2, rows, chans), BF16),
            pltpu.VMEM((8, wide, 2 * chans), BF16),
            pltpu.VMEM((wide, 3 * chans), BF16),
            pltpu.VMEM((8, wide, 3 * chans), F32),
            pltpu.VMEM((groups, 2, rows, chans), BF16),
            pltpu.VMEM((length, chans), F32),
            pltpu.VMEM((chans, length), F32),
            pltpu.VMEM((3, parts, rows + HALO, 128), F32),
            pltpu.VMEM((3, TAPS, 8, chans), F32),
            pltpu.VMEM((2, 4 * rows, chans), BF16),
            pltpu.VMEM((EXTRA, chans), BF16),
            pltpu.SemaphoreType.DMA((groups,)),
            pltpu.SemaphoreType.DMA((1,)),
            pltpu.SemaphoreType.DMA((8,)),
            pltpu.SemaphoreType.DMA((8,)),
            pltpu.SemaphoreType.DMA((8,)),
            pltpu.SemaphoreType.DMA((1,)),
            pltpu.SemaphoreType.DMA((2,)),
            pltpu.SemaphoreType.DMA((groups,)),
        ],
        compiler_params=pltpu.CompilerParams(vmem_limit_bytes=OWNER_MIB * MIB),
        cost_estimate=pl.CostEstimate(flops=flops, bytes_accessed=24 * MIB, transcendentals=0),
        name="owner_work",
    )(me, *in_hbm(*pieces, incoming, spectrum, table, back), taps, gain, *in_hbm(*earlier))


def place_kernel(chunk, held_ref, *refs):
    output_ref, grad_ref, sems = refs[-3:]
    groups, _, part = held_ref.shape
    rows, width = output_ref.shape
    copies = []
    for owner in range(groups):
        start = owner * (width // groups) + chunk * part
        for kind in range(4):
            into, at = (output_ref, start) if kind == 0 else (grad_ref, (kind - 1) * width + start)
            copies.append(
                pltpu.make_async_copy(
                    held_ref.at[owner, pl.ds(kind * rows, rows)], into.at[:, pl.ds(at, part)], sems.at[owner, kind]
                )
            )
    wait_all(copies)


def place_columns(held, rows, chunk, earlier):
    groups, _, part = held.shape
    width = groups * part * CHUNKS
    return pl.pallas_call(
        functools.partial(place_kernel, chunk),
        input_output_aliases={1: 0, 2: 1} if earlier else {},
        out_shape=(pltpu.HBM((rows, width), BF16), pltpu.HBM((rows, 3 * width), BF16)),
        in_specs=[pl.BlockSpec(memory_space=pltpu.VMEM)] + [pl.BlockSpec(memory_space=pl.ANY)] * len(earlier),
        out_specs=(pl.BlockSpec(memory_space=pl.ANY),) * 2,
        scratch_shapes=[pltpu.SemaphoreType.DMA((groups, 4))],
        compiler_params=pltpu.CompilerParams(vmem_limit_bytes=12 * MIB),
        cost_estimate=pl.CostEstimate(flops=0, bytes_accessed=16 * rows * width, transcendentals=0),
        name="place_columns",
    )(held, *in_hbm(*earlier))


def on_device(acts, cots, kern, filt, skip):
    rows, feats_all = acts.shape[1:]
    groups = lax.axis_size("ctx")
    chans = filt.shape[1]
    part = chans // CHUNKS
    place = lax.axis_index("ctx").astype(jnp.int32)
    me = place[None]

    table, back = (jnp.asarray(one) for one in leaf_tables(rows * groups))
    spectrum = filter_spectrum(filt[0], table)
    gain = lax.dynamic_slice_in_dim(skip, place * chans, chans, axis=1)
    taps = kern[0].reshape(TAPS, 3, groups, chans)
    taps = lax.dynamic_index_in_dim(taps, place, axis=2, keepdims=False).transpose(1, 0, 2)
    taps = jnp.pad(taps, ((0, 0), (0, HALO - TAPS), (0, 0)))

    incoming = passed_along(split_columns(cots[0], groups), "section", -1)
    came = handed_over(leaving_pieces(me, acts[0], groups, 3), 0, 1)
    pieces = pieces_for_owners(me, acts[0], came, groups)
    pieces = [handed_over(piece, 1, 2 * chip) for chip, piece in enumerate(pieces)]
    incoming, pieces[:GATE] = lax.optimization_barrier((incoming, pieces[:GATE]))
    incoming = lax.all_to_all(incoming, "ctx", split_axis=0, concat_axis=0, tiled=True)

    filters, skips, results, tap_sums = [], [], (), []
    for chunk in range(CHUNKS):
        span = slice(chunk * part, chunk * part + part)
        ready, *filters, skip_grad = owner_work(
            me, pieces, incoming, spectrum, table, back, taps[:, :, span], gain[:, span], chunk, filters
        )
        ready = lax.all_to_all(ready, "ctx", split_axis=0, concat_axis=0, tiled=True)
        results = place_columns(ready, rows, chunk, results)
        skips.append(skip_grad)
        sums = ready[:, 4 * rows : 4 * rows + 3 * HALO].reshape(groups, 3, HALO, part)[:, :, :TAPS]
        tap_sums.append(sums.transpose(2, 1, 0, 3).astype(F32))
    kern_grad = jnp.stack(tap_sums, axis=3).reshape(TAPS, feats_all)
    skip_grad = jnp.concatenate(skips, axis=1)
    output, input_grad = results
    return (output[None], input_grad[None], kern_grad[None], filters[0][None], skip_grad)


def solution(mesh):
    return jax.shard_map(
        on_device,
        mesh=mesh,
        in_specs=(
            P("section", "ctx", None),
            P("section", "ctx", None),
            P("section", None, None),
            P("section", "ctx", None),
            P("section", None),
        ),
        out_specs=(
            P("section", "ctx", None),
            P("section", "ctx", None),
            P("section", None, None),
            P("section", "ctx", None),
            P("section", "ctx"),
        ),
        check_vma=False,
    )
```

time: 261 us -> 221 us (0.85)
  blocking collectives: 55.6 us -> 0 us
  waiting for transfers between devices: 45.4 us -> 101 us
  Pallas kernels: 89.6 us -> 67.2 us
  starting transfers between devices: 53.5 us -> 41.8 us
  local copies, waits for them, and re-layouts: 11.4 us -> 6.97 us
    all_to_all x1 -> x0, blocking collectives: 55.6 us -> none  [on_device(): lax.all_to_all(ready, 'ctx', split_axis=0, concat_axis=0, tiled=True)]
    ppermute x1, waiting for transfers between devices: 0.01 us -> 43.3 us  [passed_along(): return lax.ppermute(value, axis, pairs)]
    all_to_all x0 -> x2, waiting for transfers between devices: none -> 34.6 us  [on_device(): lax.all_to_all(ready, 'ctx', split_axis=0, concat_axis=0, tiled=True)]
    ppermute x16 -> x9, starting transfers between devices: 42.9 us -> 20.4 us  [handed_over(): return lax.ppermute(value, ('section', 'ctx'), pairs)]
    pallas_call x6 -> x7, Pallas kernels: 80.5 us -> 58.1 us  [the longest x2 46.7 us: owner_work(): pl.pallas_call(functools.partial(owner_kernel, chunk, groups), input_outp...]
    ppermute x16 -> x9, waiting for transfers between devices: 45.4 us -> 23.2 us  [handed_over(): return lax.ppermute(value, ('section', 'ctx'), pairs)]
    all_to_all x0 -> x2, starting transfers between devices: none -> 9.66 us  [on_device(): lax.all_to_all(ready, 'ctx', split_axis=0, concat_axis=0, tiled=True)]
    unnamed x26 -> x14, local copies, waits for them, and re-layouts: 8.75 us -> 3.51 us
  transfers between devices with their start and end apart: 18 -> 13, of which waited for: 7 -> 7; matrix products, arithmetic and copies ran while one was open for 2% -> 2% of each run, Pallas kernels for 4% -> 17%
where the time goes in v4:
time: 221 us; the launch traced here: 220 us
  waiting for transfers between devices  101 us (46%)
  Pallas kernels  67.2 us (30%)
  starting transfers between devices  41.8 us (19%)
  local copies, waits for them, and re-layouts  6.97 us (3%)
  other arithmetic  2.39 us (1%)
    pallas_call x2, Pallas kernels, owner_work(): pl.pallas_call(functools.partial(owner_kernel, chunk, groups), input_outp...  46.7 us
    ppermute x1, waiting for transfers between devices, passed_along(): return lax.ppermute(value, axis, pairs)  43.3 us
    all_to_all x2, waiting for transfers between devices, on_device(): lax.all_to_all(ready, 'ctx', split_axis=0, concat_axis=0, tiled=True)  34.6 us
    ppermute x9, waiting for transfers between devices, handed_over(): return lax.ppermute(value, ('section', 'ctx'), pairs)  23.2 us
    ppermute x9, starting transfers between devices, handed_over(): return lax.ppermute(value, ('section', 'ctx'), pairs)  20.4 us
    all_to_all x2, starting transfers between devices, on_device(): lax.all_to_all(ready, 'ctx', split_axis=0, concat_axis=0, tiled=True)  9.66 us
    pallas_call x1, Pallas kernels, filter_spectrum(): pl.pallas_call(filter_kernel, out_shape=pltpu.HBM((8, wide, chans), F32),...  9.06 us
    ppermute x1, starting transfers between devices, passed_along(): return lax.ppermute(value, axis, pairs)  5.94 us
  transfers between devices with their start and end apart: 13, of which 7 were waited for; matrix products, arithmetic and copies ran while one was open for 2% of the time, Pallas kernels for 17%

profile of v4, /device:TPU:1, one launch (start us, length us, event | category | flops | bytes accessed | tf_op | source)
XLA Modules:
  0.0 220.1 jit_solution(5853688940639695723)
XLA Ops:
  0.6 1.6 leaving_pieces.1
  2.3 1.5 collective-permute-start.1
  3.8 1.4 split_columns.1
  5.2 5.9 %collective-permute-start = (bf16[16,128,256]{2,1,0:T(8,128)(2,1)S(1)}, bf16[16,128,256]{2,1,0:T(8,128)(2,1)S(1)}, u32[]{:S(2)}, u32[]{:S(2)}) collective-permute-start(bf16[16,128,256]{2,1,0:T(8,128)(2,1)S(1)} %split_columns.1), channel_id=1, source_target_pairs={{0,112},{16,0},{32,16},{48,32},{64,48},{80,64},{96,80},{112,96},{1... | collective-permute-start | bytes 3145736 | tf_op jit(solution)/shard_map/ppermute | solution.py:32
  11.1 0.0 collective-permute-done.1.came_ref
  11.1 3.1 %pieces_for_owners.1 = (bf16[2,3,128,256]{3,2,1,0:T(8,128)(2,1)S(1)}, bf16[2,3,128,256]{3,2,1,0:T(8,128)(2,1)S(1)}, bf16[2,3,128,256]{3,2,1,0:T(8,128)(2,1)S(1)}...) custom-call(s32[1]{0:T(128)} %bitcast.me_ref, ...), custom_call_target="tpu_custom_call" | custom-call | bytes 6291456 | tf_op jit(solution)/shard_map/pieces_for_owners/pallas_call | solution.py:210
  14.2 0.1 collective-permute-start.2
  14.3 2.7 %collective-permute-start.3 = (bf16[2,3,128,256]{3,2,1,0:T(8,128)(2,1)S(1)}, bf16[2,3,128,256]{3,2,1,0:T(8,128)(2,1)S(1)}, u32[]{:S(2)}, u32[]{:S(2)}) collective-permute-start(bf16[2,3,128,256]{3,2,1,0:T(8,128)(2,1)S(1)} %get-tuple-element.29), channel_id=1, source_target_pairs={{0,18},{1,19},{2,16},{3,17},{4,22},{5,23},{6,20},{7,21},{8,26},{9,... | collective-permute-start | bytes 1179656 | tf_op jit(solution)/shard_map/ppermute | solution.py:42
  17.0 3.9 %collective-permute-start.4 = (bf16[2,3,128,256]{3,2,1,0:T(8,128)(2,1)S(1)}, bf16[2,3,128,256]{3,2,1,0:T(8,128)(2,1)S(1)}, u32[]{:S(2)}, u32[]{:S(2)}) collective-permute-start(bf16[2,3,128,256]{3,2,1,0:T(8,128)(2,1)S(1)} %get-tuple-element.30), channel_id=1, source_target_pairs={{0,20},{1,21},{2,22},{3,23},{4,16},{5,17},{6,18},{7,19},{8,28},{9,... | collective-permute-start | bytes 1179656 | tf_op jit(solution)/shard_map/ppermute | solution.py:42
  20.9 2.0 collective-permute-start.5
  22.9 43.3 %collective-permute-done = bf16[16,128,256]{2,1,0:T(8,128)(2,1)S(1)} collective-permute-done((bf16[16,128,256]{2,1,0:T(8,128)(2,1)S(1)}, bf16[16,128,256]{2,1,0:T(8,128)(2,1)S(1)}, u32[]{:S(2)}, u32[]{:S(2)}) %collective-permute-start) | collective-permute-done | bytes 1048608 | tf_op jit(solution)/shard_map/ppermute | solution.py:32
  66.1 0.0 copy-start.5
  66.1 0.3 collective-permute-done.2.refs_0_
  66.5 0.0 collective-permute-done.3.refs_1_
  66.5 0.0 collective-permute-done.4.refs_2_
  66.5 0.8 copy-done.5
  67.2 0.0 collective-permute-done.5.refs_3_
  67.3 0.0 copy-done.2
  67.3 0.7 copy-done.3
  68.0 0.2 copy-done.4
  68.2 5.8 %all-to-all-start = ((bf16[16,128,256]{2,1,0:T(8,128)(2,1)}), bf16[16,128,256]{2,1,0:T(8,128)(2,1)S(1)}, u32[]{:S(2)}, u32[]{:S(2)}) async-start(bf16[16,128,256]{2,1,0:T(8,128)(2,1)} %copy-done.5), calls=%async_computation | async-start | bytes 2097152 | tf_op jit(solution)/shard_map/all_to_all | solution.py:580
  74.0 1.8 reduce
  75.8 0.8 copy.28
  76.6 3.5 %collective-permute-start.6 = (bf16[2,3,128,256]{3,2,1,0:T(8,128)(2,1)S(1)}, bf16[2,3,128,256]{3,2,1,0:T(8,128)(2,1)}, u32[]{:S(2)}, u32[]{:S(2)}) collective-permute-start(bf16[2,3,128,256]{3,2,1,0:T(8,128)(2,1)S(1)} %get-tuple-element.36), channel_id=1, source_target_pairs={{0,24},{1,25},{2,26},{3,27},{4,28},{5,29},{6,30},{7,31},{8,16},{9,... | collective-permute-start | bytes 1179656 | tf_op jit(solution)/shard_map/ppermute | solution.py:42
  80.1 1.3 collective-permute-start.7
  81.3 5.4 %collective-permute-start.8 = (bf16[2,3,128,256]{3,2,1,0:T(8,128)(2,1)S(1)}, bf16[2,3,128,256]{3,2,1,0:T(8,128)(2,1)}, u32[]{:S(2)}, u32[]{:S(2)}) collective-permute-start(bf16[2,3,128,256]{3,2,1,0:T(8,128)(2,1)S(1)} %get-tuple-element.38), channel_id=1, source_target_pairs={{0,28},{1,29},{2,30},{3,31},{4,24},{5,25},{6,26},{7,27},{8,20},{9,... | collective-permute-start | bytes 1179656 | tf_op jit(solution)/shard_map/ppermute | solution.py:42
  86.7 0.2 collective-permute-start.9
  86.9 0.9 constant_dynamic-slice_fusion.2
  87.8 9.1 %filter_spectrum.1.refs_9_ = f32[8,512,256]{2,1,0:T(8,128)} custom-call(bf16[256,2048]{1,0:T(8,128)(2,1)} %bitcast.35, bf16[8,512,512]{2,1,0:T(8,128)(2,1)} %constant.21.clone.table_ref.refs_10_), custom_call_target="tpu_custom_call" | custom-call | flops 1073741824 | bytes 10485760 | tf_op jit(solution)/shard_map/filter_spectrum/pallas_call | solution.py:140
  96.9 0.0 copy-done.1
  96.9 0.7 constant_dynamic-slice_fusion.1
  97.5 7.4 %collective-permute-done.6.refs_4_ = bf16[2,3,128,256]{3,2,1,0:T(8,128)(2,1)} collective-permute-done((bf16[2,3,128,256]{3,2,1,0:T(8,128)(2,1)S(1)}, bf16[2,3,128,256]{3,2,1,0:T(8,128)(2,1)}, u32[]{:S(2)}, u32[]{:S(2)}) %collective-permute-start.6) | collective-permute-done | bytes 393248 | tf_op jit(solution)/shard_map/ppermute | solution.py:42
  104.9 0.0 collective-permute-done.7.refs_5_
  104.9 7.1 %collective-permute-done.8.refs_6_ = bf16[2,3,128,256]{3,2,1,0:T(8,128)(2,1)} collective-permute-done((bf16[2,3,128,256]{3,2,1,0:T(8,128)(2,1)S(1)}, bf16[2,3,128,256]{3,2,1,0:T(8,128)(2,1)}, u32[]{:S(2)}, u32[]{:S(2)}) %collective-permute-start.8) | collective-permute-done | bytes 393248 | tf_op jit(solution)/shard_map/ppermute | solution.py:42
  112.0 8.4 %collective-permute-done.9.refs_7_ = bf16[2,3,128,256]{3,2,1,0:T(8,128)(2,1)} collective-permute-done((bf16[2,3,128,256]{3,2,1,0:T(8,128)(2,1)S(1)}, bf16[2,3,128,256]{3,2,1,0:T(8,128)(2,1)}, u32[]{:S(2)}, u32[]{:S(2)}) %collective-permute-start.9) | collective-permute-done | bytes 393248 | tf_op jit(solution)/shard_map/ppermute | solution.py:42
  120.4 0.0 all-to-all-done.refs_8_
  120.4 1.0 copy-done
  121.4 23.2 %owner_work.2 = (bf16[16,544,128]{2,1,0:T(8,128)(2,1)}, f32[256,2048]{1,0:T(8,128)}, f32[1,128]{1,0:T(1,128)S(1)}) custom-call(s32[1]{0:T(128)} %bitcast.me_ref, bf16[2,3,128,256]{3,2,1,0:T(8,128)(2,1)} %copy-done.1, bf16[2,3,128,256]{3,2,1,0:T(8,128)(2,1)} %copy-done.2, bf16[2,3,128,256]{3,2,1,0:T(8,128)(2,1)} %copy-done.3, ...), custom_call_target="tpu_custom_call" | custom-call | flops 2736783360 | bytes 25165824 | tf_op jit(solution)/shard_map/owner_work/pallas_call | solution.py:476
  144.6 4.4 %all-to-all-start.2 = ((bf16[16,544,128]{2,1,0:T(8,128)(2,1)}), bf16[16,544,128]{2,1,0:T(8,128)(2,1)S(1)}, u32[]{:S(2)}, u32[]{:S(2)}) async-start(bf16[16,544,128]{2,1,0:T(8,128)(2,1)} %get-tuple-element.43), calls=%async_computation.2 | async-start | bytes 4456448 | tf_op jit(solution)/shard_map/all_to_all | solution.py:588
  149.1 23.5 %owner_work.3 = (bf16[16,544,128]{2,1,0:T(8,128)(2,1)}, f32[256,2048]{1,0:T(8,128)}, f32[1,128]{1,0:T(1,128)S(1)}) custom-call(s32[1]{0:T(128)} %bitcast.me_ref, bf16[2,3,128,256]{3,2,1,0:T(8,128)(2,1)} %copy-done.1, bf16[2,3,128,256]{3,2,1,0:T(8,128)(2,1)} %copy-done.2, bf16[2,3,128,256]{3,2,1,0:T(8,128)(2,1)} %copy-done.3, ...), custom_call_target="tpu_custom_call", output_to_operand_aliasing={{1}: (15, {})} | custom-call | flops 2736783360 | bytes 25165824 | tf_op jit(solution)/shard_map/owner_work/pallas_call | solution.py:476
  172.5 5.8 %all-to-all-done.2.held_ref = bf16[16,544,128]{2,1,0:T(8,128)(2,1)S(1)} async-done(((bf16[16,544,128]{2,1,0:T(8,128)(2,1)}), bf16[16,544,128]{2,1,0:T(8,128)(2,1)S(1)}, u32[]{:S(2)}, u32[]{:S(2)}) %all-to-all-start.2) | async-done | bytes 2228256 | tf_op jit(solution)/shard_map/all_to_all | solution.py:588
  178.3 5.2 %all-to-all-start.1 = ((bf16[16,544,128]{2,1,0:T(8,128)(2,1)}), bf16[16,544,128]{2,1,0:T(8,128)(2,1)}, u32[]{:S(2)}, u32[]{:S(2)}) async-start(bf16[16,544,128]{2,1,0:T(8,128)(2,1)} %get-tuple-element.42), calls=%async_computation.1 | async-start | bytes 4456448 | tf_op jit(solution)/shard_map/all_to_all | solution.py:588
  183.5 0.6 pad_maximum_fusion
  184.1 28.8 %all-to-all-done.1.held_ref = bf16[16,544,128]{2,1,0:T(8,128)(2,1)} async-done(((bf16[16,544,128]{2,1,0:T(8,128)(2,1)}), bf16[16,544,128]{2,1,0:T(8,128)(2,1)}, u32[]{:S(2)}, u32[]{:S(2)}) %all-to-all-start.1) | async-done | bytes 2228256 | tf_op jit(solution)/shard_map/all_to_all | solution.py:588
  212.9 0.9 slice_bitcast_fusion
  213.9 0.9 copy.23
  214.8 1.8 place_columns.2
  216.6 3.5 %place_columns.3 = (bf16[128,4096]{1,0:T(8,128)(2,1)}, bf16[128,12288]{1,0:T(8,128)(2,1)}) custom-call(bf16[16,544,128]{2,1,0:T(8,128)(2,1)} %all-to-all-done.1.held_ref, bf16[128,4096]{1,0:T(8,128)(2,1)} %get-tuple-element.44.refs_0_, bf16[128,12288]{1,0:T(8,128)(2,1)} %get-tuple-element.45.refs_1_), custom_call_target="tpu_custom_call", output_to_operand_aliasing={{0}: (1, {}), {1}: (2, {})} | custom-call | bytes 8388608 | tf_op jit(solution)/shard_map/place_columns/pallas_call | solution.py:547
  (10 shorter events, 0.1 us)
Async XLA Ops:
  2.3 8.8 %collective-permute-start.1 = (bf16[8,3,128,256]{3,2,1,0:T(8,128)(2,1)S(1)}, bf16[8,3,128,256]{3,2,1,0:T(8,128)(2,1)S(1)}, u32[]{:S(2)}, u32[]{:S(2)}) collective-permute-start(bf16[8,3,128,256]{3,2,1,0:T(8,128)(2,1)S(1)} %leaving_pieces.1), channel_id=1, source_target_pairs={{0,1},{1,0},{2,3},{3,2},{4,5},{5,4},{6,7},{7,6},{8,9},{9,8},{10,11... | collective-permute-start | bytes 4718600 | tf_op jit(solution)/shard_map/ppermute | solution.py:42
  5.2 61.0 %collective-permute-start = (bf16[16,128,256]{2,1,0:T(8,128)(2,1)S(1)}, bf16[16,128,256]{2,1,0:T(8,128)(2,1)S(1)}, u32[]{:S(2)}, u32[]{:S(2)}) collective-permute-start(bf16[16,128,256]{2,1,0:T(8,128)(2,1)S(1)} %split_columns.1), channel_id=1, source_target_pairs={{0,112},{16,0},{32,16},{48,32},{64,48},{80,64},{96,80},{112,96},{1... | collective-permute-start | bytes 3145736 | tf_op jit(solution)/shard_map/ppermute | solution.py:32
  14.2 52.2 %collective-permute-start.2 = (bf16[2,3,128,256]{3,2,1,0:T(8,128)(2,1)S(1)}, bf16[2,3,128,256]{3,2,1,0:T(8,128)(2,1)S(1)}, u32[]{:S(2)}, u32[]{:S(2)}) collective-permute-start(bf16[2,3,128,256]{3,2,1,0:T(8,128)(2,1)S(1)} %get-tuple-element.28), channel_id=1, source_target_pairs={{0,16},{1,17},{2,18},{3,19},{4,20},{5,21},{6,22},{7,23},{8,24},{9,... | collective-permute-start | bytes 1179656 | tf_op jit(solution)/shard_map/ppermute | solution.py:42
  14.3 52.1 %collective-permute-start.3 = (bf16[2,3,128,256]{3,2,1,0:T(8,128)(2,1)S(1)}, bf16[2,3,128,256]{3,2,1,0:T(8,128)(2,1)S(1)}, u32[]{:S(2)}, u32[]{:S(2)}) collective-permute-start(bf16[2,3,128,256]{3,2,1,0:T(8,128)(2,1)S(1)} %get-tuple-element.29), channel_id=1, source_target_pairs={{0,18},{1,19},{2,16},{3,17},{4,22},{5,23},{6,20},{7,21},{8,26},{9,... | collective-permute-start | bytes 1179656 | tf_op jit(solution)/shard_map/ppermute | solution.py:42
  17.0 49.5 %collective-permute-start.4 = (bf16[2,3,128,256]{3,2,1,0:T(8,128)(2,1)S(1)}, bf16[2,3,128,256]{3,2,1,0:T(8,128)(2,1)S(1)}, u32[]{:S(2)}, u32[]{:S(2)}) collective-permute-start(bf16[2,3,128,256]{3,2,1,0:T(8,128)(2,1)S(1)} %get-tuple-element.30), channel_id=1, source_target_pairs={{0,20},{1,21},{2,22},{3,23},{4,16},{5,17},{6,18},{7,19},{8,28},{9,... | collective-permute-start | bytes 1179656 | tf_op jit(solution)/shard_map/ppermute | solution.py:42
  20.9 46.3 %collective-permute-start.5 = (bf16[2,3,128,256]{3,2,1,0:T(8,128)(2,1)S(1)}, bf16[2,3,128,256]{3,2,1,0:T(8,128)(2,1)S(1)}, u32[]{:S(2)}, u32[]{:S(2)}) collective-permute-start(bf16[2,3,128,256]{3,2,1,0:T(8,128)(2,1)S(1)} %get-tuple-element.31), channel_id=1, source_target_pairs={{0,22},{1,23},{2,20},{3,21},{4,18},{5,19},{6,16},{7,17},{8,30},{9,... | collective-permute-start | bytes 1179656 | tf_op jit(solution)/shard_map/ppermute | solution.py:42
  66.1 1.1 copy-start.5
  66.5 30.4 %copy-start.1 = (bf16[2,3,128,256]{3,2,1,0:T(8,128)(2,1)}, bf16[2,3,128,256]{3,2,1,0:T(8,128)(2,1)S(1)}, u32[]{:S(2)}) copy-start(bf16[2,3,128,256]{3,2,1,0:T(8,128)(2,1)S(1)} %collective-permute-done.2.refs_0_) | copy-start | bytes 1179652
  66.5 0.8 copy-start.2
  67.2 0.8 copy-start.3
  67.3 0.9 copy-start.4
  68.2 52.2 %all-to-all-start = ((bf16[16,128,256]{2,1,0:T(8,128)(2,1)}), bf16[16,128,256]{2,1,0:T(8,128)(2,1)S(1)}, u32[]{:S(2)}, u32[]{:S(2)}) async-start(bf16[16,128,256]{2,1,0:T(8,128)(2,1)} %copy-done.5), calls=%async_computation | async-start | bytes 2097152 | tf_op jit(solution)/shard_map/all_to_all | solution.py:580
  76.6 28.3 %collective-permute-start.6 = (bf16[2,3,128,256]{3,2,1,0:T(8,128)(2,1)S(1)}, bf16[2,3,128,256]{3,2,1,0:T(8,128)(2,1)}, u32[]{:S(2)}, u32[]{:S(2)}) collective-permute-start(bf16[2,3,128,256]{3,2,1,0:T(8,128)(2,1)S(1)} %get-tuple-element.36), channel_id=1, source_target_pairs={{0,24},{1,25},{2,26},{3,27},{4,28},{5,29},{6,30},{7,31},{8,16},{9,... | collective-permute-start | bytes 1179656 | tf_op jit(solution)/shard_map/ppermute | solution.py:42
  80.1 24.9 %collective-permute-start.7 = (bf16[2,3,128,256]{3,2,1,0:T(8,128)(2,1)S(1)}, bf16[2,3,128,256]{3,2,1,0:T(8,128)(2,1)}, u32[]{:S(2)}, u32[]{:S(2)}) collective-permute-start(bf16[2,3,128,256]{3,2,1,0:T(8,128)(2,1)S(1)} %get-tuple-element.37), channel_id=1, source_target_pairs={{0,26},{1,27},{2,24},{3,25},{4,30},{5,31},{6,28},{7,29},{8,18},{9,... | collective-permute-start | bytes 1179656 | tf_op jit(solution)/shard_map/ppermute | solution.py:42
  81.3 30.7 %collective-permute-start.8 = (bf16[2,3,128,256]{3,2,1,0:T(8,128)(2,1)S(1)}, bf16[2,3,128,256]{3,2,1,0:T(8,128)(2,1)}, u32[]{:S(2)}, u32[]{:S(2)}) collective-permute-start(bf16[2,3,128,256]{3,2,1,0:T(8,128)(2,1)S(1)} %get-tuple-element.38), channel_id=1, source_target_pairs={{0,28},{1,29},{2,30},{3,31},{4,24},{5,25},{6,26},{7,27},{8,20},{9,... | collective-permute-start | bytes 1179656 | tf_op jit(solution)/shard_map/ppermute | solution.py:42
  86.7 33.7 %collective-permute-start.9 = (bf16[2,3,128,256]{3,2,1,0:T(8,128)(2,1)S(1)}, bf16[2,3,128,256]{3,2,1,0:T(8,128)(2,1)}, u32[]{:S(2)}, u32[]{:S(2)}) collective-permute-start(bf16[2,3,128,256]{3,2,1,0:T(8,128)(2,1)S(1)} %get-tuple-element.39), channel_id=1, source_target_pairs={{0,30},{1,31},{2,28},{3,29},{4,26},{5,27},{6,24},{7,25},{8,22},{9,... | collective-permute-start | bytes 1179656 | tf_op jit(solution)/shard_map/ppermute | solution.py:42
  120.4 1.0 copy-start
  144.6 33.7 %all-to-all-start.2 = ((bf16[16,544,128]{2,1,0:T(8,128)(2,1)}), bf16[16,544,128]{2,1,0:T(8,128)(2,1)S(1)}, u32[]{:S(2)}, u32[]{:S(2)}) async-start(bf16[16,544,128]{2,1,0:T(8,128)(2,1)} %get-tuple-element.43), calls=%async_computation.2 | async-start | bytes 4456448 | tf_op jit(solution)/shard_map/all_to_all | solution.py:588
  178.3 34.6 %all-to-all-start.1 = ((bf16[16,544,128]{2,1,0:T(8,128)(2,1)}), bf16[16,544,128]{2,1,0:T(8,128)(2,1)}, u32[]{:S(2)}, u32[]{:S(2)}) async-start(bf16[16,544,128]{2,1,0:T(8,128)(2,1)} %get-tuple-element.42), calls=%async_computation.1 | async-start | bytes 4456448 | tf_op jit(solution)/shard_map/all_to_all | solution.py:588

commit v5 on v4

v5 whole, which is shorter than its diff:
```python
import functools
import math

import jax
import jax.numpy as jnp
import ml_dtypes
import numpy as np
from jax import lax
from jax.experimental import pallas as pl
from jax.experimental.pallas import tpu as pltpu
from jax.sharding import PartitionSpec as P

TAPS = 7
HALO = 8
EXTRA = 32
LATE = 4
ROOT = math.sqrt(0.5)
F32 = jnp.float32
BF16 = jnp.bfloat16
MIB = 1 << 20


def in_hbm(*arrays):
    return [pltpu.with_memory_space_constraint(array, pltpu.HBM) for array in arrays]


def passed_along(value, axis, steps):
    count = lax.axis_size(axis)
    pairs = [(source, (source + steps) % count) for source in range(count)]
    return lax.ppermute(value, axis, pairs)


def handed_over(value, steps, partner):
    sections, groups = lax.axis_size("section"), lax.axis_size("ctx")
    pairs = [
        (section * groups + place, (section + steps) % sections * groups + (place ^ partner))
        for section in range(sections)
        for place in range(groups)
    ]
    return lax.ppermute(value, ("section", "ctx"), pairs)


def leaf_angles():
    angles = [math.pi / 2]
    for _ in range(3):
        angles = [half for angle in angles for half in (angle / 2, angle / 2 + math.pi)]
    return angles


def leaf_tables(length):
    leaf = length // 8
    order = np.arange(leaf)
    tables = []
    for angle in leaf_angles():
        phase = (angle + 2.0 * np.pi * order[:, None]) / leaf * order[None, :]
        real, imag = np.cos(phase), np.sin(phase)
        tables.append(np.block([[real, -imag], [imag, real]]))
    table = np.stack(tables)
    back = table.transpose(0, 2, 1) / length
    return table.astype(ml_dtypes.bfloat16), back.astype(ml_dtypes.bfloat16)


def turned(pair, angle):
    real, imag = pair
    cos, sin = math.cos(angle), math.sin(angle)
    return real * cos - imag * sin, real * sin + imag * cos


def split_rings(parts):
    low, high = [], []
    for lower, upper in zip(parts[:4], parts[4:]):
        scaled = upper * ROOT
        low.append((lower + scaled, scaled))
        high.append((lower - scaled, -scaled))
    rings = [(math.pi / 4, low), (math.pi / 4 + math.pi, high)]
    while len(rings[0][1]) > 1:
        finer = []
        for angle, pieces in rings:
            half = len(pieces) // 2
            plus, minus = [], []
            for lower, upper in zip(pieces[:half], pieces[half:]):
                real, imag = turned(upper, angle / 2)
                plus.append((lower[0] + real, lower[1] + imag))
                minus.append((lower[0] - real, lower[1] - imag))
            finer += [(angle / 2, plus), (angle / 2 + math.pi, minus)]
        rings = finer
    return [pieces[0] for _, pieces in rings]


def join_rings(leaves):
    angles = [math.pi / 4, math.pi / 4 + math.pi]
    angles = [half for angle in angles for half in (angle / 2, angle / 2 + math.pi)]
    groups = [[leaf] for leaf in leaves]
    while len(groups) > 2:
        merged = []
        for index in range(0, len(groups), 2):
            angle = angles[index // 2] if len(groups) == 8 else [math.pi / 4, math.pi / 4 + math.pi][index // 2]
            lower, upper = [], []
            for plus, minus in zip(groups[index], groups[index + 1]):
                lower.append((plus[0] + minus[0], plus[1] + minus[1]))
                upper.append(turned((plus[0] - minus[0], plus[1] - minus[1]), -angle / 2))
            merged.append(lower + upper)
        groups = merged
    lower, upper = [], []
    for plus, minus in zip(groups[0], groups[1]):
        lower.append(plus[0] + minus[0])
        upper.append(((plus[0] - minus[0]) + (plus[1] - minus[1])) * ROOT)
    return lower + upper


def filter_kernel(filt_ref, table_ref, spec_ref, rings):
    chans, length = filt_ref.shape
    leaf = length // 8
    step = pl.program_id(0)

    @pl.when(step == 0)
    def _():
        @pl.loop(0, chans // 16)
        def _(strip):
            rows = pl.ds(pl.multiple_of(strip * 16, 16), 16)
            for lane in range(0, leaf, 128):
                parts = [
                    filt_ref[rows, piece * leaf + lane : piece * leaf + lane + 128].astype(F32)
                    for piece in range(8)
                ]
                for index, (real, imag) in enumerate(split_rings(parts)):
                    rings[index, rows, lane : lane + 128] = real.astype(BF16)
                    rings[index, rows, leaf + lane : leaf + lane + 128] = imag.astype(BF16)

    spec_ref[0] = lax.dot_general(
        table_ref[0], rings[step], (((1,), (1,)), ((), ())), preferred_element_type=F32
    )


def filter_spectrum(filt, table):
    chans, length = filt.shape
    wide = length // 4
    return pl.pallas_call(
        filter_kernel,
        out_shape=pltpu.HBM((8, wide, chans), F32),
        grid=(8,),
        in_specs=[
            pl.BlockSpec((chans, length), lambda j: (0, 0)),
            pl.BlockSpec((1, wide, wide), lambda j: (j, 0, 0)),
        ],
        out_specs=pl.BlockSpec((1, wide, chans), lambda j: (j, 0, 0)),
        scratch_shapes=[pltpu.VMEM((8, chans, wide), BF16)],
        compiler_params=pltpu.CompilerParams(vmem_limit_bytes=12 * MIB),
        cost_estimate=pl.CostEstimate(
            flops=16 * wide * wide * chans, bytes_accessed=10 * MIB, transcendentals=0
        ),
        name="filter_spectrum",
    )(*in_hbm(filt, table))


def wait_all(copies):
    for copy in copies:
        copy.start()
    for copy in copies:
        copy.wait()


def leave_kernel(me_ref, wide_ref, leaving_ref, sems):
    chips, roles, _, chans = leaving_ref.shape
    width = wide_ref.shape[1] // 3
    copies = []
    for chip in range(chips):
        start = (me_ref[0] ^ (2 * chip + 1)) * chans
        for role in range(roles):
            columns = pl.ds(pl.multiple_of((role + 1) * width + start, 128), chans)
            copies.append(
                pltpu.make_async_copy(wide_ref.at[:, columns], leaving_ref.at[chip, role], sems.at[chip, role])
            )
    wait_all(copies)


def piece_kernel(me_ref, wide_ref, came_ref, *refs):
    *pieces, sems = refs
    _, roles, _, chans = pieces[0].shape
    width = wide_ref.shape[1] // 3
    copies = []
    for chip, piece in enumerate(pieces):
        start = (me_ref[0] ^ (2 * chip)) * chans
        for role in range(roles):
            columns = pl.ds(pl.multiple_of((role + 1) * width + start, 128), chans)
            copies.append(pltpu.make_async_copy(wide_ref.at[:, columns], piece.at[0, role], sems.at[chip, role]))
        copies.append(pltpu.make_async_copy(came_ref.at[chip], piece.at[1], sems.at[chip, roles]))
    wait_all(copies)


def leaving_pieces(me, wide, groups, roles):
    rows, width = wide.shape
    chans = width // 3 // groups
    return pl.pallas_call(
        leave_kernel,
        out_shape=jax.ShapeDtypeStruct((groups // 2, roles, rows, chans), BF16),
        in_specs=[pl.BlockSpec(memory_space=pltpu.SMEM), pl.BlockSpec(memory_space=pl.ANY)],
        out_specs=pl.BlockSpec(memory_space=pltpu.VMEM),
        scratch_shapes=[pltpu.SemaphoreType.DMA((groups // 2, roles))],
        compiler_params=pltpu.CompilerParams(vmem_limit_bytes=4 * MIB),
        cost_estimate=pl.CostEstimate(flops=0, bytes_accessed=2 * rows * width, transcendentals=0),
        name="leaving_pieces",
    )(me, *in_hbm(wide))


def pieces_for_owners(me, wide, came, groups):
    chips, roles, rows, chans = came.shape
    return pl.pallas_call(
        piece_kernel,
        out_shape=[jax.ShapeDtypeStruct((2, roles, rows, chans), BF16)] * chips,
        in_specs=[pl.BlockSpec(memory_space=pltpu.SMEM), pl.BlockSpec(memory_space=pl.ANY), pl.BlockSpec(memory_space=pltpu.VMEM)],
        out_specs=[pl.BlockSpec(memory_space=pltpu.VMEM)] * chips,
        scratch_shapes=[pltpu.SemaphoreType.DMA((chips, roles + 1))],
        compiler_params=pltpu.CompilerParams(vmem_limit_bytes=8 * MIB),
        cost_estimate=pl.CostEstimate(flops=0, bytes_accessed=8 * chips * roles * rows * chans, transcendentals=0),
        name="pieces_for_owners",
    )(me, *in_hbm(wide), came)


def tap_sum(held, part, taps, row):
    total = taps[0] * held[part, HALO + row : HALO + row + 16, :]
    for tap in range(1, TAPS):
        total = total + taps[tap] * held[part, HALO + row - tap : HALO + row - tap + 16, :]
    return total


def hold(held, part, block):
    rows = block.shape[0]
    held[part, 0:HALO, :] = held[part, rows : rows + HALO, :]
    held[part, HALO:, :] = block.astype(F32)


def tap_rows(taps_ref, role, lanes):
    return [taps_ref[role, tap : tap + 1, lanes] for tap in range(TAPS)]


def split_signal(signal, rings):
    groups, rows, chans = signal.shape
    leaf = groups * rows // 8
    per_piece = leaf // rows

    @pl.loop(0, rows // 16)
    def _(strip):
        inside = pl.ds(pl.multiple_of(strip * 16, 16), 16)
        for part in range(per_piece):
            real_rows = pl.ds(pl.multiple_of(part * rows + strip * 16, 16), 16)
            imag_rows = pl.ds(pl.multiple_of(leaf + part * rows + strip * 16, 16), 16)
            for lane in range(0, chans, 128):
                lanes = slice(lane, lane + 128)
                parts = [signal[piece * per_piece + part, inside, lanes].astype(F32) for piece in range(8)]
                for index, (real, imag) in enumerate(split_rings(parts)):
                    rings[index, real_rows, lanes] = real.astype(BF16)
                    rings[index, imag_rows, lanes] = imag.astype(BF16)


def join_signal(joined, first, rows, place):
    leaf = joined.shape[1] // 2
    per_piece = leaf // rows
    chans = 256 if joined.shape[2] % 256 == 0 else 128

    @pl.loop(0, rows // 16)
    def _(strip):
        inside = pl.ds(pl.multiple_of(strip * 16, 16), 16)
        for part in range(per_piece):
            real_rows = pl.ds(pl.multiple_of(part * rows + strip * 16, 16), 16)
            imag_rows = pl.ds(pl.multiple_of(leaf + part * rows + strip * 16, 16), 16)
            for lane in range(0, chans, 128):
                column = slice(first + lane, first + lane + 128)
                leaves = [
                    (joined[index, real_rows, column], joined[index, imag_rows, column]) for index in range(8)
                ]
                for piece, result in enumerate(join_rings(leaves)):
                    place(piece * per_piece + part, strip, inside, slice(lane, lane + 128), result)


def back_taps(grads, source_block, part, taps, place, sums, role, lanes):
    rows = grads.shape[1] - HALO
    parts = [jnp.zeros((16, 128), F32) for _ in range(TAPS)]
    for row in range(0, rows, 16):
        here = source_block(row).astype(F32)
        total = jnp.zeros((16, 128), F32)
        for tap in range(TAPS):
            ahead = grads[part, row + tap : row + tap + 16, :]
            total = total + taps[tap] * ahead
            parts[tap] = parts[tap] + here * ahead
        place(row, total.astype(BF16))
    for tap in range(TAPS):
        sums[role, tap, :, lanes] += parts[tap][0:8] + parts[tap][8:16]


def sum_rows(sums, roles):
    rows_out = []
    chans = sums.shape[3]
    for role in range(roles):
        for tap in range(TAPS):
            rows_out.append(jnp.sum(sums[role, tap], axis=0, keepdims=True))
        rows_out.append(jnp.zeros((HALO - TAPS, chans), F32))
    return rows_out


def mixed_kernel(groups, me_ref, *refs):
    pieces = refs[: groups // 2]
    spec_hbm, table_hbm, back_hbm, taps_ref, gain_ref = refs[groups // 2 : groups // 2 + 5]
    (
        feats_hbm, gated_hbm, inner_ref, ring_hbm,
        source, spec, table, back, held, feats, gated, rings, products, joined, ring,
        piece_sems, load_sems, feats_sems, gated_sem, ring_sems,
    ) = refs[groups // 2 + 5 :]
    _, _, rows, chans = source.shape
    for partner in range(groups):
        block = me_ref[0] ^ partner
        piece = pieces[partner // 2].at[partner % 2]
        pltpu.make_async_copy(piece, source.at[block], piece_sems.at[block]).start()
    loads = []
    for index in range(8):
        for kind, (from_ref, into) in enumerate(((table_hbm, table), (spec_hbm, spec), (back_hbm, back))):
            loads.append(pltpu.make_async_copy(from_ref.at[index], into.at[index], load_sems.at[kind, index]))
            loads[-1].start()
    held[:, :, rows:, :] = jnp.zeros((2, chans // 128, HALO, 128), F32)

    def feats_copy(block):
        return pltpu.make_async_copy(feats.at[block], feats_hbm.at[block], feats_sems.at[block])

    @pl.loop(0, groups)
    def _(step):
        pltpu.make_async_copy(pieces[0].at[0], source.at[step], piece_sems.at[step]).wait()
        for part in range(chans // 128):
            lanes = slice(part * 128, part * 128 + 128)
            for role in range(2):
                hold(held.at[role], part, source[step, role, :, lanes])
            taps = [tap_rows(taps_ref, role + 1, lanes) for role in range(2)]
            for row in range(0, rows, 16):
                span = slice(row, row + 16)
                keyed, value = [tap_sum(held.at[role], part, taps[role], row) for role in range(2)]
                feats[step, 0, span, lanes] = keyed
                feats[step, 1, span, lanes] = value
                gated[step, span, lanes] = (keyed * value).astype(BF16)
        feats_copy(step).start()

    gated_copy = pltpu.make_async_copy(gated, gated_hbm, gated_sem.at[0])
    gated_copy.start()
    split_signal(gated, rings)
    leaf = spec.shape[1] // 2

    def ring_copy(index):
        return pltpu.make_async_copy(ring.at[index], ring_hbm.at[index], ring_sems.at[index])

    @pl.loop(0, 8)
    def _(index):
        for kind, (from_ref, into) in enumerate(((table_hbm, table), (spec_hbm, spec), (back_hbm, back))):
            pltpu.make_async_copy(from_ref.at[index], into.at[index], load_sems.at[kind, index]).wait()
        ring[index] = jnp.dot(table[index], rings[index], preferred_element_type=F32)
        g_real, g_imag = ring[index, :leaf], ring[index, leaf:]
        f_real, f_imag = spec[index, :leaf], spec[index, leaf:]
        products[:leaf] = (g_real * f_real - g_imag * f_imag).astype(BF16)
        products[leaf:] = (g_real * f_imag + g_imag * f_real).astype(BF16)
        joined[index] = jnp.dot(back[index], products[...], preferred_element_type=F32)
        ring_copy(index).start()

    def place(owner, strip, inside, lanes, result):
        total = result + gain_ref[0:1, lanes] * gated[owner, inside, lanes].astype(F32)
        inner_ref[owner, inside, lanes] = total.astype(BF16)

    join_signal(joined, 0, rows, place)
    for owner in range(groups - 1):
        inner_ref[owner, rows:, :] = inner_ref[owner + 1, 0:HALO, :]
    inner_ref[groups - 1, rows:, :] = jnp.zeros((HALO, chans), BF16)

    @pl.loop(0, groups)
    def _(step):
        feats_copy(step).wait()

    gated_copy.wait()

    @pl.loop(0, 8)
    def _(index):
        ring_copy(index).wait()


def inner_work(me, pieces, spectrum, table, back, taps, gain):
    groups = 2 * len(pieces)
    _, _, rows, chans = pieces[0].shape
    length = groups * rows
    wide = length // 4
    parts = chans // 128
    return pl.pallas_call(
        functools.partial(mixed_kernel, groups),
        out_shape=(
            pltpu.HBM((groups, 2, rows, chans), F32),
            pltpu.HBM((groups, rows, chans), BF16),
            jax.ShapeDtypeStruct((groups, rows + HALO, chans), BF16),
            pltpu.HBM((8, wide, chans), F32),
        ),
        in_specs=[pl.BlockSpec(memory_space=pltpu.SMEM)]
        + [pl.BlockSpec(memory_space=pl.ANY)] * (groups // 2 + 3)
        + [pl.BlockSpec(memory_space=pltpu.VMEM)] * 2,
        out_specs=(
            pl.BlockSpec(memory_space=pl.ANY),
            pl.BlockSpec(memory_space=pl.ANY),
            pl.BlockSpec(memory_space=pltpu.VMEM),
            pl.BlockSpec(memory_space=pl.ANY),
        ),
        scratch_shapes=[
            pltpu.VMEM((groups, 2, rows, chans), BF16),
            pltpu.VMEM((8, wide, chans), F32),
            pltpu.VMEM((8, wide, wide), BF16),
            pltpu.VMEM((8, wide, wide), BF16),
            pltpu.VMEM((2, parts, HALO + rows, 128), F32),
            pltpu.VMEM((groups, 2, rows, chans), F32),
            pltpu.VMEM((groups, rows, chans), BF16),
            pltpu.VMEM((8, wide, chans), BF16),
            pltpu.VMEM((wide, chans), BF16),
            pltpu.VMEM((8, wide, chans), F32),
            pltpu.VMEM((8, wide, chans), F32),
            pltpu.SemaphoreType.DMA((groups,)),
            pltpu.SemaphoreType.DMA((3, 8)),
            pltpu.SemaphoreType.DMA((groups,)),
            pltpu.SemaphoreType.DMA((1,)),
            pltpu.SemaphoreType.DMA((8,)),
        ],
        compiler_params=pltpu.CompilerParams(vmem_limit_bytes=40 * MIB),
        cost_estimate=pl.CostEstimate(
            flops=32 * wide * wide * chans + 60 * length * chans, bytes_accessed=24 * MIB, transcendentals=0
        ),
        name="inner_values",
    )(me, *in_hbm(*pieces, spectrum, table, back), taps, gain)


def query_kernel(source, before, incoming, taps_ref, mix_grad, features, held):
    groups, rows, chans = mix_grad.shape

    @pl.loop(0, groups)
    def _(owner):
        for part in range(chans // 128):
            columns = pl.ds(pl.multiple_of(owner * chans + part * 128, 128), 128)
            lanes = slice(part * 128, part * 128 + 128)
            held[part, 0:HALO, :] = before[:, columns].astype(F32)
            held[part, HALO:, :] = source[:, columns].astype(F32)
            taps = [taps_ref[tap : tap + 1, columns] for tap in range(TAPS)]
            for row in range(0, rows, 16):
                span = slice(row, row + 16)
                total = tap_sum(held, part, taps, row)
                features[span, columns] = total
                mix_grad[owner, span, lanes] = (incoming[span, columns].astype(F32) * total).astype(BF16)


def query_features(source, before, incoming, taps, groups):
    rows, width = source.shape
    chans = width // groups
    return pl.pallas_call(
        query_kernel,
        out_shape=(
            jax.ShapeDtypeStruct((groups, rows, chans), BF16),
            jax.ShapeDtypeStruct((rows, width), F32),
        ),
        in_specs=[pl.BlockSpec(memory_space=pltpu.VMEM)] * 4,
        out_specs=(pl.BlockSpec(memory_space=pltpu.VMEM),) * 2,
        scratch_shapes=[pltpu.VMEM((chans // 128, HALO + rows, 128), F32)],
        compiler_params=pltpu.CompilerParams(vmem_limit_bytes=10 * MIB),
        cost_estimate=pl.CostEstimate(flops=15 * rows * width, bytes_accessed=10 * rows * width, transcendentals=0),
        name="query_features",
    )(source, before, incoming, taps)


def output_kernel(
    source, incoming, later, features, inner, taps_ref, output_hbm, grad_hbm, sums_ref, grads, sums, slots, slot_sems
):
    groups, _, chans = inner.shape
    rows = source.shape[0]

    def write_back(owner, slot):
        columns = pl.ds(pl.multiple_of(owner * chans, 128), chans)
        return [
            pltpu.make_async_copy(slots.at[slot, kind], into.at[:, columns], slot_sems.at[slot, kind])
            for kind, into in enumerate((output_hbm, grad_hbm))
        ]

    @pl.loop(0, groups)
    def _(owner):
        slot = lax.rem(owner, 2)

        @pl.when(owner >= 2)
        def _():
            for copy in write_back(owner - 2, slot):
                copy.wait()

        sums[...] = jnp.zeros_like(sums)
        for part in range(chans // 128):
            columns = pl.ds(pl.multiple_of(owner * chans + part * 128, 128), 128)
            lanes = slice(part * 128, part * 128 + 128)
            for row in range(0, rows, 16):
                span = slice(row, row + 16)
                values = inner[owner, span, lanes].astype(F32)
                grads[part, span, :] = incoming[span, columns].astype(F32) * values
                slots[slot, 0, span, lanes] = (features[span, columns] * values).astype(BF16)
            ahead = inner[owner, rows : rows + HALO, lanes].astype(F32)
            grads[part, rows:, :] = later[:, columns].astype(F32) * ahead

            def place(row, values, lanes=lanes):
                slots[slot, 1, row : row + 16, lanes] = values

            def source_block(row, columns=columns):
                return source[row : row + 16, columns]

            taps = [taps_ref[tap : tap + 1, columns] for tap in range(TAPS)]
            back_taps(grads, source_block, part, taps, place, sums, 0, lanes)
        sums_ref[owner] = jnp.concatenate(sum_rows(sums, 1), axis=0).astype(BF16)
        for copy in write_back(owner, slot):
            copy.start()

    for owner in (groups - 2, groups - 1):
        for copy in write_back(owner, owner % 2):
            copy.wait()


def query_outputs(source, incoming, later, features, inner, taps):
    rows, width = source.shape
    groups, _, chans = inner.shape
    return pl.pallas_call(
        output_kernel,
        out_shape=(
            pltpu.HBM((rows, width), BF16),
            pltpu.HBM((rows, 3 * width), BF16),
            jax.ShapeDtypeStruct((groups, HALO, chans), BF16),
        ),
        in_specs=[pl.BlockSpec(memory_space=pltpu.VMEM)] * 6,
        out_specs=(
            pl.BlockSpec(memory_space=pl.ANY),
            pl.BlockSpec(memory_space=pl.ANY),
            pl.BlockSpec(memory_space=pltpu.VMEM),
        ),
        scratch_shapes=[
            pltpu.VMEM((chans // 128, rows + HALO, 128), F32),
            pltpu.VMEM((1, TAPS, 8, chans), F32),
            pltpu.VMEM((2, 2, rows, chans), BF16),
            pltpu.SemaphoreType.DMA((2, 2)),
        ],
        compiler_params=pltpu.CompilerParams(vmem_limit_bytes=12 * MIB),
        cost_estimate=pl.CostEstimate(flops=35 * rows * width, bytes_accessed=14 * rows * width, transcendentals=0),
        name="query_outputs",
    )(source, incoming, later, features, inner, taps)


def through_kernel(groups, me_ref, *refs):
    pieces = refs[: groups // 2]
    (
        grad_hbm, feats_hbm, spec_hbm, table_hbm, back_hbm, taps_ref, gain_ref,
        ready_hbm, ring_hbm,
        source, mix_grad, feats, spec, ring, table, back, rings, products, joined, through,
        grads, sums, slots, last,
        piece_sems, signal_sem, feats_sems, load_sems, ring_sems, slot_sems, last_sems,
    ) = refs[groups // 2 :]
    _, rows, chans = through.shape
    signal = pltpu.make_async_copy(grad_hbm, mix_grad, signal_sem.at[0])
    signal.start()
    kinds = ((table_hbm, table), (spec_hbm, spec), (back_hbm, back))
    for index in range(8):
        for kind, (from_ref, into) in enumerate(kinds):
            pltpu.make_async_copy(from_ref.at[index], into.at[index], load_sems.at[kind, index]).start()
    for partner in range(groups):
        block = me_ref[0] ^ partner
        piece = pieces[partner // 2].at[partner % 2]
        pltpu.make_async_copy(piece, source.at[block], piece_sems.at[block]).start()

    def feats_copy(block):
        return pltpu.make_async_copy(feats_hbm.at[block], feats.at[block], feats_sems.at[block])

    for block in range(groups):
        feats_copy(block).start()
    grads[:, :, 0:HALO, :] = jnp.zeros((2, chans // 128, HALO, 128), F32)
    sums[...] = jnp.zeros_like(sums)
    signal.wait()
    split_signal(mix_grad, rings)
    leaf = spec.shape[1] // 2

    def ring_copy(index):
        return pltpu.make_async_copy(ring.at[index], ring_hbm.at[index], ring_sems.at[index])

    @pl.loop(0, 8)
    def _(index):
        for kind, (from_ref, into) in enumerate(kinds):
            pltpu.make_async_copy(from_ref.at[index], into.at[index], load_sems.at[kind, index]).wait()
        ring[index] = jnp.dot(table[index], rings[index], preferred_element_type=F32)
        d_real, d_imag = ring[index, :leaf], ring[index, leaf:]
        f_real, f_imag = spec[index, :leaf], spec[index, leaf:]
        products[:leaf] = (d_real * f_real + d_imag * f_imag).astype(BF16)
        products[leaf:] = (d_imag * f_real - d_real * f_imag).astype(BF16)
        joined[index] = jnp.dot(back[index], products[...], preferred_element_type=F32)
        ring_copy(index).start()

    def place_through(owner, strip, inside, lanes, result):
        grad = mix_grad[owner, inside, lanes].astype(F32)
        through[owner, inside, lanes] = (result + gain_ref[0:1, lanes] * grad).astype(BF16)

    join_signal(joined, 0, rows, place_through)

    @pl.loop(0, groups)
    def _(block):
        pltpu.make_async_copy(pieces[0].at[0], source.at[block], piece_sems.at[block]).wait()
        feats_copy(block).wait()

    def write_back(slot_at, block_at):
        return pltpu.make_async_copy(
            slots.at[slot_at], ready_hbm.at[block_at, pl.ds(0, 2 * rows)], slot_sems.at[slot_at]
        )

    @pl.loop(0, groups)
    def _(step):
        block = groups - 1 - step
        slot = lax.rem(step, 2)

        @pl.when(step >= 2)
        def _():
            write_back(slot, block + 2).wait()

        for part in range(chans // 128):
            lanes = slice(part * 128, part * 128 + 128)
            for role in range(2):
                grads[role, part, rows : rows + HALO, :] = grads[role, part, 0:HALO, :]
            for row in range(0, rows, 16):
                span = slice(row, row + 16)
                values = through[block, span, lanes].astype(F32)
                grads[0, part, span, :] = values * feats[block, 1, span, lanes]
                grads[1, part, span, :] = values * feats[block, 0, span, lanes]
            for role in range(2):

                def place(row, values, role=role, lanes=lanes):
                    slots[slot, role * rows + row : role * rows + row + 16, lanes] = values

                def source_block(row, role=role, lanes=lanes):
                    return source[block, role, row : row + 16, lanes]

                taps = tap_rows(taps_ref, role + 1, lanes)
                back_taps(grads.at[role], source_block, part, taps, place, sums, role, lanes)
        write_back(slot, block).start()

    rows_out = [jnp.zeros((HALO, chans), F32)] + sum_rows(sums, 2)
    rows_out.append(jnp.zeros((EXTRA - 3 * HALO, chans), F32))
    last[...] = jnp.concatenate(rows_out, axis=0).astype(BF16)
    wait_all(
        [
            pltpu.make_async_copy(last, ready_hbm.at[owner, pl.ds(2 * rows, EXTRA)], last_sems.at[owner])
            for owner in range(groups)
        ]
    )
    write_back(groups % 2, 1).wait()
    write_back((groups + 1) % 2, 0).wait()

    @pl.loop(0, 8)
    def _(index):
        ring_copy(index).wait()


def through_work(me, pieces, mix_grad, feats, spectrum, table, back, taps, gain):
    groups, rows, chans = mix_grad.shape
    length = groups * rows
    wide = length // 4
    parts = chans // 128
    return pl.pallas_call(
        functools.partial(through_kernel, groups),
        out_shape=(
            pltpu.HBM((groups, 2 * rows + EXTRA, chans), BF16),
            pltpu.HBM((8, wide, chans), F32),
        ),
        in_specs=[pl.BlockSpec(memory_space=pltpu.SMEM)]
        + [pl.BlockSpec(memory_space=pl.ANY)] * (groups // 2 + 5)
        + [pl.BlockSpec(memory_space=pltpu.VMEM)] * 2,
        out_specs=(pl.BlockSpec(memory_space=pl.ANY),) * 2,
        scratch_shapes=[
            pltpu.VMEM((groups, 2, rows, chans), BF16),
            pltpu.VMEM((groups, rows, chans), BF16),
            pltpu.VMEM((groups, 2, rows, chans), F32),
            pltpu.VMEM((8, wide, chans), F32),
            pltpu.VMEM((8, wide, chans), F32),
            pltpu.VMEM((8, wide, wide), BF16),
            pltpu.VMEM((8, wide, wide), BF16),
            pltpu.VMEM((8, wide, chans), BF16),
            pltpu.VMEM((wide, chans), BF16),
            pltpu.VMEM((8, wide, chans), F32),
            pltpu.VMEM((groups, rows, chans), BF16),
            pltpu.VMEM((2, parts, rows + HALO, 128), F32),
            pltpu.VMEM((2, TAPS, 8, chans), F32),
            pltpu.VMEM((2, 2 * rows, chans), BF16),
            pltpu.VMEM((EXTRA, chans), BF16),
            pltpu.SemaphoreType.DMA((groups,)),
            pltpu.SemaphoreType.DMA((1,)),
            pltpu.SemaphoreType.DMA((groups,)),
            pltpu.SemaphoreType.DMA((3, 8)),
            pltpu.SemaphoreType.DMA((8,)),
            pltpu.SemaphoreType.DMA((2,)),
            pltpu.SemaphoreType.DMA((groups,)),
        ],
        compiler_params=pltpu.CompilerParams(vmem_limit_bytes=40 * MIB),
        cost_estimate=pl.CostEstimate(
            flops=32 * wide * wide * chans + 100 * length * chans, bytes_accessed=28 * MIB, transcendentals=0
        ),
        name="through_values",
    )(me, *in_hbm(*pieces), mix_grad, *in_hbm(feats, spectrum, table, back), taps, gain)


def filter_grad_kernel(
    grad_hbm, gated_hbm, d_hbm, g_hbm, back_hbm, filt_hbm, skip_ref,
    mix_grad, gated, d_ring, g_ring, back, products, joined, flat, turned_flat, signal_sems, load_sems, filt_sem,
):
    groups, rows, chans = mix_grad.shape
    signals = [
        pltpu.make_async_copy(grad_hbm, mix_grad, signal_sems.at[0]),
        pltpu.make_async_copy(gated_hbm, gated, signal_sems.at[1]),
    ]
    kinds = ((d_hbm, d_ring), (g_hbm, g_ring), (back_hbm, back))
    for index in range(8):
        for kind, (from_ref, into) in enumerate(kinds):
            pltpu.make_async_copy(from_ref.at[index], into.at[index], load_sems.at[kind, index]).start()
    for copy in signals:
        copy.start()
    leaf = d_ring.shape[1] // 2

    @pl.loop(0, 8)
    def _(index):
        for kind, (from_ref, into) in enumerate(kinds):
            pltpu.make_async_copy(from_ref.at[index], into.at[index], load_sems.at[kind, index]).wait()
        d_real, d_imag = d_ring[index, :leaf], d_ring[index, leaf:]
        g_real, g_imag = g_ring[index, :leaf], g_ring[index, leaf:]
        products[:leaf] = (d_real * g_real + d_imag * g_imag).astype(BF16)
        products[leaf:] = (d_imag * g_real - d_real * g_imag).astype(BF16)
        joined[index] = jnp.dot(back[index], products[...], preferred_element_type=F32)

    for copy in signals:
        copy.wait()
    skip_ref[...] = jnp.zeros_like(skip_ref)

    @pl.loop(0, groups)
    def _(block):
        for lane in range(0, chans, 128):
            lanes = slice(lane, lane + 128)
            total = jnp.zeros((16, 128), F32)
            for row in range(0, rows, 16):
                span = slice(row, row + 16)
                total = total + mix_grad[block, span, lanes].astype(F32) * gated[block, span, lanes].astype(F32)
            skip_ref[0:1, lanes] += jnp.sum(total, axis=0, keepdims=True)

    def place_filter(owner, strip, inside, lanes, result):
        flat[pl.ds(pl.multiple_of(owner * rows + strip * 16, 16), 16), lanes] = result

    join_signal(joined, 0, rows, place_filter)
    for block in range(groups):
        span = slice(block * rows, (block + 1) * rows)
        turned_flat[:, span] = flat[span, :].T
    wait_all([pltpu.make_async_copy(turned_flat, filt_hbm, filt_sem.at[0])])


def filter_gradient(mix_grad, gated, d_ring, g_ring, back):
    groups, rows, chans = mix_grad.shape
    length = groups * rows
    wide = length // 4
    return pl.pallas_call(
        filter_grad_kernel,
        out_shape=(pltpu.HBM((chans, length), F32), jax.ShapeDtypeStruct((1, chans), F32)),
        in_specs=[pl.BlockSpec(memory_space=pl.ANY)] * 5,
        out_specs=(pl.BlockSpec(memory_space=pl.ANY), pl.BlockSpec(memory_space=pltpu.VMEM)),
        scratch_shapes=[
            pltpu.VMEM((groups, rows, chans), BF16),
            pltpu.VMEM((groups, rows, chans), BF16),
            pltpu.VMEM((8, wide, chans), F32),
            pltpu.VMEM((8, wide, chans), F32),
            pltpu.VMEM((8, wide, wide), BF16),
            pltpu.VMEM((wide, chans), BF16),
            pltpu.VMEM((8, wide, chans), F32),
            pltpu.VMEM((length, chans), F32),
            pltpu.VMEM((chans, length), F32),
            pltpu.SemaphoreType.DMA((2,)),
            pltpu.SemaphoreType.DMA((3, 8)),
            pltpu.SemaphoreType.DMA((1,)),
        ],
        compiler_params=pltpu.CompilerParams(vmem_limit_bytes=28 * MIB),
        cost_estimate=pl.CostEstimate(
            flops=16 * wide * wide * chans + 40 * length * chans, bytes_accessed=16 * MIB, transcendentals=0
        ),
        name="filter_gradient",
    )(mix_grad, *in_hbm(gated, d_ring, g_ring, back))


def place_kernel(columns, held_ref, *refs):
    *wide_refs, sems = refs
    groups, _, chans = held_ref.shape
    rows = wide_refs[-1].shape[0]
    wide_refs = wide_refs[-1 - max(index for index, _ in columns) :]
    copies = []
    for owner in range(groups):
        for kind, (index, first) in enumerate(columns):
            copies.append(
                pltpu.make_async_copy(
                    held_ref.at[owner, pl.ds(kind * rows, rows)],
                    wide_refs[index].at[:, pl.ds(first * groups * chans + owner * chans, chans)],
                    sems.at[owner, kind],
                )
            )
    wait_all(copies)


def place_columns(held, rows, columns, earlier):
    groups, _, chans = held.shape
    width = groups * chans
    shapes = [(rows, 3 * width)]
    return pl.pallas_call(
        functools.partial(place_kernel, columns),
        input_output_aliases={1: 0} if earlier else {},
        out_shape=[pltpu.HBM(shape, BF16) for shape in shapes],
        in_specs=[pl.BlockSpec(memory_space=pltpu.VMEM)] + [pl.BlockSpec(memory_space=pl.ANY)] * len(earlier),
        out_specs=[pl.BlockSpec(memory_space=pl.ANY)] * len(shapes),
        scratch_shapes=[pltpu.SemaphoreType.DMA((groups, 2))],
        compiler_params=pltpu.CompilerParams(vmem_limit_bytes=6 * MIB),
        cost_estimate=pl.CostEstimate(flops=0, bytes_accessed=8 * rows * width, transcendentals=0),
        name="place_columns",
    )(held, *in_hbm(*earlier))


def from_behind(block, axis, distance):
    devices = range(lax.axis_size(axis))
    route = [(i - distance, i) for i in devices if i - distance in devices]
    return lax.ppermute(block, axis, route)


def on_device(acts, cots, kern, filt, skip):
    rows, feats_all = acts.shape[1:]
    groups = lax.axis_size("ctx")
    chans = filt.shape[1]
    width = groups * chans
    place = lax.axis_index("ctx").astype(jnp.int32)
    me = place[None]

    table, back = (jnp.asarray(one) for one in leaf_tables(rows * groups))
    spectrum = filter_spectrum(filt[0], table)
    gain = lax.dynamic_slice_in_dim(skip, place * chans, chans, axis=1)
    taps = kern[0].reshape(TAPS, 3, groups, chans)
    taps = lax.dynamic_index_in_dim(taps, place, axis=2, keepdims=False).transpose(1, 0, 2)
    taps = jnp.pad(taps, ((0, 0), (0, HALO - TAPS), (0, 0)))
    query_taps = jnp.pad(kern[0, :, :width], ((0, HALO - TAPS), (0, 0)))

    came = handed_over(leaving_pieces(me, acts[0], groups, 2), 0, 1)
    pieces = pieces_for_owners(me, acts[0], came, groups)
    pieces = [handed_over(piece, 1, 2 * chip) for chip, piece in enumerate(pieces)]
    query, incoming = acts[0, :, :width], cots[0]
    query, incoming, pieces[:LATE] = lax.optimization_barrier((query, incoming, pieces[:LATE]))
    query = passed_along(query, "section", 1)
    incoming = passed_along(incoming, "section", -1)

    feats, gated, inner, g_ring = inner_work(me, pieces, spectrum, table, back, taps, gain)
    inner = lax.all_to_all(inner, "ctx", split_axis=0, concat_axis=0, tiled=True)

    before = from_behind(query[rows - HALO :], "ctx", 1)
    later = from_behind(incoming[:HALO], "ctx", -1)
    mix_grad, features = query_features(query, before, incoming, query_taps, groups)
    mix_grad = lax.all_to_all(mix_grad, "ctx", split_axis=0, concat_axis=0, tiled=True)
    output, input_grad, partial = query_outputs(query, incoming, later, features, inner, query_taps)
    partial, mix_grad = lax.optimization_barrier((partial, mix_grad))
    partial = lax.all_to_all(partial, "ctx", split_axis=0, concat_axis=0, tiled=True)
    query_sums = jnp.sum(partial.astype(F32), axis=0)

    ready, d_ring = through_work(me, pieces, mix_grad, feats, spectrum, table, back, taps, gain)
    query_rows = jnp.broadcast_to(query_sums.astype(BF16), (groups, HALO, chans))
    ready = lax.dynamic_update_slice(ready, query_rows, (0, 2 * rows, 0))
    ready = lax.all_to_all(ready, "ctx", split_axis=0, concat_axis=0, tiled=True)
    filt_grad, skip_grad = filter_gradient(mix_grad, gated, d_ring, g_ring, back)
    (input_grad,) = place_columns(ready, rows, ((0, 1), (0, 2)), (input_grad,))
    sums = ready[:, 2 * rows : 2 * rows + 3 * HALO].reshape(groups, 3, HALO, chans)[:, :, :TAPS]
    kern_grad = sums.transpose(2, 1, 0, 3).reshape(TAPS, feats_all).astype(F32)
    return (output[None], input_grad[None], kern_grad[None], filt_grad[None], skip_grad)


def solution(mesh):
    return jax.shard_map(
        on_device,
        mesh=mesh,
        in_specs=(
            P("section", "ctx", None),
            P("section", "ctx", None),
            P("section", None, None),
            P("section", "ctx", None),
            P("section", None),
        ),
        out_specs=(
            P("section", "ctx", None),
            P("section", "ctx", None),
            P("section", None, None),
            P("section", "ctx", None),
            P("section", "ctx"),
        ),
        check_vma=False,
    )
```

time: 221 us -> 224 us (1.014)
  waiting for transfers between devices: 101 us -> 54.2 us
  starting transfers between devices: 41.8 us -> 85.5 us
  local copies, waits for them, and re-layouts: 6.97 us -> 13.9 us
    ppermute x1 -> x2, waiting for transfers between devices: 43.3 us -> 0.01 us  [passed_along(): return lax.ppermute(value, axis, pairs)]
    ppermute x1 -> x2, starting transfers between devices: 5.94 us -> 30.3 us  [passed_along(): return lax.ppermute(value, axis, pairs)]
    ppermute x0 -> x2, waiting for transfers between devices: none -> 23.3 us  [from_behind(): return lax.ppermute(block, axis, route)]
    ppermute x9, waiting for transfers between devices: 23.2 us -> 8.62 us  [handed_over(): return lax.ppermute(value, ('section', 'ctx'), pairs)]
    all_to_all x2 -> x1, waiting for transfers between devices: 34.6 us -> 22.3 us  [on_device(): lax.all_to_all(ready, 'ctx', split_axis=0, concat_axis=0, tiled=True)]
    all_to_all x1 -> x3, starting transfers between devices: 5.8 us -> 17.3 us  [the longest x1 6.64 us: on_device(): lax.all_to_all(inner, 'ctx', split_axis=0, concat_axis=0, tiled=True)]
    ppermute x9, starting transfers between devices: 20.4 us -> 26.7 us  [handed_over(): return lax.ppermute(value, ('section', 'ctx'), pairs)]
    ppermute x0 -> x2, starting transfers between devices: none -> 5.55 us  [from_behind(): return lax.ppermute(block, axis, route)]
  transfers between devices with their start and end apart: 13 -> 17, of which waited for: 7 -> 5; matrix products, arithmetic and copies ran while one was open for 2% -> 3% of each run, Pallas kernels for 17% -> 27%
where the time goes in v5:
time: 224 us; the launch traced here: 223 us
  starting transfers between devices  85.5 us (38%)
  Pallas kernels  66.3 us (30%)
  waiting for transfers between devices  54.2 us (24%)
  local copies, waits for them, and re-layouts  13.9 us (6%)
    ppermute x2, starting transfers between devices, passed_along(): return lax.ppermute(value, axis, pairs)  30.3 us
    ppermute x9, starting transfers between devices, handed_over(): return lax.ppermute(value, ('section', 'ctx'), pairs)  26.7 us
    ppermute x2, waiting for transfers between devices, from_behind(): return lax.ppermute(block, axis, route)  23.3 us
    all_to_all x1, waiting for transfers between devices, on_device(): lax.all_to_all(ready, 'ctx', split_axis=0, concat_axis=0, tiled=True)  22.3 us
    pallas_call x1, Pallas kernels, through_work(): pl.pallas_call(functools.partial(through_kernel, groups), out_shape=(pltp...  18.1 us
    pallas_call x1, Pallas kernels, inner_work(): pl.pallas_call(functools.partial(mixed_kernel, groups), out_shape=(pltpu....  15.8 us
    pallas_call x1, Pallas kernels, filter_spectrum(): pl.pallas_call(filter_kernel, out_shape=pltpu.HBM((8, wide, chans), F32),...  9.09 us
    pallas_call x1, Pallas kernels, filter_gradient(): pl.pallas_call(filter_grad_kernel, out_shape=(pltpu.HBM((chans, length),...  9.03 us
  transfers between devices with their start and end apart: 17, of which 5 were waited for; matrix products, arithmetic and copies ran while one was open for 3% of the time, Pallas kernels for 27%

profile of v5, /device:TPU:1, one launch (start us, length us, event | category | flops | bytes accessed | tf_op | source)
XLA Modules:
  0.0 222.8 jit_solution(13072925490125548884)
XLA Ops:
  0.6 0.0 copy-start
  0.7 1.4 leaving_pieces.1
  2.1 1.5 collective-permute-start
  3.6 2.3 %collective-permute-done.came_ref = bf16[8,2,128,256]{3,2,1,0:T(8,128)(2,1)S(1)} collective-permute-done((bf16[8,2,128,256]{3,2,1,0:T(8,128)(2,1)S(1)}, bf16[8,2,128,256]{3,2,1,0:T(8,128)(2,1)S(1)}, u32[]{:S(2)}, u32[]{:S(2)}) %collective-permute-start) | collective-permute-done | bytes 1048608 | tf_op jit(solution)/shard_map/ppermute | solution.py:40
  5.8 2.4 %pieces_for_owners.1 = (bf16[2,2,128,256]{3,2,1,0:T(8,128)(2,1)S(1)}, bf16[2,2,128,256]{3,2,1,0:T(8,128)(2,1)S(1)}, bf16[2,2,128,256]{3,2,1,0:T(8,128)(2,1)S(1)}...) custom-call(s32[1]{0:T(128)} %bitcast.2.me_ref, ...), custom_call_target="tpu_custom_call" | custom-call | bytes 4194304 | tf_op jit(solution)/shard_map/pieces_for_owners/pallas_call | solution.py:208
  8.2 3.7 %collective-permute-start.1 = (bf16[2,2,128,256]{3,2,1,0:T(8,128)(2,1)S(1)}, bf16[2,2,128,256]{3,2,1,0:T(8,128)(2,1)S(1)}, u32[]{:S(2)}, u32[]{:S(2)}) collective-permute-start(bf16[2,2,128,256]{3,2,1,0:T(8,128)(2,1)S(1)} %get-tuple-element.34), channel_id=1, source_target_pairs={{0,16},{1,17},{2,18},{3,19},{4,20},{5,21},{6,22},{7,23},{8,24},{9,... | collective-permute-start | bytes 786440 | tf_op jit(solution)/shard_map/ppermute | solution.py:40
  12.0 1.3 collective-permute-start.2
  13.3 5.9 %collective-permute-start.3 = (bf16[2,2,128,256]{3,2,1,0:T(8,128)(2,1)S(1)}, bf16[2,2,128,256]{3,2,1,0:T(8,128)(2,1)S(1)}, u32[]{:S(2)}, u32[]{:S(2)}) collective-permute-start(bf16[2,2,128,256]{3,2,1,0:T(8,128)(2,1)S(1)} %get-tuple-element.36), channel_id=1, source_target_pairs={{0,20},{1,21},{2,22},{3,23},{4,16},{5,17},{6,18},{7,19},{8,28},{9,... | collective-permute-start | bytes 786440 | tf_op jit(solution)/shard_map/ppermute | solution.py:40
  19.2 2.3 %slice_bitcast_fusion = bf16[128,4096]{1,0:T(8,128)(2,1)} fusion(bf16[1,128,12288]{2,1,0:T(8,128)(2,1)} %param.7), kind=kLoop, calls=%fused_computation | loop fusion | bytes 2097152 | tf_op jit(solution)/shard_map/squeeze | solution.py:843
  21.5 1.8 reduce.1
  23.3 0.8 copy.18
  24.1 3.7 %collective-permute-start.9 = (bf16[2,2,128,256]{3,2,1,0:T(8,128)(2,1)S(1)}, bf16[2,2,128,256]{3,2,1,0:T(8,128)(2,1)}, u32[]{:S(2)}, u32[]{:S(2)}) collective-permute-start(bf16[2,2,128,256]{3,2,1,0:T(8,128)(2,1)S(1)} %get-tuple-element.45), channel_id=1, source_target_pairs={{0,24},{1,25},{2,26},{3,27},{4,28},{5,29},{6,30},{7,31},{8,16},{9,... | collective-permute-start | bytes 786440 | tf_op jit(solution)/shard_map/ppermute | solution.py:40
  27.9 6.3 %collective-permute-done.1.refs_0_ = bf16[2,2,128,256]{3,2,1,0:T(8,128)(2,1)S(1)} collective-permute-done((bf16[2,2,128,256]{3,2,1,0:T(8,128)(2,1)S(1)}, bf16[2,2,128,256]{3,2,1,0:T(8,128)(2,1)S(1)}, u32[]{:S(2)}, u32[]{:S(2)}) %collective-permute-start.1) | collective-permute-done | bytes 262176 | tf_op jit(solution)/shard_map/ppermute | solution.py:40
  34.2 4.9 %collective-permute-start.10 = (bf16[2,2,128,256]{3,2,1,0:T(8,128)(2,1)S(1)}, bf16[2,2,128,256]{3,2,1,0:T(8,128)(2,1)}, u32[]{:S(2)}, u32[]{:S(2)}) collective-permute-start(bf16[2,2,128,256]{3,2,1,0:T(8,128)(2,1)S(1)} %get-tuple-element.46), channel_id=1, source_target_pairs={{0,26},{1,27},{2,24},{3,25},{4,30},{5,31},{6,28},{7,29},{8,18},{9,... | collective-permute-start | bytes 786440 | tf_op jit(solution)/shard_map/ppermute | solution.py:40
  39.1 2.1 collective-permute-start.11
  41.1 3.5 %collective-permute-start.12 = (bf16[2,2,128,256]{3,2,1,0:T(8,128)(2,1)S(1)}, bf16[2,2,128,256]{3,2,1,0:T(8,128)(2,1)}, u32[]{:S(2)}, u32[]{:S(2)}) collective-permute-start(bf16[2,2,128,256]{3,2,1,0:T(8,128)(2,1)S(1)} %get-tuple-element.48), channel_id=1, source_target_pairs={{0,30},{1,31},{2,28},{3,29},{4,26},{5,27},{6,24},{7,25},{8,22},{9,... | collective-permute-start | bytes 786440 | tf_op jit(solution)/shard_map/ppermute | solution.py:40
  44.7 0.9 constant_dynamic-slice_fusion.1
  45.6 9.1 %filter_spectrum.1.refs_8_.refs_10_ = f32[8,512,256]{2,1,0:T(8,128)} custom-call(bf16[256,2048]{1,0:T(8,128)(2,1)} %bitcast.30, bf16[8,512,512]{2,1,0:T(8,128)(2,1)} %constant.24.clone.table_ref.refs_9_.refs_11_), custom_call_target="tpu_custom_call" | custom-call | flops 1073741824 | bytes 10485760 | tf_op jit(solution)/shard_map/filter_spectrum/pallas_call | solution.py:138
  54.8 0.0 copy-start.9
  54.8 0.0 copy-start.14
  54.8 0.7 copy-done.14
  55.5 30.3 %collective-permute-start.6 = (bf16[128,4096]{1,0:T(8,128)(2,1)}, bf16[128,4096]{1,0:T(8,128)(2,1)S(1)}, u32[]{:S(2)}, u32[]{:S(2)}) collective-permute-start(bf16[128,4096]{1,0:T(8,128)(2,1)} %bitcast.1), channel_id=1, source_target_pairs={{0,112},{16,0},{32,16},{48,32},{64,48},{80,64},{96,80},{112,96},{1... | collective-permute-start | bytes 3145736 | tf_op jit(solution)/shard_map/ppermute | solution.py:30
  85.8 15.8 %inner_values.1 = (f32[16,2,128,256]{3,2,1,0:T(8,128)}, bf16[16,128,256]{2,1,0:T(8,128)(2,1)}, bf16[16,136,256]{2,1,0:T(8,128)(2,1)S(1)}, f32[8,512,256]{2,1,0:T(8,128)}) custom-call(s32[1]{0:T(128)} %bitcast.2.me_ref, bf16[2,2,128,256]{3,2,1,0:T(8,128)(2,1)} %copy-done.11, bf16[2,2,128,256]{3,2,1,0:T(8,128)(2,1)} %copy-done.12, ...), custom_call_target="tpu_custom_call" | custom-call | flops 2178940928 | bytes 25165824 | tf_op jit(solution)/shard_map/inner_values/pallas_call | solution.py:386
  101.6 1.0 copy-done.5
  102.6 6.6 %all-to-all-start = ((bf16[16,136,256]{2,1,0:T(8,128)(2,1)}), bf16[16,136,256]{2,1,0:T(8,128)(2,1)S(1)}, u32[]{:S(2)}, u32[]{:S(2)}) async-start(bf16[16,136,256]{2,1,0:T(8,128)(2,1)} %copy-done.5), calls=%async_computation | async-start | bytes 2228224 | tf_op jit(solution)/shard_map/all_to_all | solution.py:849
  109.3 3.5 %collective-permute-start.8 = (bf16[8,4096]{1,0:T(8,128)(2,1)S(1)}, bf16[8,4096]{1,0:T(8,128)(2,1)S(1)}, u32[]{:S(2)}, u32[]{:S(2)}) collective-permute-start(bf16[8,4096]{1,0:T(8,128)(2,1)S(1)} %slice.25), channel_id=1, source_target_pairs={{0,1},{1,2},{2,3},{3,4},{4,5},{5,6},{6,7},{7,8},{8,9},{9,10},{10,1... | collective-permute-start | bytes 196616 | tf_op jit(solution)/shard_map/ppermute | solution.py:821
  112.8 0.1 copy.21
  113.0 10.5 %collective-permute-done.8.before = bf16[8,4096]{1,0:T(8,128)(2,1)S(1)} collective-permute-done((bf16[8,4096]{1,0:T(8,128)(2,1)S(1)}, bf16[8,4096]{1,0:T(8,128)(2,1)S(1)}, u32[]{:S(2)}, u32[]{:S(2)}) %collective-permute-start.8) | collective-permute-done | bytes 65568 | tf_op jit(solution)/shard_map/ppermute | solution.py:821
  123.5 1.6 query_features.1
  125.1 1.3 copy-done.3
  126.4 1.0 copy-done.6
  127.4 1.0 copy-done.1
  128.4 5.9 %all-to-all-start.1 = ((bf16[16,128,256]{2,1,0:T(8,128)(2,1)}), bf16[16,128,256]{2,1,0:T(8,128)(2,1)S(1)}, u32[]{:S(2)}, u32[]{:S(2)}) async-start(bf16[16,128,256]{2,1,0:T(8,128)(2,1)} %copy-done.6), calls=%async_computation.1 | async-start | bytes 2097152 | tf_op jit(solution)/shard_map/all_to_all | solution.py:854
  134.3 0.0 copy-start.10
  134.4 2.0 collective-permute-start.7
  136.4 12.7 %collective-permute-done.7.later = bf16[8,4096]{1,0:T(8,128)(2,1)S(1)} collective-permute-done((bf16[8,4096]{1,0:T(8,128)(2,1)S(1)}, bf16[8,4096]{1,0:T(8,128)(2,1)S(1)}, u32[]{:S(2)}, u32[]{:S(2)}) %collective-permute-start.7) | collective-permute-done | bytes 65568 | tf_op jit(solution)/shard_map/ppermute | solution.py:821
  149.1 1.2 copy-done.2
  150.4 1.6 copy-done.4
  152.0 7.4 %query_outputs.1 = (bf16[128,4096]{1,0:T(8,128)(2,1)}, bf16[128,12288]{1,0:T(8,128)(2,1)}, bf16[16,8,256]{2,1,0:T(8,128)(2,1)}) custom-call(bf16[128,4096]{1,0:T(8,128)(2,1)S(1)} %collective-permute-done.5.source, bf16[128,4096]{1,0:T(8,128)(2,1)S(1)} %collective-permute-done.6.incoming, bf16[8,4096]{1,0:T(8,128)(2,1)S(1)} %collective-permute-done.7.later, ...), custom_call_target="tpu_custom_call" | custom-call | flops 18350080 | bytes 7340032 | tf_op jit(solution)/shard_map/query_outputs/pallas_call | solution.py:519
  159.4 4.7 %all-to-all-start.2 = ((bf16[16,8,256]{2,1,0:T(8,128)(2,1)}), bf16[16,8,256]{2,1,0:T(8,128)(2,1)S(1)}, u32[]{:S(2)}, u32[]{:S(2)}) async-start(bf16[16,8,256]{2,1,0:T(8,128)(2,1)} %get-tuple-element.56), calls=%async_computation.2 | async-start | bytes 131072 | tf_op jit(solution)/shard_map/all_to_all | solution.py:857
  164.1 18.1 %through_values.1 = (bf16[16,288,256]{2,1,0:T(8,128)(2,1)}, f32[8,512,256]{2,1,0:T(8,128)}) custom-call(s32[1]{0:T(128)} %bitcast.2.me_ref, bf16[2,2,128,256]{3,2,1,0:T(8,128)(2,1)} %copy-done.11, bf16[2,2,128,256]{3,2,1,0:T(8,128)(2,1)} %copy-done.12, bf16[2,2,128,256]{3,2,1,0:T(8,128)(2,1)} %copy-done.13, bf16[2,2,128,256]{3,2,1,0:T(8,128)(2,1)} %copy-done.14, ...), custom_call_target="tpu_custom_call" | custom-call | flops 2199912448 | bytes 29360128 | tf_op jit(solution)/shard_map/through_values/pallas_call | solution.py:659
  182.2 0.6 broadcast_dynamic-update-slice_fusion
  182.8 5.7 %all-to-all-start.3 = ((bf16[16,288,256]{2,1,0:T(8,128)(2,1)}), bf16[16,288,256]{2,1,0:T(8,128)(2,1)S(1)}, u32[]{:S(2)}, u32[]{:S(2)}) async-start(bf16[16,288,256]{2,1,0:T(8,128)(2,1)} %broadcast_dynamic-update-slice_fusion), calls=%async_computation.3 | async-start | bytes 4718592 | tf_op jit(solution)/shard_map/all_to_all | solution.py:863
  188.6 9.0 %filter_gradient.1 = (f32[256,2048]{1,0:T(8,128)}, f32[1,256]{1,0:T(1,128)}) custom-call(bf16[16,128,256]{2,1,0:T(8,128)(2,1)S(1)} %all-to-all-done.1.refs_8_.grad_hbm, bf16[16,128,256]{2,1,0:T(8,128)(2,1)} %get-tuple-element.58.gated_hbm, f32[8,512,256]{2,1,0:T(8,128)} %get-tuple-element.59.d_hbm, f32[8,512,256]{2,1,0:T(8,128)} %get-tuple-element.60.g_hbm, ...), custom_call_target="tpu_custom_call" | custom-call | flops 1094713344 | bytes 16777216 | tf_op jit(solution)/shard_map/filter_gradient/pallas_call | solution.py:756
  197.6 22.3 %all-to-all-done.3.held_ref = bf16[16,288,256]{2,1,0:T(8,128)(2,1)S(1)} async-done(((bf16[16,288,256]{2,1,0:T(8,128)(2,1)}), bf16[16,288,256]{2,1,0:T(8,128)(2,1)S(1)}, u32[]{:S(2)}, u32[]{:S(2)}) %all-to-all-start.3) | async-done | bytes 2359328 | tf_op jit(solution)/shard_map/all_to_all | solution.py:863
  220.0 0.1 copy.15
  220.1 1.1 reshape.27
  221.2 1.6 place_columns.1
  (44 shorter events, 0.2 us)
Async XLA Ops:
  0.6 54.1 %copy-start = (f32[1,4096]{1,0:T(1,128)S(1)}, f32[1,4096]{1,0:T(1,128)}, u32[]{:S(2)}) copy-start(f32[1,4096]{1,0:T(1,128)} %param.11) | copy-start | bytes 49156
  2.1 3.8 %collective-permute-start = (bf16[8,2,128,256]{3,2,1,0:T(8,128)(2,1)S(1)}, bf16[8,2,128,256]{3,2,1,0:T(8,128)(2,1)S(1)}, u32[]{:S(2)}, u32[]{:S(2)}) collective-permute-start(bf16[8,2,128,256]{3,2,1,0:T(8,128)(2,1)S(1)} %leaving_pieces.1), channel_id=1, source_target_pairs={{0,1},{1,0},{2,3},{3,2},{4,5},{5,4},{6,7},{7,6},{8,9},{9,8},{10,11... | collective-permute-start | bytes 3145736 | tf_op jit(solution)/shard_map/ppermute | solution.py:40
  8.2 26.0 %collective-permute-start.1 = (bf16[2,2,128,256]{3,2,1,0:T(8,128)(2,1)S(1)}, bf16[2,2,128,256]{3,2,1,0:T(8,128)(2,1)S(1)}, u32[]{:S(2)}, u32[]{:S(2)}) collective-permute-start(bf16[2,2,128,256]{3,2,1,0:T(8,128)(2,1)S(1)} %get-tuple-element.34), channel_id=1, source_target_pairs={{0,16},{1,17},{2,18},{3,19},{4,20},{5,21},{6,22},{7,23},{8,24},{9,... | collective-permute-start | bytes 786440 | tf_op jit(solution)/shard_map/ppermute | solution.py:40
  12.0 27.1 %collective-permute-start.2 = (bf16[2,2,128,256]{3,2,1,0:T(8,128)(2,1)S(1)}, bf16[2,2,128,256]{3,2,1,0:T(8,128)(2,1)S(1)}, u32[]{:S(2)}, u32[]{:S(2)}) collective-permute-start(bf16[2,2,128,256]{3,2,1,0:T(8,128)(2,1)S(1)} %get-tuple-element.35), channel_id=1, source_target_pairs={{0,18},{1,19},{2,16},{3,17},{4,22},{5,23},{6,20},{7,21},{8,26},{9,... | collective-permute-start | bytes 786440 | tf_op jit(solution)/shard_map/ppermute | solution.py:40
  13.3 27.9 %collective-permute-start.3 = (bf16[2,2,128,256]{3,2,1,0:T(8,128)(2,1)S(1)}, bf16[2,2,128,256]{3,2,1,0:T(8,128)(2,1)S(1)}, u32[]{:S(2)}, u32[]{:S(2)}) collective-permute-start(bf16[2,2,128,256]{3,2,1,0:T(8,128)(2,1)S(1)} %get-tuple-element.36), channel_id=1, source_target_pairs={{0,20},{1,21},{2,22},{3,23},{4,16},{5,17},{6,18},{7,19},{8,28},{9,... | collective-permute-start | bytes 786440 | tf_op jit(solution)/shard_map/ppermute | solution.py:40
  24.1 30.7 %collective-permute-start.4 = (bf16[2,2,128,256]{3,2,1,0:T(8,128)(2,1)S(1)}, bf16[2,2,128,256]{3,2,1,0:T(8,128)(2,1)S(1)}, u32[]{:S(2)}, u32[]{:S(2)}) collective-permute-start(bf16[2,2,128,256]{3,2,1,0:T(8,128)(2,1)S(1)} %get-tuple-element.37), channel_id=1, source_target_pairs={{0,22},{1,23},{2,20},{3,21},{4,18},{5,19},{6,16},{7,17},{8,30},{9,... | collective-permute-start | bytes 786440 | tf_op jit(solution)/shard_map/ppermute | solution.py:40
  24.1 31.4 %collective-permute-start.9 = (bf16[2,2,128,256]{3,2,1,0:T(8,128)(2,1)S(1)}, bf16[2,2,128,256]{3,2,1,0:T(8,128)(2,1)}, u32[]{:S(2)}, u32[]{:S(2)}) collective-permute-start(bf16[2,2,128,256]{3,2,1,0:T(8,128)(2,1)S(1)} %get-tuple-element.45), channel_id=1, source_target_pairs={{0,24},{1,25},{2,26},{3,27},{4,28},{5,29},{6,30},{7,31},{8,16},{9,... | collective-permute-start | bytes 786440 | tf_op jit(solution)/shard_map/ppermute | solution.py:40
  34.2 20.6 %copy-start.11 = (bf16[2,2,128,256]{3,2,1,0:T(8,128)(2,1)}, bf16[2,2,128,256]{3,2,1,0:T(8,128)(2,1)S(1)}, u32[]{:S(2)}) copy-start(bf16[2,2,128,256]{3,2,1,0:T(8,128)(2,1)S(1)} %collective-permute-done.1.refs_0_) | copy-start | bytes 786436
  34.2 51.6 %collective-permute-start.10 = (bf16[2,2,128,256]{3,2,1,0:T(8,128)(2,1)S(1)}, bf16[2,2,128,256]{3,2,1,0:T(8,128)(2,1)}, u32[]{:S(2)}, u32[]{:S(2)}) collective-permute-start(bf16[2,2,128,256]{3,2,1,0:T(8,128)(2,1)S(1)} %get-tuple-element.46), channel_id=1, source_target_pairs={{0,26},{1,27},{2,24},{3,25},{4,30},{5,31},{6,28},{7,29},{8,18},{9,... | collective-permute-start | bytes 786440 | tf_op jit(solution)/shard_map/ppermute | solution.py:40
  39.1 15.7 %copy-start.12 = (bf16[2,2,128,256]{3,2,1,0:T(8,128)(2,1)}, bf16[2,2,128,256]{3,2,1,0:T(8,128)(2,1)S(1)}, u32[]{:S(2)}) copy-start(bf16[2,2,128,256]{3,2,1,0:T(8,128)(2,1)S(1)} %collective-permute-done.2.refs_1_) | copy-start | bytes 786436
  39.1 46.7 %collective-permute-start.11 = (bf16[2,2,128,256]{3,2,1,0:T(8,128)(2,1)S(1)}, bf16[2,2,128,256]{3,2,1,0:T(8,128)(2,1)}, u32[]{:S(2)}, u32[]{:S(2)}) collective-permute-start(bf16[2,2,128,256]{3,2,1,0:T(8,128)(2,1)S(1)} %get-tuple-element.47), channel_id=1, source_target_pairs={{0,28},{1,29},{2,30},{3,31},{4,24},{5,25},{6,26},{7,27},{8,20},{9,... | collective-permute-start | bytes 786440 | tf_op jit(solution)/shard_map/ppermute | solution.py:40
  41.1 13.6 %copy-start.13 = (bf16[2,2,128,256]{3,2,1,0:T(8,128)(2,1)}, bf16[2,2,128,256]{3,2,1,0:T(8,128)(2,1)S(1)}, u32[]{:S(2)}) copy-start(bf16[2,2,128,256]{3,2,1,0:T(8,128)(2,1)S(1)} %collective-permute-done.3.refs_2_) | copy-start | bytes 786436
  41.1 44.7 %collective-permute-start.12 = (bf16[2,2,128,256]{3,2,1,0:T(8,128)(2,1)S(1)}, bf16[2,2,128,256]{3,2,1,0:T(8,128)(2,1)}, u32[]{:S(2)}, u32[]{:S(2)}) collective-permute-start(bf16[2,2,128,256]{3,2,1,0:T(8,128)(2,1)S(1)} %get-tuple-element.48), channel_id=1, source_target_pairs={{0,30},{1,31},{2,28},{3,29},{4,26},{5,27},{6,24},{7,25},{8,22},{9,... | collective-permute-start | bytes 786440 | tf_op jit(solution)/shard_map/ppermute | solution.py:40
  45.6 40.2 %copy-start.7 = (f32[3,8,256]{2,1,0:T(8,128)}, f32[3,8,256]{2,1,0:T(8,128)S(1)}, u32[]{:S(2)}) copy-start(f32[3,8,256]{2,1,0:T(8,128)S(1)} %pad.9.refs_11_.refs_13_) | copy-start | bytes 73732
  54.8 46.8 %copy-start.9 = (f32[1,256]{1,0:T(1,128)}, f32[1,256]{1,0:T(1,128)S(1)}, u32[]{:S(2)}) copy-start(f32[1,256]{1,0:T(1,128)S(1)} %constant_dynamic-slice_fusion.refs_12_.refs_14_) | copy-start | bytes 3076
  54.8 0.7 copy-start.14
  55.5 57.3 %slice-start = ((f32[1,7,12288]{2,0,1:T(1,128)}), f32[1,7,4096]{2,0,1:T(1,128)S(1)}, s32[]{:S(2)}) async-start(f32[1,7,12288]{2,0,1:T(1,128)} %param.9), calls=%async_computation.4 | async-start | bytes 229376 | tf_op jit(solution)/shard_map/slice | solution.py:838
  55.5 53.8 %collective-permute-start.5 = (bf16[128,4096]{1,0:T(8,128)(2,1)}, bf16[128,4096]{1,0:T(8,128)(2,1)S(1)}, u32[]{:S(2)}, u32[]{:S(2)}) collective-permute-start(bf16[128,4096]{1,0:T(8,128)(2,1)} %slice_bitcast_fusion), channel_id=1, source_target_pairs={{0,16},{16,32},{32,48},{48,64},{64,80},{80,96},{96,112},{112,0},{1... | collective-permute-start | bytes 3145736 | tf_op jit(solution)/shard_map/ppermute | solution.py:30
  55.5 57.4 %collective-permute-start.6 = (bf16[128,4096]{1,0:T(8,128)(2,1)}, bf16[128,4096]{1,0:T(8,128)(2,1)S(1)}, u32[]{:S(2)}, u32[]{:S(2)}) collective-permute-start(bf16[128,4096]{1,0:T(8,128)(2,1)} %bitcast.1), channel_id=1, source_target_pairs={{0,112},{16,0},{32,16},{48,32},{64,48},{80,64},{96,80},{112,96},{1... | collective-permute-start | bytes 3145736 | tf_op jit(solution)/shard_map/ppermute | solution.py:30
  101.6 1.0 copy-start.5
  102.6 24.8 %all-to-all-start = ((bf16[16,136,256]{2,1,0:T(8,128)(2,1)}), bf16[16,136,256]{2,1,0:T(8,128)(2,1)S(1)}, u32[]{:S(2)}, u32[]{:S(2)}) async-start(bf16[16,136,256]{2,1,0:T(8,128)(2,1)} %copy-done.5), calls=%async_computation | async-start | bytes 2228224 | tf_op jit(solution)/shard_map/all_to_all | solution.py:849
  109.3 14.2 %collective-permute-start.8 = (bf16[8,4096]{1,0:T(8,128)(2,1)S(1)}, bf16[8,4096]{1,0:T(8,128)(2,1)S(1)}, u32[]{:S(2)}, u32[]{:S(2)}) collective-permute-start(bf16[8,4096]{1,0:T(8,128)(2,1)S(1)} %slice.25), channel_id=1, source_target_pairs={{0,1},{1,2},{2,3},{3,4},{4,5},{5,6},{6,7},{7,8},{8,9},{9,10},{10,1... | collective-permute-start | bytes 196616 | tf_op jit(solution)/shard_map/ppermute | solution.py:821
  125.1 1.3 copy-start.3
  126.4 1.0 copy-start.6
  127.4 1.0 copy-start.1
  128.4 31.0 %all-to-all-start.1 = ((bf16[16,128,256]{2,1,0:T(8,128)(2,1)}), bf16[16,128,256]{2,1,0:T(8,128)(2,1)S(1)}, u32[]{:S(2)}, u32[]{:S(2)}) async-start(bf16[16,128,256]{2,1,0:T(8,128)(2,1)} %copy-done.6), calls=%async_computation.1 | async-start | bytes 2097152 | tf_op jit(solution)/shard_map/all_to_all | solution.py:854
  134.3 29.7 %copy-start.8 = (f32[3,8,256]{2,1,0:T(8,128)S(1)}, f32[3,8,256]{2,1,0:T(8,128)}, u32[]{:S(2)}) copy-start(f32[3,8,256]{2,1,0:T(8,128)} %copy-done.7) | copy-start | bytes 73732
  134.3 29.7 %copy-start.10 = (f32[1,256]{1,0:T(1,128)S(1)}, f32[1,256]{1,0:T(1,128)}, u32[]{:S(2)}) copy-start(f32[1,256]{1,0:T(1,128)} %copy-done.9) | copy-start | bytes 3076
  134.4 14.7 %collective-permute-start.7 = (bf16[8,4096]{1,0:T(8,128)(2,1)S(1)}, bf16[8,4096]{1,0:T(8,128)(2,1)S(1)}, u32[]{:S(2)}, u32[]{:S(2)}) collective-permute-start(bf16[8,4096]{1,0:T(8,128)(2,1)S(1)} %slice.24), channel_id=1, source_target_pairs={{1,0},{2,1},{3,2},{4,3},{5,4},{6,5},{7,6},{8,7},{9,8},{10,9},{11,1... | collective-permute-start | bytes 196616 | tf_op jit(solution)/shard_map/ppermute | solution.py:821
  149.1 1.2 copy-start.2
  150.4 1.6 copy-start.4
  159.4 22.8 %all-to-all-start.2 = ((bf16[16,8,256]{2,1,0:T(8,128)(2,1)}), bf16[16,8,256]{2,1,0:T(8,128)(2,1)S(1)}, u32[]{:S(2)}, u32[]{:S(2)}) async-start(bf16[16,8,256]{2,1,0:T(8,128)(2,1)} %get-tuple-element.56), calls=%async_computation.2 | async-start | bytes 131072 | tf_op jit(solution)/shard_map/all_to_all | solution.py:857
  182.8 37.1 %all-to-all-start.3 = ((bf16[16,288,256]{2,1,0:T(8,128)(2,1)}), bf16[16,288,256]{2,1,0:T(8,128)(2,1)S(1)}, u32[]{:S(2)}, u32[]{:S(2)}) async-start(bf16[16,288,256]{2,1,0:T(8,128)(2,1)} %broadcast_dynamic-update-slice_fusion), calls=%async_computation.3 | async-start | bytes 4718592 | tf_op jit(solution)/shard_map/all_to_all | solution.py:863

commit v6 on v5

--- a/solution.py
+++ b/solution.py
@@ -12,8 +12,8 @@
 
 TAPS = 7
 HALO = 8
-EXTRA = 32
-LATE = 4
+EXTRA = 24
+LATE = 6
 ROOT = math.sqrt(0.5)
 F32 = jnp.float32
 BF16 = jnp.bfloat16
@@ -418,7 +418,7 @@
             pltpu.SemaphoreType.DMA((1,)),
             pltpu.SemaphoreType.DMA((8,)),
         ],
-        compiler_params=pltpu.CompilerParams(vmem_limit_bytes=40 * MIB),
+        compiler_params=pltpu.CompilerParams(vmem_limit_bytes=33 * MIB),
         cost_estimate=pl.CostEstimate(
             flops=32 * wide * wide * chans + 60 * length * chans, bytes_accessed=24 * MIB, transcendentals=0
         ),
@@ -426,8 +426,17 @@
     )(me, *in_hbm(*pieces, spectrum, table, back), taps, gain)
 
 
-def query_kernel(source, before, incoming, taps_ref, mix_grad, features, held):
+def query_kernel(
+    source, before, incoming, taps_ref, grad_hbm, features_hbm, mix_grad, features, held, grad_sems, features_sems
+):
     groups, rows, chans = mix_grad.shape
+
+    def write_back(owner):
+        columns = pl.ds(pl.multiple_of(owner * chans, 128), chans)
+        return (
+            pltpu.make_async_copy(mix_grad.at[owner], grad_hbm.at[owner], grad_sems.at[owner]),
+            pltpu.make_async_copy(features.at[:, columns], features_hbm.at[:, columns], features_sems.at[owner]),
+        )
 
     @pl.loop(0, groups)
     def _(owner):
@@ -442,6 +451,13 @@
                 total = tap_sum(held, part, taps, row)
                 features[span, columns] = total
                 mix_grad[owner, span, lanes] = (incoming[span, columns].astype(F32) * total).astype(BF16)
+        for copy in write_back(owner):
+            copy.start()
+
+    @pl.loop(0, groups)
+    def _(owner):
+        for copy in write_back(owner):
+            copy.wait()
 
 
 def query_features(source, before, incoming, taps, groups):
@@ -450,12 +466,18 @@
     return pl.pallas_call(
         query_kernel,
         out_shape=(
-            jax.ShapeDtypeStruct((groups, rows, chans), BF16),
-            jax.ShapeDtypeStruct((rows, width), F32),
+            pltpu.HBM((groups, rows, chans), BF16),
+            pltpu.HBM((rows, width), F32),
         ),
         in_specs=[pl.BlockSpec(memory_space=pltpu.VMEM)] * 4,
-        out_specs=(pl.BlockSpec(memory_space=pltpu.VMEM),) * 2,
-        scratch_shapes=[pltpu.VMEM((chans // 128, HALO + rows, 128), F32)],
+        out_specs=(pl.BlockSpec(memory_space=pl.ANY),) * 2,
+        scratch_shapes=[
+            pltpu.VMEM((groups, rows, chans), BF16),
+            pltpu.VMEM((rows, width), F32),
+            pltpu.VMEM((chans // 128, HALO + rows, 128), F32),
+            pltpu.SemaphoreType.DMA((groups,)),
+            pltpu.SemaphoreType.DMA((groups,)),
+        ],
         compiler_params=pltpu.CompilerParams(vmem_limit_bytes=10 * MIB),
         cost_estimate=pl.CostEstimate(flops=15 * rows * width, bytes_accessed=10 * rows * width, transcendentals=0),
         name="query_features",
@@ -635,7 +657,6 @@
         write_back(slot, block).start()
 
     rows_out = [jnp.zeros((HALO, chans), F32)] + sum_rows(sums, 2)
-    rows_out.append(jnp.zeros((EXTRA - 3 * HALO, chans), F32))
     last[...] = jnp.concatenate(rows_out, axis=0).astype(BF16)
     wait_all(
         [
@@ -690,7 +711,7 @@
             pltpu.SemaphoreType.DMA((2,)),
             pltpu.SemaphoreType.DMA((groups,)),
         ],
-        compiler_params=pltpu.CompilerParams(vmem_limit_bytes=40 * MIB),
+        compiler_params=pltpu.CompilerParams(vmem_limit_bytes=34 * MIB),
         cost_estimate=pl.CostEstimate(
             flops=32 * wide * wide * chans + 100 * length * chans, bytes_accessed=28 * MIB, transcendentals=0
         ),
@@ -815,10 +836,15 @@
     )(held, *in_hbm(*earlier))
 
 
-def from_behind(block, axis, distance):
-    devices = range(lax.axis_size(axis))
-    route = [(i - distance, i) for i in devices if i - distance in devices]
-    return lax.ppermute(block, axis, route)
+def edge_of(block, steps):
+    sections, groups = lax.axis_size("section"), lax.axis_size("ctx")
+    pairs = [
+        (section * groups + place, (section + steps) % sections * groups + place + steps)
+        for section in range(sections)
+        for place in range(groups)
+        if 0 <= place + steps < groups
+    ]
+    return lax.ppermute(block, ("section", "ctx"), pairs)
 
 
 def on_device(acts, cots, kern, filt, skip):
@@ -848,8 +874,9 @@
     feats, gated, inner, g_ring = inner_work(me, pieces, spectrum, table, back, taps, gain)
     inner = lax.all_to_all(inner, "ctx", split_axis=0, concat_axis=0, tiled=True)
 
-    before = from_behind(query[rows - HALO :], "ctx", 1)
-    later = from_behind(incoming[:HALO], "ctx", -1)
+    before = edge_of(acts[0, rows - HALO :, :width], 1)
+    later = edge_of(cots[0, :HALO], -1)
+    before, later = lax.optimization_barrier((before, later))
     mix_grad, features = query_features(query, before, incoming, query_taps, groups)
     mix_grad = lax.all_to_all(mix_grad, "ctx", split_axis=0, concat_axis=0, tiled=True)
     output, input_grad, partial = query_outputs(query, incoming, later, features, inner, query_taps)

time: 224 us -> 212 us (0.946)
  starting transfers between devices: 85.5 us -> 69.9 us
    ppermute x2, starting transfers between devices: 30.3 us -> 7.82 us  [passed_along(): return lax.ppermute(value, axis, pairs)]
    ppermute x2, waiting for transfers between devices: 23.3 us -> 4.96 us  [edge_of(): return lax.ppermute(block, ('section', 'ctx'), pairs)]
    ppermute x2, waiting for transfers between devices: 0.01 us -> 16.5 us  [passed_along(): return lax.ppermute(value, axis, pairs)]
    all_to_all x1, waiting for transfers between devices: 0.01 us -> 4.8 us  [on_device(): lax.all_to_all(mix_grad, 'ctx', split_axis=0, concat_axis=0, tiled=True)]
    all_to_all x1, starting transfers between devices: 5.94 us -> 9.86 us  [on_device(): lax.all_to_all(mix_grad, 'ctx', split_axis=0, concat_axis=0, tiled=True)]
    ppermute x2, starting transfers between devices: 5.55 us -> 9.15 us  [edge_of(): return lax.ppermute(block, ('section', 'ctx'), pairs)]
    unnamed x33 -> x27, local copies, waits for them, and re-layouts: 8.75 us -> 6.97 us
  transfers between devices with their start and end apart: 17 -> 17, of which waited for: 5 -> 8; matrix products, arithmetic and copies ran while one was open for 3% -> 4% of each run, Pallas kernels for 27% -> 29%
where the time goes in v6:
time: 212 us; the launch traced here: 211 us
  starting transfers between devices  69.9 us (33%)
  Pallas kernels  67.3 us (32%)
  waiting for transfers between devices  56.3 us (27%)
  local copies, waits for them, and re-layouts  14.7 us (7%)
    ppermute x9, starting transfers between devices, handed_over(): return lax.ppermute(value, ('section', 'ctx'), pairs)  26.7 us
    all_to_all x1, waiting for transfers between devices, on_device(): lax.all_to_all(ready, 'ctx', split_axis=0, concat_axis=0, tiled=True)  21.4 us
    pallas_call x1, Pallas kernels, through_work(): pl.pallas_call(functools.partial(through_kernel, groups), out_shape=(pltp...  18 us
    ppermute x2, waiting for transfers between devices, passed_along(): return lax.ppermute(value, axis, pairs)  16.5 us
    pallas_call x1, Pallas kernels, inner_work(): pl.pallas_call(functools.partial(mixed_kernel, groups), out_shape=(pltpu....  15.8 us
    all_to_all x1, starting transfers between devices, on_device(): lax.all_to_all(mix_grad, 'ctx', split_axis=0, concat_axis=0, tiled=True)  9.86 us
    ppermute x2, starting transfers between devices, edge_of(): return lax.ppermute(block, ('section', 'ctx'), pairs)  9.15 us
    pallas_call x1, Pallas kernels, filter_spectrum(): pl.pallas_call(filter_kernel, out_shape=pltpu.HBM((8, wide, chans), F32),...  9.12 us
  transfers between devices with their start and end apart: 17, of which 8 were waited for; matrix products, arithmetic and copies ran while one was open for 4% of the time, Pallas kernels for 29%

profile of v6, /device:TPU:1, one launch (start us, length us, event | category | flops | bytes accessed | tf_op | source)
XLA Modules:
  0.0 210.8 jit_solution(17585892133890567200)
XLA Ops:
  0.7 1.4 leaving_pieces.1
  2.1 1.5 collective-permute-start
  3.6 2.3 %collective-permute-done.came_ref = bf16[8,2,128,256]{3,2,1,0:T(8,128)(2,1)S(1)} collective-permute-done((bf16[8,2,128,256]{3,2,1,0:T(8,128)(2,1)S(1)}, bf16[8,2,128,256]{3,2,1,0:T(8,128)(2,1)S(1)}, u32[]{:S(2)}, u32[]{:S(2)}) %collective-permute-start) | collective-permute-done | bytes 1048608 | tf_op jit(solution)/shard_map/ppermute | solution.py:40
  5.8 2.4 %pieces_for_owners.1 = (bf16[2,2,128,256]{3,2,1,0:T(8,128)(2,1)S(1)}, bf16[2,2,128,256]{3,2,1,0:T(8,128)(2,1)S(1)}, bf16[2,2,128,256]{3,2,1,0:T(8,128)(2,1)S(1)}...) custom-call(s32[1]{0:T(128)} %bitcast.2.me_ref, ...), custom_call_target="tpu_custom_call" | custom-call | bytes 4194304 | tf_op jit(solution)/shard_map/pieces_for_owners/pallas_call | solution.py:208
  8.2 3.7 %collective-permute-start.1 = (bf16[2,2,128,256]{3,2,1,0:T(8,128)(2,1)S(1)}, bf16[2,2,128,256]{3,2,1,0:T(8,128)(2,1)S(1)}, u32[]{:S(2)}, u32[]{:S(2)}) collective-permute-start(bf16[2,2,128,256]{3,2,1,0:T(8,128)(2,1)S(1)} %get-tuple-element.38), channel_id=1, source_target_pairs={{0,16},{1,17},{2,18},{3,19},{4,20},{5,21},{6,22},{7,23},{8,24},{9,... | collective-permute-start | bytes 786440 | tf_op jit(solution)/shard_map/ppermute | solution.py:40
  12.0 1.3 collective-permute-start.2
  13.3 5.9 %collective-permute-start.3 = (bf16[2,2,128,256]{3,2,1,0:T(8,128)(2,1)S(1)}, bf16[2,2,128,256]{3,2,1,0:T(8,128)(2,1)S(1)}, u32[]{:S(2)}, u32[]{:S(2)}) collective-permute-start(bf16[2,2,128,256]{3,2,1,0:T(8,128)(2,1)S(1)} %get-tuple-element.40), channel_id=1, source_target_pairs={{0,20},{1,21},{2,22},{3,23},{4,16},{5,17},{6,18},{7,19},{8,28},{9,... | collective-permute-start | bytes 786440 | tf_op jit(solution)/shard_map/ppermute | solution.py:40
  19.2 2.3 %slice_bitcast_fusion = bf16[128,4096]{1,0:T(8,128)(2,1)} fusion(bf16[1,128,12288]{2,1,0:T(8,128)(2,1)} %param.7), kind=kLoop, calls=%fused_computation | loop fusion | bytes 2097152 | tf_op jit(solution)/shard_map/squeeze | solution.py:869
  21.5 1.8 reduce.1
  23.3 0.8 copy.18
  24.1 3.7 %collective-permute-start.5 = (bf16[2,2,128,256]{3,2,1,0:T(8,128)(2,1)S(1)}, bf16[2,2,128,256]{3,2,1,0:T(8,128)(2,1)}, u32[]{:S(2)}, u32[]{:S(2)}) collective-permute-start(bf16[2,2,128,256]{3,2,1,0:T(8,128)(2,1)S(1)} %get-tuple-element.42), channel_id=1, source_target_pairs={{0,24},{1,25},{2,26},{3,27},{4,28},{5,29},{6,30},{7,31},{8,16},{9,... | collective-permute-start | bytes 786440 | tf_op jit(solution)/shard_map/ppermute | solution.py:40
  27.9 6.3 %collective-permute-done.1.refs_0_ = bf16[2,2,128,256]{3,2,1,0:T(8,128)(2,1)S(1)} collective-permute-done((bf16[2,2,128,256]{3,2,1,0:T(8,128)(2,1)S(1)}, bf16[2,2,128,256]{3,2,1,0:T(8,128)(2,1)S(1)}, u32[]{:S(2)}, u32[]{:S(2)}) %collective-permute-start.1) | collective-permute-done | bytes 262176 | tf_op jit(solution)/shard_map/ppermute | solution.py:40
  34.2 4.9 %collective-permute-start.6 = (bf16[2,2,128,256]{3,2,1,0:T(8,128)(2,1)S(1)}, bf16[2,2,128,256]{3,2,1,0:T(8,128)(2,1)S(1)}, u32[]{:S(2)}, u32[]{:S(2)}) collective-permute-start(bf16[2,2,128,256]{3,2,1,0:T(8,128)(2,1)S(1)} %get-tuple-element.43), channel_id=1, source_target_pairs={{0,26},{1,27},{2,24},{3,25},{4,30},{5,31},{6,28},{7,29},{8,18},{9,... | collective-permute-start | bytes 786440 | tf_op jit(solution)/shard_map/ppermute | solution.py:40
  39.1 2.1 collective-permute-start.11
  41.1 3.5 %collective-permute-start.12 = (bf16[2,2,128,256]{3,2,1,0:T(8,128)(2,1)S(1)}, bf16[2,2,128,256]{3,2,1,0:T(8,128)(2,1)}, u32[]{:S(2)}, u32[]{:S(2)}) collective-permute-start(bf16[2,2,128,256]{3,2,1,0:T(8,128)(2,1)S(1)} %get-tuple-element.56), channel_id=1, source_target_pairs={{0,30},{1,31},{2,28},{3,29},{4,26},{5,27},{6,24},{7,25},{8,22},{9,... | collective-permute-start | bytes 786440 | tf_op jit(solution)/shard_map/ppermute | solution.py:40
  44.7 0.9 constant_dynamic-slice_fusion.1
  45.6 9.1 %filter_spectrum.1.refs_8_.refs_10_ = f32[8,512,256]{2,1,0:T(8,128)} custom-call(bf16[256,2048]{1,0:T(8,128)(2,1)} %bitcast.34, bf16[8,512,512]{2,1,0:T(8,128)(2,1)} %constant.24.clone.table_ref.refs_9_.refs_11_), custom_call_target="tpu_custom_call" | custom-call | flops 1073741824 | bytes 10485760 | tf_op jit(solution)/shard_map/filter_spectrum/pallas_call | solution.py:138
  54.8 0.7 copy-done.10
  55.5 0.7 copy-done.11
  56.2 5.6 %collective-permute-start.7 = (bf16[128,4096]{1,0:T(8,128)(2,1)}, bf16[128,4096]{1,0:T(8,128)(2,1)S(1)}, u32[]{:S(2)}, u32[]{:S(2)}) collective-permute-start(bf16[128,4096]{1,0:T(8,128)(2,1)} %slice_bitcast_fusion), channel_id=1, source_target_pairs={{0,16},{16,32},{32,48},{48,64},{64,80},{80,96},{96,112},{112,0},{1... | collective-permute-start | bytes 3145736 | tf_op jit(solution)/shard_map/ppermute | solution.py:30
  61.9 2.2 %collective-permute-start.8 = (bf16[128,4096]{1,0:T(8,128)(2,1)}, bf16[128,4096]{1,0:T(8,128)(2,1)S(1)}, u32[]{:S(2)}, u32[]{:S(2)}) collective-permute-start(bf16[128,4096]{1,0:T(8,128)(2,1)} %bitcast.1), channel_id=1, source_target_pairs={{0,112},{16,0},{32,16},{48,32},{64,48},{80,64},{96,80},{112,96},{1... | collective-permute-start | bytes 3145736 | tf_op jit(solution)/shard_map/ppermute | solution.py:30
  64.1 15.8 %inner_values.1 = (f32[16,2,128,256]{3,2,1,0:T(8,128)}, bf16[16,128,256]{2,1,0:T(8,128)(2,1)}, bf16[16,136,256]{2,1,0:T(8,128)(2,1)S(1)}, f32[8,512,256]{2,1,0:T(8,128)}) custom-call(s32[1]{0:T(128)} %bitcast.2.me_ref, bf16[2,2,128,256]{3,2,1,0:T(8,128)(2,1)} %copy-done.7, bf16[2,2,128,256]{3,2,1,0:T(8,128)(2,1)} %copy-done.8, ...), custom_call_target="tpu_custom_call" | custom-call | flops 2178940928 | bytes 25165824 | tf_op jit(solution)/shard_map/inner_values/pallas_call | solution.py:386
  79.9 1.0 copy-done.4
  80.8 6.6 %all-to-all-start = ((bf16[16,136,256]{2,1,0:T(8,128)(2,1)}), bf16[16,136,256]{2,1,0:T(8,128)(2,1)S(1)}, u32[]{:S(2)}, u32[]{:S(2)}) async-start(bf16[16,136,256]{2,1,0:T(8,128)(2,1)} %copy-done.4), calls=%async_computation | async-start | bytes 2228224 | tf_op jit(solution)/shard_map/all_to_all | solution.py:875
  87.4 0.8 slice_bitcast_fusion.3
  88.2 4.9 %collective-permute-start.9 = (bf16[8,4096]{1,0:T(8,128)(2,1)S(1)}, bf16[8,4096]{1,0:T(8,128)(2,1)S(1)}, u32[]{:S(2)}, u32[]{:S(2)}) collective-permute-start(bf16[8,4096]{1,0:T(8,128)(2,1)S(1)} %slice_bitcast_fusion.3), channel_id=1, source_target_pairs={{0,17},{1,18},{2,19},{3,20},{4,21},{5,22},{6,23},{7,24},{8,25},{9,... | collective-permute-start | bytes 196616 | tf_op jit(solution)/shard_map/ppermute | solution.py:847
  93.1 0.8 slice_bitcast_fusion.2
  94.0 4.2 %collective-permute-start.10 = (bf16[8,4096]{1,0:T(8,128)(2,1)S(1)}, bf16[8,4096]{1,0:T(8,128)(2,1)S(1)}, u32[]{:S(2)}, u32[]{:S(2)}) collective-permute-start(bf16[8,4096]{1,0:T(8,128)(2,1)S(1)} %slice_bitcast_fusion.2), channel_id=1, source_target_pairs={{1,112},{2,113},{3,114},{4,115},{5,116},{6,117},{7,118},{8,119},{9... | collective-permute-start | bytes 196616 | tf_op jit(solution)/shard_map/ppermute | solution.py:847
  98.2 0.9 slice.21
  99.2 2.4 %collective-permute-done.9.before = bf16[8,4096]{1,0:T(8,128)(2,1)S(1)} collective-permute-done((bf16[8,4096]{1,0:T(8,128)(2,1)S(1)}, bf16[8,4096]{1,0:T(8,128)(2,1)S(1)}, u32[]{:S(2)}, u32[]{:S(2)}) %collective-permute-start.9) | collective-permute-done | bytes 65568 | tf_op jit(solution)/shard_map/ppermute | solution.py:847
  101.6 2.6 %collective-permute-done.10.later = bf16[8,4096]{1,0:T(8,128)(2,1)S(1)} collective-permute-done((bf16[8,4096]{1,0:T(8,128)(2,1)S(1)}, bf16[8,4096]{1,0:T(8,128)(2,1)S(1)}, u32[]{:S(2)}, u32[]{:S(2)}) %collective-permute-start.10) | collective-permute-done | bytes 65568 | tf_op jit(solution)/shard_map/ppermute | solution.py:847
  104.2 12.8 %collective-permute-done.7.source = bf16[128,4096]{1,0:T(8,128)(2,1)S(1)} collective-permute-done((bf16[128,4096]{1,0:T(8,128)(2,1)}, bf16[128,4096]{1,0:T(8,128)(2,1)S(1)}, u32[]{:S(2)}, u32[]{:S(2)}) %collective-permute-start.7) | collective-permute-done | bytes 1048608 | tf_op jit(solution)/shard_map/ppermute | solution.py:30
  117.0 3.7 %collective-permute-done.8.incoming = bf16[128,4096]{1,0:T(8,128)(2,1)S(1)} collective-permute-done((bf16[128,4096]{1,0:T(8,128)(2,1)}, bf16[128,4096]{1,0:T(8,128)(2,1)S(1)}, u32[]{:S(2)}, u32[]{:S(2)}) %collective-permute-start.8) | collective-permute-done | bytes 1048608 | tf_op jit(solution)/shard_map/ppermute | solution.py:30
  120.7 2.6 %query_features.1 = (bf16[16,128,256]{2,1,0:T(8,128)(2,1)}, f32[128,4096]{1,0:T(8,128)}) custom-call(bf16[128,4096]{1,0:T(8,128)(2,1)S(1)} %collective-permute-done.7.source, bf16[8,4096]{1,0:T(8,128)(2,1)S(1)} %collective-permute-done.9.before, bf16[128,4096]{1,0:T(8,128)(2,1)S(1)} %collective-permute-done.8.incoming, f32[8,4096]{1,0:T(8,128)S(1)} %pad.8.taps_ref), custom_call_target="tpu_custom_call" | custom-call | flops 7864320 | bytes 5242880 | tf_op jit(solution)/shard_map/query_features/pallas_call | solution.py:466
  123.3 9.9 %all-to-all-start.1 = ((bf16[16,128,256]{2,1,0:T(8,128)(2,1)}), bf16[16,128,256]{2,1,0:T(8,128)(2,1)S(1)}, u32[]{:S(2)}, u32[]{:S(2)}) async-start(bf16[16,128,256]{2,1,0:T(8,128)(2,1)} %get-tuple-element.60), calls=%async_computation.1 | async-start | bytes 2097152 | tf_op jit(solution)/shard_map/all_to_all | solution.py:881
  133.2 1.2 copy-done.2
  134.4 1.6 copy-done.3
  136.0 0.8 copy-done.6
  136.8 7.4 %query_outputs.1 = (bf16[128,4096]{1,0:T(8,128)(2,1)}, bf16[128,12288]{1,0:T(8,128)(2,1)}, bf16[16,8,256]{2,1,0:T(8,128)(2,1)}) custom-call(bf16[128,4096]{1,0:T(8,128)(2,1)S(1)} %collective-permute-done.7.source, bf16[128,4096]{1,0:T(8,128)(2,1)S(1)} %copy-done.2, bf16[8,4096]{1,0:T(8,128)(2,1)S(1)} %copy-done.6, f32[128,4096]{1,0:T(8,128)S(1)} %copy-done.3, ...), custom_call_target="tpu_custom_call" | custom-call | flops 18350080 | bytes 7340032 | tf_op jit(solution)/shard_map/query_outputs/pallas_call | solution.py:541
  144.2 4.8 %all-to-all-done.1.refs_8_.grad_hbm = bf16[16,128,256]{2,1,0:T(8,128)(2,1)S(1)} async-done(((bf16[16,128,256]{2,1,0:T(8,128)(2,1)}), bf16[16,128,256]{2,1,0:T(8,128)(2,1)S(1)}, u32[]{:S(2)}, u32[]{:S(2)}) %all-to-all-start.1) | async-done | bytes 1048608 | tf_op jit(solution)/shard_map/all_to_all | solution.py:881
  149.0 4.0 %all-to-all-start.2 = ((bf16[16,8,256]{2,1,0:T(8,128)(2,1)}), bf16[16,8,256]{2,1,0:T(8,128)(2,1)S(1)}, u32[]{:S(2)}, u32[]{:S(2)}) async-start(bf16[16,8,256]{2,1,0:T(8,128)(2,1)} %get-tuple-element.64), calls=%async_computation.2 | async-start | bytes 131072 | tf_op jit(solution)/shard_map/all_to_all | solution.py:884
  153.0 18.0 %through_values.1 = (bf16[16,280,256]{2,1,0:T(8,128)(2,1)}, f32[8,512,256]{2,1,0:T(8,128)}) custom-call(s32[1]{0:T(128)} %bitcast.2.me_ref, bf16[2,2,128,256]{3,2,1,0:T(8,128)(2,1)} %copy-done.7, bf16[2,2,128,256]{3,2,1,0:T(8,128)(2,1)} %copy-done.8, bf16[2,2,128,256]{3,2,1,0:T(8,128)(2,1)} %copy-done.9, bf16[2,2,128,256]{3,2,1,0:T(8,128)(2,1)} %copy-done.10, ...), custom_call_target="tpu_custom_call" | custom-call | flops 2199912448 | bytes 29360128 | tf_op jit(solution)/shard_map/through_values/pallas_call | solution.py:680
  171.1 0.6 broadcast_dynamic-update-slice_fusion
  171.8 5.8 %all-to-all-start.3 = ((bf16[16,280,256]{2,1,0:T(8,128)(2,1)}), bf16[16,280,256]{2,1,0:T(8,128)(2,1)S(1)}, u32[]{:S(2)}, u32[]{:S(2)}) async-start(bf16[16,280,256]{2,1,0:T(8,128)(2,1)} %broadcast_dynamic-update-slice_fusion), calls=%async_computation.3 | async-start | bytes 4587520 | tf_op jit(solution)/shard_map/all_to_all | solution.py:890
  177.6 9.0 %filter_gradient.1 = (f32[256,2048]{1,0:T(8,128)}, f32[1,256]{1,0:T(1,128)}) custom-call(bf16[16,128,256]{2,1,0:T(8,128)(2,1)S(1)} %all-to-all-done.1.refs_8_.grad_hbm, bf16[16,128,256]{2,1,0:T(8,128)(2,1)} %get-tuple-element.66.gated_hbm, f32[8,512,256]{2,1,0:T(8,128)} %get-tuple-element.67.d_hbm, f32[8,512,256]{2,1,0:T(8,128)} %get-tuple-element.68.g_hbm, ...), custom_call_target="tpu_custom_call" | custom-call | flops 1094713344 | bytes 16777216 | tf_op jit(solution)/shard_map/filter_gradient/pallas_call | solution.py:777
  186.6 21.4 %all-to-all-done.3.held_ref = bf16[16,280,256]{2,1,0:T(8,128)(2,1)S(1)} async-done(((bf16[16,280,256]{2,1,0:T(8,128)(2,1)}), bf16[16,280,256]{2,1,0:T(8,128)(2,1)S(1)}, u32[]{:S(2)}, u32[]{:S(2)}) %all-to-all-start.3) | async-done | bytes 2293792 | tf_op jit(solution)/shard_map/all_to_all | solution.py:890
  208.2 1.1 reshape.27
  209.3 1.6 place_columns.1
  (37 shorter events, 0.4 us)
Async XLA Ops:
  0.6 54.1 %copy-start = (f32[1,4096]{1,0:T(1,128)S(1)}, f32[1,4096]{1,0:T(1,128)}, u32[]{:S(2)}) copy-start(f32[1,4096]{1,0:T(1,128)} %param.11) | copy-start | bytes 49156
  2.1 3.8 %collective-permute-start = (bf16[8,2,128,256]{3,2,1,0:T(8,128)(2,1)S(1)}, bf16[8,2,128,256]{3,2,1,0:T(8,128)(2,1)S(1)}, u32[]{:S(2)}, u32[]{:S(2)}) collective-permute-start(bf16[8,2,128,256]{3,2,1,0:T(8,128)(2,1)S(1)} %leaving_pieces.1), channel_id=1, source_target_pairs={{0,1},{1,0},{2,3},{3,2},{4,5},{5,4},{6,7},{7,6},{8,9},{9,8},{10,11... | collective-permute-start | bytes 3145736 | tf_op jit(solution)/shard_map/ppermute | solution.py:40
  8.2 26.0 %collective-permute-start.1 = (bf16[2,2,128,256]{3,2,1,0:T(8,128)(2,1)S(1)}, bf16[2,2,128,256]{3,2,1,0:T(8,128)(2,1)S(1)}, u32[]{:S(2)}, u32[]{:S(2)}) collective-permute-start(bf16[2,2,128,256]{3,2,1,0:T(8,128)(2,1)S(1)} %get-tuple-element.38), channel_id=1, source_target_pairs={{0,16},{1,17},{2,18},{3,19},{4,20},{5,21},{6,22},{7,23},{8,24},{9,... | collective-permute-start | bytes 786440 | tf_op jit(solution)/shard_map/ppermute | solution.py:40
  12.0 27.1 %collective-permute-start.2 = (bf16[2,2,128,256]{3,2,1,0:T(8,128)(2,1)S(1)}, bf16[2,2,128,256]{3,2,1,0:T(8,128)(2,1)S(1)}, u32[]{:S(2)}, u32[]{:S(2)}) collective-permute-start(bf16[2,2,128,256]{3,2,1,0:T(8,128)(2,1)S(1)} %get-tuple-element.39), channel_id=1, source_target_pairs={{0,18},{1,19},{2,16},{3,17},{4,22},{5,23},{6,20},{7,21},{8,26},{9,... | collective-permute-start | bytes 786440 | tf_op jit(solution)/shard_map/ppermute | solution.py:40
  13.3 27.9 %collective-permute-start.3 = (bf16[2,2,128,256]{3,2,1,0:T(8,128)(2,1)S(1)}, bf16[2,2,128,256]{3,2,1,0:T(8,128)(2,1)S(1)}, u32[]{:S(2)}, u32[]{:S(2)}) collective-permute-start(bf16[2,2,128,256]{3,2,1,0:T(8,128)(2,1)S(1)} %get-tuple-element.40), channel_id=1, source_target_pairs={{0,20},{1,21},{2,22},{3,23},{4,16},{5,17},{6,18},{7,19},{8,28},{9,... | collective-permute-start | bytes 786440 | tf_op jit(solution)/shard_map/ppermute | solution.py:40
  24.1 30.7 %collective-permute-start.4 = (bf16[2,2,128,256]{3,2,1,0:T(8,128)(2,1)S(1)}, bf16[2,2,128,256]{3,2,1,0:T(8,128)(2,1)S(1)}, u32[]{:S(2)}, u32[]{:S(2)}) collective-permute-start(bf16[2,2,128,256]{3,2,1,0:T(8,128)(2,1)S(1)} %get-tuple-element.41), channel_id=1, source_target_pairs={{0,22},{1,23},{2,20},{3,21},{4,18},{5,19},{6,16},{7,17},{8,30},{9,... | collective-permute-start | bytes 786440 | tf_op jit(solution)/shard_map/ppermute | solution.py:40
  24.1 30.7 %collective-permute-start.5 = (bf16[2,2,128,256]{3,2,1,0:T(8,128)(2,1)S(1)}, bf16[2,2,128,256]{3,2,1,0:T(8,128)(2,1)}, u32[]{:S(2)}, u32[]{:S(2)}) collective-permute-start(bf16[2,2,128,256]{3,2,1,0:T(8,128)(2,1)S(1)} %get-tuple-element.42), channel_id=1, source_target_pairs={{0,24},{1,25},{2,26},{3,27},{4,28},{5,29},{6,30},{7,31},{8,16},{9,... | collective-permute-start | bytes 786440 | tf_op jit(solution)/shard_map/ppermute | solution.py:40
  34.2 20.6 %copy-start.7 = (bf16[2,2,128,256]{3,2,1,0:T(8,128)(2,1)}, bf16[2,2,128,256]{3,2,1,0:T(8,128)(2,1)S(1)}, u32[]{:S(2)}) copy-start(bf16[2,2,128,256]{3,2,1,0:T(8,128)(2,1)S(1)} %collective-permute-done.1.refs_0_) | copy-start | bytes 786436
  34.2 20.7 %collective-permute-start.6 = (bf16[2,2,128,256]{3,2,1,0:T(8,128)(2,1)S(1)}, bf16[2,2,128,256]{3,2,1,0:T(8,128)(2,1)S(1)}, u32[]{:S(2)}, u32[]{:S(2)}) collective-permute-start(bf16[2,2,128,256]{3,2,1,0:T(8,128)(2,1)S(1)} %get-tuple-element.43), channel_id=1, source_target_pairs={{0,26},{1,27},{2,24},{3,25},{4,30},{5,31},{6,28},{7,29},{8,18},{9,... | collective-permute-start | bytes 786440 | tf_op jit(solution)/shard_map/ppermute | solution.py:40
  39.1 15.7 %copy-start.8 = (bf16[2,2,128,256]{3,2,1,0:T(8,128)(2,1)}, bf16[2,2,128,256]{3,2,1,0:T(8,128)(2,1)S(1)}, u32[]{:S(2)}) copy-start(bf16[2,2,128,256]{3,2,1,0:T(8,128)(2,1)S(1)} %collective-permute-done.2.refs_1_) | copy-start | bytes 786436
  39.1 25.0 %collective-permute-start.11 = (bf16[2,2,128,256]{3,2,1,0:T(8,128)(2,1)S(1)}, bf16[2,2,128,256]{3,2,1,0:T(8,128)(2,1)}, u32[]{:S(2)}, u32[]{:S(2)}) collective-permute-start(bf16[2,2,128,256]{3,2,1,0:T(8,128)(2,1)S(1)} %get-tuple-element.55), channel_id=1, source_target_pairs={{0,28},{1,29},{2,30},{3,31},{4,24},{5,25},{6,26},{7,27},{8,20},{9,... | collective-permute-start | bytes 786440 | tf_op jit(solution)/shard_map/ppermute | solution.py:40
  41.1 13.6 %copy-start.9 = (bf16[2,2,128,256]{3,2,1,0:T(8,128)(2,1)}, bf16[2,2,128,256]{3,2,1,0:T(8,128)(2,1)S(1)}, u32[]{:S(2)}) copy-start(bf16[2,2,128,256]{3,2,1,0:T(8,128)(2,1)S(1)} %collective-permute-done.3.refs_2_) | copy-start | bytes 786436
  41.1 22.9 %collective-permute-start.12 = (bf16[2,2,128,256]{3,2,1,0:T(8,128)(2,1)S(1)}, bf16[2,2,128,256]{3,2,1,0:T(8,128)(2,1)}, u32[]{:S(2)}, u32[]{:S(2)}) collective-permute-start(bf16[2,2,128,256]{3,2,1,0:T(8,128)(2,1)S(1)} %get-tuple-element.56), channel_id=1, source_target_pairs={{0,30},{1,31},{2,28},{3,29},{4,26},{5,27},{6,24},{7,25},{8,22},{9,... | collective-permute-start | bytes 786440 | tf_op jit(solution)/shard_map/ppermute | solution.py:40
  54.8 0.7 copy-start.10
  55.5 0.7 copy-start.11
  56.2 60.8 %collective-permute-start.7 = (bf16[128,4096]{1,0:T(8,128)(2,1)}, bf16[128,4096]{1,0:T(8,128)(2,1)S(1)}, u32[]{:S(2)}, u32[]{:S(2)}) collective-permute-start(bf16[128,4096]{1,0:T(8,128)(2,1)} %slice_bitcast_fusion), channel_id=1, source_target_pairs={{0,16},{16,32},{32,48},{48,64},{64,80},{80,96},{96,112},{112,0},{1... | collective-permute-start | bytes 3145736 | tf_op jit(solution)/shard_map/ppermute | solution.py:30
  61.9 58.9 %collective-permute-start.8 = (bf16[128,4096]{1,0:T(8,128)(2,1)}, bf16[128,4096]{1,0:T(8,128)(2,1)S(1)}, u32[]{:S(2)}, u32[]{:S(2)}) collective-permute-start(bf16[128,4096]{1,0:T(8,128)(2,1)} %bitcast.1), channel_id=1, source_target_pairs={{0,112},{16,0},{32,16},{48,32},{64,48},{80,64},{96,80},{112,96},{1... | collective-permute-start | bytes 3145736 | tf_op jit(solution)/shard_map/ppermute | solution.py:30
  79.8 1.0 copy-start.4
  80.8 42.5 %all-to-all-start = ((bf16[16,136,256]{2,1,0:T(8,128)(2,1)}), bf16[16,136,256]{2,1,0:T(8,128)(2,1)S(1)}, u32[]{:S(2)}, u32[]{:S(2)}) async-start(bf16[16,136,256]{2,1,0:T(8,128)(2,1)} %copy-done.4), calls=%async_computation | async-start | bytes 2228224 | tf_op jit(solution)/shard_map/all_to_all | solution.py:875
  88.2 13.4 %collective-permute-start.9 = (bf16[8,4096]{1,0:T(8,128)(2,1)S(1)}, bf16[8,4096]{1,0:T(8,128)(2,1)S(1)}, u32[]{:S(2)}, u32[]{:S(2)}) collective-permute-start(bf16[8,4096]{1,0:T(8,128)(2,1)S(1)} %slice_bitcast_fusion.3), channel_id=1, source_target_pairs={{0,17},{1,18},{2,19},{3,20},{4,21},{5,22},{6,23},{7,24},{8,25},{9,... | collective-permute-start | bytes 196616 | tf_op jit(solution)/shard_map/ppermute | solution.py:847
  94.0 10.2 %collective-permute-start.10 = (bf16[8,4096]{1,0:T(8,128)(2,1)S(1)}, bf16[8,4096]{1,0:T(8,128)(2,1)S(1)}, u32[]{:S(2)}, u32[]{:S(2)}) collective-permute-start(bf16[8,4096]{1,0:T(8,128)(2,1)S(1)} %slice_bitcast_fusion.2), channel_id=1, source_target_pairs={{1,112},{2,113},{3,114},{4,115},{5,116},{6,117},{7,118},{8,119},{9... | collective-permute-start | bytes 196616 | tf_op jit(solution)/shard_map/ppermute | solution.py:847
  104.2 19.1 %copy-start.5 = (bf16[8,4096]{1,0:T(8,128)(2,1)}, bf16[8,4096]{1,0:T(8,128)(2,1)S(1)}, u32[]{:S(2)}) copy-start(bf16[8,4096]{1,0:T(8,128)(2,1)S(1)} %collective-permute-done.10.later) | copy-start | bytes 196612
  120.7 2.6 %copy-start.1 = (bf16[128,4096]{1,0:T(8,128)(2,1)}, bf16[128,4096]{1,0:T(8,128)(2,1)S(1)}, u32[]{:S(2)}) copy-start(bf16[128,4096]{1,0:T(8,128)(2,1)S(1)} %collective-permute-done.8.incoming) | copy-start | bytes 3145732
  123.3 25.7 %all-to-all-start.1 = ((bf16[16,128,256]{2,1,0:T(8,128)(2,1)}), bf16[16,128,256]{2,1,0:T(8,128)(2,1)S(1)}, u32[]{:S(2)}, u32[]{:S(2)}) async-start(bf16[16,128,256]{2,1,0:T(8,128)(2,1)} %get-tuple-element.60), calls=%async_computation.1 | async-start | bytes 2097152 | tf_op jit(solution)/shard_map/all_to_all | solution.py:881
  133.2 1.2 copy-start.2
  134.4 1.6 copy-start.3
  136.0 0.8 copy-start.6
  149.0 22.1 %all-to-all-start.2 = ((bf16[16,8,256]{2,1,0:T(8,128)(2,1)}), bf16[16,8,256]{2,1,0:T(8,128)(2,1)S(1)}, u32[]{:S(2)}, u32[]{:S(2)}) async-start(bf16[16,8,256]{2,1,0:T(8,128)(2,1)} %get-tuple-element.64), calls=%async_computation.2 | async-start | bytes 131072 | tf_op jit(solution)/shard_map/all_to_all | solution.py:884
  171.8 36.2 %all-to-all-start.3 = ((bf16[16,280,256]{2,1,0:T(8,128)(2,1)}), bf16[16,280,256]{2,1,0:T(8,128)(2,1)S(1)}, u32[]{:S(2)}, u32[]{:S(2)}) async-start(bf16[16,280,256]{2,1,0:T(8,128)(2,1)} %broadcast_dynamic-update-slice_fusion), calls=%async_computation.3 | async-start | bytes 4587520 | tf_op jit(solution)/shard_map/all_to_all | solution.py:890

commit v7 on v6

--- a/solution.py
+++ b/solution.py
@@ -13,7 +13,7 @@
 TAPS = 7
 HALO = 8
 EXTRA = 24
-LATE = 6
+LATE = 3
 ROOT = math.sqrt(0.5)
 F32 = jnp.float32
 BF16 = jnp.bfloat16
@@ -174,11 +174,11 @@
     wait_all(copies)
 
 
-def piece_kernel(me_ref, wide_ref, came_ref, *refs):
-    *pieces, sems = refs
+def piece_kernel(me_ref, wide_ref, came_ref, query_ref, *refs):
+    *pieces, sems, query_sem = refs
     _, roles, _, chans = pieces[0].shape
     width = wide_ref.shape[1] // 3
-    copies = []
+    copies = [pltpu.make_async_copy(wide_ref.at[:, pl.ds(0, width)], query_ref, query_sem.at[0])]
     for chip, piece in enumerate(pieces):
         start = (me_ref[0] ^ (2 * chip)) * chans
         for role in range(roles):
@@ -207,10 +207,11 @@
     chips, roles, rows, chans = came.shape
     return pl.pallas_call(
         piece_kernel,
-        out_shape=[jax.ShapeDtypeStruct((2, roles, rows, chans), BF16)] * chips,
+        out_shape=[jax.ShapeDtypeStruct((rows, wide.shape[1] // 3), BF16)]
+        + [jax.ShapeDtypeStruct((2, roles, rows, chans), BF16)] * chips,
         in_specs=[pl.BlockSpec(memory_space=pltpu.SMEM), pl.BlockSpec(memory_space=pl.ANY), pl.BlockSpec(memory_space=pltpu.VMEM)],
-        out_specs=[pl.BlockSpec(memory_space=pltpu.VMEM)] * chips,
-        scratch_shapes=[pltpu.SemaphoreType.DMA((chips, roles + 1))],
+        out_specs=[pl.BlockSpec(memory_space=pltpu.VMEM)] * (chips + 1),
+        scratch_shapes=[pltpu.SemaphoreType.DMA((chips, roles + 1)), pltpu.SemaphoreType.DMA((1,))],
         compiler_params=pltpu.CompilerParams(vmem_limit_bytes=8 * MIB),
         cost_estimate=pl.CostEstimate(flops=0, bytes_accessed=8 * chips * roles * rows * chans, transcendentals=0),
         name="pieces_for_owners",
@@ -858,15 +859,15 @@
     table, back = (jnp.asarray(one) for one in leaf_tables(rows * groups))
     spectrum = filter_spectrum(filt[0], table)
     gain = lax.dynamic_slice_in_dim(skip, place * chans, chans, axis=1)
+    came = handed_over(leaving_pieces(me, acts[0], groups, 2), 0, 1)
+    query, *pieces = pieces_for_owners(me, acts[0], came, groups)
+    pieces = [handed_over(piece, 1, 2 * chip) for chip, piece in enumerate(pieces)]
+    incoming = cots[0]
+    kern, pieces[0] = lax.optimization_barrier((kern, pieces[0]))
     taps = kern[0].reshape(TAPS, 3, groups, chans)
     taps = lax.dynamic_index_in_dim(taps, place, axis=2, keepdims=False).transpose(1, 0, 2)
     taps = jnp.pad(taps, ((0, 0), (0, HALO - TAPS), (0, 0)))
     query_taps = jnp.pad(kern[0, :, :width], ((0, HALO - TAPS), (0, 0)))
-
-    came = handed_over(leaving_pieces(me, acts[0], groups, 2), 0, 1)
-    pieces = pieces_for_owners(me, acts[0], came, groups)
-    pieces = [handed_over(piece, 1, 2 * chip) for chip, piece in enumerate(pieces)]
-    query, incoming = acts[0, :, :width], cots[0]
     query, incoming, pieces[:LATE] = lax.optimization_barrier((query, incoming, pieces[:LATE]))
     query = passed_along(query, "section", 1)
     incoming = passed_along(incoming, "section", -1)

time: 212 us -> 210 us (level)
  waiting for transfers between devices: 56.3 us -> 65.2 us
  starting transfers between devices: 69.9 us -> 63.2 us
  local copies, waits for them, and re-layouts: 14.7 us -> 9.56 us
    ppermute x2, waiting for transfers between devices: 4.96 us -> 9.4 us  [edge_of(): return lax.ppermute(block, ('section', 'ctx'), pairs)]
    ppermute x9, waiting for transfers between devices: 8.62 us -> 12.7 us  [handed_over(): return lax.ppermute(value, ('section', 'ctx'), pairs)]
    all_to_all x1, starting transfers between devices: 9.86 us -> 6.91 us  [on_device(): lax.all_to_all(mix_grad, 'ctx', split_axis=0, concat_axis=0, tiled=True)]
    ppermute x2, starting transfers between devices: 7.82 us -> 5.15 us  [passed_along(): return lax.ppermute(value, axis, pairs)]
    squeeze x1, local copies, waits for them, and re-layouts: 2.29 us -> 0.01 us  [on_device(): query_taps = jnp.pad(kern[0, :, :width], ((0, HALO - TAPS), (0, 0)))]
    unnamed x27 -> x28, local copies, waits for them, and re-layouts: 6.97 us -> 4.79 us
  transfers between devices with their start and end apart: 17 -> 17, of which waited for: 8 -> 7; matrix products, arithmetic and copies ran while one was open for 4% -> 2% of each run, Pallas kernels for 29% -> 30%
where the time goes in v7:
time: 210 us; the launch traced here: 208 us
  Pallas kernels  68.4 us (33%)
  waiting for transfers between devices  65.2 us (31%)
  starting transfers between devices  63.2 us (30%)
  local copies, waits for them, and re-layouts  9.56 us (5%)
    ppermute x9, starting transfers between devices, handed_over(): return lax.ppermute(value, ('section', 'ctx'), pairs)  26.7 us
    all_to_all x1, waiting for transfers between devices, on_device(): lax.all_to_all(ready, 'ctx', split_axis=0, concat_axis=0, tiled=True)  21.4 us
    pallas_call x1, Pallas kernels, through_work(): pl.pallas_call(functools.partial(through_kernel, groups), out_shape=(pltp...  18.1 us
    ppermute x2, waiting for transfers between devices, passed_along(): return lax.ppermute(value, axis, pairs)  17 us
    pallas_call x1, Pallas kernels, inner_work(): pl.pallas_call(functools.partial(mixed_kernel, groups), out_shape=(pltpu....  15.8 us
    ppermute x9, waiting for transfers between devices, handed_over(): return lax.ppermute(value, ('section', 'ctx'), pairs)  12.7 us
    ppermute x2, waiting for transfers between devices, edge_of(): return lax.ppermute(block, ('section', 'ctx'), pairs)  9.4 us
    pallas_call x1, Pallas kernels, filter_spectrum(): pl.pallas_call(filter_kernel, out_shape=pltpu.HBM((8, wide, chans), F32),...  9.18 us
  transfers between devices with their start and end apart: 17, of which 7 were waited for; matrix products, arithmetic and copies ran while one was open for 2% of the time, Pallas kernels for 30%

profile of v7, /device:TPU:1, one launch (start us, length us, event | category | flops | bytes accessed | tf_op | source)
XLA Modules:
  0.0 208.1 jit_solution(11612046212300143885)
XLA Ops:
  0.6 0.0 copy-start
  0.7 1.4 leaving_pieces.1
  2.1 1.5 collective-permute-start
  3.6 2.3 %collective-permute-done.came_ref = bf16[8,2,128,256]{3,2,1,0:T(8,128)(2,1)S(1)} collective-permute-done((bf16[8,2,128,256]{3,2,1,0:T(8,128)(2,1)S(1)}, bf16[8,2,128,256]{3,2,1,0:T(8,128)(2,1)S(1)}, u32[]{:S(2)}, u32[]{:S(2)}) %collective-permute-start) | collective-permute-done | bytes 1048608 | tf_op jit(solution)/shard_map/ppermute | solution.py:40
  5.8 3.4 %pieces_for_owners.1 = (bf16[128,4096]{1,0:T(8,128)(2,1)}, bf16[2,2,128,256]{3,2,1,0:T(8,128)(2,1)S(1)}, bf16[2,2,128,256]{3,2,1,0:T(8,128)(2,1)S(1)}, bf16[2,2,...) custom-call(s32[1]{0:T(128)} %bitcast.me_ref, ...), custom_call_target="tpu_custom_call" | custom-call | bytes 4194304 | tf_op jit(solution)/shard_map/pieces_for_owners/pallas_call | solution.py:208
  9.2 3.7 %collective-permute-start.1 = (bf16[2,2,128,256]{3,2,1,0:T(8,128)(2,1)S(1)}, bf16[2,2,128,256]{3,2,1,0:T(8,128)(2,1)S(1)}, u32[]{:S(2)}, u32[]{:S(2)}) collective-permute-start(bf16[2,2,128,256]{3,2,1,0:T(8,128)(2,1)S(1)} %get-tuple-element.39), channel_id=1, source_target_pairs={{0,16},{1,17},{2,18},{3,19},{4,20},{5,21},{6,22},{7,23},{8,24},{9,... | collective-permute-start | bytes 786440 | tf_op jit(solution)/shard_map/ppermute | solution.py:40
  13.0 1.3 collective-permute-start.2
  14.3 5.9 %collective-permute-start.3 = (bf16[2,2,128,256]{3,2,1,0:T(8,128)(2,1)S(1)}, bf16[2,2,128,256]{3,2,1,0:T(8,128)(2,1)S(1)}, u32[]{:S(2)}, u32[]{:S(2)}) collective-permute-start(bf16[2,2,128,256]{3,2,1,0:T(8,128)(2,1)S(1)} %get-tuple-element.42), channel_id=1, source_target_pairs={{0,20},{1,21},{2,22},{3,23},{4,16},{5,17},{6,18},{7,19},{8,28},{9,... | collective-permute-start | bytes 786440 | tf_op jit(solution)/shard_map/ppermute | solution.py:40
  20.2 0.8 slice_bitcast_fusion.2
  21.1 3.7 %collective-permute-start.9 = (bf16[2,2,128,256]{3,2,1,0:T(8,128)(2,1)S(1)}, bf16[2,2,128,256]{3,2,1,0:T(8,128)(2,1)S(1)}, u32[]{:S(2)}, u32[]{:S(2)}) collective-permute-start(bf16[2,2,128,256]{3,2,1,0:T(8,128)(2,1)S(1)} %get-tuple-element.53), channel_id=1, source_target_pairs={{0,24},{1,25},{2,26},{3,27},{4,28},{5,29},{6,30},{7,31},{8,16},{9,... | collective-permute-start | bytes 786440 | tf_op jit(solution)/shard_map/ppermute | solution.py:40
  24.8 10.4 %collective-permute-done.1.refs_0_ = bf16[2,2,128,256]{3,2,1,0:T(8,128)(2,1)S(1)} collective-permute-done((bf16[2,2,128,256]{3,2,1,0:T(8,128)(2,1)S(1)}, bf16[2,2,128,256]{3,2,1,0:T(8,128)(2,1)S(1)}, u32[]{:S(2)}, u32[]{:S(2)}) %collective-permute-start.1) | collective-permute-done | bytes 262176 | tf_op jit(solution)/shard_map/ppermute | solution.py:40
  35.2 4.9 %collective-permute-start.10 = (bf16[2,2,128,256]{3,2,1,0:T(8,128)(2,1)S(1)}, bf16[2,2,128,256]{3,2,1,0:T(8,128)(2,1)}, u32[]{:S(2)}, u32[]{:S(2)}) collective-permute-start(bf16[2,2,128,256]{3,2,1,0:T(8,128)(2,1)S(1)} %get-tuple-element.54), channel_id=1, source_target_pairs={{0,26},{1,27},{2,24},{3,25},{4,30},{5,31},{6,28},{7,29},{8,18},{9,... | collective-permute-start | bytes 786440 | tf_op jit(solution)/shard_map/ppermute | solution.py:40
  40.1 2.1 collective-permute-start.11
  42.1 0.0 collective-permute-done.3.refs_2_
  42.1 3.5 %collective-permute-start.12 = (bf16[2,2,128,256]{3,2,1,0:T(8,128)(2,1)S(1)}, bf16[2,2,128,256]{3,2,1,0:T(8,128)(2,1)}, u32[]{:S(2)}, u32[]{:S(2)}) collective-permute-start(bf16[2,2,128,256]{3,2,1,0:T(8,128)(2,1)S(1)} %get-tuple-element.56), channel_id=1, source_target_pairs={{0,30},{1,31},{2,28},{3,29},{4,26},{5,27},{6,24},{7,25},{8,22},{9,... | collective-permute-start | bytes 786440 | tf_op jit(solution)/shard_map/ppermute | solution.py:40
  45.7 9.2 %filter_spectrum.1.refs_8_.refs_10_ = f32[8,512,256]{2,1,0:T(8,128)} custom-call(bf16[256,2048]{1,0:T(8,128)(2,1)} %bitcast.31, bf16[8,512,512]{2,1,0:T(8,128)(2,1)} %constant.24.clone.table_ref.refs_9_.refs_11_), custom_call_target="tpu_custom_call" | custom-call | flops 1073741824 | bytes 10485760 | tf_op jit(solution)/shard_map/filter_spectrum/pallas_call | solution.py:138
  54.9 0.8 reduce.1
  55.7 0.1 copy.17
  55.9 0.0 collective-permute-done.8.refs_3_
  55.9 4.4 %collective-permute-start.7 = (bf16[8,4096]{1,0:T(8,128)(2,1)S(1)}, bf16[8,4096]{1,0:T(8,128)(2,1)S(1)}, u32[]{:S(2)}, u32[]{:S(2)}) collective-permute-start(bf16[8,4096]{1,0:T(8,128)(2,1)S(1)} %slice_bitcast_fusion.2), channel_id=1, source_target_pairs={{1,112},{2,113},{3,114},{4,115},{5,116},{6,117},{7,118},{8,119},{9... | collective-permute-start | bytes 196616 | tf_op jit(solution)/shard_map/ppermute | solution.py:848
  60.4 2.5 %collective-permute-start.4 = (bf16[128,4096]{1,0:T(8,128)(2,1)}, bf16[128,4096]{1,0:T(8,128)(2,1)S(1)}, u32[]{:S(2)}, u32[]{:S(2)}) collective-permute-start(bf16[128,4096]{1,0:T(8,128)(2,1)} %get-tuple-element.43), channel_id=1, source_target_pairs={{0,16},{16,32},{32,48},{48,64},{64,80},{80,96},{96,112},{112,0},{1... | collective-permute-start | bytes 3145736 | tf_op jit(solution)/shard_map/ppermute | solution.py:30
  62.9 2.6 %collective-permute-start.5 = (bf16[128,4096]{1,0:T(8,128)(2,1)}, bf16[128,4096]{1,0:T(8,128)(2,1)S(1)}, u32[]{:S(2)}, u32[]{:S(2)}) collective-permute-start(bf16[128,4096]{1,0:T(8,128)(2,1)} %bitcast.34), channel_id=1, source_target_pairs={{0,112},{16,0},{32,16},{48,32},{64,48},{80,64},{96,80},{112,96},{1... | collective-permute-start | bytes 3145736 | tf_op jit(solution)/shard_map/ppermute | solution.py:30
  65.5 15.8 %inner_values.1 = (f32[16,2,128,256]{3,2,1,0:T(8,128)}, bf16[16,128,256]{2,1,0:T(8,128)(2,1)}, bf16[16,136,256]{2,1,0:T(8,128)(2,1)S(1)}, f32[8,512,256]{2,1,0:T(8,128)}) custom-call(s32[1]{0:T(128)} %bitcast.me_ref, bf16[2,2,128,256]{3,2,1,0:T(8,128)(2,1)} %copy-done.8, bf16[2,2,128,256]{3,2,1,0:T(8,128)(2,1)} %copy-done.9, ...), custom_call_target="tpu_custom_call" | custom-call | flops 2178940928 | bytes 25165824 | tf_op jit(solution)/shard_map/inner_values/pallas_call | solution.py:387
  81.3 0.0 copy-start.4
  81.3 1.0 copy-done.4
  82.3 6.2 %all-to-all-start = ((bf16[16,136,256]{2,1,0:T(8,128)(2,1)}), bf16[16,136,256]{2,1,0:T(8,128)(2,1)S(1)}, u32[]{:S(2)}, u32[]{:S(2)}) async-start(bf16[16,136,256]{2,1,0:T(8,128)(2,1)} %copy-done.4), calls=%async_computation | async-start | bytes 2228224 | tf_op jit(solution)/shard_map/all_to_all | solution.py:876
  88.5 0.8 slice_bitcast_fusion.3
  89.4 4.0 %collective-permute-start.6 = (bf16[8,4096]{1,0:T(8,128)(2,1)S(1)}, bf16[8,4096]{1,0:T(8,128)(2,1)S(1)}, u32[]{:S(2)}, u32[]{:S(2)}) collective-permute-start(bf16[8,4096]{1,0:T(8,128)(2,1)S(1)} %slice_bitcast_fusion.3), channel_id=1, source_target_pairs={{0,17},{1,18},{2,19},{3,20},{4,21},{5,22},{6,23},{7,24},{8,25},{9,... | collective-permute-start | bytes 196616 | tf_op jit(solution)/shard_map/ppermute | solution.py:848
  93.4 9.4 %collective-permute-done.6.before = bf16[8,4096]{1,0:T(8,128)(2,1)S(1)} collective-permute-done((bf16[8,4096]{1,0:T(8,128)(2,1)S(1)}, bf16[8,4096]{1,0:T(8,128)(2,1)S(1)}, u32[]{:S(2)}, u32[]{:S(2)}) %collective-permute-start.6) | collective-permute-done | bytes 65568 | tf_op jit(solution)/shard_map/ppermute | solution.py:848
  102.8 1.2 copy.13
  104.0 13.5 %collective-permute-done.4.source = bf16[128,4096]{1,0:T(8,128)(2,1)S(1)} collective-permute-done((bf16[128,4096]{1,0:T(8,128)(2,1)}, bf16[128,4096]{1,0:T(8,128)(2,1)S(1)}, u32[]{:S(2)}, u32[]{:S(2)}) %collective-permute-start.4) | collective-permute-done | bytes 1048608 | tf_op jit(solution)/shard_map/ppermute | solution.py:30
  117.5 3.5 %collective-permute-done.5.incoming = bf16[128,4096]{1,0:T(8,128)(2,1)S(1)} collective-permute-done((bf16[128,4096]{1,0:T(8,128)(2,1)}, bf16[128,4096]{1,0:T(8,128)(2,1)S(1)}, u32[]{:S(2)}, u32[]{:S(2)}) %collective-permute-start.5) | collective-permute-done | bytes 1048608 | tf_op jit(solution)/shard_map/ppermute | solution.py:30
  120.9 2.6 %query_features.1 = (bf16[16,128,256]{2,1,0:T(8,128)(2,1)}, f32[128,4096]{1,0:T(8,128)}) custom-call(bf16[128,4096]{1,0:T(8,128)(2,1)S(1)} %collective-permute-done.4.source, bf16[8,4096]{1,0:T(8,128)(2,1)S(1)} %collective-permute-done.6.before, bf16[128,4096]{1,0:T(8,128)(2,1)S(1)} %collective-permute-done.5.incoming, f32[8,4096]{1,0:T(8,128)S(1)} %pad.8.taps_ref), custom_call_target="tpu_custom_call" | custom-call | flops 7864320 | bytes 5242880 | tf_op jit(solution)/shard_map/query_features/pallas_call | solution.py:467
  123.6 6.9 %all-to-all-start.1 = ((bf16[16,128,256]{2,1,0:T(8,128)(2,1)}), bf16[16,128,256]{2,1,0:T(8,128)(2,1)S(1)}, u32[]{:S(2)}, u32[]{:S(2)}) async-start(bf16[16,128,256]{2,1,0:T(8,128)(2,1)} %get-tuple-element.60), calls=%async_computation.1 | async-start | bytes 2097152 | tf_op jit(solution)/shard_map/all_to_all | solution.py:882
  130.5 1.2 copy-done.2
  131.7 1.6 copy-done.3
  133.3 0.8 copy-done.6
  134.1 7.4 %query_outputs.1 = (bf16[128,4096]{1,0:T(8,128)(2,1)}, bf16[128,12288]{1,0:T(8,128)(2,1)}, bf16[16,8,256]{2,1,0:T(8,128)(2,1)}) custom-call(bf16[128,4096]{1,0:T(8,128)(2,1)S(1)} %collective-permute-done.4.source, bf16[128,4096]{1,0:T(8,128)(2,1)S(1)} %copy-done.2, bf16[8,4096]{1,0:T(8,128)(2,1)S(1)} %copy-done.6, f32[128,4096]{1,0:T(8,128)S(1)} %copy-done.3, ...), custom_call_target="tpu_custom_call" | custom-call | flops 18350080 | bytes 7340032 | tf_op jit(solution)/shard_map/query_outputs/pallas_call | solution.py:542
  141.5 4.8 %all-to-all-done.1.refs_8_.grad_hbm = bf16[16,128,256]{2,1,0:T(8,128)(2,1)S(1)} async-done(((bf16[16,128,256]{2,1,0:T(8,128)(2,1)}), bf16[16,128,256]{2,1,0:T(8,128)(2,1)S(1)}, u32[]{:S(2)}, u32[]{:S(2)}) %all-to-all-start.1) | async-done | bytes 1048608 | tf_op jit(solution)/shard_map/all_to_all | solution.py:882
  146.3 4.0 %all-to-all-start.2 = ((bf16[16,8,256]{2,1,0:T(8,128)(2,1)}), bf16[16,8,256]{2,1,0:T(8,128)(2,1)S(1)}, u32[]{:S(2)}, u32[]{:S(2)}) async-start(bf16[16,8,256]{2,1,0:T(8,128)(2,1)} %get-tuple-element.64), calls=%async_computation.2 | async-start | bytes 131072 | tf_op jit(solution)/shard_map/all_to_all | solution.py:885
  150.3 18.1 %through_values.1 = (bf16[16,280,256]{2,1,0:T(8,128)(2,1)}, f32[8,512,256]{2,1,0:T(8,128)}) custom-call(s32[1]{0:T(128)} %bitcast.me_ref, bf16[2,2,128,256]{3,2,1,0:T(8,128)(2,1)} %copy-done.8, bf16[2,2,128,256]{3,2,1,0:T(8,128)(2,1)} %copy-done.9, bf16[2,2,128,256]{3,2,1,0:T(8,128)(2,1)} %copy-done.10, bf16[2,2,128,256]{3,2,1,0:T(8,128)(2,1)} %copy-done.11, ...), custom_call_target="tpu_custom_call" | custom-call | flops 2199912448 | bytes 29360128 | tf_op jit(solution)/shard_map/through_values/pallas_call | solution.py:681
  168.5 0.6 broadcast_dynamic-update-slice_fusion
  169.1 5.8 %all-to-all-start.3 = ((bf16[16,280,256]{2,1,0:T(8,128)(2,1)}), bf16[16,280,256]{2,1,0:T(8,128)(2,1)S(1)}, u32[]{:S(2)}, u32[]{:S(2)}) async-start(bf16[16,280,256]{2,1,0:T(8,128)(2,1)} %broadcast_dynamic-update-slice_fusion), calls=%async_computation.3 | async-start | bytes 4587520 | tf_op jit(solution)/shard_map/all_to_all | solution.py:891
  174.9 9.0 %filter_gradient.1 = (f32[256,2048]{1,0:T(8,128)}, f32[1,256]{1,0:T(1,128)}) custom-call(bf16[16,128,256]{2,1,0:T(8,128)(2,1)S(1)} %all-to-all-done.1.refs_8_.grad_hbm, bf16[16,128,256]{2,1,0:T(8,128)(2,1)} %get-tuple-element.66.gated_hbm, f32[8,512,256]{2,1,0:T(8,128)} %get-tuple-element.67.d_hbm, f32[8,512,256]{2,1,0:T(8,128)} %get-tuple-element.68.g_hbm, ...), custom_call_target="tpu_custom_call" | custom-call | flops 1094713344 | bytes 16777216 | tf_op jit(solution)/shard_map/filter_gradient/pallas_call | solution.py:778
  183.9 21.4 %all-to-all-done.3.held_ref = bf16[16,280,256]{2,1,0:T(8,128)(2,1)S(1)} async-done(((bf16[16,280,256]{2,1,0:T(8,128)(2,1)}), bf16[16,280,256]{2,1,0:T(8,128)(2,1)S(1)}, u32[]{:S(2)}, u32[]{:S(2)}) %all-to-all-start.3) | async-done | bytes 2293792 | tf_op jit(solution)/shard_map/all_to_all | solution.py:891
  205.4 0.1 copy.15
  205.5 1.1 reshape.27
  206.6 1.6 place_columns.1
  (38 shorter events, 0.2 us)
Async XLA Ops:
  0.6 54.2 %copy-start = (f32[1,4096]{1,0:T(1,128)S(1)}, f32[1,4096]{1,0:T(1,128)}, u32[]{:S(2)}) copy-start(f32[1,4096]{1,0:T(1,128)} %param.11) | copy-start | bytes 49156
  2.1 3.8 %collective-permute-start = (bf16[8,2,128,256]{3,2,1,0:T(8,128)(2,1)S(1)}, bf16[8,2,128,256]{3,2,1,0:T(8,128)(2,1)S(1)}, u32[]{:S(2)}, u32[]{:S(2)}) collective-permute-start(bf16[8,2,128,256]{3,2,1,0:T(8,128)(2,1)S(1)} %leaving_pieces.1), channel_id=1, source_target_pairs={{0,1},{1,0},{2,3},{3,2},{4,5},{5,4},{6,7},{7,6},{8,9},{9,8},{10,11... | collective-permute-start | bytes 3145736 | tf_op jit(solution)/shard_map/ppermute | solution.py:40
  9.2 26.0 %collective-permute-start.1 = (bf16[2,2,128,256]{3,2,1,0:T(8,128)(2,1)S(1)}, bf16[2,2,128,256]{3,2,1,0:T(8,128)(2,1)S(1)}, u32[]{:S(2)}, u32[]{:S(2)}) collective-permute-start(bf16[2,2,128,256]{3,2,1,0:T(8,128)(2,1)S(1)} %get-tuple-element.39), channel_id=1, source_target_pairs={{0,16},{1,17},{2,18},{3,19},{4,20},{5,21},{6,22},{7,23},{8,24},{9,... | collective-permute-start | bytes 786440 | tf_op jit(solution)/shard_map/ppermute | solution.py:40
  13.0 27.1 %collective-permute-start.2 = (bf16[2,2,128,256]{3,2,1,0:T(8,128)(2,1)S(1)}, bf16[2,2,128,256]{3,2,1,0:T(8,128)(2,1)S(1)}, u32[]{:S(2)}, u32[]{:S(2)}) collective-permute-start(bf16[2,2,128,256]{3,2,1,0:T(8,128)(2,1)S(1)} %get-tuple-element.41), channel_id=1, source_target_pairs={{0,18},{1,19},{2,16},{3,17},{4,22},{5,23},{6,20},{7,21},{8,26},{9,... | collective-permute-start | bytes 786440 | tf_op jit(solution)/shard_map/ppermute | solution.py:40
  14.3 27.9 %collective-permute-start.3 = (bf16[2,2,128,256]{3,2,1,0:T(8,128)(2,1)S(1)}, bf16[2,2,128,256]{3,2,1,0:T(8,128)(2,1)S(1)}, u32[]{:S(2)}, u32[]{:S(2)}) collective-permute-start(bf16[2,2,128,256]{3,2,1,0:T(8,128)(2,1)S(1)} %get-tuple-element.42), channel_id=1, source_target_pairs={{0,20},{1,21},{2,22},{3,23},{4,16},{5,17},{6,18},{7,19},{8,28},{9,... | collective-permute-start | bytes 786440 | tf_op jit(solution)/shard_map/ppermute | solution.py:40
  21.1 34.8 %collective-permute-start.8 = (bf16[2,2,128,256]{3,2,1,0:T(8,128)(2,1)S(1)}, bf16[2,2,128,256]{3,2,1,0:T(8,128)(2,1)S(1)}, u32[]{:S(2)}, u32[]{:S(2)}) collective-permute-start(bf16[2,2,128,256]{3,2,1,0:T(8,128)(2,1)S(1)} %get-tuple-element.52), channel_id=1, source_target_pairs={{0,22},{1,23},{2,20},{3,21},{4,18},{5,19},{6,16},{7,17},{8,30},{9,... | collective-permute-start | bytes 786440 | tf_op jit(solution)/shard_map/ppermute | solution.py:40
  21.1 39.3 %collective-permute-start.9 = (bf16[2,2,128,256]{3,2,1,0:T(8,128)(2,1)S(1)}, bf16[2,2,128,256]{3,2,1,0:T(8,128)(2,1)S(1)}, u32[]{:S(2)}, u32[]{:S(2)}) collective-permute-start(bf16[2,2,128,256]{3,2,1,0:T(8,128)(2,1)S(1)} %get-tuple-element.53), channel_id=1, source_target_pairs={{0,24},{1,25},{2,26},{3,27},{4,28},{5,29},{6,30},{7,31},{8,16},{9,... | collective-permute-start | bytes 786440 | tf_op jit(solution)/shard_map/ppermute | solution.py:40
  35.2 10.5 %copy-start.8 = (bf16[2,2,128,256]{3,2,1,0:T(8,128)(2,1)}, bf16[2,2,128,256]{3,2,1,0:T(8,128)(2,1)S(1)}, u32[]{:S(2)}) copy-start(bf16[2,2,128,256]{3,2,1,0:T(8,128)(2,1)S(1)} %collective-permute-done.1.refs_0_) | copy-start | bytes 786436
  35.2 27.7 %collective-permute-start.10 = (bf16[2,2,128,256]{3,2,1,0:T(8,128)(2,1)S(1)}, bf16[2,2,128,256]{3,2,1,0:T(8,128)(2,1)}, u32[]{:S(2)}, u32[]{:S(2)}) collective-permute-start(bf16[2,2,128,256]{3,2,1,0:T(8,128)(2,1)S(1)} %get-tuple-element.54), channel_id=1, source_target_pairs={{0,26},{1,27},{2,24},{3,25},{4,30},{5,31},{6,28},{7,29},{8,18},{9,... | collective-permute-start | bytes 786440 | tf_op jit(solution)/shard_map/ppermute | solution.py:40
  40.1 5.6 %copy-start.9 = (bf16[2,2,128,256]{3,2,1,0:T(8,128)(2,1)}, bf16[2,2,128,256]{3,2,1,0:T(8,128)(2,1)S(1)}, u32[]{:S(2)}) copy-start(bf16[2,2,128,256]{3,2,1,0:T(8,128)(2,1)S(1)} %collective-permute-done.2.refs_1_) | copy-start | bytes 786436
  40.1 25.5 %collective-permute-start.11 = (bf16[2,2,128,256]{3,2,1,0:T(8,128)(2,1)S(1)}, bf16[2,2,128,256]{3,2,1,0:T(8,128)(2,1)}, u32[]{:S(2)}, u32[]{:S(2)}) collective-permute-start(bf16[2,2,128,256]{3,2,1,0:T(8,128)(2,1)S(1)} %get-tuple-element.55), channel_id=1, source_target_pairs={{0,28},{1,29},{2,30},{3,31},{4,24},{5,25},{6,26},{7,27},{8,20},{9,... | collective-permute-start | bytes 786440 | tf_op jit(solution)/shard_map/ppermute | solution.py:40
  42.1 3.5 %copy-start.10 = (bf16[2,2,128,256]{3,2,1,0:T(8,128)(2,1)}, bf16[2,2,128,256]{3,2,1,0:T(8,128)(2,1)S(1)}, u32[]{:S(2)}) copy-start(bf16[2,2,128,256]{3,2,1,0:T(8,128)(2,1)S(1)} %collective-permute-done.3.refs_2_) | copy-start | bytes 786436
  42.1 23.4 %collective-permute-start.12 = (bf16[2,2,128,256]{3,2,1,0:T(8,128)(2,1)S(1)}, bf16[2,2,128,256]{3,2,1,0:T(8,128)(2,1)}, u32[]{:S(2)}, u32[]{:S(2)}) collective-permute-start(bf16[2,2,128,256]{3,2,1,0:T(8,128)(2,1)S(1)} %get-tuple-element.56), channel_id=1, source_target_pairs={{0,30},{1,31},{2,28},{3,29},{4,26},{5,27},{6,24},{7,25},{8,22},{9,... | collective-permute-start | bytes 786440 | tf_op jit(solution)/shard_map/ppermute | solution.py:40
  45.7 9.2 %copy-start.7 = (f32[1,7,12288]{2,0,1:T(1,128)S(1)}, f32[1,7,12288]{2,0,1:T(1,128)}, u32[]{:S(2)}) copy-start(f32[1,7,12288]{2,0,1:T(1,128)} %param.9) | copy-start | bytes 1032196
  55.9 4.4 %copy-start.11 = (bf16[2,2,128,256]{3,2,1,0:T(8,128)(2,1)}, bf16[2,2,128,256]{3,2,1,0:T(8,128)(2,1)S(1)}, u32[]{:S(2)}) copy-start(bf16[2,2,128,256]{3,2,1,0:T(8,128)(2,1)S(1)} %collective-permute-done.8.refs_3_) | copy-start | bytes 786436
  55.9 37.5 %collective-permute-start.7 = (bf16[8,4096]{1,0:T(8,128)(2,1)S(1)}, bf16[8,4096]{1,0:T(8,128)(2,1)S(1)}, u32[]{:S(2)}, u32[]{:S(2)}) collective-permute-start(bf16[8,4096]{1,0:T(8,128)(2,1)S(1)} %slice_bitcast_fusion.2), channel_id=1, source_target_pairs={{1,112},{2,113},{3,114},{4,115},{5,116},{6,117},{7,118},{8,119},{9... | collective-permute-start | bytes 196616 | tf_op jit(solution)/shard_map/ppermute | solution.py:848
  60.3 2.5 %copy-start.12 = (bf16[2,2,128,256]{3,2,1,0:T(8,128)(2,1)}, bf16[2,2,128,256]{3,2,1,0:T(8,128)(2,1)S(1)}, u32[]{:S(2)}) copy-start(bf16[2,2,128,256]{3,2,1,0:T(8,128)(2,1)S(1)} %collective-permute-done.9.refs_4_) | copy-start | bytes 786436
  60.4 57.1 %collective-permute-start.4 = (bf16[128,4096]{1,0:T(8,128)(2,1)}, bf16[128,4096]{1,0:T(8,128)(2,1)S(1)}, u32[]{:S(2)}, u32[]{:S(2)}) collective-permute-start(bf16[128,4096]{1,0:T(8,128)(2,1)} %get-tuple-element.43), channel_id=1, source_target_pairs={{0,16},{16,32},{32,48},{48,64},{64,80},{80,96},{96,112},{112,0},{1... | collective-permute-start | bytes 3145736 | tf_op jit(solution)/shard_map/ppermute | solution.py:30
  62.9 58.1 %collective-permute-start.5 = (bf16[128,4096]{1,0:T(8,128)(2,1)}, bf16[128,4096]{1,0:T(8,128)(2,1)S(1)}, u32[]{:S(2)}, u32[]{:S(2)}) collective-permute-start(bf16[128,4096]{1,0:T(8,128)(2,1)} %bitcast.34), channel_id=1, source_target_pairs={{0,112},{16,0},{32,16},{48,32},{64,48},{80,64},{96,80},{112,96},{1... | collective-permute-start | bytes 3145736 | tf_op jit(solution)/shard_map/ppermute | solution.py:30
  81.3 1.0 copy-start.4
  82.3 41.2 %all-to-all-start = ((bf16[16,136,256]{2,1,0:T(8,128)(2,1)}), bf16[16,136,256]{2,1,0:T(8,128)(2,1)S(1)}, u32[]{:S(2)}, u32[]{:S(2)}) async-start(bf16[16,136,256]{2,1,0:T(8,128)(2,1)} %copy-done.4), calls=%async_computation | async-start | bytes 2228224 | tf_op jit(solution)/shard_map/all_to_all | solution.py:876
  89.4 13.4 %collective-permute-start.6 = (bf16[8,4096]{1,0:T(8,128)(2,1)S(1)}, bf16[8,4096]{1,0:T(8,128)(2,1)S(1)}, u32[]{:S(2)}, u32[]{:S(2)}) collective-permute-start(bf16[8,4096]{1,0:T(8,128)(2,1)S(1)} %slice_bitcast_fusion.3), channel_id=1, source_target_pairs={{0,17},{1,18},{2,19},{3,20},{4,21},{5,22},{6,23},{7,24},{8,25},{9,... | collective-permute-start | bytes 196616 | tf_op jit(solution)/shard_map/ppermute | solution.py:848
  93.4 30.2 %copy-start.5 = (bf16[8,4096]{1,0:T(8,128)(2,1)}, bf16[8,4096]{1,0:T(8,128)(2,1)S(1)}, u32[]{:S(2)}) copy-start(bf16[8,4096]{1,0:T(8,128)(2,1)S(1)} %collective-permute-done.7.later) | copy-start | bytes 196612
  120.9 2.6 %copy-start.1 = (bf16[128,4096]{1,0:T(8,128)(2,1)}, bf16[128,4096]{1,0:T(8,128)(2,1)S(1)}, u32[]{:S(2)}) copy-start(bf16[128,4096]{1,0:T(8,128)(2,1)S(1)} %collective-permute-done.5.incoming) | copy-start | bytes 3145732
  123.6 22.8 %all-to-all-start.1 = ((bf16[16,128,256]{2,1,0:T(8,128)(2,1)}), bf16[16,128,256]{2,1,0:T(8,128)(2,1)S(1)}, u32[]{:S(2)}, u32[]{:S(2)}) async-start(bf16[16,128,256]{2,1,0:T(8,128)(2,1)} %get-tuple-element.60), calls=%async_computation.1 | async-start | bytes 2097152 | tf_op jit(solution)/shard_map/all_to_all | solution.py:882
  130.5 1.2 copy-start.2
  131.7 1.6 copy-start.3
  133.3 0.8 copy-start.6
  146.3 22.1 %all-to-all-start.2 = ((bf16[16,8,256]{2,1,0:T(8,128)(2,1)}), bf16[16,8,256]{2,1,0:T(8,128)(2,1)S(1)}, u32[]{:S(2)}, u32[]{:S(2)}) async-start(bf16[16,8,256]{2,1,0:T(8,128)(2,1)} %get-tuple-element.64), calls=%async_computation.2 | async-start | bytes 131072 | tf_op jit(solution)/shard_map/all_to_all | solution.py:885
  169.1 36.2 %all-to-all-start.3 = ((bf16[16,280,256]{2,1,0:T(8,128)(2,1)}), bf16[16,280,256]{2,1,0:T(8,128)(2,1)S(1)}, u32[]{:S(2)}, u32[]{:S(2)}) async-start(bf16[16,280,256]{2,1,0:T(8,128)(2,1)} %broadcast_dynamic-update-slice_fusion), calls=%async_computation.3 | async-start | bytes 4587520 | tf_op jit(solution)/shard_map/all_to_all | solution.py:891

commit v8 on v7

--- a/solution.py
+++ b/solution.py
@@ -568,10 +568,10 @@
     pieces = refs[: groups // 2]
     (
         grad_hbm, feats_hbm, spec_hbm, table_hbm, back_hbm, taps_ref, gain_ref,
-        ready_hbm, ring_hbm,
+        ready_hbm, ring_hbm, sums_ref,
         source, mix_grad, feats, spec, ring, table, back, rings, products, joined, through,
-        grads, sums, slots, last,
-        piece_sems, signal_sem, feats_sems, load_sems, ring_sems, slot_sems, last_sems,
+        grads, sums, slots,
+        piece_sems, signal_sem, feats_sems, load_sems, ring_sems, slot_sems,
     ) = refs[groups // 2 :]
     _, rows, chans = through.shape
     signal = pltpu.make_async_copy(grad_hbm, mix_grad, signal_sem.at[0])
@@ -657,14 +657,7 @@
                 back_taps(grads.at[role], source_block, part, taps, place, sums, role, lanes)
         write_back(slot, block).start()
 
-    rows_out = [jnp.zeros((HALO, chans), F32)] + sum_rows(sums, 2)
-    last[...] = jnp.concatenate(rows_out, axis=0).astype(BF16)
-    wait_all(
-        [
-            pltpu.make_async_copy(last, ready_hbm.at[owner, pl.ds(2 * rows, EXTRA)], last_sems.at[owner])
-            for owner in range(groups)
-        ]
-    )
+    sums_ref[...] = jnp.concatenate(sum_rows(sums, 2), axis=0)
     write_back(groups % 2, 1).wait()
     write_back((groups + 1) % 2, 0).wait()
 
@@ -683,11 +676,12 @@
         out_shape=(
             pltpu.HBM((groups, 2 * rows + EXTRA, chans), BF16),
             pltpu.HBM((8, wide, chans), F32),
+            jax.ShapeDtypeStruct((2 * HALO, chans), F32),
         ),
         in_specs=[pl.BlockSpec(memory_space=pltpu.SMEM)]
         + [pl.BlockSpec(memory_space=pl.ANY)] * (groups // 2 + 5)
         + [pl.BlockSpec(memory_space=pltpu.VMEM)] * 2,
-        out_specs=(pl.BlockSpec(memory_space=pl.ANY),) * 2,
+        out_specs=(pl.BlockSpec(memory_space=pl.ANY),) * 2 + (pl.BlockSpec(memory_space=pltpu.VMEM),),
         scratch_shapes=[
             pltpu.VMEM((groups, 2, rows, chans), BF16),
             pltpu.VMEM((groups, rows, chans), BF16),
@@ -703,14 +697,12 @@
             pltpu.VMEM((2, parts, rows + HALO, 128), F32),
             pltpu.VMEM((2, TAPS, 8, chans), F32),
             pltpu.VMEM((2, 2 * rows, chans), BF16),
-            pltpu.VMEM((EXTRA, chans), BF16),
             pltpu.SemaphoreType.DMA((groups,)),
             pltpu.SemaphoreType.DMA((1,)),
             pltpu.SemaphoreType.DMA((groups,)),
             pltpu.SemaphoreType.DMA((3, 8)),
             pltpu.SemaphoreType.DMA((8,)),
             pltpu.SemaphoreType.DMA((2,)),
-            pltpu.SemaphoreType.DMA((groups,)),
         ],
         compiler_params=pltpu.CompilerParams(vmem_limit_bytes=34 * MIB),
         cost_estimate=pl.CostEstimate(
@@ -885,9 +877,10 @@
     partial = lax.all_to_all(partial, "ctx", split_axis=0, concat_axis=0, tiled=True)
     query_sums = jnp.sum(partial.astype(F32), axis=0)
 
-    ready, d_ring = through_work(me, pieces, mix_grad, feats, spectrum, table, back, taps, gain)
-    query_rows = jnp.broadcast_to(query_sums.astype(BF16), (groups, HALO, chans))
-    ready = lax.dynamic_update_slice(ready, query_rows, (0, 2 * rows, 0))
+    ready, d_ring, value_sums = through_work(me, pieces, mix_grad, feats, spectrum, table, back, taps, gain)
+    tap_sums = jnp.concatenate([query_sums, value_sums], axis=0).astype(BF16)
+    tap_sums = jnp.broadcast_to(tap_sums, (groups, EXTRA, chans))
+    ready = lax.dynamic_update_slice(ready, tap_sums, (0, 2 * rows, 0))
     ready = lax.all_to_all(ready, "ctx", split_axis=0, concat_axis=0, tiled=True)
     filt_grad, skip_grad = filter_gradient(mix_grad, gated, d_ring, g_ring, back)
     (input_grad,) = place_columns(ready, rows, ((0, 1), (0, 2)), (input_grad,))

time: 210 us -> 210 us (level)
  no operation moved by 1% of the time
where the time goes in v8:
time: 210 us; the launch traced here: 208 us
  Pallas kernels  68.1 us (32%)
  waiting for transfers between devices  65.2 us (31%)
  starting transfers between devices  63.2 us (30%)
  local copies, waits for them, and re-layouts  9.64 us (5%)
    ppermute x9, starting transfers between devices, handed_over(): return lax.ppermute(value, ('section', 'ctx'), pairs)  26.7 us
    all_to_all x1, waiting for transfers between devices, on_device(): lax.all_to_all(ready, 'ctx', split_axis=0, concat_axis=0, tiled=True)  21.4 us
    pallas_call x1, Pallas kernels, through_work(): pl.pallas_call(functools.partial(through_kernel, groups), out_shape=(pltp...  17.9 us
    ppermute x2, waiting for transfers between devices, passed_along(): return lax.ppermute(value, axis, pairs)  17 us
    pallas_call x1, Pallas kernels, inner_work(): pl.pallas_call(functools.partial(mixed_kernel, groups), out_shape=(pltpu....  15.8 us
    ppermute x9, waiting for transfers between devices, handed_over(): return lax.ppermute(value, ('section', 'ctx'), pairs)  12.7 us
    ppermute x2, waiting for transfers between devices, edge_of(): return lax.ppermute(block, ('section', 'ctx'), pairs)  9.4 us
    pallas_call x1, Pallas kernels, filter_spectrum(): pl.pallas_call(filter_kernel, out_shape=pltpu.HBM((8, wide, chans), F32),...  9.18 us
  transfers between devices with their start and end apart: 17, of which 7 were waited for; matrix products, arithmetic and copies ran while one was open for 2% of the time, Pallas kernels for 30%

profile of v8, /device:TPU:1, one launch (start us, length us, event | category | flops | bytes accessed | tf_op | source)
XLA Modules:
  0.0 208.0 jit_solution(2036228951198888731)
XLA Ops:
  0.6 0.0 copy-start
  0.7 1.4 leaving_pieces.1
  2.1 1.5 collective-permute-start
  3.6 2.3 %collective-permute-done.came_ref = bf16[8,2,128,256]{3,2,1,0:T(8,128)(2,1)S(1)} collective-permute-done((bf16[8,2,128,256]{3,2,1,0:T(8,128)(2,1)S(1)}, bf16[8,2,128,256]{3,2,1,0:T(8,128)(2,1)S(1)}, u32[]{:S(2)}, u32[]{:S(2)}) %collective-permute-start) | collective-permute-done | bytes 1048608 | tf_op jit(solution)/shard_map/ppermute | solution.py:40
  5.8 3.4 %pieces_for_owners.1 = (bf16[128,4096]{1,0:T(8,128)(2,1)}, bf16[2,2,128,256]{3,2,1,0:T(8,128)(2,1)S(1)}, bf16[2,2,128,256]{3,2,1,0:T(8,128)(2,1)S(1)}, bf16[2,2,...) custom-call(s32[1]{0:T(128)} %bitcast.me_ref, ...), custom_call_target="tpu_custom_call" | custom-call | bytes 4194304 | tf_op jit(solution)/shard_map/pieces_for_owners/pallas_call | solution.py:208
  9.2 3.7 %collective-permute-start.1 = (bf16[2,2,128,256]{3,2,1,0:T(8,128)(2,1)S(1)}, bf16[2,2,128,256]{3,2,1,0:T(8,128)(2,1)S(1)}, u32[]{:S(2)}, u32[]{:S(2)}) collective-permute-start(bf16[2,2,128,256]{3,2,1,0:T(8,128)(2,1)S(1)} %get-tuple-element.40), channel_id=1, source_target_pairs={{0,16},{1,17},{2,18},{3,19},{4,20},{5,21},{6,22},{7,23},{8,24},{9,... | collective-permute-start | bytes 786440 | tf_op jit(solution)/shard_map/ppermute | solution.py:40
  13.0 1.3 collective-permute-start.2
  14.3 5.9 %collective-permute-start.3 = (bf16[2,2,128,256]{3,2,1,0:T(8,128)(2,1)S(1)}, bf16[2,2,128,256]{3,2,1,0:T(8,128)(2,1)S(1)}, u32[]{:S(2)}, u32[]{:S(2)}) collective-permute-start(bf16[2,2,128,256]{3,2,1,0:T(8,128)(2,1)S(1)} %get-tuple-element.43), channel_id=1, source_target_pairs={{0,20},{1,21},{2,22},{3,23},{4,16},{5,17},{6,18},{7,19},{8,28},{9,... | collective-permute-start | bytes 786440 | tf_op jit(solution)/shard_map/ppermute | solution.py:40
  20.2 0.8 slice_bitcast_fusion.2
  21.1 0.0 collective-permute-start.8
  21.1 3.7 %collective-permute-start.9 = (bf16[2,2,128,256]{3,2,1,0:T(8,128)(2,1)S(1)}, bf16[2,2,128,256]{3,2,1,0:T(8,128)(2,1)S(1)}, u32[]{:S(2)}, u32[]{:S(2)}) collective-permute-start(bf16[2,2,128,256]{3,2,1,0:T(8,128)(2,1)S(1)} %get-tuple-element.54), channel_id=1, source_target_pairs={{0,24},{1,25},{2,26},{3,27},{4,28},{5,29},{6,30},{7,31},{8,16},{9,... | collective-permute-start | bytes 786440 | tf_op jit(solution)/shard_map/ppermute | solution.py:40
  24.8 10.4 %collective-permute-done.1.refs_0_ = bf16[2,2,128,256]{3,2,1,0:T(8,128)(2,1)S(1)} collective-permute-done((bf16[2,2,128,256]{3,2,1,0:T(8,128)(2,1)S(1)}, bf16[2,2,128,256]{3,2,1,0:T(8,128)(2,1)S(1)}, u32[]{:S(2)}, u32[]{:S(2)}) %collective-permute-start.1) | collective-permute-done | bytes 262176 | tf_op jit(solution)/shard_map/ppermute | solution.py:40
  35.2 4.9 %collective-permute-start.10 = (bf16[2,2,128,256]{3,2,1,0:T(8,128)(2,1)S(1)}, bf16[2,2,128,256]{3,2,1,0:T(8,128)(2,1)}, u32[]{:S(2)}, u32[]{:S(2)}) collective-permute-start(bf16[2,2,128,256]{3,2,1,0:T(8,128)(2,1)S(1)} %get-tuple-element.55), channel_id=1, source_target_pairs={{0,26},{1,27},{2,24},{3,25},{4,30},{5,31},{6,28},{7,29},{8,18},{9,... | collective-permute-start | bytes 786440 | tf_op jit(solution)/shard_map/ppermute | solution.py:40
  40.1 0.0 collective-permute-done.2.refs_1_
  40.1 2.1 collective-permute-start.11
  42.1 3.5 %collective-permute-start.12 = (bf16[2,2,128,256]{3,2,1,0:T(8,128)(2,1)S(1)}, bf16[2,2,128,256]{3,2,1,0:T(8,128)(2,1)}, u32[]{:S(2)}, u32[]{:S(2)}) collective-permute-start(bf16[2,2,128,256]{3,2,1,0:T(8,128)(2,1)S(1)} %get-tuple-element.57), channel_id=1, source_target_pairs={{0,30},{1,31},{2,28},{3,29},{4,26},{5,27},{6,24},{7,25},{8,22},{9,... | collective-permute-start | bytes 786440 | tf_op jit(solution)/shard_map/ppermute | solution.py:40
  45.7 9.2 %filter_spectrum.1.refs_8_.refs_10_ = f32[8,512,256]{2,1,0:T(8,128)} custom-call(bf16[256,2048]{1,0:T(8,128)(2,1)} %bitcast.31, bf16[8,512,512]{2,1,0:T(8,128)(2,1)} %constant.22.clone.table_ref.refs_9_.refs_11_), custom_call_target="tpu_custom_call" | custom-call | flops 1073741824 | bytes 10485760 | tf_op jit(solution)/shard_map/filter_spectrum/pallas_call | solution.py:138
  54.9 0.8 reduce.1
  55.7 0.1 copy.17
  55.9 4.4 %collective-permute-start.7 = (bf16[8,4096]{1,0:T(8,128)(2,1)S(1)}, bf16[8,4096]{1,0:T(8,128)(2,1)S(1)}, u32[]{:S(2)}, u32[]{:S(2)}) collective-permute-start(bf16[8,4096]{1,0:T(8,128)(2,1)S(1)} %slice_bitcast_fusion.2), channel_id=1, source_target_pairs={{1,112},{2,113},{3,114},{4,115},{5,116},{6,117},{7,118},{8,119},{9... | collective-permute-start | bytes 196616 | tf_op jit(solution)/shard_map/ppermute | solution.py:840
  60.4 2.5 %collective-permute-start.4 = (bf16[128,4096]{1,0:T(8,128)(2,1)}, bf16[128,4096]{1,0:T(8,128)(2,1)S(1)}, u32[]{:S(2)}, u32[]{:S(2)}) collective-permute-start(bf16[128,4096]{1,0:T(8,128)(2,1)} %get-tuple-element.44), channel_id=1, source_target_pairs={{0,16},{16,32},{32,48},{48,64},{64,80},{80,96},{96,112},{112,0},{1... | collective-permute-start | bytes 3145736 | tf_op jit(solution)/shard_map/ppermute | solution.py:30
  62.9 2.6 %collective-permute-start.5 = (bf16[128,4096]{1,0:T(8,128)(2,1)}, bf16[128,4096]{1,0:T(8,128)(2,1)S(1)}, u32[]{:S(2)}, u32[]{:S(2)}) collective-permute-start(bf16[128,4096]{1,0:T(8,128)(2,1)} %bitcast.34), channel_id=1, source_target_pairs={{0,112},{16,0},{32,16},{48,32},{64,48},{80,64},{96,80},{112,96},{1... | collective-permute-start | bytes 3145736 | tf_op jit(solution)/shard_map/ppermute | solution.py:30
  65.5 15.8 %inner_values.1 = (f32[16,2,128,256]{3,2,1,0:T(8,128)}, bf16[16,128,256]{2,1,0:T(8,128)(2,1)}, bf16[16,136,256]{2,1,0:T(8,128)(2,1)S(1)}, f32[8,512,256]{2,1,0:T(8,128)}) custom-call(s32[1]{0:T(128)} %bitcast.me_ref, bf16[2,2,128,256]{3,2,1,0:T(8,128)(2,1)} %copy-done.8, bf16[2,2,128,256]{3,2,1,0:T(8,128)(2,1)} %copy-done.9, ...), custom_call_target="tpu_custom_call" | custom-call | flops 2178940928 | bytes 25165824 | tf_op jit(solution)/shard_map/inner_values/pallas_call | solution.py:387
  81.3 0.0 copy-start.4
  81.3 1.0 copy-done.4
  82.3 6.2 %all-to-all-start = ((bf16[16,136,256]{2,1,0:T(8,128)(2,1)}), bf16[16,136,256]{2,1,0:T(8,128)(2,1)S(1)}, u32[]{:S(2)}, u32[]{:S(2)}) async-start(bf16[16,136,256]{2,1,0:T(8,128)(2,1)} %copy-done.4), calls=%async_computation | async-start | bytes 2228224 | tf_op jit(solution)/shard_map/all_to_all | solution.py:868
  88.5 0.8 slice_bitcast_fusion.3
  89.4 4.0 %collective-permute-start.6 = (bf16[8,4096]{1,0:T(8,128)(2,1)S(1)}, bf16[8,4096]{1,0:T(8,128)(2,1)S(1)}, u32[]{:S(2)}, u32[]{:S(2)}) collective-permute-start(bf16[8,4096]{1,0:T(8,128)(2,1)S(1)} %slice_bitcast_fusion.3), channel_id=1, source_target_pairs={{0,17},{1,18},{2,19},{3,20},{4,21},{5,22},{6,23},{7,24},{8,25},{9,... | collective-permute-start | bytes 196616 | tf_op jit(solution)/shard_map/ppermute | solution.py:840
  93.4 9.4 %collective-permute-done.6.before = bf16[8,4096]{1,0:T(8,128)(2,1)S(1)} collective-permute-done((bf16[8,4096]{1,0:T(8,128)(2,1)S(1)}, bf16[8,4096]{1,0:T(8,128)(2,1)S(1)}, u32[]{:S(2)}, u32[]{:S(2)}) %collective-permute-start.6) | collective-permute-done | bytes 65568 | tf_op jit(solution)/shard_map/ppermute | solution.py:840
  102.8 1.2 copy.13
  104.0 13.5 %collective-permute-done.4.source = bf16[128,4096]{1,0:T(8,128)(2,1)S(1)} collective-permute-done((bf16[128,4096]{1,0:T(8,128)(2,1)}, bf16[128,4096]{1,0:T(8,128)(2,1)S(1)}, u32[]{:S(2)}, u32[]{:S(2)}) %collective-permute-start.4) | collective-permute-done | bytes 1048608 | tf_op jit(solution)/shard_map/ppermute | solution.py:30
  117.5 3.5 %collective-permute-done.5.incoming = bf16[128,4096]{1,0:T(8,128)(2,1)S(1)} collective-permute-done((bf16[128,4096]{1,0:T(8,128)(2,1)}, bf16[128,4096]{1,0:T(8,128)(2,1)S(1)}, u32[]{:S(2)}, u32[]{:S(2)}) %collective-permute-start.5) | collective-permute-done | bytes 1048608 | tf_op jit(solution)/shard_map/ppermute | solution.py:30
  120.9 2.6 %query_features.1 = (bf16[16,128,256]{2,1,0:T(8,128)(2,1)}, f32[128,4096]{1,0:T(8,128)}) custom-call(bf16[128,4096]{1,0:T(8,128)(2,1)S(1)} %collective-permute-done.4.source, bf16[8,4096]{1,0:T(8,128)(2,1)S(1)} %collective-permute-done.6.before, bf16[128,4096]{1,0:T(8,128)(2,1)S(1)} %collective-permute-done.5.incoming, f32[8,4096]{1,0:T(8,128)S(1)} %pad.8.taps_ref), custom_call_target="tpu_custom_call" | custom-call | flops 7864320 | bytes 5242880 | tf_op jit(solution)/shard_map/query_features/pallas_call | solution.py:467
  123.6 6.9 %all-to-all-start.1 = ((bf16[16,128,256]{2,1,0:T(8,128)(2,1)}), bf16[16,128,256]{2,1,0:T(8,128)(2,1)S(1)}, u32[]{:S(2)}, u32[]{:S(2)}) async-start(bf16[16,128,256]{2,1,0:T(8,128)(2,1)} %get-tuple-element.61), calls=%async_computation.1 | async-start | bytes 2097152 | tf_op jit(solution)/shard_map/all_to_all | solution.py:874
  130.5 1.2 copy-done.2
  131.7 1.6 copy-done.3
  133.3 0.8 copy-done.6
  134.1 7.4 %query_outputs.1 = (bf16[128,4096]{1,0:T(8,128)(2,1)}, bf16[128,12288]{1,0:T(8,128)(2,1)}, bf16[16,8,256]{2,1,0:T(8,128)(2,1)}) custom-call(bf16[128,4096]{1,0:T(8,128)(2,1)S(1)} %collective-permute-done.4.source, bf16[128,4096]{1,0:T(8,128)(2,1)S(1)} %copy-done.2, bf16[8,4096]{1,0:T(8,128)(2,1)S(1)} %copy-done.6, f32[128,4096]{1,0:T(8,128)S(1)} %copy-done.3, ...), custom_call_target="tpu_custom_call" | custom-call | flops 18350080 | bytes 7340032 | tf_op jit(solution)/shard_map/query_outputs/pallas_call | solution.py:542
  141.5 4.8 %all-to-all-done.1.refs_8_.grad_hbm = bf16[16,128,256]{2,1,0:T(8,128)(2,1)S(1)} async-done(((bf16[16,128,256]{2,1,0:T(8,128)(2,1)}), bf16[16,128,256]{2,1,0:T(8,128)(2,1)S(1)}, u32[]{:S(2)}, u32[]{:S(2)}) %all-to-all-start.1) | async-done | bytes 1048608 | tf_op jit(solution)/shard_map/all_to_all | solution.py:874
  146.3 4.0 %all-to-all-start.2 = ((bf16[16,8,256]{2,1,0:T(8,128)(2,1)}), bf16[16,8,256]{2,1,0:T(8,128)(2,1)S(1)}, u32[]{:S(2)}, u32[]{:S(2)}) async-start(bf16[16,8,256]{2,1,0:T(8,128)(2,1)} %get-tuple-element.65), calls=%async_computation.2 | async-start | bytes 131072 | tf_op jit(solution)/shard_map/all_to_all | solution.py:877
  150.3 17.9 %through_values.1 = (bf16[16,280,256]{2,1,0:T(8,128)(2,1)}, f32[8,512,256]{2,1,0:T(8,128)}, f32[16,256]{1,0:T(8,128)S(1)}) custom-call(s32[1]{0:T(128)} %bitcast.me_ref, bf16[2,2,128,256]{3,2,1,0:T(8,128)(2,1)} %copy-done.8, bf16[2,2,128,256]{3,2,1,0:T(8,128)(2,1)} %copy-done.9, bf16[2,2,128,256]{3,2,1,0:T(8,128)(2,1)} %copy-done.10, ...), custom_call_target="tpu_custom_call" | custom-call | flops 2199912448 | bytes 29360128 | tf_op jit(solution)/shard_map/through_values/pallas_call | solution.py:674
  168.3 0.7 broadcast_dynamic-update-slice_fusion
  169.0 5.8 %all-to-all-start.3 = ((bf16[16,280,256]{2,1,0:T(8,128)(2,1)}), bf16[16,280,256]{2,1,0:T(8,128)(2,1)S(1)}, u32[]{:S(2)}, u32[]{:S(2)}) async-start(bf16[16,280,256]{2,1,0:T(8,128)(2,1)} %broadcast_dynamic-update-slice_fusion), calls=%async_computation.3 | async-start | bytes 4587520 | tf_op jit(solution)/shard_map/all_to_all | solution.py:884
  174.8 9.0 %filter_gradient.1 = (f32[256,2048]{1,0:T(8,128)}, f32[1,256]{1,0:T(1,128)}) custom-call(bf16[16,128,256]{2,1,0:T(8,128)(2,1)S(1)} %all-to-all-done.1.refs_8_.grad_hbm, bf16[16,128,256]{2,1,0:T(8,128)(2,1)} %get-tuple-element.68.gated_hbm, f32[8,512,256]{2,1,0:T(8,128)} %get-tuple-element.69.d_hbm, f32[8,512,256]{2,1,0:T(8,128)} %get-tuple-element.70.g_hbm, ...), custom_call_target="tpu_custom_call" | custom-call | flops 1094713344 | bytes 16777216 | tf_op jit(solution)/shard_map/filter_gradient/pallas_call | solution.py:770
  183.8 21.4 %all-to-all-done.3.held_ref = bf16[16,280,256]{2,1,0:T(8,128)(2,1)S(1)} async-done(((bf16[16,280,256]{2,1,0:T(8,128)(2,1)}), bf16[16,280,256]{2,1,0:T(8,128)(2,1)S(1)}, u32[]{:S(2)}, u32[]{:S(2)}) %all-to-all-start.3) | async-done | bytes 2293792 | tf_op jit(solution)/shard_map/all_to_all | solution.py:884
  205.3 0.1 copy.15
  205.4 1.1 reshape.27
  206.5 1.6 place_columns.1
  (40 shorter events, 0.2 us)
Async XLA Ops:
  0.6 54.2 %copy-start = (f32[1,4096]{1,0:T(1,128)S(1)}, f32[1,4096]{1,0:T(1,128)}, u32[]{:S(2)}) copy-start(f32[1,4096]{1,0:T(1,128)} %param.11) | copy-start | bytes 49156
  2.1 3.8 %collective-permute-start = (bf16[8,2,128,256]{3,2,1,0:T(8,128)(2,1)S(1)}, bf16[8,2,128,256]{3,2,1,0:T(8,128)(2,1)S(1)}, u32[]{:S(2)}, u32[]{:S(2)}) collective-permute-start(bf16[8,2,128,256]{3,2,1,0:T(8,128)(2,1)S(1)} %leaving_pieces.1), channel_id=1, source_target_pairs={{0,1},{1,0},{2,3},{3,2},{4,5},{5,4},{6,7},{7,6},{8,9},{9,8},{10,11... | collective-permute-start | bytes 3145736 | tf_op jit(solution)/shard_map/ppermute | solution.py:40
  9.2 26.0 %collective-permute-start.1 = (bf16[2,2,128,256]{3,2,1,0:T(8,128)(2,1)S(1)}, bf16[2,2,128,256]{3,2,1,0:T(8,128)(2,1)S(1)}, u32[]{:S(2)}, u32[]{:S(2)}) collective-permute-start(bf16[2,2,128,256]{3,2,1,0:T(8,128)(2,1)S(1)} %get-tuple-element.40), channel_id=1, source_target_pairs={{0,16},{1,17},{2,18},{3,19},{4,20},{5,21},{6,22},{7,23},{8,24},{9,... | collective-permute-start | bytes 786440 | tf_op jit(solution)/shard_map/ppermute | solution.py:40
  13.0 27.1 %collective-permute-start.2 = (bf16[2,2,128,256]{3,2,1,0:T(8,128)(2,1)S(1)}, bf16[2,2,128,256]{3,2,1,0:T(8,128)(2,1)S(1)}, u32[]{:S(2)}, u32[]{:S(2)}) collective-permute-start(bf16[2,2,128,256]{3,2,1,0:T(8,128)(2,1)S(1)} %get-tuple-element.42), channel_id=1, source_target_pairs={{0,18},{1,19},{2,16},{3,17},{4,22},{5,23},{6,20},{7,21},{8,26},{9,... | collective-permute-start | bytes 786440 | tf_op jit(solution)/shard_map/ppermute | solution.py:40
  14.3 27.9 %collective-permute-start.3 = (bf16[2,2,128,256]{3,2,1,0:T(8,128)(2,1)S(1)}, bf16[2,2,128,256]{3,2,1,0:T(8,128)(2,1)S(1)}, u32[]{:S(2)}, u32[]{:S(2)}) collective-permute-start(bf16[2,2,128,256]{3,2,1,0:T(8,128)(2,1)S(1)} %get-tuple-element.43), channel_id=1, source_target_pairs={{0,20},{1,21},{2,22},{3,23},{4,16},{5,17},{6,18},{7,19},{8,28},{9,... | collective-permute-start | bytes 786440 | tf_op jit(solution)/shard_map/ppermute | solution.py:40
  21.1 34.8 %collective-permute-start.8 = (bf16[2,2,128,256]{3,2,1,0:T(8,128)(2,1)S(1)}, bf16[2,2,128,256]{3,2,1,0:T(8,128)(2,1)S(1)}, u32[]{:S(2)}, u32[]{:S(2)}) collective-permute-start(bf16[2,2,128,256]{3,2,1,0:T(8,128)(2,1)S(1)} %get-tuple-element.53), channel_id=1, source_target_pairs={{0,22},{1,23},{2,20},{3,21},{4,18},{5,19},{6,16},{7,17},{8,30},{9,... | collective-permute-start | bytes 786440 | tf_op jit(solution)/shard_map/ppermute | solution.py:40
  21.1 39.3 %collective-permute-start.9 = (bf16[2,2,128,256]{3,2,1,0:T(8,128)(2,1)S(1)}, bf16[2,2,128,256]{3,2,1,0:T(8,128)(2,1)S(1)}, u32[]{:S(2)}, u32[]{:S(2)}) collective-permute-start(bf16[2,2,128,256]{3,2,1,0:T(8,128)(2,1)S(1)} %get-tuple-element.54), channel_id=1, source_target_pairs={{0,24},{1,25},{2,26},{3,27},{4,28},{5,29},{6,30},{7,31},{8,16},{9,... | collective-permute-start | bytes 786440 | tf_op jit(solution)/shard_map/ppermute | solution.py:40
  35.2 10.5 %copy-start.8 = (bf16[2,2,128,256]{3,2,1,0:T(8,128)(2,1)}, bf16[2,2,128,256]{3,2,1,0:T(8,128)(2,1)S(1)}, u32[]{:S(2)}) copy-start(bf16[2,2,128,256]{3,2,1,0:T(8,128)(2,1)S(1)} %collective-permute-done.1.refs_0_) | copy-start | bytes 786436
  35.2 27.7 %collective-permute-start.10 = (bf16[2,2,128,256]{3,2,1,0:T(8,128)(2,1)S(1)}, bf16[2,2,128,256]{3,2,1,0:T(8,128)(2,1)}, u32[]{:S(2)}, u32[]{:S(2)}) collective-permute-start(bf16[2,2,128,256]{3,2,1,0:T(8,128)(2,1)S(1)} %get-tuple-element.55), channel_id=1, source_target_pairs={{0,26},{1,27},{2,24},{3,25},{4,30},{5,31},{6,28},{7,29},{8,18},{9,... | collective-permute-start | bytes 786440 | tf_op jit(solution)/shard_map/ppermute | solution.py:40
  40.1 5.6 %copy-start.9 = (bf16[2,2,128,256]{3,2,1,0:T(8,128)(2,1)}, bf16[2,2,128,256]{3,2,1,0:T(8,128)(2,1)S(1)}, u32[]{:S(2)}) copy-start(bf16[2,2,128,256]{3,2,1,0:T(8,128)(2,1)S(1)} %collective-permute-done.2.refs_1_) | copy-start | bytes 786436
  40.1 25.5 %collective-permute-start.11 = (bf16[2,2,128,256]{3,2,1,0:T(8,128)(2,1)S(1)}, bf16[2,2,128,256]{3,2,1,0:T(8,128)(2,1)}, u32[]{:S(2)}, u32[]{:S(2)}) collective-permute-start(bf16[2,2,128,256]{3,2,1,0:T(8,128)(2,1)S(1)} %get-tuple-element.56), channel_id=1, source_target_pairs={{0,28},{1,29},{2,30},{3,31},{4,24},{5,25},{6,26},{7,27},{8,20},{9,... | collective-permute-start | bytes 786440 | tf_op jit(solution)/shard_map/ppermute | solution.py:40
  42.1 3.5 %copy-start.10 = (bf16[2,2,128,256]{3,2,1,0:T(8,128)(2,1)}, bf16[2,2,128,256]{3,2,1,0:T(8,128)(2,1)S(1)}, u32[]{:S(2)}) copy-start(bf16[2,2,128,256]{3,2,1,0:T(8,128)(2,1)S(1)} %collective-permute-done.3.refs_2_) | copy-start | bytes 786436
  42.1 23.4 %collective-permute-start.12 = (bf16[2,2,128,256]{3,2,1,0:T(8,128)(2,1)S(1)}, bf16[2,2,128,256]{3,2,1,0:T(8,128)(2,1)}, u32[]{:S(2)}, u32[]{:S(2)}) collective-permute-start(bf16[2,2,128,256]{3,2,1,0:T(8,128)(2,1)S(1)} %get-tuple-element.57), channel_id=1, source_target_pairs={{0,30},{1,31},{2,28},{3,29},{4,26},{5,27},{6,24},{7,25},{8,22},{9,... | collective-permute-start | bytes 786440 | tf_op jit(solution)/shard_map/ppermute | solution.py:40
  45.7 9.2 %copy-start.7 = (f32[1,7,12288]{2,0,1:T(1,128)S(1)}, f32[1,7,12288]{2,0,1:T(1,128)}, u32[]{:S(2)}) copy-start(f32[1,7,12288]{2,0,1:T(1,128)} %param.9) | copy-start | bytes 1032196
  55.9 4.4 %copy-start.11 = (bf16[2,2,128,256]{3,2,1,0:T(8,128)(2,1)}, bf16[2,2,128,256]{3,2,1,0:T(8,128)(2,1)S(1)}, u32[]{:S(2)}) copy-start(bf16[2,2,128,256]{3,2,1,0:T(8,128)(2,1)S(1)} %collective-permute-done.8.refs_3_) | copy-start | bytes 786436
  55.9 37.5 %collective-permute-start.7 = (bf16[8,4096]{1,0:T(8,128)(2,1)S(1)}, bf16[8,4096]{1,0:T(8,128)(2,1)S(1)}, u32[]{:S(2)}, u32[]{:S(2)}) collective-permute-start(bf16[8,4096]{1,0:T(8,128)(2,1)S(1)} %slice_bitcast_fusion.2), channel_id=1, source_target_pairs={{1,112},{2,113},{3,114},{4,115},{5,116},{6,117},{7,118},{8,119},{9... | collective-permute-start | bytes 196616 | tf_op jit(solution)/shard_map/ppermute | solution.py:840
  60.3 2.5 %copy-start.12 = (bf16[2,2,128,256]{3,2,1,0:T(8,128)(2,1)}, bf16[2,2,128,256]{3,2,1,0:T(8,128)(2,1)S(1)}, u32[]{:S(2)}) copy-start(bf16[2,2,128,256]{3,2,1,0:T(8,128)(2,1)S(1)} %collective-permute-done.9.refs_4_) | copy-start | bytes 786436
  60.4 57.1 %collective-permute-start.4 = (bf16[128,4096]{1,0:T(8,128)(2,1)}, bf16[128,4096]{1,0:T(8,128)(2,1)S(1)}, u32[]{:S(2)}, u32[]{:S(2)}) collective-permute-start(bf16[128,4096]{1,0:T(8,128)(2,1)} %get-tuple-element.44), channel_id=1, source_target_pairs={{0,16},{16,32},{32,48},{48,64},{64,80},{80,96},{96,112},{112,0},{1... | collective-permute-start | bytes 3145736 | tf_op jit(solution)/shard_map/ppermute | solution.py:30
  62.9 58.1 %collective-permute-start.5 = (bf16[128,4096]{1,0:T(8,128)(2,1)}, bf16[128,4096]{1,0:T(8,128)(2,1)S(1)}, u32[]{:S(2)}, u32[]{:S(2)}) collective-permute-start(bf16[128,4096]{1,0:T(8,128)(2,1)} %bitcast.34), channel_id=1, source_target_pairs={{0,112},{16,0},{32,16},{48,32},{64,48},{80,64},{96,80},{112,96},{1... | collective-permute-start | bytes 3145736 | tf_op jit(solution)/shard_map/ppermute | solution.py:30
  81.3 1.0 copy-start.4
  82.3 41.2 %all-to-all-start = ((bf16[16,136,256]{2,1,0:T(8,128)(2,1)}), bf16[16,136,256]{2,1,0:T(8,128)(2,1)S(1)}, u32[]{:S(2)}, u32[]{:S(2)}) async-start(bf16[16,136,256]{2,1,0:T(8,128)(2,1)} %copy-done.4), calls=%async_computation | async-start | bytes 2228224 | tf_op jit(solution)/shard_map/all_to_all | solution.py:868
  89.4 13.4 %collective-permute-start.6 = (bf16[8,4096]{1,0:T(8,128)(2,1)S(1)}, bf16[8,4096]{1,0:T(8,128)(2,1)S(1)}, u32[]{:S(2)}, u32[]{:S(2)}) collective-permute-start(bf16[8,4096]{1,0:T(8,128)(2,1)S(1)} %slice_bitcast_fusion.3), channel_id=1, source_target_pairs={{0,17},{1,18},{2,19},{3,20},{4,21},{5,22},{6,23},{7,24},{8,25},{9,... | collective-permute-start | bytes 196616 | tf_op jit(solution)/shard_map/ppermute | solution.py:840
  93.4 30.2 %copy-start.5 = (bf16[8,4096]{1,0:T(8,128)(2,1)}, bf16[8,4096]{1,0:T(8,128)(2,1)S(1)}, u32[]{:S(2)}) copy-start(bf16[8,4096]{1,0:T(8,128)(2,1)S(1)} %collective-permute-done.7.later) | copy-start | bytes 196612
  120.9 2.6 %copy-start.1 = (bf16[128,4096]{1,0:T(8,128)(2,1)}, bf16[128,4096]{1,0:T(8,128)(2,1)S(1)}, u32[]{:S(2)}) copy-start(bf16[128,4096]{1,0:T(8,128)(2,1)S(1)} %collective-permute-done.5.incoming) | copy-start | bytes 3145732
  123.6 22.8 %all-to-all-start.1 = ((bf16[16,128,256]{2,1,0:T(8,128)(2,1)}), bf16[16,128,256]{2,1,0:T(8,128)(2,1)S(1)}, u32[]{:S(2)}, u32[]{:S(2)}) async-start(bf16[16,128,256]{2,1,0:T(8,128)(2,1)} %get-tuple-element.61), calls=%async_computation.1 | async-start | bytes 2097152 | tf_op jit(solution)/shard_map/all_to_all | solution.py:874
  130.5 1.2 copy-start.2
  131.7 1.6 copy-start.3
  133.3 0.8 copy-start.6
  146.3 21.9 %all-to-all-start.2 = ((bf16[16,8,256]{2,1,0:T(8,128)(2,1)}), bf16[16,8,256]{2,1,0:T(8,128)(2,1)S(1)}, u32[]{:S(2)}, u32[]{:S(2)}) async-start(bf16[16,8,256]{2,1,0:T(8,128)(2,1)} %get-tuple-element.65), calls=%async_computation.2 | async-start | bytes 131072 | tf_op jit(solution)/shard_map/all_to_all | solution.py:877
  169.0 36.2 %all-to-all-start.3 = ((bf16[16,280,256]{2,1,0:T(8,128)(2,1)}), bf16[16,280,256]{2,1,0:T(8,128)(2,1)S(1)}, u32[]{:S(2)}, u32[]{:S(2)}) async-start(bf16[16,280,256]{2,1,0:T(8,128)(2,1)} %broadcast_dynamic-update-slice_fusion), calls=%async_computation.3 | async-start | bytes 4587520 | tf_op jit(solution)/shard_map/all_to_all | solution.py:884
